TPU v7x, 32 devices: a whole 2x2x4 slice. The times are simulated.
32 devices in a mesh: ctx: 4 (over y, core), ch: 8 (over z, x).
Axes of the slice: x: 2, y: 2, z: 4, core: 2. Of those that a mesh axis runs over, the one named last changes fastest.
Arguments:
- q_branch: bfloat16 [1, 2048, 8192], P(None, 'ctx', 'ch'), may hold values from -6 to 6
- k_branch: bfloat16 [1, 2048, 8192], P(None, 'ctx', 'ch'), may hold values from -6 to 6
- out_gate: bfloat16 [1, 2048, 8192], P(None, 'ctx', 'ch'), may hold values from -6 to 6
- filters: bfloat16 [512, 2048], P('ch'), may hold values from -1.1 to 1.1
- grad_out: bfloat16 [1, 2048, 8192], P(None, 'ctx', 'ch'), may hold values from -6 to 6
Outputs:
- grad_q: bfloat16 [1, 2048, 8192], P(None, 'ctx', 'ch')
- grad_k: bfloat16 [1, 2048, 8192], P(None, 'ctx', 'ch')
- grad_filters: float32 [512, 2048], P('ch', 'ctx')
All inputs are finite; a program needn't handle non-finite values.
Results may differ from a plain program's by a relative error of at most 0.005.
Values may be sent and summed in bfloat16 or wider, within the bound.
No kernel may reach another device: no remote copies, remote signals or barrier semaphores. Data moves between devices by JAX's collectives and lax.ppermute only.
A program may use at most 128 MiB of HBM per device.

v0:
```python
import math

import jax
import jax.numpy as jnp
from jax import lax
from jax.sharding import PartitionSpec as P

WIDTH = 8192
GROUP = 16


def pair_terms(taps_pad, offset, grad_rows, prod_rev, block_len):
    window = lax.dynamic_slice_in_dim(taps_pad, offset * block_len, 2 * block_len + 1, 1)

    def one_group(pieces):
        taps_one, grad_one, prod_one = pieces
        repeated = jnp.broadcast_to(taps_one[None, :], (block_len, 2 * block_len + 1))
        repeated = repeated.reshape(block_len * (2 * block_len + 1))
        toeplitz = repeated[: 2 * block_len * block_len].reshape(block_len, 2 * block_len)
        toeplitz = toeplitz[:, block_len:]
        grad_part = jnp.einsum(
            "st,bct->bcs", toeplitz, grad_one, preferred_element_type=jnp.float32
        )
        products = jnp.einsum("bct,bcr->tr", grad_one, prod_one, preferred_element_type=jnp.float32)
        padded = jnp.pad(products, ((0, 0), (1, block_len)))
        skewed = padded.reshape(block_len * (2 * block_len + 1))[: 2 * block_len * block_len]
        skewed = skewed.reshape(block_len, 2 * block_len)
        return (grad_part, jnp.sum(skewed, axis=0))

    return lax.map(one_group, (window, grad_rows, prod_rev))


def add_lags(lag_acc, lag_part, offset, block_len):
    slot_ids = jnp.arange(lag_acc.shape[0], dtype=jnp.int32)
    at_block = (slot_ids == offset).astype(jnp.float32)[:, None, None]
    at_before = (slot_ids == offset - 1).astype(jnp.float32)[:, None, None]
    upper_half = lag_part[:, block_len:]
    lower_half = lag_part[:, :block_len]
    return lag_acc + at_block * upper_half[None] + at_before * lower_half[None]


def on_device(q_branch, k_branch, out_gate, filters, grad_out):
    seq_count, block_len, chan_dev = q_branch.shape
    cycle_size = lax.axis_size("ctx")
    position = lax.axis_index("ctx")
    gated_grad = (grad_out.astype(jnp.float32) * out_gate.astype(jnp.float32)).astype(jnp.bfloat16)
    scale = 4.0 / math.sqrt(seq_count * GROUP)
    gathered = (
        lax.all_to_all(gated_grad, "ctx", split_axis=2, concat_axis=1, tiled=True),
        lax.all_to_all(q_branch, "ctx", split_axis=2, concat_axis=1, tiled=True),
        lax.all_to_all(k_branch, "ctx", split_axis=2, concat_axis=1, tiled=True),
    )
    grad_whole, q_whole, k_whole = gathered
    group_here = grad_whole.shape[2] // GROUP
    prod_whole = (q_whole.astype(jnp.float32) * k_whole.astype(jnp.float32)).astype(jnp.bfloat16)
    grad_blocks = jnp.transpose(
        grad_whole.reshape(seq_count, cycle_size, block_len, group_here, GROUP), (3, 0, 1, 4, 2)
    )
    prod_blocks = jnp.transpose(
        prod_whole.reshape(seq_count, cycle_size, block_len, group_here, GROUP), (3, 0, 1, 4, 2)
    )
    prod_rev = prod_blocks[..., ::-1].reshape(group_here, seq_count * cycle_size, GROUP, block_len)
    grad_padded = jnp.concatenate([grad_blocks, jnp.zeros_like(grad_blocks)], axis=2)
    taps_here = lax.dynamic_slice_in_dim(filters, position * group_here, group_here, 0)
    taps_pad = jnp.pad(taps_here, ((0, 0), (block_len, block_len)))

    def advance(offset, state_now):
        grad_acc, lag_acc = state_now
        chosen = lax.dynamic_slice_in_dim(grad_padded, offset, cycle_size, 2)
        chosen = chosen.reshape(group_here, seq_count * cycle_size, GROUP, block_len)
        grad_part, lag_part = pair_terms(taps_pad, offset, chosen, prod_rev, block_len)
        return (grad_acc + grad_part, add_lags(lag_acc, lag_part, offset, block_len))

    start_state = (
        jnp.zeros((group_here, seq_count * cycle_size, GROUP, block_len), jnp.float32),
        jnp.zeros((cycle_size, group_here, block_len), jnp.float32),
    )
    grad_acc, lag_acc = lax.fori_loop(0, cycle_size, advance, start_state)
    grad_prod = jnp.transpose(
        grad_acc.reshape(group_here, seq_count, cycle_size, GROUP, block_len), (1, 2, 4, 0, 3)
    ).reshape(seq_count, cycle_size * block_len, group_here * GROUP)
    grad_q_whole = (grad_prod * k_whole.astype(jnp.float32)).astype(jnp.bfloat16)
    grad_k_whole = (grad_prod * q_whole.astype(jnp.float32)).astype(jnp.bfloat16)
    grad_q, grad_k = (
        lax.all_to_all(grad_q_whole, "ctx", split_axis=1, concat_axis=2, tiled=True),
        lax.all_to_all(grad_k_whole, "ctx", split_axis=1, concat_axis=2, tiled=True),
    )
    raw_here = jnp.transpose(lag_acc, (1, 0, 2)).reshape(group_here, cycle_size * block_len) * scale
    raw = lax.all_to_all(raw_here, "ctx", split_axis=1, concat_axis=0, tiled=True)
    squares = lax.psum(jnp.sum(raw * raw), ("ctx", "ch"))
    threshold = math.sqrt(WIDTH // GROUP * block_len * cycle_size)
    factor = jnp.minimum(1.0, threshold / jnp.sqrt(squares + 1e-06))
    return (grad_q, grad_k, raw * factor)


def solution(mesh):
    return jax.shard_map(
        on_device,
        mesh=mesh,
        in_specs=(
            P(None, "ctx", "ch"),
            P(None, "ctx", "ch"),
            P(None, "ctx", "ch"),
            P("ch", None),
            P(None, "ctx", "ch"),
        ),
        out_specs=(P(None, "ctx", "ch"), P(None, "ctx", "ch"), P("ch", "ctx")),
        check_vma=False,
    )
```

profile of v0, /device:TPU:0, one launch (start us, length us, event | category | flops | bytes accessed | tf_op | source)
XLA Modules:
  0.0 1042.7 jit_solution(12327060089122882641)
XLA Ops:
  0.6 4.7 copy.97
  5.8 6.9 reduce.5
  14.8 4.8 all-to-all-start.1
  19.6 4.6 copy.99
  24.2 7.9 reduce.6
  32.1 3.9 reshape.191
  36.0 4.4 all-to-all-start.2
  42.7 8.0 reduce.4
  50.7 3.7 reshape.187
  55.5 3.7 all-to-all-start
  59.2 4.0 reshape.192
  66.3 3.7 rev.3
  77.0 840.0 %while.63 = (s32[]{:T(128)}, f32[16,4,16,512]{3,2,1,0:T(8,128)}, f32[4,16,512]{2,1,0:T(8,128)}, bf16[16,3072]{1,0:T(8,128)(2,1)S(1)}, bf16[16,1,8,16,512]{4,3,0,...) while((s32[]{:T(128)}, f32[16,4,16,512]{3,2,1,0:T(8,128)}, ...), condition=%wide.region_4.5_spmd.clone.clone, body=%wide.region_0.4_spmd.clone.sunk.clone | while | flops 68844568 | bytes 54883932 | solution.py:78
  78.7 202.6 %while.62 = (s32[]{:T(128)}, f32[16,4,16,512]{3,2,1,0:T(8,128)}, f32[16,1024]{1,0:T(8,128)S(1)}, bf16[16,4,16,512]{3,2,1,0:T(8,128)(2,1)}, bf16[16,1025]{1,0:T(8...) while((s32[]{:T(128)}, f32[16,4,16,512]{3,2,1,0:T(8,128)}, ...), condition=%wide.region_3.3_spmd, body=%wide.region_1.2_spmd.sunk | while | flops 67632128 | bytes 29193356 | solution.py:30
  282.1 3.8 select_add_fusion.4
  287.6 202.6 %while.62 = (s32[]{:T(128)}, f32[16,4,16,512]{3,2,1,0:T(8,128)}, f32[16,1024]{1,0:T(8,128)S(1)}, bf16[16,4,16,512]{3,2,1,0:T(8,128)(2,1)}, bf16[16,1025]{1,0:T(8...) while((s32[]{:T(128)}, f32[16,4,16,512]{3,2,1,0:T(8,128)}, ...), condition=%wide.region_3.3_spmd, body=%wide.region_1.2_spmd.sunk | while | flops 67632128 | bytes 29193356 | solution.py:30
  491.8 4.4 select_add_fusion.4
  498.0 202.6 %while.62 = (s32[]{:T(128)}, f32[16,4,16,512]{3,2,1,0:T(8,128)}, f32[16,1024]{1,0:T(8,128)S(1)}, bf16[16,4,16,512]{3,2,1,0:T(8,128)(2,1)}, bf16[16,1025]{1,0:T(8...) while((s32[]{:T(128)}, f32[16,4,16,512]{3,2,1,0:T(8,128)}, ...), condition=%wide.region_3.3_spmd, body=%wide.region_1.2_spmd.sunk | while | flops 67632128 | bytes 29193356 | solution.py:30
  702.2 4.4 select_add_fusion.4
  708.3 202.6 %while.62 = (s32[]{:T(128)}, f32[16,4,16,512]{3,2,1,0:T(8,128)}, f32[16,1024]{1,0:T(8,128)S(1)}, bf16[16,4,16,512]{3,2,1,0:T(8,128)(2,1)}, bf16[16,1025]{1,0:T(8...) while((s32[]{:T(128)}, f32[16,4,16,512]{3,2,1,0:T(8,128)}, ...), condition=%wide.region_3.3_spmd, body=%wide.region_1.2_spmd.sunk | while | flops 67632128 | bytes 29193356 | solution.py:30
  912.6 4.4 select_add_fusion.4
  917.0 3.7 all-to-all-start.5
  920.8 4.3 copy.103
  925.1 3.8 reshape.178
  938.7 3.9 multiply_convert_fusion
  944.3 10.5 %reduce.8 = bf16[2048,256]{1,0:T(8,128)(2,1)S(1)} reduce(bf16[2048,1,256]{2,1,0:T(2,128)(2,1)S(1)} %bitcast.104, bf16[]{:T(256)} %broadcast.69), dimensions={1}, to_apply=%bitcast.69.reduce_sub_computation | reduce | bytes 2097154
  956.5 3.5 all-to-all-start.4
  960.0 4.6 copy.106
  964.6 11.5 %reduce.7 = bf16[2048,256]{1,0:T(8,128)(2,1)} reduce(bf16[2048,1,256]{2,1,0:T(2,128)(2,1)S(1)} %bitcast.100, bf16[]{:T(256)} %broadcast.69), dimensions={1}, to_apply=%bitcast.67.reduce_sub_computation | reduce | bytes 2097154
  976.1 3.5 reshape.193
  979.6 4.2 all-to-all-start.3
  984.4 48.9 %psum.7 = f32[]{:T(128)} all-reduce(f32[]{:T(128)} %multiply_reduce_fusion), channel_id=1, replica_groups=mesh['ctx'=4,'ch'=8] {'ctx','ch'}, use_global_device_ids=true, to_apply=%region_6.7 | all-reduce | flops 1 | bytes 8 | tf_op jit(solution)/shard_map/psum | solution.py:90
  (998 shorter events, 857.6 us)
Async XLA Ops:
  0.6 53.8 %copy-start = (bf16[64,2048]{1,0:T(8,128)(2,1)S(1)}, bf16[64,2048]{1,0:T(8,128)(2,1)}, u32[]{:S(2)}) copy-start(bf16[64,2048]{1,0:T(8,128)(2,1)} %param.12) | copy-start | bytes 786436
  14.8 21.2 %all-to-all-start.1 = ((bf16[4,2,65536]{2,1,0:T(2,128)(2,1)}), bf16[4,2,65536]{2,1,0:T(2,128)(2,1)S(1)}, u32[]{:S(2)}, u32[]{:S(2)}) async-start(bf16[4,2,65536]{2,1,0:T(2,128)(2,1)} %reshape.189), calls=%async_computation.1 | async-start | bytes 2097152 | tf_op jit(solution)/shard_map/all_to_all | solution.py:50
  32.1 8.3 copy-start.10
  32.1 8.4 copy-start.11
  36.0 4.5 copy-start.8
  36.0 19.5 %all-to-all-start.2 = ((bf16[4,2,65536]{2,1,0:T(2,128)(2,1)}), bf16[4,2,65536]{2,1,0:T(2,128)(2,1)}, u32[]{:S(2)}, u32[]{:S(2)}) async-start(bf16[4,2,65536]{2,1,0:T(2,128)(2,1)} %reshape.191), calls=%async_computation.2 | async-start | bytes 2097152 | tf_op jit(solution)/shard_map/all_to_all | solution.py:51
  42.7 11.8 %copy-start.9 = (bf16[4,2,65536]{2,1,0:T(2,128)(2,1)S(1)}, bf16[4,2,65536]{2,1,0:T(2,128)(2,1)}, u32[]{:S(2)}) copy-start(bf16[4,2,65536]{2,1,0:T(2,128)(2,1)} %copy-done.8) | copy-start | bytes 3145732
  55.5 20.0 %all-to-all-start = ((bf16[4,2,65536]{2,1,0:T(2,128)(2,1)}), bf16[4,2,65536]{2,1,0:T(2,128)(2,1)S(1)}, u32[]{:S(2)}, u32[]{:S(2)}) async-start(bf16[4,2,65536]{2,1,0:T(2,128)(2,1)} %reshape.187), calls=%async_computation | async-start | bytes 2097152 | tf_op jit(solution)/shard_map/all_to_all | solution.py:49
  70.0 2.4 copy-start.4
  77.0 1.7 copy-start.2
  82.6 1.6 slice-start
  95.3 1.6 slice-start
  108.0 1.6 slice-start
  120.6 1.6 slice-start
  158.6 1.6 slice-start
  171.3 1.6 slice-start
  183.9 1.6 slice-start
  209.2 1.6 slice-start
  282.1 3.8 copy-start.3
  285.9 1.7 copy-start.2
  491.8 4.4 copy-start.3
  496.3 1.7 copy-start.2
  702.2 4.4 copy-start.3
  706.7 1.7 copy-start.2
  912.6 4.4 copy-start.3
  917.0 39.5 %all-to-all-start.5 = ((f32[16,4,512]{2,0,1:T(8,128)}), f32[16,4,512]{2,0,1:T(8,128)S(1)}, u32[]{:S(2)}, u32[]{:S(2)}) async-start(f32[16,4,512]{2,0,1:T(8,128)} %bitcast.26), calls=%async_computation.5 | async-start | bytes 262144 | tf_op jit(solution)/shard_map/all_to_all | solution.py:89
  925.1 3.8 copy-start.6
  930.8 3.1 copy-start.5
  935.7 3.0 copy-start.7
  956.5 23.1 %all-to-all-start.4 = ((bf16[4,2,65536]{2,1,0:T(2,128)(2,1)}), bf16[4,2,65536]{2,1,0:T(2,128)(2,1)S(1)}, u32[]{:S(2)}, u32[]{:S(2)}) async-start(bf16[4,2,65536]{2,1,0:T(2,128)(2,1)} %reshape.195), calls=%async_computation.4 | async-start | bytes 2097152 | tf_op jit(solution)/shard_map/all_to_all | solution.py:86
  979.6 58.2 %all-to-all-start.3 = ((bf16[4,2,65536]{2,1,0:T(2,128)(2,1)}), bf16[4,2,65536]{2,1,0:T(2,128)(2,1)}, u32[]{:S(2)}, u32[]{:S(2)}) async-start(bf16[4,2,65536]{2,1,0:T(2,128)(2,1)} %reshape.193), calls=%async_computation.3 | async-start | bytes 2097152 | tf_op jit(solution)/shard_map/all_to_all | solution.py:85
  1040.6 1.9 copy-start.1
  (56 other events, 89.1 us)
where the time goes:
time: 1060 us; the launch traced here: 1040 us
  local copies, waits for them, and re-layouts  584 us (55%)
  other arithmetic  191 us (18%)
  matrix products  190 us (18%)
  blocking collectives  48.9 us (5%)
  starting transfers between devices  24.4 us (2%)
    reshape x64, local copies, waits for them, and re-layouts, one_group(): padded.reshape(block_len * (2 * block_len + 1))[:2 * block_len * block_len]  147 us
    dot_general x64, matrix products, one_group(): jnp.einsum('st,bct->bcs', toeplitz, grad_one, preferred_element_type=jnp....  114 us
    reduce_sum x64, other arithmetic, one_group(): return (grad_part, jnp.sum(skewed, axis=0))  111 us
    slice x128, local copies, waits for them, and re-layouts, one_group(): padded.reshape(block_len * (2 * block_len + 1))[:2 * block_len * block_len]  102 us
    reshape x64, local copies, waits for them, and re-layouts, one_group(): skewed = skewed.reshape(block_len, 2 * block_len)  95.2 us
    reshape x64, local copies, waits for them, and re-layouts, one_group(): repeated = repeated.reshape(block_len * (2 * block_len + 1))  85.2 us
    dot_general x64, matrix products, one_group(): jnp.einsum('bct,bcr->tr', grad_one, prod_one, preferred_element_type=jnp....  75.8 us
    psum x1, blocking collectives, on_device(): squares = lax.psum(jnp.sum(raw * raw), ('ctx', 'ch'))  48.9 us
  transfers between devices with their start and end apart: 6, of which 0 were waited for; matrix products, arithmetic and copies ran while one was open for 10% of the time, Pallas kernels for 0%

commit v1 on v0

v1 whole, which is shorter than its diff:
```python
import functools
import math

import jax
import jax.numpy as jnp
from jax import lax
from jax.experimental import pallas as pl
from jax.experimental.pallas import tpu as pltpu
from jax.sharding import PartitionSpec as P

WIDTH = 8192
GROUP = 16
LANES = 128
NT = (((1,), (1,)), ((), ()))


def gate_kernel(q_ref, k_ref, gate_ref, grad_ref, out_ref):
    groups = out_ref.shape[0]
    pairs = ((grad_ref, gate_ref), (q_ref, k_ref))
    for slot, (left, right) in enumerate(pairs):
        value = left[0].astype(jnp.float32) * right[0].astype(jnp.float32)
        value = value.T.astype(jnp.bfloat16)
        out_ref[:, slot, 0, 0] = value.reshape(groups, GROUP, LANES)


def ungate_kernel(grad_ref, q_ref, k_ref, gq_ref, gk_ref):
    groups = grad_ref.shape[0]
    grad = grad_ref[:, 0, 0].reshape(groups * GROUP, LANES).astype(jnp.float32).T
    gq_ref[0] = (grad * k_ref[0].astype(jnp.float32)).astype(jnp.bfloat16)
    gk_ref[0] = (grad * q_ref[0].astype(jnp.float32)).astype(jnp.bfloat16)


def group_kernel(
    pos_ref, data_ref, filt_ref, grad_ref, raw_ref, sq_ref, toep_ref, pad_ref, *, scale
):
    step = pl.program_id(0)
    per_device = pl.num_programs(0)
    blocks = raw_ref.shape[0] * raw_ref.shape[2]
    rows = data_ref.shape[0] * data_ref.shape[4] * GROUP
    row_id = lax.broadcasted_iota(jnp.int32, (LANES, LANES), 0)
    col_id = lax.broadcasted_iota(jnp.int32, (LANES, LANES), 1)

    @pl.when(step == 0)
    def _():
        toep_ref[:, :LANES] = jnp.zeros((LANES, LANES), jnp.bfloat16)
        pad_ref[:, rows:] = jnp.zeros((2, rows, LANES), jnp.bfloat16)
        sq_ref[...] = jnp.zeros_like(sq_ref)

    for half in range(2):
        pad_ref[half, :rows] = data_ref[:, 0, 0, half].reshape(rows, LANES)
    row = pos_ref[0] * per_device + step
    pick = lax.broadcasted_iota(jnp.int32, (8, filt_ref.shape[0]), 1) == row
    picked = jnp.dot(pick.astype(jnp.bfloat16), filt_ref[...], preferred_element_type=jnp.float32)
    upper = col_id >= row_id
    before = jnp.zeros((LANES, LANES), jnp.float32)
    for block in range(blocks):
        taps = jnp.concatenate([picked[:, block * LANES : (block + 1) * LANES]] * (LANES // 8), axis=0)
        rolled = pltpu.roll(taps, 0, 1, stride=1, stride_axis=0)
        toep_ref[:, (block + 1) * LANES : (block + 2) * LANES] = jnp.where(
            upper, rolled, before
        ).astype(jnp.bfloat16)
        before = rolled

    acc = jnp.zeros((rows, 2 * LANES), jnp.float32)
    for pair in range(blocks // 2):
        start = pair * GROUP
        left = jnp.concatenate([pad_ref[half, start:rows] for half in range(2)], axis=1)
        at = 2 * pair * LANES
        right = jnp.concatenate(
            [toep_ref[:, at + LANES : at + 3 * LANES], toep_ref[:, at : at + 2 * LANES]], axis=0
        )
        part = lax.dot_general(left, right, NT, preferred_element_type=jnp.float32)
        if start:
            part = jnp.concatenate([part, jnp.zeros((start, 2 * LANES), jnp.float32)], axis=0)
        acc = acc + part
    for half in range(2):
        value = acc[:, half * LANES : (half + 1) * LANES].astype(jnp.bfloat16)
        grad_ref[:, 0, half] = value.reshape(grad_ref.shape[0], grad_ref.shape[3], GROUP, LANES)

    flip = (row_id + col_id == LANES - 1).astype(jnp.bfloat16)
    prod = jnp.concatenate(
        [
            lax.dot_general(
                flip, data_ref[:, 0, 1, half].reshape(rows, LANES), NT, preferred_element_type=jnp.float32
            )
            for half in range(2)
        ],
        axis=1,
    ).astype(jnp.bfloat16)
    wraps = col_id <= row_id
    after = jnp.zeros((LANES, LANES), jnp.float32)
    per_owner = raw_ref.shape[2]
    squares = jnp.zeros((1, LANES), jnp.float32)
    for pair in reversed(range(blocks // 2)):
        start = pair * GROUP
        even = jnp.concatenate([pad_ref[0, start : start + rows], pad_ref[1, start : start + rows]], axis=0)
        odd = jnp.concatenate(
            [pad_ref[1, start : start + rows], pad_ref[0, start + GROUP : start + GROUP + rows]], axis=0
        )
        right = jnp.concatenate([even, odd], axis=1)
        both = jnp.dot(prod, right, preferred_element_type=jnp.float32)
        for half in (1, 0):
            block = 2 * pair + half
            rolled = pltpu.roll(both[:, half * LANES : (half + 1) * LANES], 1, 1, stride=1, stride_axis=0)
            lags = jnp.sum(jnp.where(wraps, rolled, after), axis=0, keepdims=True) * scale
            after = rolled
            raw_ref[block // per_owner, 0, block % per_owner : block % per_owner + 1] = lags
            squares = squares + lags * lags
    sq_ref[...] += jnp.broadcast_to(squares, sq_ref.shape)


def on_device(q_branch, k_branch, out_gate, filters, grad_out):
    seqs, block_len, chans = q_branch.shape
    owners = lax.axis_size("ctx")
    groups = chans // GROUP
    per_device = groups // owners
    local = block_len // LANES
    length = owners * block_len
    blocks = length // LANES
    wide = min(256, chans)
    scale = 4.0 / math.sqrt(seqs * GROUP)
    bf16, f32 = jnp.bfloat16, jnp.float32

    plain = pl.BlockSpec((1, LANES, wide), lambda i, j: (0, i, j))
    sent = pl.pallas_call(
        gate_kernel,
        grid=(local, chans // wide),
        in_specs=[plain] * 4,
        out_specs=pl.BlockSpec(
            (wide // GROUP, 2, 1, 1, GROUP, LANES), lambda i, j: (j, 0, i % 2, i // 2, 0, 0)
        ),
        out_shape=jax.ShapeDtypeStruct((groups, 2, 2, local // 2, GROUP, LANES), bf16),
        name="gate",
    )(q_branch, k_branch, out_gate, grad_out)
    got = lax.all_to_all(sent, "ctx", 0, 0, tiled=True)
    got = got.reshape(owners, per_device, 2, 2, local // 2, GROUP, LANES)
    rows = length * GROUP // (2 * LANES)
    pos = lax.axis_index("ctx").astype(jnp.int32).reshape(1)
    grad, raw, squares = pl.pallas_call(
        functools.partial(group_kernel, scale=scale),
        grid_spec=pltpu.PrefetchScalarGridSpec(
            num_scalar_prefetch=1,
            grid=(per_device,),
            in_specs=[
                pl.BlockSpec(
                    (owners, 1, 2, 2, local // 2, GROUP, LANES), lambda f, p: (0, f, 0, 0, 0, 0, 0)
                ),
                pl.BlockSpec((groups, length), lambda f, p: (0, 0)),
            ],
            out_specs=[
                pl.BlockSpec((owners, 1, 2, local // 2, GROUP, LANES), lambda f, p: (0, f, 0, 0, 0, 0)),
                pl.BlockSpec((owners, 1, blocks // owners, LANES), lambda f, p: (0, f, 0, 0)),
                pl.BlockSpec((8, LANES), lambda f, p: (0, 0)),
            ],
            scratch_shapes=[
                pltpu.VMEM((LANES, length + LANES), bf16),
                pltpu.VMEM((2, 2 * rows, LANES), bf16),
            ],
        ),
        out_shape=[
            jax.ShapeDtypeStruct((owners, per_device, 2, local // 2, GROUP, LANES), bf16),
            jax.ShapeDtypeStruct((owners, per_device, blocks // owners, LANES), f32),
            jax.ShapeDtypeStruct((8, LANES), f32),
        ],
        name="groups",
    )(pos, got, filters)

    back = lax.all_to_all(grad.reshape(groups, 2, local // 2, GROUP, LANES), "ctx", 0, 0, tiled=True)
    raw = lax.all_to_all(raw, "ctx", 0, 0, tiled=True).reshape(groups, length // owners)
    both = ("ctx", "ch")
    count = lax.axis_size(both)
    spread = jnp.broadcast_to(squares[:1], (count, LANES))
    total = jnp.sum(lax.all_to_all(spread, both, 0, 0, tiled=True))
    threshold = math.sqrt(WIDTH // GROUP * length)
    factor = jnp.minimum(1.0, threshold / jnp.sqrt(total + 1e-06))
    grad_q, grad_k = pl.pallas_call(
        ungate_kernel,
        grid=(local, chans // wide),
        in_specs=[
            pl.BlockSpec((wide // GROUP, 1, 1, GROUP, LANES), lambda i, j: (j, i % 2, i // 2, 0, 0)),
            plain,
            plain,
        ],
        out_specs=[plain] * 2,
        out_shape=[jax.ShapeDtypeStruct(q_branch.shape, bf16)] * 2,
        name="ungate",
    )(back, q_branch, k_branch)
    return (grad_q, grad_k, raw * factor)


def solution(mesh):
    return jax.shard_map(
        on_device,
        mesh=mesh,
        in_specs=(
            P(None, "ctx", "ch"),
            P(None, "ctx", "ch"),
            P(None, "ctx", "ch"),
            P("ch", None),
            P(None, "ctx", "ch"),
        ),
        out_specs=(P(None, "ctx", "ch"), P(None, "ctx", "ch"), P("ch", "ctx")),
        check_vma=False,
    )
```

time: 1060 us -> 112 us (0.11); the launches traced: 1040 us -> 110 us
  local copies, waits for them, and re-layouts: 584 us -> 3.68 us
  other arithmetic: 191 us -> 0.62 us
  matrix products: 190 us -> 0 us
  Pallas kernels: 0 us -> 38.2 us
  waiting for transfers between devices: 0.02 us -> 38.1 us
  blocking collectives: 48.9 us -> 20.5 us
  starting transfers between devices: 24.4 us -> 7.75 us
    reshape x261 -> x0, local copies, waits for them, and re-layouts: 368 us -> none  [the longest x64 147 us: one_group(): padded.reshape(block_len * (2 * block_len + 1))[:2 * block_len * block_len]]
    dot_general x128 -> x0, matrix products: 190 us -> none  [the longest x64 114 us: one_group(): jnp.einsum('st,bct->bcs', toeplitz, grad_one, preferred_element_type=jnp....]
    reduce_sum x65 -> x1, other arithmetic: 112 us -> 0.6 us  [on_device(): total = jnp.sum(lax.all_to_all(spread, both, 0, 0, tiled=True))]
    slice x196 -> x1, local copies, waits for them, and re-layouts: 106 us -> 0.69 us  [on_device(): spread = jnp.broadcast_to(squares[:1], (count, LANES))]
    psum x1 -> x0, blocking collectives: 48.9 us -> none  [on_device(): squares = lax.psum(jnp.sum(raw * raw), ('ctx', 'ch'))]
    unnamed x7 -> x0, other arithmetic: 44.8 us -> none
    pallas_call x0 -> x3, Pallas kernels: none -> 38.2 us  [the longest x1 17.6 us: on_device(): pl.pallas_call(functools.partial(group_kernel, scale=scale), grid_spec=pl...]
    all_to_all x6 -> x2, waiting for transfers between devices: 0.02 us -> 38.1 us  [the longest x1 25.7 us: on_device(): got = lax.all_to_all(sent, 'ctx', 0, 0, tiled=True)]
  transfers between devices with their start and end apart: 6 -> 2, of which waited for: 0 -> 2; matrix products, arithmetic and copies ran while one was open for 10% -> 1% of each run, Pallas kernels for 0% -> 0%
where the time goes in v1:
time: 112 us; the launch traced here: 110 us
  Pallas kernels  38.2 us (34%)
  waiting for transfers between devices  38.1 us (34%)
  blocking collectives  20.5 us (18%)
  starting transfers between devices  7.75 us (7%)
  local copies, waits for them, and re-layouts  3.68 us (3%)
  between operations  1.35 us (1%)
    all_to_all x1, waiting for transfers between devices, on_device(): got = lax.all_to_all(sent, 'ctx', 0, 0, tiled=True)  25.7 us
    pallas_call x1, Pallas kernels, on_device(): pl.pallas_call(functools.partial(group_kernel, scale=scale), grid_spec=pl...  17.6 us
    all_to_all x1, blocking collectives, on_device(): total = jnp.sum(lax.all_to_all(spread, both, 0, 0, tiled=True))  12.6 us
    all_to_all x1, waiting for transfers between devices, on_device(): lax.all_to_all(grad.reshape(groups, 2, local // 2, GROUP, LANES), 'ctx',...  12.4 us
    pallas_call x1, Pallas kernels, on_device(): pl.pallas_call(gate_kernel, grid=(local, chans // wide), in_specs=[plain]...  10.5 us
    pallas_call x1, Pallas kernels, on_device(): pl.pallas_call(ungate_kernel, grid=(local, chans // wide), in_specs=[pl.B...  10.1 us
    all_to_all x1, blocking collectives, on_device(): lax.all_to_all(raw, 'ctx', 0, 0, tiled=True)  7.92 us
    all_to_all x1, starting transfers between devices, on_device(): got = lax.all_to_all(sent, 'ctx', 0, 0, tiled=True)  4.24 us
  transfers between devices with their start and end apart: 2, of which 2 were waited for; matrix products, arithmetic and copies ran while one was open for 1% of the time, Pallas kernels for 0%

profile of v1, /device:TPU:0, one launch (start us, length us, event | category | flops | bytes accessed | tf_op | source)
XLA Modules:
  0.0 110.3 jit_solution(3595464158875968136)
XLA Ops:
  0.6 10.5 %gate.1 = bf16[64,2,2,2,16,128]{5,4,3,2,1,0:T(8,128)(2,1)} custom-call(bf16[1,512,1024]{2,1,0:T(8,128)(2,1)} %q_ref.3, bf16[1,512,1024]{2,1,0:T(8,128)(2,1)} %k_ref.3, bf16[1,512,1024]{2,1,0:T(8,128)(2,1)} %gate_ref.1, bf16[1,512,1024]{2,1,0:T(8,128)(2,1)} %grad_ref.1), custom_call_target="tpu_custom_call" | custom-call | tf_op jit(solution)/shard_map/gate/pallas_call | solution.py:125
  11.1 4.2 %all-to-all-start = ((bf16[64,2,2,2,16,128]{5,4,3,2,1,0:T(8,128)(2,1)}), bf16[64,2,2,2,16,128]{5,4,3,2,1,0:T(8,128)(2,1)S(1)}, u32[]{:S(2)}, u32[]{:S(2)}) async-start(bf16[64,2,2,2,16,128]{5,4,3,2,1,0:T(8,128)(2,1)} %gate.1), calls=%async_computation | async-start | bytes 4194304 | tf_op jit(solution)/shard_map/all_to_all | solution.py:135
  15.4 25.7 %all-to-all-done = bf16[64,2,2,2,16,128]{5,4,3,2,1,0:T(8,128)(2,1)S(1)} async-done(((bf16[64,2,2,2,16,128]{5,4,3,2,1,0:T(8,128)(2,1)}), bf16[64,2,2,2,16,128]{5,4,3,2,1,0:T(8,128)(2,1)S(1)}, u32[]{:S(2)}, u32[]{:S(2)}) %all-to-all-start) | async-done | bytes 2097184 | tf_op jit(solution)/shard_map/all_to_all | solution.py:135
  41.1 0.0 copy-start
  41.1 1.3 %copy-done = bf16[64,2,2,2,16,128]{5,4,3,2,1,0:T(8,128)(2,1)} copy-done((bf16[64,2,2,2,16,128]{5,4,3,2,1,0:T(8,128)(2,1)}, bf16[64,2,2,2,16,128]{5,4,3,2,1,0:T(8,128)(2,1)S(1)}, u32[]{:S(2)}) %copy-start) | copy-done | bytes 2097176
  42.4 17.6 %groups.1 = (bf16[4,16,2,2,16,128]{5,4,3,2,1,0:T(8,128)(2,1)}, f32[4,16,4,128]{3,2,1,0:T(4,128)}, f32[8,128]{1,0:T(8,128)}) custom-call(s32[1]{0:T(128)} %bitcast.pos_ref, bf16[4,16,2,2,2,16,128]{6,5,4,3,2,1,0:T(8,128)(2,1)} %bitcast.13, bf16[64,2048]{1,0:T(8,128)(2,1)} %filt_ref.1), custom_call_target="tpu_custom_call" | custom-call | tf_op jit(solution)/shard_map/groups/pallas_call | solution.py:139
  60.0 0.7 slice_bitcast_fusion
  60.7 12.6 %all_to_all.21 = f32[32,1,128]{2,1,0:T(1,128)S(1)} all-to-all(f32[32,1,128]{2,1,0:T(1,128)S(1)} %broadcast_in_dim.2), channel_id=1, replica_groups=mesh['ctx'=4,'ch'=8] {'ctx','ch'}, dimensions={0} | all-to-all | bytes 32768 | tf_op jit(solution)/shard_map/all_to_all | solution.py:173
  73.3 7.9 %all_to_all.22 = f32[4,16,4,128]{3,2,1,0:T(4,128)S(1)} all-to-all(f32[4,16,4,128]{3,2,1,0:T(4,128)} %get-tuple-element.11), channel_id=1, replica_groups=mesh['ctx'=4,'ch'=8] {'ctx'}, dimensions={0} | all-to-all | bytes 262144 | tf_op jit(solution)/shard_map/all_to_all | solution.py:169
  81.3 3.5 %all-to-all-start.1 = ((bf16[64,2,2,16,128]{4,3,2,1,0:T(8,128)(2,1)}), bf16[64,2,2,16,128]{4,3,2,1,0:T(8,128)(2,1)S(1)}, u32[]{:S(2)}, u32[]{:S(2)}) async-start(bf16[64,2,2,16,128]{4,3,2,1,0:T(8,128)(2,1)} %bitcast.14), calls=%async_computation.1 | async-start | bytes 2097152 | tf_op jit(solution)/shard_map/all_to_all | solution.py:168
  84.8 0.6 reduce_sum.9
  86.1 0.7 copy.11
  86.8 12.4 %all-to-all-done.1.grad_ref = bf16[64,2,2,16,128]{4,3,2,1,0:T(8,128)(2,1)S(1)} async-done(((bf16[64,2,2,16,128]{4,3,2,1,0:T(8,128)(2,1)}), bf16[64,2,2,16,128]{4,3,2,1,0:T(8,128)(2,1)S(1)}, u32[]{:S(2)}, u32[]{:S(2)}) %all-to-all-start.1) | async-done | bytes 1048608 | tf_op jit(solution)/shard_map/all_to_all | solution.py:168
  99.2 0.0 copy-start.1
  99.2 1.0 copy-done.1
  100.2 10.1 %ungate.1 = (bf16[1,512,1024]{2,1,0:T(8,128)(2,1)}, bf16[1,512,1024]{2,1,0:T(8,128)(2,1)}) custom-call(bf16[64,2,2,16,128]{4,3,2,1,0:T(8,128)(2,1)} %copy-done.1, bf16[1,512,1024]{2,1,0:T(8,128)(2,1)} %q_ref.3, bf16[1,512,1024]{2,1,0:T(8,128)(2,1)} %k_ref.3), custom_call_target="tpu_custom_call" | custom-call | tf_op jit(solution)/shard_map/ungate/pallas_call | solution.py:176
  (2 shorter events, 0.0 us)
Async XLA Ops:
  11.1 29.9 %all-to-all-start = ((bf16[64,2,2,2,16,128]{5,4,3,2,1,0:T(8,128)(2,1)}), bf16[64,2,2,2,16,128]{5,4,3,2,1,0:T(8,128)(2,1)S(1)}, u32[]{:S(2)}, u32[]{:S(2)}) async-start(bf16[64,2,2,2,16,128]{5,4,3,2,1,0:T(8,128)(2,1)} %gate.1), calls=%async_computation | async-start | bytes 4194304 | tf_op jit(solution)/shard_map/all_to_all | solution.py:135
  41.1 1.3 %copy-start = (bf16[64,2,2,2,16,128]{5,4,3,2,1,0:T(8,128)(2,1)}, bf16[64,2,2,2,16,128]{5,4,3,2,1,0:T(8,128)(2,1)S(1)}, u32[]{:S(2)}) copy-start(bf16[64,2,2,2,16,128]{5,4,3,2,1,0:T(8,128)(2,1)S(1)} %all-to-all-done) | copy-start | bytes 6291460
  81.3 18.0 %all-to-all-start.1 = ((bf16[64,2,2,16,128]{4,3,2,1,0:T(8,128)(2,1)}), bf16[64,2,2,16,128]{4,3,2,1,0:T(8,128)(2,1)S(1)}, u32[]{:S(2)}, u32[]{:S(2)}) async-start(bf16[64,2,2,16,128]{4,3,2,1,0:T(8,128)(2,1)} %bitcast.14), calls=%async_computation.1 | async-start | bytes 2097152 | tf_op jit(solution)/shard_map/all_to_all | solution.py:168
  99.2 1.0 copy-start.1

commit v2 on v0

v2 whole, which is shorter than its diff:
```python
import functools
import math

import jax
import jax.numpy as jnp
from jax import lax
from jax.experimental import pallas as pl
from jax.experimental.pallas import tpu as pltpu
from jax.sharding import PartitionSpec as P

WIDTH = 8192
GROUP = 16
LANES = 128
NT = (((1,), (1,)), ((), ()))
BF16, F32 = jnp.bfloat16, jnp.float32


def gate_kernel(pos_ref, left_ref, right_ref, *refs):
    *outs, left, right, out, in_sem, out_sem = refs
    local = left.shape[0] // LANES
    per_device = outs[0].shape[0]
    copies = []
    for i in range(local):
        here = pl.ds(i * LANES, LANES)
        copies.append(
            (
                pltpu.make_async_copy(left_ref.at[0, here], left.at[here], in_sem.at[i, 0]),
                pltpu.make_async_copy(right_ref.at[0, here], right.at[here], in_sem.at[i, 1]),
            )
        )
    for pair in copies:
        for copy in pair:
            copy.start()
    sends = []
    for i in range(local):
        for copy in copies[i]:
            copy.wait()
        rows = slice(i * LANES, (i + 1) * LANES)
        value = (left[rows].astype(F32) * right[rows].astype(F32)).astype(BF16).T
        out[i % 2, i // 2] = value.reshape(out.shape[2:])
        for k, target in enumerate(outs):
            first = jnp.bitwise_xor(pos_ref[0], k) * per_device
            send = pltpu.make_async_copy(
                out.at[i % 2, i // 2, pl.ds(first, per_device)],
                target.at[:, i % 2, i // 2],
                out_sem.at[i, k],
            )
            send.start()
            sends.append(send)
    for send in sends:
        send.wait()


def ungate_kernel(pos_ref, q_ref, k_ref, *refs):
    *grads, gq_ref, gk_ref, grad, q_in, k_in, gq, gk, in_sem, out_sem = refs
    local = q_in.shape[0] // LANES
    per_device = grads[0].shape[0]
    owners = len(grads)
    copies, sends = [], []
    for i in range(local):
        here = pl.ds(i * LANES, LANES)
        row = [
            pltpu.make_async_copy(q_ref.at[0, here], q_in.at[here], in_sem.at[i, owners]),
            pltpu.make_async_copy(k_ref.at[0, here], k_in.at[here], in_sem.at[i, owners + 1]),
        ]
        for k, source in enumerate(grads):
            first = jnp.bitwise_xor(pos_ref[0], k) * per_device
            row.append(
                pltpu.make_async_copy(
                    source.at[:, i % 2, i // 2], grad.at[i, pl.ds(first, per_device)], in_sem.at[i, k]
                )
            )
        copies.append(row)
    for row in copies:
        for copy in row:
            copy.start()
    for i in range(local):
        for copy in copies[i]:
            copy.wait()
        here = pl.ds(i * LANES, LANES)
        rows = slice(i * LANES, (i + 1) * LANES)
        value = grad[i].reshape(q_in.shape[1], LANES).T.astype(F32)
        gq[rows] = (value * k_in[rows].astype(F32)).astype(BF16)
        gk[rows] = (value * q_in[rows].astype(F32)).astype(BF16)
        for n, (source, target) in enumerate(((gq, gq_ref), (gk, gk_ref))):
            send = pltpu.make_async_copy(source.at[here], target.at[0, here], out_sem.at[i, n])
            send.start()
            sends.append(send)
    for send in sends:
        send.wait()


def clip_kernel(pos_ref, total_ref, *refs, threshold):
    *parts, _, out_ref, stage = refs
    per_device, each = stage.shape[1:3]
    for k, part in enumerate(parts):
        stage[jnp.bitwise_xor(pos_ref[0], k)] = part[...]
    total = jnp.sum(total_ref[...], axis=(0, 1, 2), keepdims=True)[0]
    factor = jnp.minimum(1.0, threshold / jnp.sqrt(total + 1e-06))
    for owner in range(stage.shape[0]):
        for n in range(each):
            rows = slice(owner * per_device, (owner + 1) * per_device)
            out_ref[rows, n * LANES : (n + 1) * LANES] = stage[owner, :, n] * factor


def fetch(pos_ref, sources, target, sem, *at):
    return [
        pltpu.make_async_copy(source, target.at[jnp.bitwise_xor(pos_ref[0], k)], sem.at[(k,) + at])
        for k, source in enumerate(sources)
    ]


def store(pos_ref, source, targets, sem, *at):
    return [
        pltpu.make_async_copy(source.at[jnp.bitwise_xor(pos_ref[0], k)], target, sem.at[(k,) + at])
        for k, target in enumerate(targets)
    ]


def conv_kernel(pos_ref, filt_ref, *refs):
    *refs, grad_v, out_v, taps, toep, pad, sem = refs
    ins, outs = refs[: len(refs) // 2], refs[len(refs) // 2 :]
    per_device, blocks = taps.shape[0], taps.shape[1] - 1
    owners, half_blocks = grad_v.shape[0], grad_v.shape[3]
    rows = pad.shape[1]
    copies = fetch(pos_ref, ins, grad_v, sem)
    for copy in copies:
        copy.start()
    groups = filt_ref.shape[0]
    picks = max(per_device, 8)
    row_id = lax.broadcasted_iota(jnp.int32, (picks, groups), 0)
    col_id = lax.broadcasted_iota(jnp.int32, (picks, groups), 1)
    pick = (col_id == row_id + pos_ref[0] * per_device).astype(BF16)
    mine = jnp.dot(pick, filt_ref[...], preferred_element_type=F32).astype(BF16)
    empty = jnp.zeros((picks, LANES), BF16)
    mine = jnp.concatenate([empty, mine, empty], axis=1)
    row_id = lax.broadcasted_iota(jnp.int32, (2 * LANES, LANES), 0)
    col_id = lax.broadcasted_iota(jnp.int32, (2 * LANES, LANES), 1)
    flip = (row_id + col_id == LANES).astype(BF16)
    for block in range(blocks + 1):
        near = mine[:, block * LANES : (block + 2) * LANES]
        back = jnp.dot(near, flip, preferred_element_type=F32)
        for f in range(per_device):
            taps[f, block] = back[f : f + 1]
    toep[0] = jnp.zeros((LANES, LANES), BF16)
    row_id = lax.broadcasted_iota(jnp.int32, (LANES, LANES), 0)
    col_id = lax.broadcasted_iota(jnp.int32, (LANES, LANES), 1)
    upper = col_id >= row_id

    def one(f, carry):
        for half in range(2):
            pad[half] = grad_v[:, f, half].reshape(rows, LANES)
        before = None
        for block in range(blocks + 1):
            tap = jnp.broadcast_to(taps[f, block], (LANES, LANES))
            rolled = pltpu.roll(tap, 0, 1, stride=1, stride_axis=0)
            if block:
                toep[block] = jnp.where(upper, before, rolled).astype(BF16)
            before = rolled
        acc = jnp.zeros((rows, 2 * LANES), F32)
        for pair in range(blocks // 2):
            start = pair * GROUP
            left = jnp.concatenate([pad[0, start:], pad[1, start:]], axis=1)
            at = 2 * pair + 1
            top = jnp.concatenate([toep[at], toep[at - 1]], axis=1)
            low = jnp.concatenate([toep[at + 1], toep[at]], axis=1)
            right = jnp.concatenate([top, low], axis=0)
            part = jnp.dot(left, right, preferred_element_type=F32)
            if start:
                part = jnp.concatenate([part, jnp.zeros((start, 2 * LANES), F32)], axis=0)
            acc = acc + part
        for half in range(2):
            value = acc[:, half * LANES : (half + 1) * LANES].astype(BF16)
            out_v[:, f, half] = value.reshape(owners, half_blocks, GROUP, LANES)
        return carry

    for copy in copies:
        copy.wait()
    lax.fori_loop(0, per_device, one, 0)
    sends = store(pos_ref, out_v, outs, sem)
    for send in sends:
        send.start()
    for send in sends:
        send.wait()


def lag_kernel(pos_ref, *refs, scale):
    *refs, sq_ref, grad_v, prod_v, raw_v, pad, sem = refs
    owners, per_device, per_owner = raw_v.shape[:3]
    blocks = owners * per_owner
    grads, prods, raws = refs[:owners], refs[owners : 2 * owners], refs[-owners:]
    rows = pad.shape[1] // 2
    copies = fetch(pos_ref, grads, grad_v, sem, 0) + fetch(pos_ref, prods, prod_v, sem, 1)
    for copy in copies:
        copy.start()
    pad[:, rows:] = jnp.zeros((2, rows, LANES), BF16)
    sq_ref[...] = jnp.zeros_like(sq_ref)
    row_id = lax.broadcasted_iota(jnp.int32, (LANES, LANES), 0)
    col_id = lax.broadcasted_iota(jnp.int32, (LANES, LANES), 1)
    flip = (row_id + col_id == LANES - 1).astype(BF16)
    wraps = col_id <= row_id

    def one(f, carry):
        for half in range(2):
            pad[half, :rows] = grad_v[:, f, half].reshape(rows, LANES)
        prod = jnp.concatenate(
            [
                lax.dot_general(
                    flip, prod_v[:, f, half].reshape(rows, LANES), NT, preferred_element_type=F32
                )
                for half in range(2)
            ],
            axis=1,
        ).astype(BF16)
        after = jnp.zeros((LANES, LANES), F32)
        squares = jnp.zeros((1, LANES), F32)
        for pair in reversed(range(blocks // 2)):
            start = pair * GROUP
            here, later = slice(start, start + rows), slice(start + GROUP, start + GROUP + rows)
            even = jnp.concatenate([pad[0, here], pad[1, here]], axis=0)
            odd = jnp.concatenate([pad[1, here], pad[0, later]], axis=0)
            both = jnp.dot(
                prod, jnp.concatenate([even, odd], axis=1), preferred_element_type=F32
            )
            for half in (1, 0):
                block = 2 * pair + half
                rolled = pltpu.roll(
                    both[:, half * LANES : (half + 1) * LANES], 1, 1, stride=1, stride_axis=0
                )
                lags = jnp.sum(jnp.where(wraps, rolled, after), axis=0, keepdims=True) * scale
                after = rolled
                raw_v[block // per_owner, f, block % per_owner : block % per_owner + 1] = lags
                squares = squares + lags * lags
        sq_ref[...] += jnp.broadcast_to(squares, sq_ref.shape)
        return carry

    for copy in copies:
        copy.wait()
    lax.fori_loop(0, per_device, one, 0)
    sends = store(pos_ref, raw_v, raws, sem, 0)
    for send in sends:
        send.start()
    for send in sends:
        send.wait()


def cost(flops, moved):
    return pl.CostEstimate(flops=int(flops), bytes_accessed=int(moved), transcendentals=0)


def on_device(q_branch, k_branch, out_gate, filters, grad_out):
    seqs, block_len, chans = q_branch.shape
    owners = lax.axis_size("ctx")
    groups = chans // GROUP
    per_device = groups // owners
    local = block_len // LANES
    length = owners * block_len
    blocks = length // LANES
    rows = length * GROUP // (2 * LANES)
    scale = 4.0 / math.sqrt(seqs * GROUP)
    size = block_len * chans * 2
    anywhere = pl.BlockSpec(memory_space=pl.ANY)
    vmem = pl.BlockSpec(memory_space=pltpu.VMEM)
    smem = pl.BlockSpec(memory_space=pltpu.SMEM)
    tail = (2, local // 2, GROUP, LANES)
    whole = (owners, per_device) + tail
    pos = lax.axis_index("ctx").astype(jnp.int32).reshape(1)
    piece = jax.ShapeDtypeStruct((per_device,) + tail, BF16)
    lag_piece = jax.ShapeDtypeStruct((per_device, blocks // owners, LANES), F32)

    def gate(left, right, limit, name):
        return pl.pallas_call(
            gate_kernel,
            in_specs=[smem] + [pl.BlockSpec(memory_space=pltpu.HBM)] * 2,
            out_specs=[anywhere] * owners,
            out_shape=[piece] * owners,
            scratch_shapes=[
                pltpu.VMEM((block_len, chans), BF16),
                pltpu.VMEM((block_len, chans), BF16),
                pltpu.VMEM((2, local // 2, groups, GROUP, LANES), BF16),
                pltpu.SemaphoreType.DMA((local, 2)),
                pltpu.SemaphoreType.DMA((local, owners)),
            ],
            cost_estimate=cost(block_len * chans, 3 * size),
            compiler_params=pltpu.CompilerParams(vmem_limit_bytes=limit << 20),
            name=name,
        )(pos, left, right)

    def swap(values):
        out = [values[0]]
        for k in range(1, owners):
            out.append(lax.ppermute(values[k], "ctx", [(i, i ^ k) for i in range(owners)]))
        return out

    grad_got = swap(gate(grad_out, out_gate, 56, "gate_grad"))
    prod_got = swap(gate(q_branch, k_branch, 12, "gate_prod"))
    conv = pl.pallas_call(
        conv_kernel,
        in_specs=[smem, vmem] + [anywhere] * owners,
        out_specs=[anywhere] * owners,
        out_shape=[piece] * owners,
        scratch_shapes=[
            pltpu.VMEM(whole, BF16),
            pltpu.VMEM(whole, BF16),
            pltpu.VMEM((per_device, blocks + 1, 1, LANES), F32),
            pltpu.VMEM((blocks + 1, LANES, LANES), BF16),
            pltpu.VMEM((2, rows, LANES), BF16),
            pltpu.SemaphoreType.DMA((owners,)),
        ],
        cost_estimate=cost(per_device * rows * length * 4096, 2 * size + groups * length * 2),
        compiler_params=pltpu.CompilerParams(vmem_limit_bytes=16 << 20),
        name="conv",
    )(pos, filters, *grad_got)
    back = swap(conv)
    *raw, squares = pl.pallas_call(
        functools.partial(lag_kernel, scale=scale),
        in_specs=[smem] + [anywhere] * (2 * owners + 1),
        out_specs=[anywhere] * owners + [vmem],
        out_shape=[lag_piece] * owners + [jax.ShapeDtypeStruct((8, LANES), F32)],
        scratch_shapes=[
            pltpu.VMEM(whole, BF16),
            pltpu.VMEM(whole, BF16),
            pltpu.VMEM((owners, per_device, blocks // owners, LANES), F32),
            pltpu.VMEM((2, 2 * rows, LANES), BF16),
            pltpu.SemaphoreType.DMA((owners, 2)),
        ],
        cost_estimate=cost(per_device * 2 * rows * length * 2048, 2 * size + per_device * length * 4),
        compiler_params=pltpu.CompilerParams(vmem_limit_bytes=16 << 20),
        name="lags",
    )(pos, *grad_got, *prod_got, conv[0])

    raw = swap(raw)
    both = ("ctx", "ch")
    count = lax.axis_size(both)
    spread = jnp.broadcast_to(squares[:1], (count, 1, LANES))
    total = lax.all_to_all(spread, both, 0, 0, tiled=True)
    threshold = math.sqrt(WIDTH // GROUP * length)
    grad_q, grad_k = pl.pallas_call(
        ungate_kernel,
        in_specs=[smem] + [anywhere] * (2 + owners),
        out_specs=[anywhere] * 2,
        out_shape=[jax.ShapeDtypeStruct(q_branch.shape, BF16)] * 2,
        scratch_shapes=[
            pltpu.VMEM((local, groups, GROUP, LANES), BF16),
            pltpu.VMEM((block_len, chans), BF16),
            pltpu.VMEM((block_len, chans), BF16),
            pltpu.VMEM((block_len, chans), BF16),
            pltpu.VMEM((block_len, chans), BF16),
            pltpu.SemaphoreType.DMA((local, owners + 2)),
            pltpu.SemaphoreType.DMA((local, 2)),
        ],
        cost_estimate=cost(2 * block_len * chans, 5 * size),
        compiler_params=pltpu.CompilerParams(vmem_limit_bytes=16 << 20),
        name="ungate",
    )(pos, q_branch, k_branch, *back)
    grad_filters = pl.pallas_call(
        functools.partial(clip_kernel, threshold=threshold),
        in_specs=[smem] + [vmem] * (1 + owners) + [anywhere],
        out_specs=vmem,
        out_shape=jax.ShapeDtypeStruct((groups, length // owners), F32),
        scratch_shapes=[pltpu.VMEM((owners, per_device, blocks // owners, LANES), F32)],
        cost_estimate=cost(groups * length, groups * length * 4),
        compiler_params=pltpu.CompilerParams(vmem_limit_bytes=60 << 20),
        name="clip",
    )(pos, total, *raw, grad_q)
    return (grad_q, grad_k, grad_filters)


def solution(mesh):
    return jax.shard_map(
        on_device,
        mesh=mesh,
        in_specs=(
            P(None, "ctx", "ch"),
            P(None, "ctx", "ch"),
            P(None, "ctx", "ch"),
            P("ch", None),
            P(None, "ctx", "ch"),
        ),
        out_specs=(P(None, "ctx", "ch"), P(None, "ctx", "ch"), P("ch", "ctx")),
        check_vma=False,
    )
```

time: 1060 us -> 59.9 us (0.06); the launches traced: 1040 us -> 59.6 us
  local copies, waits for them, and re-layouts: 584 us -> 1.82 us
  other arithmetic: 191 us -> 0 us
  matrix products: 190 us -> 0 us
  blocking collectives: 48.9 us -> 0 us
  Pallas kernels: 0 us -> 26.6 us
  waiting for transfers between devices: 0.02 us -> 14.9 us
    reshape x261 -> x0, local copies, waits for them, and re-layouts: 368 us -> none  [the longest x64 147 us: one_group(): padded.reshape(block_len * (2 * block_len + 1))[:2 * block_len * block_len]]
    dot_general x128 -> x0, matrix products: 190 us -> none  [the longest x64 114 us: one_group(): jnp.einsum('st,bct->bcs', toeplitz, grad_one, preferred_element_type=jnp....]
    reduce_sum x65 -> x0, other arithmetic: 112 us -> none  [the longest x64 111 us: one_group(): return (grad_part, jnp.sum(skewed, axis=0))]
    slice x196 -> x1, local copies, waits for them, and re-layouts: 106 us -> 0.01 us  [on_device(): spread = jnp.broadcast_to(squares[:1], (count, 1, LANES))]
    psum x1 -> x0, blocking collectives: 48.9 us -> none  [on_device(): squares = lax.psum(jnp.sum(raw * raw), ('ctx', 'ch'))]
    unnamed x7 -> x0, other arithmetic: 44.8 us -> none
    unnamed x39 -> x14, local copies, waits for them, and re-layouts: 39.7 us -> 1.2 us
    pallas_call x0 -> x6, Pallas kernels: none -> 26.6 us  [the longest x1 10.9 us: on_device(): pl.pallas_call(functools.partial(lag_kernel, scale=scale), in_specs=[smem...]
  transfers between devices with their start and end apart: 6 -> 13, of which waited for: 0 -> 4; matrix products, arithmetic and copies ran while one was open for 10% -> 1% of each run, Pallas kernels for 0% -> 37%
where the time goes in v2:
time: 59.9 us; the launch traced here: 59.6 us
  Pallas kernels  26.6 us (44%)
  starting transfers between devices  15.5 us (26%)
  waiting for transfers between devices  14.9 us (25%)
  local copies, waits for them, and re-layouts  1.82 us (3%)
  between operations  0.75 us (1%)
    pallas_call x1, Pallas kernels, on_device(): pl.pallas_call(functools.partial(lag_kernel, scale=scale), in_specs=[smem...  10.9 us
    ppermute x12, waiting for transfers between devices, swap(): lax.ppermute(values[k], 'ctx', [(i, i ^ k) for i in range(owners)])  10 us
    ppermute x12, starting transfers between devices, swap(): lax.ppermute(values[k], 'ctx', [(i, i ^ k) for i in range(owners)])  9.46 us
    pallas_call x1, Pallas kernels, on_device(): pl.pallas_call(conv_kernel, in_specs=[smem, vmem] + [anywhere] * owners,...  8.15 us
    all_to_all x1, starting transfers between devices, on_device(): total = lax.all_to_all(spread, both, 0, 0, tiled=True)  6.04 us
    all_to_all x1, waiting for transfers between devices, on_device(): total = lax.all_to_all(spread, both, 0, 0, tiled=True)  4.94 us
    pallas_call x2, Pallas kernels, gate(): pl.pallas_call(gate_kernel, in_specs=[smem] + [pl.BlockSpec(memory_space=...  3.73 us
    pallas_call x1, Pallas kernels, on_device(): pl.pallas_call(ungate_kernel, in_specs=[smem] + [anywhere] * (2 + owners)...  2.07 us
  transfers between devices with their start and end apart: 13, of which 4 were waited for; matrix products, arithmetic and copies ran while one was open for 1% of the time, Pallas kernels for 37%

profile of v2, /device:TPU:0, one launch (start us, length us, event | category | flops | bytes accessed | tf_op | source)
XLA Modules:
  0.0 59.6 jit_solution(9008913146205081350)
XLA Ops:
  0.7 2.7 %gate_grad.1 = (bf16[16,2,2,16,128]{4,3,2,1,0:T(8,128)(2,1)}, bf16[16,2,2,16,128]{4,3,2,1,0:T(8,128)(2,1)}, bf16[16,2,2,16,128]{4,3,2,1,0:T(8,128)(2,1)}, bf16[16,2,2,16,128]{4,3,2,1,0:T(8,128)(2,1)}) custom-call(s32[1]{0:T(128)} %bitcast.pos_ref, bf16[1,512,1024]{2,1,0:T(8,128)(2,1)} %left_ref.2, bf16[1,512,1024]{2,1,0:T(8,128)(2,1)} %right_ref.2), custom_call_target="tpu_custom_call" | custom-call | flops 524288 | bytes 3145728 | tf_op jit(solution)/shard_map/gate_grad/pallas_call | solution.py:272
  3.3 0.5 collective-permute-start
  3.9 2.6 %collective-permute-start.1 = (bf16[16,2,2,16,128]{4,3,2,1,0:T(8,128)(2,1)}, bf16[16,2,2,16,128]{4,3,2,1,0:T(8,128)(2,1)S(1)}, u32[]{:S(2)}, u32[]{:S(2)}) collective-permute-start(bf16[16,2,2,16,128]{4,3,2,1,0:T(8,128)(2,1)} %get-tuple-element.24), channel_id=1, source_target_pairs={{0,16},{8,24},{16,0},{24,8},{1,17},{9,25},{17,1},{25,9},{2,18},{10... | collective-permute-start | bytes 786440 | tf_op jit(solution)/shard_map/ppermute | solution.py:292
  6.5 0.1 collective-permute-start.2
  6.5 1.1 %gate_prod.1 = (bf16[16,2,2,16,128]{4,3,2,1,0:T(8,128)(2,1)S(1)}, bf16[16,2,2,16,128]{4,3,2,1,0:T(8,128)(2,1)S(1)}, bf16[16,2,2,16,128]{4,3,2,1,0:T(8,128)(2,1)S(1)}, bf16[16,2,2,16,128]{4,3,2,1,0:T(8,128)(2,1)S(1)}) custom-call(s32[1]{0:T(128)} %bitcast.pos_ref, bf16[1,512,1024]{2,1,0:T(8,128)(2,1)S(1)} %copy-done, bf16[1,512,1024]{2,1,0:T(8,128)(2,1)S(1)} %copy-done.1), custom_call_target="tpu_custom_call" | custom-call | flops 524288 | bytes 3145728 | tf_op jit(solution)/shard_map/gate_prod/pallas_call | solution.py:272
  7.6 0.2 collective-permute-start.6
  7.8 1.9 %collective-permute-start.7 = (bf16[16,2,2,16,128]{4,3,2,1,0:T(8,128)(2,1)S(1)}, bf16[16,2,2,16,128]{4,3,2,1,0:T(8,128)(2,1)S(1)}, u32[]{:S(2)}, u32[]{:S(2)}) collective-permute-start(bf16[16,2,2,16,128]{4,3,2,1,0:T(8,128)(2,1)S(1)} %get-tuple-element.34), channel_id=1, source_target_pairs={{0,16},{8,24},{16,0},{24,8},{1,17},{9,25},{17,1},{25,9},{2,18},{10... | collective-permute-start | bytes 786440 | tf_op jit(solution)/shard_map/ppermute | solution.py:292
  9.7 0.0 collective-permute-start.8
  9.7 4.1 %collective-permute-done.1.refs_2_ = bf16[16,2,2,16,128]{4,3,2,1,0:T(8,128)(2,1)S(1)} collective-permute-done((bf16[16,2,2,16,128]{4,3,2,1,0:T(8,128)(2,1)}, bf16[16,2,2,16,128]{4,3,2,1,0:T(8,128)(2,1)S(1)}, u32[]{:S(2)}, u32[]{:S(2)}) %collective-permute-start.1) | collective-permute-done | bytes 262176 | tf_op jit(solution)/shard_map/ppermute | solution.py:292
  13.8 5.2 %collective-permute-done.2.refs_3_ = bf16[16,2,2,16,128]{4,3,2,1,0:T(8,128)(2,1)S(1)} collective-permute-done((bf16[16,2,2,16,128]{4,3,2,1,0:T(8,128)(2,1)}, bf16[16,2,2,16,128]{4,3,2,1,0:T(8,128)(2,1)S(1)}, u32[]{:S(2)}, u32[]{:S(2)}) %collective-permute-start.2) | collective-permute-done | bytes 262176 | tf_op jit(solution)/shard_map/ppermute | solution.py:292
  19.0 8.2 %conv.1 = (bf16[16,2,2,16,128]{4,3,2,1,0:T(8,128)(2,1)S(1)}, bf16[16,2,2,16,128]{4,3,2,1,0:T(8,128)(2,1)S(1)}, bf16[16,2,2,16,128]{4,3,2,1,0:T(8,128)(2,1)}, bf16[16,2,2,16,128]{4,3,2,1,0:T(8,128)(2,1)S(1)}) custom-call(s32[1]{0:T(128)} %bitcast.pos_ref, bf16[64,2048]{1,0:T(8,128)(2,1)S(1)} %copy-done.3, bf16[16,2,2,16,128]{4,3,2,1,0:T(8,128)(2,1)S(1)} %copy-done.4, ...), custom_call_target="tpu_custom_call" | custom-call | flops 17179869184 | bytes 2359296 | tf_op jit(solution)/shard_map/conv/pallas_call | solution.py:297
  27.2 0.3 collective-permute-start.3
  27.5 1.9 %collective-permute-start.4 = (bf16[16,2,2,16,128]{4,3,2,1,0:T(8,128)(2,1)}, bf16[16,2,2,16,128]{4,3,2,1,0:T(8,128)(2,1)S(1)}, u32[]{:S(2)}, u32[]{:S(2)}) collective-permute-start(bf16[16,2,2,16,128]{4,3,2,1,0:T(8,128)(2,1)} %get-tuple-element.28), channel_id=1, source_target_pairs={{0,16},{8,24},{16,0},{24,8},{1,17},{9,25},{17,1},{25,9},{2,18},{10... | collective-permute-start | bytes 786440 | tf_op jit(solution)/shard_map/ppermute | solution.py:292
  29.4 0.0 collective-permute-done.6.refs_5_
  29.4 0.0 collective-permute-start.5
  29.4 0.0 collective-permute-done.7.refs_6_
  29.4 0.7 %collective-permute-done.8.refs_7_ = bf16[16,2,2,16,128]{4,3,2,1,0:T(8,128)(2,1)S(1)} collective-permute-done((bf16[16,2,2,16,128]{4,3,2,1,0:T(8,128)(2,1)S(1)}, bf16[16,2,2,16,128]{4,3,2,1,0:T(8,128)(2,1)S(1)}, u32[]{:S(2)}, u32[]{:S(2)}) %collective-permute-start.8) | collective-permute-done | bytes 262176 | tf_op jit(solution)/shard_map/ppermute | solution.py:292
  30.1 10.9 %lags.1 = (f32[16,4,128]{2,1,0:T(4,128)S(1)}, f32[16,4,128]{2,1,0:T(4,128)S(1)}, f32[16,4,128]{2,1,0:T(4,128)S(1)}, f32[16,4,128]{2,1,0:T(4,128)S(1)}, f32[8,128]{1,0:T(8,128)S(1)}) custom-call(s32[1]{0:T(128)} %bitcast.pos_ref, bf16[16,2,2,16,128]{4,3,2,1,0:T(8,128)(2,1)S(1)} %copy-done.4, bf16[16,2,2,16,128]{4,3,2,1,0:T(8,128)(2,1)S(1)} %collective-permute-done.refs_1_, ...), custom_call_target="tpu_custom_call" | custom-call | flops 17179869184 | bytes 2228224 | tf_op jit(solution)/shard_map/lags/pallas_call | solution.py:315
  41.1 0.6 copy-done.2
  41.7 0.1 collective-permute-start.9
  41.8 1.7 %collective-permute-start.10 = (f32[16,4,128]{2,1,0:T(4,128)S(1)}, f32[16,4,128]{2,1,0:T(4,128)}, u32[]{:S(2)}, u32[]{:S(2)}) collective-permute-start(f32[16,4,128]{2,1,0:T(4,128)S(1)} %get-tuple-element.39), channel_id=1, source_target_pairs={{0,16},{8,24},{16,0},{24,8},{1,17},{9,25},{17,1},{25,9},{2,18},{10... | collective-permute-start | bytes 98312 | tf_op jit(solution)/shard_map/ppermute | solution.py:292
  43.5 0.0 collective-permute-done.3.refs_1_
  43.5 0.0 collective-permute-start.11
  43.6 0.6 %broadcast_in_dim.3 = f32[32,1,128]{2,1,0:T(1,128)} broadcast(f32[128]{0:T(128)S(1)} %slice_bitcast_fusion), dimensions={2} | broadcast | bytes 16896 | tf_op jit(solution)/shard_map/broadcast_in_dim | solution.py:335
  44.2 6.0 %all-to-all-start = ((f32[32,1,128]{2,1,0:T(1,128)}), f32[32,1,128]{2,1,0:T(1,128)S(1)}, u32[]{:S(2)}, u32[]{:S(2)}) async-start(f32[32,1,128]{2,1,0:T(1,128)} %broadcast_in_dim.3), calls=%async_computation | async-start | bytes 32768 | tf_op jit(solution)/shard_map/all_to_all | solution.py:336
  50.2 0.0 collective-permute-done.5.refs_3_
  50.3 2.1 %ungate.1 = (bf16[1,512,1024]{2,1,0:T(8,128)(2,1)}, bf16[1,512,1024]{2,1,0:T(8,128)(2,1)}) custom-call(s32[1]{0:T(128)} %bitcast.pos_ref, bf16[1,512,1024]{2,1,0:T(8,128)(2,1)S(1)} %copy-done, bf16[1,512,1024]{2,1,0:T(8,128)(2,1)S(1)} %copy-done.1, bf16[16,2,2,16,128]{4,3,2,1,0:T(8,128)(2,1)S(1)} %get-tuple-element.26.refs_0_.refs_8_, ...), custom_call_target="tpu_custom_call" | custom-call | flops 1048576 | bytes 5242880 | tf_op jit(solution)/shard_map/ungate/pallas_call | solution.py:338
  52.3 4.9 %all-to-all-done.total_ref = f32[32,1,128]{2,1,0:T(1,128)S(1)} async-done(((f32[32,1,128]{2,1,0:T(1,128)}), f32[32,1,128]{2,1,0:T(1,128)S(1)}, u32[]{:S(2)}, u32[]{:S(2)}) %all-to-all-start) | async-done | bytes 16416 | tf_op jit(solution)/shard_map/all_to_all | solution.py:336
  57.3 0.0 collective-permute-done.10.refs_2_
  57.3 0.6 copy-done.5
  57.9 0.0 copy-done.6
  57.9 1.7 %clip.1 = f32[64,512]{1,0:T(8,128)} custom-call(s32[1]{0:T(128)} %bitcast.pos_ref, f32[32,1,128]{2,1,0:T(1,128)} %copy-done.5, f32[16,4,128]{2,1,0:T(4,128)} %copy-done.2, f32[16,4,128]{2,1,0:T(4,128)} %copy-done.6, f32[16,4,128]{2,1,0:T(4,128)} %collective-permute-done.10.refs_2_, f32[16,4,128]{2,1,0:T(4,128)} %collective-permute-done.11.refs_3_, ...), custom_call_target="tpu_custom_call" | custom-call | flops 131072 | bytes 524288 | tf_op jit(solution)/shard_map/clip/pallas_call | solution.py:356
  (16 shorter events, 0.0 us)
Async XLA Ops:
  0.6 5.9 %copy-start = (bf16[1,512,1024]{2,1,0:T(8,128)(2,1)S(1)}, bf16[1,512,1024]{2,1,0:T(8,128)(2,1)}, u32[]{:S(2)}) copy-start(bf16[1,512,1024]{2,1,0:T(8,128)(2,1)} %left_ref.3) | copy-start | bytes 3145732
  0.6 5.9 %copy-start.1 = (bf16[1,512,1024]{2,1,0:T(8,128)(2,1)S(1)}, bf16[1,512,1024]{2,1,0:T(8,128)(2,1)}, u32[]{:S(2)}) copy-start(bf16[1,512,1024]{2,1,0:T(8,128)(2,1)} %right_ref.3) | copy-start | bytes 3145732
  3.3 6.4 %collective-permute-start = (bf16[16,2,2,16,128]{4,3,2,1,0:T(8,128)(2,1)}, bf16[16,2,2,16,128]{4,3,2,1,0:T(8,128)(2,1)S(1)}, u32[]{:S(2)}, u32[]{:S(2)}) collective-permute-start(bf16[16,2,2,16,128]{4,3,2,1,0:T(8,128)(2,1)} %get-tuple-element.23), channel_id=1, source_target_pairs={{0,8},{8,0},{16,24},{24,16},{1,9},{9,1},{17,25},{25,17},{2,10},{10... | collective-permute-start | bytes 786440 | tf_op jit(solution)/shard_map/ppermute | solution.py:292
  3.9 10.0 %collective-permute-start.1 = (bf16[16,2,2,16,128]{4,3,2,1,0:T(8,128)(2,1)}, bf16[16,2,2,16,128]{4,3,2,1,0:T(8,128)(2,1)S(1)}, u32[]{:S(2)}, u32[]{:S(2)}) collective-permute-start(bf16[16,2,2,16,128]{4,3,2,1,0:T(8,128)(2,1)} %get-tuple-element.24), channel_id=1, source_target_pairs={{0,16},{8,24},{16,0},{24,8},{1,17},{9,25},{17,1},{25,9},{2,18},{10... | collective-permute-start | bytes 786440 | tf_op jit(solution)/shard_map/ppermute | solution.py:292
  6.4 12.6 %copy-start.3 = (bf16[64,2048]{1,0:T(8,128)(2,1)S(1)}, bf16[64,2048]{1,0:T(8,128)(2,1)}, u32[]{:S(2)}) copy-start(bf16[64,2048]{1,0:T(8,128)(2,1)} %filt_ref.1) | copy-start | bytes 786436
  6.5 12.6 %copy-start.4 = (bf16[16,2,2,16,128]{4,3,2,1,0:T(8,128)(2,1)S(1)}, bf16[16,2,2,16,128]{4,3,2,1,0:T(8,128)(2,1)}, u32[]{:S(2)}) copy-start(bf16[16,2,2,16,128]{4,3,2,1,0:T(8,128)(2,1)} %get-tuple-element.22.refs_0_) | copy-start | bytes 786436
  6.5 12.6 %collective-permute-start.2 = (bf16[16,2,2,16,128]{4,3,2,1,0:T(8,128)(2,1)}, bf16[16,2,2,16,128]{4,3,2,1,0:T(8,128)(2,1)S(1)}, u32[]{:S(2)}, u32[]{:S(2)}) collective-permute-start(bf16[16,2,2,16,128]{4,3,2,1,0:T(8,128)(2,1)} %get-tuple-element.25), channel_id=1, source_target_pairs={{0,24},{8,16},{16,8},{24,0},{1,25},{9,17},{17,9},{25,1},{2,26},{10... | collective-permute-start | bytes 786440 | tf_op jit(solution)/shard_map/ppermute | solution.py:292
  7.6 21.9 %collective-permute-start.6 = (bf16[16,2,2,16,128]{4,3,2,1,0:T(8,128)(2,1)S(1)}, bf16[16,2,2,16,128]{4,3,2,1,0:T(8,128)(2,1)S(1)}, u32[]{:S(2)}, u32[]{:S(2)}) collective-permute-start(bf16[16,2,2,16,128]{4,3,2,1,0:T(8,128)(2,1)S(1)} %get-tuple-element.33), channel_id=1, source_target_pairs={{0,8},{8,0},{16,24},{24,16},{1,9},{9,1},{17,25},{25,17},{2,10},{10... | collective-permute-start | bytes 786440 | tf_op jit(solution)/shard_map/ppermute | solution.py:292
  7.8 21.6 %collective-permute-start.7 = (bf16[16,2,2,16,128]{4,3,2,1,0:T(8,128)(2,1)S(1)}, bf16[16,2,2,16,128]{4,3,2,1,0:T(8,128)(2,1)S(1)}, u32[]{:S(2)}, u32[]{:S(2)}) collective-permute-start(bf16[16,2,2,16,128]{4,3,2,1,0:T(8,128)(2,1)S(1)} %get-tuple-element.34), channel_id=1, source_target_pairs={{0,16},{8,24},{16,0},{24,8},{1,17},{9,25},{17,1},{25,9},{2,18},{10... | collective-permute-start | bytes 786440 | tf_op jit(solution)/shard_map/ppermute | solution.py:292
  9.7 20.4 %collective-permute-start.8 = (bf16[16,2,2,16,128]{4,3,2,1,0:T(8,128)(2,1)S(1)}, bf16[16,2,2,16,128]{4,3,2,1,0:T(8,128)(2,1)S(1)}, u32[]{:S(2)}, u32[]{:S(2)}) collective-permute-start(bf16[16,2,2,16,128]{4,3,2,1,0:T(8,128)(2,1)S(1)} %get-tuple-element.35), channel_id=1, source_target_pairs={{0,24},{8,16},{16,8},{24,0},{1,25},{9,17},{17,9},{25,1},{2,26},{10... | collective-permute-start | bytes 786440 | tf_op jit(solution)/shard_map/ppermute | solution.py:292
  27.2 16.4 %collective-permute-start.3 = (bf16[16,2,2,16,128]{4,3,2,1,0:T(8,128)(2,1)S(1)}, bf16[16,2,2,16,128]{4,3,2,1,0:T(8,128)(2,1)S(1)}, u32[]{:S(2)}, u32[]{:S(2)}) collective-permute-start(bf16[16,2,2,16,128]{4,3,2,1,0:T(8,128)(2,1)S(1)} %get-tuple-element.27), channel_id=1, source_target_pairs={{0,8},{8,0},{16,24},{24,16},{1,9},{9,1},{17,25},{25,17},{2,10},{10... | collective-permute-start | bytes 786440 | tf_op jit(solution)/shard_map/ppermute | solution.py:292
  27.5 22.7 %collective-permute-start.4 = (bf16[16,2,2,16,128]{4,3,2,1,0:T(8,128)(2,1)}, bf16[16,2,2,16,128]{4,3,2,1,0:T(8,128)(2,1)S(1)}, u32[]{:S(2)}, u32[]{:S(2)}) collective-permute-start(bf16[16,2,2,16,128]{4,3,2,1,0:T(8,128)(2,1)} %get-tuple-element.28), channel_id=1, source_target_pairs={{0,16},{8,24},{16,0},{24,8},{1,17},{9,25},{17,1},{25,9},{2,18},{10... | collective-permute-start | bytes 786440 | tf_op jit(solution)/shard_map/ppermute | solution.py:292
  29.4 20.8 %collective-permute-start.5 = (bf16[16,2,2,16,128]{4,3,2,1,0:T(8,128)(2,1)S(1)}, bf16[16,2,2,16,128]{4,3,2,1,0:T(8,128)(2,1)S(1)}, u32[]{:S(2)}, u32[]{:S(2)}) collective-permute-start(bf16[16,2,2,16,128]{4,3,2,1,0:T(8,128)(2,1)S(1)} %get-tuple-element.29), channel_id=1, source_target_pairs={{0,24},{8,16},{16,8},{24,0},{1,25},{9,17},{17,9},{25,1},{2,26},{10... | collective-permute-start | bytes 786440 | tf_op jit(solution)/shard_map/ppermute | solution.py:292
  41.1 0.6 %copy-start.2 = (f32[16,4,128]{2,1,0:T(4,128)}, f32[16,4,128]{2,1,0:T(4,128)S(1)}, u32[]{:S(2)}) copy-start(f32[16,4,128]{2,1,0:T(4,128)S(1)} %get-tuple-element.37.refs_0_) | copy-start | bytes 98308
  41.7 15.6 %collective-permute-start.9 = (f32[16,4,128]{2,1,0:T(4,128)S(1)}, f32[16,4,128]{2,1,0:T(4,128)S(1)}, u32[]{:S(2)}, u32[]{:S(2)}) collective-permute-start(f32[16,4,128]{2,1,0:T(4,128)S(1)} %get-tuple-element.38), channel_id=1, source_target_pairs={{0,8},{8,0},{16,24},{24,16},{1,9},{9,1},{17,25},{25,17},{2,10},{10... | collective-permute-start | bytes 98312 | tf_op jit(solution)/shard_map/ppermute | solution.py:292
  41.8 15.5 %collective-permute-start.10 = (f32[16,4,128]{2,1,0:T(4,128)S(1)}, f32[16,4,128]{2,1,0:T(4,128)}, u32[]{:S(2)}, u32[]{:S(2)}) collective-permute-start(f32[16,4,128]{2,1,0:T(4,128)S(1)} %get-tuple-element.39), channel_id=1, source_target_pairs={{0,16},{8,24},{16,0},{24,8},{1,17},{9,25},{17,1},{25,9},{2,18},{10... | collective-permute-start | bytes 98312 | tf_op jit(solution)/shard_map/ppermute | solution.py:292
  43.5 13.8 %collective-permute-start.11 = (f32[16,4,128]{2,1,0:T(4,128)S(1)}, f32[16,4,128]{2,1,0:T(4,128)}, u32[]{:S(2)}, u32[]{:S(2)}) collective-permute-start(f32[16,4,128]{2,1,0:T(4,128)S(1)} %get-tuple-element.40), channel_id=1, source_target_pairs={{0,24},{8,16},{16,8},{24,0},{1,25},{9,17},{17,9},{25,1},{2,26},{10... | collective-permute-start | bytes 98312 | tf_op jit(solution)/shard_map/ppermute | solution.py:292
  44.2 13.1 %all-to-all-start = ((f32[32,1,128]{2,1,0:T(1,128)}), f32[32,1,128]{2,1,0:T(1,128)S(1)}, u32[]{:S(2)}, u32[]{:S(2)}) async-start(f32[32,1,128]{2,1,0:T(1,128)} %broadcast_in_dim.3), calls=%async_computation | async-start | bytes 32768 | tf_op jit(solution)/shard_map/all_to_all | solution.py:336
  57.3 0.6 %copy-start.5 = (f32[32,1,128]{2,1,0:T(1,128)}, f32[32,1,128]{2,1,0:T(1,128)S(1)}, u32[]{:S(2)}) copy-start(f32[32,1,128]{2,1,0:T(1,128)S(1)} %all-to-all-done.total_ref) | copy-start | bytes 49156
  57.3 0.6 %copy-start.6 = (f32[16,4,128]{2,1,0:T(4,128)}, f32[16,4,128]{2,1,0:T(4,128)S(1)}, u32[]{:S(2)}) copy-start(f32[16,4,128]{2,1,0:T(4,128)S(1)} %collective-permute-done.9.refs_1_) | copy-start | bytes 98308

commit v3 on v2

--- a/solution.py
+++ b/solution.py
@@ -15,7 +15,7 @@
 BF16, F32 = jnp.bfloat16, jnp.float32
 
 
-def gate_kernel(pos_ref, left_ref, right_ref, *refs):
+def gate_kernel(pos_ref, left_ref, right_ref, *refs, reverse):
     *outs, left, right, out, in_sem, out_sem = refs
     local = left.shape[0] // LANES
     per_device = outs[0].shape[0]
@@ -36,7 +36,13 @@
         for copy in copies[i]:
             copy.wait()
         rows = slice(i * LANES, (i + 1) * LANES)
-        value = (left[rows].astype(F32) * right[rows].astype(F32)).astype(BF16).T
+        value = (left[rows].astype(F32) * right[rows].astype(F32)).astype(BF16)
+        if reverse:
+            row_id = lax.broadcasted_iota(jnp.int32, (LANES, LANES), 0)
+            col_id = lax.broadcasted_iota(jnp.int32, (LANES, LANES), 1)
+            flip = (row_id + col_id == LANES - 1).astype(BF16)
+            value = jnp.dot(flip, value, preferred_element_type=F32).astype(BF16)
+        value = value.T
         out[i % 2, i // 2] = value.reshape(out.shape[2:])
         for k, target in enumerate(outs):
             first = jnp.bitwise_xor(pos_ref[0], k) * per_device
@@ -52,10 +58,11 @@
 
 
 def ungate_kernel(pos_ref, q_ref, k_ref, *refs):
-    *grads, gq_ref, gk_ref, grad, q_in, k_in, gq, gk, in_sem, out_sem = refs
+    *grads, gq_ref, gk_ref, mark_ref, grad, q_in, k_in, gq, gk, in_sem, out_sem = refs
     local = q_in.shape[0] // LANES
     per_device = grads[0].shape[0]
     owners = len(grads)
+    mark_ref[...] = jnp.zeros_like(mark_ref)
     copies, sends = [], []
     for i in range(local):
         here = pl.ds(i * LANES, LANES)
@@ -103,29 +110,20 @@
             out_ref[rows, n * LANES : (n + 1) * LANES] = stage[owner, :, n] * factor
 
 
-def fetch(pos_ref, sources, target, sem, *at):
-    return [
-        pltpu.make_async_copy(source, target.at[jnp.bitwise_xor(pos_ref[0], k)], sem.at[(k,) + at])
-        for k, source in enumerate(sources)
-    ]
-
-
-def store(pos_ref, source, targets, sem, *at):
-    return [
-        pltpu.make_async_copy(source.at[jnp.bitwise_xor(pos_ref[0], k)], target, sem.at[(k,) + at])
-        for k, target in enumerate(targets)
-    ]
-
-
-def conv_kernel(pos_ref, filt_ref, *refs):
-    *refs, grad_v, out_v, taps, toep, pad, sem = refs
-    ins, outs = refs[: len(refs) // 2], refs[len(refs) // 2 :]
+def spread_rows(pos_ref, sources, f, target):
+    for k, source in enumerate(sources):
+        count = source.shape[2] * GROUP
+        at = pl.multiple_of(jnp.bitwise_xor(pos_ref[0], k) * count, count)
+        for half in range(2):
+            target[half, pl.ds(at, count)] = source[f, half].reshape(count, LANES)
+
+
+def conv_kernel(pos_ref, filt_ref, *refs, owners, unroll):
+    ins, outs, refs = refs[:owners], refs[owners : 2 * owners], refs[2 * owners :]
+    taps, refs = refs[0], refs[1:]
+    toeps, pads, accs = refs[:unroll], refs[unroll : 2 * unroll], refs[2 * unroll :]
     per_device, blocks = taps.shape[0], taps.shape[1] - 1
-    owners, half_blocks = grad_v.shape[0], grad_v.shape[3]
-    rows = pad.shape[1]
-    copies = fetch(pos_ref, ins, grad_v, sem)
-    for copy in copies:
-        copy.start()
+    rows = pads[0].shape[1]
     groups = filt_ref.shape[0]
     picks = max(per_device, 8)
     row_id = lax.broadcasted_iota(jnp.int32, (picks, groups), 0)
@@ -142,14 +140,13 @@
         back = jnp.dot(near, flip, preferred_element_type=F32)
         for f in range(per_device):
             taps[f, block] = back[f : f + 1]
-    toep[0] = jnp.zeros((LANES, LANES), BF16)
+    for toep in toeps:
+        toep[0] = jnp.zeros((LANES, LANES), BF16)
     row_id = lax.broadcasted_iota(jnp.int32, (LANES, LANES), 0)
     col_id = lax.broadcasted_iota(jnp.int32, (LANES, LANES), 1)
     upper = col_id >= row_id
 
-    def one(f, carry):
-        for half in range(2):
-            pad[half] = grad_v[:, f, half].reshape(rows, LANES)
+    def one(f, toep, pad, out):
         before = None
         for block in range(blocks + 1):
             tap = jnp.broadcast_to(taps[f, block], (LANES, LANES))
@@ -170,50 +167,43 @@
                 part = jnp.concatenate([part, jnp.zeros((start, 2 * LANES), F32)], axis=0)
             acc = acc + part
         for half in range(2):
-            value = acc[:, half * LANES : (half + 1) * LANES].astype(BF16)
-            out_v[:, f, half] = value.reshape(owners, half_blocks, GROUP, LANES)
+            out[half] = acc[:, half * LANES : (half + 1) * LANES].astype(BF16)
+
+    def some(i, carry):
+        for u in range(unroll):
+            spread_rows(pos_ref, ins, i * unroll + u, pads[u])
+        for u in range(unroll):
+            one(i * unroll + u, toeps[u], pads[u], accs[u])
+        for u in range(unroll):
+            for k, target in enumerate(outs):
+                count = target.shape[2] * GROUP
+                at = pl.multiple_of(jnp.bitwise_xor(pos_ref[0], k) * count, count)
+                for half in range(2):
+                    value = accs[u][half, pl.ds(at, count)]
+                    target[i * unroll + u, half] = value.reshape(target.shape[2:])
         return carry
 
-    for copy in copies:
-        copy.wait()
-    lax.fori_loop(0, per_device, one, 0)
-    sends = store(pos_ref, out_v, outs, sem)
-    for send in sends:
-        send.start()
-    for send in sends:
-        send.wait()
-
-
-def lag_kernel(pos_ref, *refs, scale):
-    *refs, sq_ref, grad_v, prod_v, raw_v, pad, sem = refs
-    owners, per_device, per_owner = raw_v.shape[:3]
+    lax.fori_loop(0, per_device // unroll, some, 0)
+
+
+def lag_kernel(pos_ref, *refs, owners, unroll, scale):
+    grads, prods, refs = refs[:owners], refs[owners : 2 * owners], refs[2 * owners + 1 :]
+    raws, sum_ref, refs = refs[:owners], refs[owners], refs[owners + 1 :]
+    pads, flips, lags_v, sq_v = refs[:unroll], refs[unroll : 2 * unroll], refs[-2], refs[-1]
+    per_device, per_owner = raws[0].shape[:2]
     blocks = owners * per_owner
-    grads, prods, raws = refs[:owners], refs[owners : 2 * owners], refs[-owners:]
-    rows = pad.shape[1] // 2
-    copies = fetch(pos_ref, grads, grad_v, sem, 0) + fetch(pos_ref, prods, prod_v, sem, 1)
-    for copy in copies:
-        copy.start()
-    pad[:, rows:] = jnp.zeros((2, rows, LANES), BF16)
-    sq_ref[...] = jnp.zeros_like(sq_ref)
+    rows = flips[0].shape[1]
+    for pad in pads:
+        pad[:, rows:] = jnp.zeros((2, rows, LANES), BF16)
+    sq_v[...] = jnp.zeros_like(sq_v)
     row_id = lax.broadcasted_iota(jnp.int32, (LANES, LANES), 0)
     col_id = lax.broadcasted_iota(jnp.int32, (LANES, LANES), 1)
-    flip = (row_id + col_id == LANES - 1).astype(BF16)
     wraps = col_id <= row_id
 
-    def one(f, carry):
-        for half in range(2):
-            pad[half, :rows] = grad_v[:, f, half].reshape(rows, LANES)
-        prod = jnp.concatenate(
-            [
-                lax.dot_general(
-                    flip, prod_v[:, f, half].reshape(rows, LANES), NT, preferred_element_type=F32
-                )
-                for half in range(2)
-            ],
-            axis=1,
-        ).astype(BF16)
+    def one(slot, pad, flipped):
+        prod = jnp.concatenate([flipped[half].T for half in range(2)], axis=1)
         after = jnp.zeros((LANES, LANES), F32)
-        squares = jnp.zeros((1, LANES), F32)
+        sums = {}
         for pair in reversed(range(blocks // 2)):
             start = pair * GROUP
             here, later = slice(start, start + rows), slice(start + GROUP, start + GROUP + rows)
@@ -223,25 +213,33 @@
                 prod, jnp.concatenate([even, odd], axis=1), preferred_element_type=F32
             )
             for half in (1, 0):
-                block = 2 * pair + half
                 rolled = pltpu.roll(
                     both[:, half * LANES : (half + 1) * LANES], 1, 1, stride=1, stride_axis=0
                 )
-                lags = jnp.sum(jnp.where(wraps, rolled, after), axis=0, keepdims=True) * scale
+                part = jnp.where(wraps, rolled, after)
+                sums[2 * pair + half] = jnp.sum(part, axis=0, keepdims=True)
                 after = rolled
-                raw_v[block // per_owner, f, block % per_owner : block % per_owner + 1] = lags
-                squares = squares + lags * lags
-        sq_ref[...] += jnp.broadcast_to(squares, sq_ref.shape)
+        for owner in range(owners):
+            lags = jnp.concatenate(
+                [sums[owner * per_owner + n] for n in range(per_owner)], axis=0
+            ) * scale
+            lags_v[slot, owner] = lags
+            sq_v[...] += lags * lags
+
+    def some(i, carry):
+        for u in range(unroll):
+            spread_rows(pos_ref, grads, i * unroll + u, pads[u])
+            spread_rows(pos_ref, prods, i * unroll + u, flips[u])
+        for u in range(unroll):
+            one(u, pads[u], flips[u])
+        for u in range(unroll):
+            for k, target in enumerate(raws):
+                target[i * unroll + u] = lags_v[u, jnp.bitwise_xor(pos_ref[0], k)]
         return carry
 
-    for copy in copies:
-        copy.wait()
-    lax.fori_loop(0, per_device, one, 0)
-    sends = store(pos_ref, raw_v, raws, sem, 0)
-    for send in sends:
-        send.start()
-    for send in sends:
-        send.wait()
+    lax.fori_loop(0, per_device // unroll, some, 0)
+    squares = jnp.sum(sq_v[...], axis=0, keepdims=True)
+    sum_ref[...] = jnp.broadcast_to(squares[None], sum_ref.shape)
 
 
 def cost(flops, moved):
@@ -268,9 +266,9 @@
     piece = jax.ShapeDtypeStruct((per_device,) + tail, BF16)
     lag_piece = jax.ShapeDtypeStruct((per_device, blocks // owners, LANES), F32)
 
-    def gate(left, right, limit, name):
+    def gate(left, right, reverse, limit, name):
         return pl.pallas_call(
-            gate_kernel,
+            functools.partial(gate_kernel, reverse=reverse),
             in_specs=[smem] + [pl.BlockSpec(memory_space=pltpu.HBM)] * 2,
             out_specs=[anywhere] * owners,
             out_shape=[piece] * owners,
@@ -292,54 +290,48 @@
             out.append(lax.ppermute(values[k], "ctx", [(i, i ^ k) for i in range(owners)]))
         return out
 
-    grad_got = swap(gate(grad_out, out_gate, 56, "gate_grad"))
-    prod_got = swap(gate(q_branch, k_branch, 12, "gate_prod"))
+    grad_got = swap(gate(grad_out, out_gate, False, 56, "gate_grad"))
+    prod_got = swap(gate(q_branch, k_branch, True, 12, "gate_prod"))
+    unroll = math.gcd(4, per_device)
     conv = pl.pallas_call(
-        conv_kernel,
-        in_specs=[smem, vmem] + [anywhere] * owners,
-        out_specs=[anywhere] * owners,
+        functools.partial(conv_kernel, owners=owners, unroll=unroll),
+        in_specs=[smem] + [vmem] * (1 + owners),
+        out_specs=[vmem] * owners,
         out_shape=[piece] * owners,
-        scratch_shapes=[
-            pltpu.VMEM(whole, BF16),
-            pltpu.VMEM(whole, BF16),
-            pltpu.VMEM((per_device, blocks + 1, 1, LANES), F32),
-            pltpu.VMEM((blocks + 1, LANES, LANES), BF16),
-            pltpu.VMEM((2, rows, LANES), BF16),
-            pltpu.SemaphoreType.DMA((owners,)),
-        ],
+        scratch_shapes=[pltpu.VMEM((per_device, blocks + 1, 1, LANES), F32)]
+        + [pltpu.VMEM((blocks + 1, LANES, LANES), BF16)] * unroll
+        + [pltpu.VMEM((2, rows, LANES), BF16)] * (2 * unroll),
         cost_estimate=cost(per_device * rows * length * 4096, 2 * size + groups * length * 2),
         compiler_params=pltpu.CompilerParams(vmem_limit_bytes=16 << 20),
         name="conv",
     )(pos, filters, *grad_got)
     back = swap(conv)
-    *raw, squares = pl.pallas_call(
-        functools.partial(lag_kernel, scale=scale),
-        in_specs=[smem] + [anywhere] * (2 * owners + 1),
-        out_specs=[anywhere] * owners + [vmem],
-        out_shape=[lag_piece] * owners + [jax.ShapeDtypeStruct((8, LANES), F32)],
-        scratch_shapes=[
-            pltpu.VMEM(whole, BF16),
-            pltpu.VMEM(whole, BF16),
-            pltpu.VMEM((owners, per_device, blocks // owners, LANES), F32),
-            pltpu.VMEM((2, 2 * rows, LANES), BF16),
-            pltpu.SemaphoreType.DMA((owners, 2)),
+    both = ("ctx", "ch")
+    count = lax.axis_size(both)
+    unroll = math.gcd(8, per_device)
+    *raw, spread = pl.pallas_call(
+        functools.partial(lag_kernel, owners=owners, unroll=unroll, scale=scale),
+        in_specs=[smem] + [vmem] * (2 * owners) + [anywhere],
+        out_specs=[vmem] * (owners + 1),
+        out_shape=[lag_piece] * owners + [jax.ShapeDtypeStruct((count, 1, LANES), F32)],
+        scratch_shapes=[pltpu.VMEM((2, 2 * rows, LANES), BF16)] * unroll
+        + [pltpu.VMEM((2, rows, LANES), BF16)] * unroll
+        + [
+            pltpu.VMEM((unroll, owners, blocks // owners, LANES), F32),
+            pltpu.VMEM((blocks // owners, LANES), F32),
         ],
         cost_estimate=cost(per_device * 2 * rows * length * 2048, 2 * size + per_device * length * 4),
         compiler_params=pltpu.CompilerParams(vmem_limit_bytes=16 << 20),
         name="lags",
     )(pos, *grad_got, *prod_got, conv[0])
-
-    raw = swap(raw)
-    both = ("ctx", "ch")
-    count = lax.axis_size(both)
-    spread = jnp.broadcast_to(squares[:1], (count, 1, LANES))
     total = lax.all_to_all(spread, both, 0, 0, tiled=True)
     threshold = math.sqrt(WIDTH // GROUP * length)
-    grad_q, grad_k = pl.pallas_call(
+    grad_q, grad_k, mark = pl.pallas_call(
         ungate_kernel,
         in_specs=[smem] + [anywhere] * (2 + owners),
-        out_specs=[anywhere] * 2,
-        out_shape=[jax.ShapeDtypeStruct(q_branch.shape, BF16)] * 2,
+        out_specs=[anywhere] * 2 + [vmem],
+        out_shape=[jax.ShapeDtypeStruct(q_branch.shape, BF16)] * 2
+        + [jax.ShapeDtypeStruct((8, LANES), F32)],
         scratch_shapes=[
             pltpu.VMEM((local, groups, GROUP, LANES), BF16),
             pltpu.VMEM((block_len, chans), BF16),
@@ -353,16 +345,18 @@
         compiler_params=pltpu.CompilerParams(vmem_limit_bytes=16 << 20),
         name="ungate",
     )(pos, q_branch, k_branch, *back)
+    raw, mark = lax.optimization_barrier((raw, mark))
+    raw = swap(raw)
     grad_filters = pl.pallas_call(
         functools.partial(clip_kernel, threshold=threshold),
-        in_specs=[smem] + [vmem] * (1 + owners) + [anywhere],
+        in_specs=[smem] + [vmem] * (2 + owners),
         out_specs=vmem,
         out_shape=jax.ShapeDtypeStruct((groups, length // owners), F32),
         scratch_shapes=[pltpu.VMEM((owners, per_device, blocks // owners, LANES), F32)],
         cost_estimate=cost(groups * length, groups * length * 4),
-        compiler_params=pltpu.CompilerParams(vmem_limit_bytes=60 << 20),
+        compiler_params=pltpu.CompilerParams(vmem_limit_bytes=8 << 20),
         name="clip",
-    )(pos, total, *raw, grad_q)
+    )(pos, total, *raw, mark)
     return (grad_q, grad_k, grad_filters)
 
 

time: 59.9 us -> 59.4 us (level)
  blocking collectives: 0 us -> 13 us
  Pallas kernels: 26.6 us -> 17.3 us
  starting transfers between devices: 15.5 us -> 9.52 us
  waiting for transfers between devices: 14.9 us -> 18.7 us
  local copies, waits for them, and re-layouts: 1.82 us -> 0.02 us
    all_to_all x0 -> x1, blocking collectives: none -> 13 us  [on_device(): total = lax.all_to_all(spread, both, 0, 0, tiled=True)]
    ppermute x12, waiting for transfers between devices: 10 us -> 18.7 us  [swap(): lax.ppermute(values[k], 'ctx', [(i, i ^ k) for i in range(owners)])]
    pallas_call x4, Pallas kernels: 22.8 us -> 14.4 us  [the longest x1 5.35 us: on_device(): pl.pallas_call(functools.partial(lag_kernel, owners=owners, unroll=unroll...]
    all_to_all x1 -> x0, starting transfers between devices: 6.04 us -> none  [on_device(): total = lax.all_to_all(spread, both, 0, 0, tiled=True)]
    all_to_all x1 -> x0, waiting for transfers between devices: 4.94 us -> none  [on_device(): total = lax.all_to_all(spread, both, 0, 0, tiled=True)]
    unnamed x14 -> x8, local copies, waits for them, and re-layouts: 1.2 us -> 0.02 us
    pallas_call x1, Pallas kernels: 1.74 us -> 0.93 us  [on_device(): pl.pallas_call(functools.partial(clip_kernel, threshold=threshold), in_sp...]
    broadcast_in_dim x1 -> x0, local copies, waits for them, and re-layouts: 0.62 us -> none  [on_device(): spread = jnp.broadcast_to(squares[:1], (count, 1, LANES))]
  transfers between devices with their start and end apart: 13 -> 12, of which waited for: 4 -> 5; matrix products, arithmetic and copies ran while one was open for 1% -> 0% of each run, Pallas kernels for 37% -> 20%
where the time goes in v3:
time: 59.4 us; the launch traced here: 59.3 us
  waiting for transfers between devices  18.7 us (31%)
  Pallas kernels  17.3 us (29%)
  blocking collectives  13 us (22%)
  starting transfers between devices  9.52 us (16%)
  between operations  0.71 us (1%)
    ppermute x12, waiting for transfers between devices, swap(): lax.ppermute(values[k], 'ctx', [(i, i ^ k) for i in range(owners)])  18.7 us
    all_to_all x1, blocking collectives, on_device(): total = lax.all_to_all(spread, both, 0, 0, tiled=True)  13 us
    ppermute x12, starting transfers between devices, swap(): lax.ppermute(values[k], 'ctx', [(i, i ^ k) for i in range(owners)])  9.52 us
    pallas_call x1, Pallas kernels, on_device(): pl.pallas_call(functools.partial(lag_kernel, owners=owners, unroll=unroll...  5.35 us
    pallas_call x1, Pallas kernels, on_device(): pl.pallas_call(functools.partial(conv_kernel, owners=owners, unroll=unrol...  4.63 us
    pallas_call x2, Pallas kernels, gate(): pl.pallas_call(functools.partial(gate_kernel, reverse=reverse), in_specs=...  4.38 us
    pallas_call x1, Pallas kernels, on_device(): pl.pallas_call(ungate_kernel, in_specs=[smem] + [anywhere] * (2 + owners)...  2.06 us
  transfers between devices with their start and end apart: 12, of which 5 were waited for; matrix products, arithmetic and copies ran while one was open for 0% of the time, Pallas kernels for 20%

profile of v3, /device:TPU:0, one launch (start us, length us, event | category | flops | bytes accessed | tf_op | source)
XLA Modules:
  0.0 59.3 jit_solution(9252277518195569369)
XLA Ops:
  0.6 0.0 copy-start
  0.7 2.7 %gate_grad.1 = (bf16[16,2,2,16,128]{4,3,2,1,0:T(8,128)(2,1)}, bf16[16,2,2,16,128]{4,3,2,1,0:T(8,128)(2,1)}, bf16[16,2,2,16,128]{4,3,2,1,0:T(8,128)(2,1)}, bf16[16,2,2,16,128]{4,3,2,1,0:T(8,128)(2,1)}) custom-call(s32[1]{0:T(128)} %bitcast.pos_ref, bf16[1,512,1024]{2,1,0:T(8,128)(2,1)} %left_ref.2, bf16[1,512,1024]{2,1,0:T(8,128)(2,1)} %right_ref.2), custom_call_target="tpu_custom_call" | custom-call | flops 524288 | bytes 3145728 | tf_op jit(solution)/shard_map/gate_grad/pallas_call | solution.py:270
  3.3 0.5 collective-permute-start
  3.9 2.6 %collective-permute-start.1 = (bf16[16,2,2,16,128]{4,3,2,1,0:T(8,128)(2,1)}, bf16[16,2,2,16,128]{4,3,2,1,0:T(8,128)(2,1)S(1)}, u32[]{:S(2)}, u32[]{:S(2)}) collective-permute-start(bf16[16,2,2,16,128]{4,3,2,1,0:T(8,128)(2,1)} %get-tuple-element.30), channel_id=1, source_target_pairs={{0,16},{8,24},{16,0},{24,8},{1,17},{9,25},{17,1},{25,9},{2,18},{10... | collective-permute-start | bytes 786440 | tf_op jit(solution)/shard_map/ppermute | solution.py:290
  6.5 0.1 collective-permute-start.2
  6.5 1.7 %gate_prod.1 = (bf16[16,2,2,16,128]{4,3,2,1,0:T(8,128)(2,1)S(1)}, bf16[16,2,2,16,128]{4,3,2,1,0:T(8,128)(2,1)S(1)}, bf16[16,2,2,16,128]{4,3,2,1,0:T(8,128)(2,1)S(1)}, bf16[16,2,2,16,128]{4,3,2,1,0:T(8,128)(2,1)S(1)}) custom-call(s32[1]{0:T(128)} %bitcast.pos_ref, bf16[1,512,1024]{2,1,0:T(8,128)(2,1)S(1)} %copy-done, bf16[1,512,1024]{2,1,0:T(8,128)(2,1)S(1)} %copy-done.1), custom_call_target="tpu_custom_call" | custom-call | flops 524288 | bytes 3145728 | tf_op jit(solution)/shard_map/gate_prod/pallas_call | solution.py:270
  8.2 0.2 collective-permute-start.6
  8.5 1.9 %collective-permute-start.7 = (bf16[16,2,2,16,128]{4,3,2,1,0:T(8,128)(2,1)S(1)}, bf16[16,2,2,16,128]{4,3,2,1,0:T(8,128)(2,1)S(1)}, u32[]{:S(2)}, u32[]{:S(2)}) collective-permute-start(bf16[16,2,2,16,128]{4,3,2,1,0:T(8,128)(2,1)S(1)} %get-tuple-element.40), channel_id=1, source_target_pairs={{0,16},{8,24},{16,0},{24,8},{1,17},{9,25},{17,1},{25,9},{2,18},{10... | collective-permute-start | bytes 786440 | tf_op jit(solution)/shard_map/ppermute | solution.py:290
  10.4 0.0 collective-permute-done.refs_1_
  10.4 0.0 collective-permute-start.8
  10.4 3.4 %collective-permute-done.1.refs_2_ = bf16[16,2,2,16,128]{4,3,2,1,0:T(8,128)(2,1)S(1)} collective-permute-done((bf16[16,2,2,16,128]{4,3,2,1,0:T(8,128)(2,1)}, bf16[16,2,2,16,128]{4,3,2,1,0:T(8,128)(2,1)S(1)}, u32[]{:S(2)}, u32[]{:S(2)}) %collective-permute-start.1) | collective-permute-done | bytes 262176 | tf_op jit(solution)/shard_map/ppermute | solution.py:290
  13.8 5.2 %collective-permute-done.2.refs_3_ = bf16[16,2,2,16,128]{4,3,2,1,0:T(8,128)(2,1)S(1)} collective-permute-done((bf16[16,2,2,16,128]{4,3,2,1,0:T(8,128)(2,1)}, bf16[16,2,2,16,128]{4,3,2,1,0:T(8,128)(2,1)S(1)}, u32[]{:S(2)}, u32[]{:S(2)}) %collective-permute-start.2) | collective-permute-done | bytes 262176 | tf_op jit(solution)/shard_map/ppermute | solution.py:290
  19.0 4.6 %conv.1 = (bf16[16,2,2,16,128]{4,3,2,1,0:T(8,128)(2,1)S(1)}, bf16[16,2,2,16,128]{4,3,2,1,0:T(8,128)(2,1)S(1)}, bf16[16,2,2,16,128]{4,3,2,1,0:T(8,128)(2,1)S(1)}, bf16[16,2,2,16,128]{4,3,2,1,0:T(8,128)(2,1)S(1)}) custom-call(s32[1]{0:T(128)} %bitcast.pos_ref, bf16[64,2048]{1,0:T(8,128)(2,1)S(1)} %copy-done.2, bf16[16,2,2,16,128]{4,3,2,1,0:T(8,128)(2,1)S(1)} %copy-done.3, ...), custom_call_target="tpu_custom_call" | custom-call | flops 17179869184 | bytes 2359296 | tf_op jit(solution)/shard_map/conv/pallas_call | solution.py:296
  23.6 0.3 collective-permute-start.3
  24.0 2.0 %collective-permute-start.4 = (bf16[16,2,2,16,128]{4,3,2,1,0:T(8,128)(2,1)S(1)}, bf16[16,2,2,16,128]{4,3,2,1,0:T(8,128)(2,1)S(1)}, u32[]{:S(2)}, u32[]{:S(2)}) collective-permute-start(bf16[16,2,2,16,128]{4,3,2,1,0:T(8,128)(2,1)S(1)} %get-tuple-element.34), channel_id=1, source_target_pairs={{0,16},{8,24},{16,0},{24,8},{1,17},{9,25},{17,1},{25,9},{2,18},{10... | collective-permute-start | bytes 786440 | tf_op jit(solution)/shard_map/ppermute | solution.py:290
  25.9 0.0 collective-permute-done.6.refs_5_
  25.9 0.0 collective-permute-start.5
  25.9 0.0 collective-permute-done.7.refs_6_
  25.9 4.2 %collective-permute-done.8.refs_7_ = bf16[16,2,2,16,128]{4,3,2,1,0:T(8,128)(2,1)S(1)} collective-permute-done((bf16[16,2,2,16,128]{4,3,2,1,0:T(8,128)(2,1)S(1)}, bf16[16,2,2,16,128]{4,3,2,1,0:T(8,128)(2,1)S(1)}, u32[]{:S(2)}, u32[]{:S(2)}) %collective-permute-start.8) | collective-permute-done | bytes 262176 | tf_op jit(solution)/shard_map/ppermute | solution.py:290
  30.1 5.3 %lags.1 = (f32[16,4,128]{2,1,0:T(4,128)S(1)}, f32[16,4,128]{2,1,0:T(4,128)S(1)}, f32[16,4,128]{2,1,0:T(4,128)S(1)}, f32[16,4,128]{2,1,0:T(4,128)S(1)}, f32[32,1,128]{2,1,0:T(1,128)S(1)}) custom-call(s32[1]{0:T(128)} %bitcast.pos_ref, bf16[16,2,2,16,128]{4,3,2,1,0:T(8,128)(2,1)S(1)} %copy-done.3, ...), custom_call_target="tpu_custom_call" | custom-call | flops 17179869184 | bytes 2228224 | tf_op jit(solution)/shard_map/lags/pallas_call | solution.py:312
  35.5 0.0 collective-permute-done.3.refs_1_
  35.5 0.8 %collective-permute-done.4.refs_2_ = bf16[16,2,2,16,128]{4,3,2,1,0:T(8,128)(2,1)S(1)} collective-permute-done((bf16[16,2,2,16,128]{4,3,2,1,0:T(8,128)(2,1)S(1)}, bf16[16,2,2,16,128]{4,3,2,1,0:T(8,128)(2,1)S(1)}, u32[]{:S(2)}, u32[]{:S(2)}) %collective-permute-start.4) | collective-permute-done | bytes 262176 | tf_op jit(solution)/shard_map/ppermute | solution.py:290
  36.3 5.1 %collective-permute-done.5.refs_3_ = bf16[16,2,2,16,128]{4,3,2,1,0:T(8,128)(2,1)S(1)} collective-permute-done((bf16[16,2,2,16,128]{4,3,2,1,0:T(8,128)(2,1)S(1)}, bf16[16,2,2,16,128]{4,3,2,1,0:T(8,128)(2,1)S(1)}, u32[]{:S(2)}, u32[]{:S(2)}) %collective-permute-start.5) | collective-permute-done | bytes 262176 | tf_op jit(solution)/shard_map/ppermute | solution.py:290
  41.4 2.1 %ungate.1 = (bf16[1,512,1024]{2,1,0:T(8,128)(2,1)}, bf16[1,512,1024]{2,1,0:T(8,128)(2,1)}, f32[8,128]{1,0:T(8,128)S(1)}) custom-call(s32[1]{0:T(128)} %bitcast.pos_ref, bf16[1,512,1024]{2,1,0:T(8,128)(2,1)S(1)} %copy-done, bf16[1,512,1024]{2,1,0:T(8,128)(2,1)S(1)} %copy-done.1, bf16[16,2,2,16,128]{4,3,2,1,0:T(8,128)(2,1)S(1)} %get-tuple-element.32.refs_0_.refs_8_, ...), custom_call_target="tpu_custom_call" | custom-call | flops 1048576 | bytes 5242880 | tf_op jit(solution)/shard_map/ungate/pallas_call | solution.py:329
  43.4 0.2 collective-permute-start.9
  43.6 1.7 %collective-permute-start.10 = (f32[16,4,128]{2,1,0:T(4,128)S(1)}, f32[16,4,128]{2,1,0:T(4,128)S(1)}, u32[]{:S(2)}, u32[]{:S(2)}) collective-permute-start(f32[16,4,128]{2,1,0:T(4,128)S(1)} %get-tuple-element.50), channel_id=1, source_target_pairs={{0,16},{8,24},{16,0},{24,8},{1,17},{9,25},{17,1},{25,9},{2,18},{10... | collective-permute-start | bytes 98312 | tf_op jit(solution)/shard_map/ppermute | solution.py:290
  45.4 0.0 collective-permute-start.11
  45.4 13.0 %all_to_all.5.total_ref = f32[32,1,128]{2,1,0:T(1,128)S(1)} all-to-all(f32[32,1,128]{2,1,0:T(1,128)S(1)} %get-tuple-element.42), channel_id=1, replica_groups=mesh['ctx'=4,'ch'=8] {'ctx','ch'}, dimensions={0} | all-to-all | bytes 32768 | tf_op jit(solution)/shard_map/all_to_all | solution.py:327
  58.3 0.0 collective-permute-done.9.refs_1_
  58.4 0.0 collective-permute-done.10.refs_2_
  58.4 0.0 collective-permute-done.11.refs_3_
  58.4 0.9 %clip.1 = f32[64,512]{1,0:T(8,128)} custom-call(s32[1]{0:T(128)} %bitcast.pos_ref, f32[32,1,128]{2,1,0:T(1,128)S(1)} %all_to_all.5.total_ref, f32[16,4,128]{2,1,0:T(4,128)S(1)} %get-tuple-element.48.refs_0_, f32[16,4,128]{2,1,0:T(4,128)S(1)} %collective-permute-done.9.refs_1_, f32[16,4,128]{2,1,0:T(4,128)S(1)} %collective-permute-done.10.refs_2_, ...), custom_call_target="tpu_custom_call" | custom-call | flops 131072 | bytes 524288 | tf_op jit(solution)/shard_map/clip/pallas_call | solution.py:350
  (7 shorter events, 0.0 us)
Async XLA Ops:
  0.6 5.9 %copy-start = (bf16[1,512,1024]{2,1,0:T(8,128)(2,1)S(1)}, bf16[1,512,1024]{2,1,0:T(8,128)(2,1)}, u32[]{:S(2)}) copy-start(bf16[1,512,1024]{2,1,0:T(8,128)(2,1)} %left_ref.3) | copy-start | bytes 3145732
  0.6 5.9 %copy-start.1 = (bf16[1,512,1024]{2,1,0:T(8,128)(2,1)S(1)}, bf16[1,512,1024]{2,1,0:T(8,128)(2,1)}, u32[]{:S(2)}) copy-start(bf16[1,512,1024]{2,1,0:T(8,128)(2,1)} %right_ref.3) | copy-start | bytes 3145732
  3.3 7.0 %collective-permute-start = (bf16[16,2,2,16,128]{4,3,2,1,0:T(8,128)(2,1)}, bf16[16,2,2,16,128]{4,3,2,1,0:T(8,128)(2,1)S(1)}, u32[]{:S(2)}, u32[]{:S(2)}) collective-permute-start(bf16[16,2,2,16,128]{4,3,2,1,0:T(8,128)(2,1)} %get-tuple-element.29), channel_id=1, source_target_pairs={{0,8},{8,0},{16,24},{24,16},{1,9},{9,1},{17,25},{25,17},{2,10},{10... | collective-permute-start | bytes 786440 | tf_op jit(solution)/shard_map/ppermute | solution.py:290
  3.9 10.0 %collective-permute-start.1 = (bf16[16,2,2,16,128]{4,3,2,1,0:T(8,128)(2,1)}, bf16[16,2,2,16,128]{4,3,2,1,0:T(8,128)(2,1)S(1)}, u32[]{:S(2)}, u32[]{:S(2)}) collective-permute-start(bf16[16,2,2,16,128]{4,3,2,1,0:T(8,128)(2,1)} %get-tuple-element.30), channel_id=1, source_target_pairs={{0,16},{8,24},{16,0},{24,8},{1,17},{9,25},{17,1},{25,9},{2,18},{10... | collective-permute-start | bytes 786440 | tf_op jit(solution)/shard_map/ppermute | solution.py:290
  6.4 12.6 %copy-start.2 = (bf16[64,2048]{1,0:T(8,128)(2,1)S(1)}, bf16[64,2048]{1,0:T(8,128)(2,1)}, u32[]{:S(2)}) copy-start(bf16[64,2048]{1,0:T(8,128)(2,1)} %filt_ref.1) | copy-start | bytes 786436
  6.5 12.6 %copy-start.3 = (bf16[16,2,2,16,128]{4,3,2,1,0:T(8,128)(2,1)S(1)}, bf16[16,2,2,16,128]{4,3,2,1,0:T(8,128)(2,1)}, u32[]{:S(2)}) copy-start(bf16[16,2,2,16,128]{4,3,2,1,0:T(8,128)(2,1)} %get-tuple-element.28.refs_0_) | copy-start | bytes 786436
  6.5 12.6 %collective-permute-start.2 = (bf16[16,2,2,16,128]{4,3,2,1,0:T(8,128)(2,1)}, bf16[16,2,2,16,128]{4,3,2,1,0:T(8,128)(2,1)S(1)}, u32[]{:S(2)}, u32[]{:S(2)}) collective-permute-start(bf16[16,2,2,16,128]{4,3,2,1,0:T(8,128)(2,1)} %get-tuple-element.31), channel_id=1, source_target_pairs={{0,24},{8,16},{16,8},{24,0},{1,25},{9,17},{17,9},{25,1},{2,26},{10... | collective-permute-start | bytes 786440 | tf_op jit(solution)/shard_map/ppermute | solution.py:290
  8.2 17.7 %collective-permute-start.6 = (bf16[16,2,2,16,128]{4,3,2,1,0:T(8,128)(2,1)S(1)}, bf16[16,2,2,16,128]{4,3,2,1,0:T(8,128)(2,1)S(1)}, u32[]{:S(2)}, u32[]{:S(2)}) collective-permute-start(bf16[16,2,2,16,128]{4,3,2,1,0:T(8,128)(2,1)S(1)} %get-tuple-element.39), channel_id=1, source_target_pairs={{0,8},{8,0},{16,24},{24,16},{1,9},{9,1},{17,25},{25,17},{2,10},{10... | collective-permute-start | bytes 786440 | tf_op jit(solution)/shard_map/ppermute | solution.py:290
  8.5 17.5 %collective-permute-start.7 = (bf16[16,2,2,16,128]{4,3,2,1,0:T(8,128)(2,1)S(1)}, bf16[16,2,2,16,128]{4,3,2,1,0:T(8,128)(2,1)S(1)}, u32[]{:S(2)}, u32[]{:S(2)}) collective-permute-start(bf16[16,2,2,16,128]{4,3,2,1,0:T(8,128)(2,1)S(1)} %get-tuple-element.40), channel_id=1, source_target_pairs={{0,16},{8,24},{16,0},{24,8},{1,17},{9,25},{17,1},{25,9},{2,18},{10... | collective-permute-start | bytes 786440 | tf_op jit(solution)/shard_map/ppermute | solution.py:290
  10.4 19.8 %collective-permute-start.8 = (bf16[16,2,2,16,128]{4,3,2,1,0:T(8,128)(2,1)S(1)}, bf16[16,2,2,16,128]{4,3,2,1,0:T(8,128)(2,1)S(1)}, u32[]{:S(2)}, u32[]{:S(2)}) collective-permute-start(bf16[16,2,2,16,128]{4,3,2,1,0:T(8,128)(2,1)S(1)} %get-tuple-element.41), channel_id=1, source_target_pairs={{0,24},{8,16},{16,8},{24,0},{1,25},{9,17},{17,9},{25,1},{2,26},{10... | collective-permute-start | bytes 786440 | tf_op jit(solution)/shard_map/ppermute | solution.py:290
  23.6 11.9 %collective-permute-start.3 = (bf16[16,2,2,16,128]{4,3,2,1,0:T(8,128)(2,1)S(1)}, bf16[16,2,2,16,128]{4,3,2,1,0:T(8,128)(2,1)S(1)}, u32[]{:S(2)}, u32[]{:S(2)}) collective-permute-start(bf16[16,2,2,16,128]{4,3,2,1,0:T(8,128)(2,1)S(1)} %get-tuple-element.33), channel_id=1, source_target_pairs={{0,8},{8,0},{16,24},{24,16},{1,9},{9,1},{17,25},{25,17},{2,10},{10... | collective-permute-start | bytes 786440 | tf_op jit(solution)/shard_map/ppermute | solution.py:290
  24.0 12.3 %collective-permute-start.4 = (bf16[16,2,2,16,128]{4,3,2,1,0:T(8,128)(2,1)S(1)}, bf16[16,2,2,16,128]{4,3,2,1,0:T(8,128)(2,1)S(1)}, u32[]{:S(2)}, u32[]{:S(2)}) collective-permute-start(bf16[16,2,2,16,128]{4,3,2,1,0:T(8,128)(2,1)S(1)} %get-tuple-element.34), channel_id=1, source_target_pairs={{0,16},{8,24},{16,0},{24,8},{1,17},{9,25},{17,1},{25,9},{2,18},{10... | collective-permute-start | bytes 786440 | tf_op jit(solution)/shard_map/ppermute | solution.py:290
  25.9 15.5 %collective-permute-start.5 = (bf16[16,2,2,16,128]{4,3,2,1,0:T(8,128)(2,1)S(1)}, bf16[16,2,2,16,128]{4,3,2,1,0:T(8,128)(2,1)S(1)}, u32[]{:S(2)}, u32[]{:S(2)}) collective-permute-start(bf16[16,2,2,16,128]{4,3,2,1,0:T(8,128)(2,1)S(1)} %get-tuple-element.35), channel_id=1, source_target_pairs={{0,24},{8,16},{16,8},{24,0},{1,25},{9,17},{17,9},{25,1},{2,26},{10... | collective-permute-start | bytes 786440 | tf_op jit(solution)/shard_map/ppermute | solution.py:290
  43.4 14.9 %collective-permute-start.9 = (f32[16,4,128]{2,1,0:T(4,128)S(1)}, f32[16,4,128]{2,1,0:T(4,128)S(1)}, u32[]{:S(2)}, u32[]{:S(2)}) collective-permute-start(f32[16,4,128]{2,1,0:T(4,128)S(1)} %get-tuple-element.49), channel_id=1, source_target_pairs={{0,8},{8,0},{16,24},{24,16},{1,9},{9,1},{17,25},{25,17},{2,10},{10... | collective-permute-start | bytes 98312 | tf_op jit(solution)/shard_map/ppermute | solution.py:290
  43.6 14.7 %collective-permute-start.10 = (f32[16,4,128]{2,1,0:T(4,128)S(1)}, f32[16,4,128]{2,1,0:T(4,128)S(1)}, u32[]{:S(2)}, u32[]{:S(2)}) collective-permute-start(f32[16,4,128]{2,1,0:T(4,128)S(1)} %get-tuple-element.50), channel_id=1, source_target_pairs={{0,16},{8,24},{16,0},{24,8},{1,17},{9,25},{17,1},{25,9},{2,18},{10... | collective-permute-start | bytes 98312 | tf_op jit(solution)/shard_map/ppermute | solution.py:290
  45.4 13.0 %collective-permute-start.11 = (f32[16,4,128]{2,1,0:T(4,128)S(1)}, f32[16,4,128]{2,1,0:T(4,128)S(1)}, u32[]{:S(2)}, u32[]{:S(2)}) collective-permute-start(f32[16,4,128]{2,1,0:T(4,128)S(1)} %get-tuple-element.51), channel_id=1, source_target_pairs={{0,24},{8,16},{16,8},{24,0},{1,25},{9,17},{17,9},{25,1},{2,26},{10... | collective-permute-start | bytes 98312 | tf_op jit(solution)/shard_map/ppermute | solution.py:290

commit v4 on v3

--- a/solution.py
+++ b/solution.py
@@ -325,6 +325,7 @@
         name="lags",
     )(pos, *grad_got, *prod_got, conv[0])
     total = lax.all_to_all(spread, both, 0, 0, tiled=True)
+    raw = swap(raw)
     threshold = math.sqrt(WIDTH // GROUP * length)
     grad_q, grad_k, mark = pl.pallas_call(
         ungate_kernel,
@@ -345,8 +346,6 @@
         compiler_params=pltpu.CompilerParams(vmem_limit_bytes=16 << 20),
         name="ungate",
     )(pos, q_branch, k_branch, *back)
-    raw, mark = lax.optimization_barrier((raw, mark))
-    raw = swap(raw)
     grad_filters = pl.pallas_call(
         functools.partial(clip_kernel, threshold=threshold),
         in_specs=[smem] + [vmem] * (2 + owners),

time: 59.4 us -> 52.7 us (0.89)
  blocking collectives: 13 us -> 0 us
  starting transfers between devices: 9.52 us -> 15.9 us
  waiting for transfers between devices: 18.7 us -> 17.2 us
  Pallas kernels: 17.3 us -> 18.7 us
    all_to_all x1 -> x0, blocking collectives: 13 us -> none  [on_device(): total = lax.all_to_all(spread, both, 0, 0, tiled=True)]
    ppermute x12, waiting for transfers between devices: 18.7 us -> 12.2 us  [swap(): lax.ppermute(values[k], 'ctx', [(i, i ^ k) for i in range(owners)])]
    all_to_all x0 -> x1, starting transfers between devices: none -> 6.08 us  [on_device(): total = lax.all_to_all(spread, both, 0, 0, tiled=True)]
    all_to_all x0 -> x1, waiting for transfers between devices: none -> 5.02 us  [on_device(): total = lax.all_to_all(spread, both, 0, 0, tiled=True)]
    pallas_call x1, Pallas kernels: 4.63 us -> 5.36 us  [on_device(): pl.pallas_call(functools.partial(conv_kernel, owners=owners, unroll=unrol...]
    pallas_call x1, Pallas kernels: 5.35 us -> 5.96 us  [on_device(): pl.pallas_call(functools.partial(lag_kernel, owners=owners, unroll=unroll...]
  transfers between devices with their start and end apart: 12 -> 13, of which waited for: 5 -> 4; matrix products, arithmetic and copies ran while one was open for 0% -> 0% of each run, Pallas kernels for 20% -> 29%
where the time goes in v4:
time: 52.7 us; the launch traced here: 52.6 us
  Pallas kernels  18.7 us (35%)
  waiting for transfers between devices  17.2 us (33%)
  starting transfers between devices  15.9 us (30%)
  between operations  0.72 us (1%)
    ppermute x12, waiting for transfers between devices, swap(): lax.ppermute(values[k], 'ctx', [(i, i ^ k) for i in range(owners)])  12.2 us
    ppermute x12, starting transfers between devices, swap(): lax.ppermute(values[k], 'ctx', [(i, i ^ k) for i in range(owners)])  9.81 us
    all_to_all x1, starting transfers between devices, on_device(): total = lax.all_to_all(spread, both, 0, 0, tiled=True)  6.08 us
    pallas_call x1, Pallas kernels, on_device(): pl.pallas_call(functools.partial(lag_kernel, owners=owners, unroll=unroll...  5.96 us
    pallas_call x1, Pallas kernels, on_device(): pl.pallas_call(functools.partial(conv_kernel, owners=owners, unroll=unrol...  5.36 us
    all_to_all x1, waiting for transfers between devices, on_device(): total = lax.all_to_all(spread, both, 0, 0, tiled=True)  5.02 us
    pallas_call x2, Pallas kernels, gate(): pl.pallas_call(functools.partial(gate_kernel, reverse=reverse), in_specs=...  4.37 us
    pallas_call x1, Pallas kernels, on_device(): pl.pallas_call(ungate_kernel, in_specs=[smem] + [anywhere] * (2 + owners)...  2.07 us
  transfers between devices with their start and end apart: 13, of which 4 were waited for; matrix products, arithmetic and copies ran while one was open for 0% of the time, Pallas kernels for 29%

profile of v4, /device:TPU:0, one launch (start us, length us, event | category | flops | bytes accessed | tf_op | source)
XLA Modules:
  0.0 52.6 jit_solution(11971659230535094088)
XLA Ops:
  0.7 2.7 %gate_grad.1 = (bf16[16,2,2,16,128]{4,3,2,1,0:T(8,128)(2,1)}, bf16[16,2,2,16,128]{4,3,2,1,0:T(8,128)(2,1)}, bf16[16,2,2,16,128]{4,3,2,1,0:T(8,128)(2,1)}, bf16[16,2,2,16,128]{4,3,2,1,0:T(8,128)(2,1)}) custom-call(s32[1]{0:T(128)} %bitcast.pos_ref, bf16[1,512,1024]{2,1,0:T(8,128)(2,1)} %left_ref.2, bf16[1,512,1024]{2,1,0:T(8,128)(2,1)} %right_ref.2), custom_call_target="tpu_custom_call" | custom-call | flops 524288 | bytes 3145728 | tf_op jit(solution)/shard_map/gate_grad/pallas_call | solution.py:270
  3.3 0.5 collective-permute-start
  3.9 2.6 %collective-permute-start.1 = (bf16[16,2,2,16,128]{4,3,2,1,0:T(8,128)(2,1)}, bf16[16,2,2,16,128]{4,3,2,1,0:T(8,128)(2,1)S(1)}, u32[]{:S(2)}, u32[]{:S(2)}) collective-permute-start(bf16[16,2,2,16,128]{4,3,2,1,0:T(8,128)(2,1)} %get-tuple-element.25), channel_id=1, source_target_pairs={{0,16},{8,24},{16,0},{24,8},{1,17},{9,25},{17,1},{25,9},{2,18},{10... | collective-permute-start | bytes 786440 | tf_op jit(solution)/shard_map/ppermute | solution.py:290
  6.5 0.1 collective-permute-start.2
  6.5 1.7 %gate_prod.1 = (bf16[16,2,2,16,128]{4,3,2,1,0:T(8,128)(2,1)S(1)}, bf16[16,2,2,16,128]{4,3,2,1,0:T(8,128)(2,1)S(1)}, bf16[16,2,2,16,128]{4,3,2,1,0:T(8,128)(2,1)S(1)}, bf16[16,2,2,16,128]{4,3,2,1,0:T(8,128)(2,1)S(1)}) custom-call(s32[1]{0:T(128)} %bitcast.pos_ref, bf16[1,512,1024]{2,1,0:T(8,128)(2,1)S(1)} %copy-done, bf16[1,512,1024]{2,1,0:T(8,128)(2,1)S(1)} %copy-done.1), custom_call_target="tpu_custom_call" | custom-call | flops 524288 | bytes 3145728 | tf_op jit(solution)/shard_map/gate_prod/pallas_call | solution.py:270
  8.2 0.2 collective-permute-start.6
  8.4 1.9 %collective-permute-start.7 = (bf16[16,2,2,16,128]{4,3,2,1,0:T(8,128)(2,1)S(1)}, bf16[16,2,2,16,128]{4,3,2,1,0:T(8,128)(2,1)S(1)}, u32[]{:S(2)}, u32[]{:S(2)}) collective-permute-start(bf16[16,2,2,16,128]{4,3,2,1,0:T(8,128)(2,1)S(1)} %get-tuple-element.35), channel_id=1, source_target_pairs={{0,16},{8,24},{16,0},{24,8},{1,17},{9,25},{17,1},{25,9},{2,18},{10... | collective-permute-start | bytes 786440 | tf_op jit(solution)/shard_map/ppermute | solution.py:290
  10.4 0.0 collective-permute-done.refs_1_
  10.4 0.0 collective-permute-start.8
  10.4 3.4 %collective-permute-done.1.refs_2_ = bf16[16,2,2,16,128]{4,3,2,1,0:T(8,128)(2,1)S(1)} collective-permute-done((bf16[16,2,2,16,128]{4,3,2,1,0:T(8,128)(2,1)}, bf16[16,2,2,16,128]{4,3,2,1,0:T(8,128)(2,1)S(1)}, u32[]{:S(2)}, u32[]{:S(2)}) %collective-permute-start.1) | collective-permute-done | bytes 262176 | tf_op jit(solution)/shard_map/ppermute | solution.py:290
  13.8 5.2 %collective-permute-done.2.refs_3_ = bf16[16,2,2,16,128]{4,3,2,1,0:T(8,128)(2,1)S(1)} collective-permute-done((bf16[16,2,2,16,128]{4,3,2,1,0:T(8,128)(2,1)}, bf16[16,2,2,16,128]{4,3,2,1,0:T(8,128)(2,1)S(1)}, u32[]{:S(2)}, u32[]{:S(2)}) %collective-permute-start.2) | collective-permute-done | bytes 262176 | tf_op jit(solution)/shard_map/ppermute | solution.py:290
  19.0 5.4 %conv.1 = (bf16[16,2,2,16,128]{4,3,2,1,0:T(8,128)(2,1)S(1)}, bf16[16,2,2,16,128]{4,3,2,1,0:T(8,128)(2,1)S(1)}, bf16[16,2,2,16,128]{4,3,2,1,0:T(8,128)(2,1)}, bf16[16,2,2,16,128]{4,3,2,1,0:T(8,128)(2,1)S(1)}) custom-call(s32[1]{0:T(128)} %bitcast.pos_ref, bf16[64,2048]{1,0:T(8,128)(2,1)S(1)} %copy-done.2, bf16[16,2,2,16,128]{4,3,2,1,0:T(8,128)(2,1)S(1)} %copy-done.3, ...), custom_call_target="tpu_custom_call" | custom-call | flops 17179869184 | bytes 2359296 | tf_op jit(solution)/shard_map/conv/pallas_call | solution.py:296
  24.4 0.2 collective-permute-start.3
  24.6 2.0 %collective-permute-start.4 = (bf16[16,2,2,16,128]{4,3,2,1,0:T(8,128)(2,1)}, bf16[16,2,2,16,128]{4,3,2,1,0:T(8,128)(2,1)S(1)}, u32[]{:S(2)}, u32[]{:S(2)}) collective-permute-start(bf16[16,2,2,16,128]{4,3,2,1,0:T(8,128)(2,1)} %get-tuple-element.29), channel_id=1, source_target_pairs={{0,16},{8,24},{16,0},{24,8},{1,17},{9,25},{17,1},{25,9},{2,18},{10... | collective-permute-start | bytes 786440 | tf_op jit(solution)/shard_map/ppermute | solution.py:290
  26.6 0.0 collective-permute-done.6.refs_5_
  26.6 0.0 collective-permute-start.5
  26.6 0.0 collective-permute-done.7.refs_6_
  26.6 3.6 %collective-permute-done.8.refs_7_ = bf16[16,2,2,16,128]{4,3,2,1,0:T(8,128)(2,1)S(1)} collective-permute-done((bf16[16,2,2,16,128]{4,3,2,1,0:T(8,128)(2,1)S(1)}, bf16[16,2,2,16,128]{4,3,2,1,0:T(8,128)(2,1)S(1)}, u32[]{:S(2)}, u32[]{:S(2)}) %collective-permute-start.8) | collective-permute-done | bytes 262176 | tf_op jit(solution)/shard_map/ppermute | solution.py:290
  30.1 6.0 %lags.1 = (f32[16,4,128]{2,1,0:T(4,128)S(1)}, f32[16,4,128]{2,1,0:T(4,128)}, f32[16,4,128]{2,1,0:T(4,128)}, f32[16,4,128]{2,1,0:T(4,128)}, f32[32,1,128]{2,1,0:T(1,128)}) custom-call(s32[1]{0:T(128)} %bitcast.pos_ref, bf16[16,2,2,16,128]{4,3,2,1,0:T(8,128)(2,1)S(1)} %copy-done.3, bf16[16,2,2,16,128]{4,3,2,1,0:T(8,128)(2,1)S(1)} %collective-permute-done.refs_1_, ...), custom_call_target="tpu_custom_call" | custom-call | flops 17179869184 | bytes 2228224 | tf_op jit(solution)/shard_map/lags/pallas_call | solution.py:312
  36.1 0.3 collective-permute-start.9
  36.5 2.0 %collective-permute-start.10 = (f32[16,4,128]{2,1,0:T(4,128)}, f32[16,4,128]{2,1,0:T(4,128)S(1)}, u32[]{:S(2)}, u32[]{:S(2)}) collective-permute-start(f32[16,4,128]{2,1,0:T(4,128)} %get-tuple-element.40), channel_id=1, source_target_pairs={{0,16},{8,24},{16,0},{24,8},{1,17},{9,25},{17,1},{25,9},{2,18},{10... | collective-permute-start | bytes 98312 | tf_op jit(solution)/shard_map/ppermute | solution.py:290
  38.4 0.0 collective-permute-done.3.refs_1_
  38.4 0.0 collective-permute-start.11
  38.4 6.1 %all-to-all-start = ((f32[32,1,128]{2,1,0:T(1,128)}), f32[32,1,128]{2,1,0:T(1,128)S(1)}, u32[]{:S(2)}, u32[]{:S(2)}) async-start(f32[32,1,128]{2,1,0:T(1,128)} %get-tuple-element.37), calls=%async_computation | async-start | bytes 32768 | tf_op jit(solution)/shard_map/all_to_all | solution.py:327
  44.5 0.0 collective-permute-done.4.refs_2_
  44.5 0.0 collective-permute-done.5.refs_3_
  44.5 2.1 %ungate.1 = (bf16[1,512,1024]{2,1,0:T(8,128)(2,1)}, bf16[1,512,1024]{2,1,0:T(8,128)(2,1)}, f32[8,128]{1,0:T(8,128)S(1)}) custom-call(s32[1]{0:T(128)} %bitcast.pos_ref, bf16[1,512,1024]{2,1,0:T(8,128)(2,1)S(1)} %copy-done, bf16[1,512,1024]{2,1,0:T(8,128)(2,1)S(1)} %copy-done.1, bf16[16,2,2,16,128]{4,3,2,1,0:T(8,128)(2,1)S(1)} %get-tuple-element.27.refs_0_.refs_8_, ...), custom_call_target="tpu_custom_call" | custom-call | flops 1048576 | bytes 5242880 | tf_op jit(solution)/shard_map/ungate/pallas_call | solution.py:330
  46.6 5.0 %all-to-all-done.total_ref = f32[32,1,128]{2,1,0:T(1,128)S(1)} async-done(((f32[32,1,128]{2,1,0:T(1,128)}), f32[32,1,128]{2,1,0:T(1,128)S(1)}, u32[]{:S(2)}, u32[]{:S(2)}) %all-to-all-start) | async-done | bytes 16416 | tf_op jit(solution)/shard_map/all_to_all | solution.py:327
  51.6 0.0 collective-permute-done.9.refs_1_
  51.6 0.0 collective-permute-done.10.refs_2_
  51.6 0.0 collective-permute-done.11.refs_3_
  51.6 0.9 %clip.1 = f32[64,512]{1,0:T(8,128)} custom-call(s32[1]{0:T(128)} %bitcast.pos_ref, f32[32,1,128]{2,1,0:T(1,128)S(1)} %all-to-all-done.total_ref, f32[16,4,128]{2,1,0:T(4,128)S(1)} %get-tuple-element.38.refs_0_, f32[16,4,128]{2,1,0:T(4,128)S(1)} %collective-permute-done.9.refs_1_, f32[16,4,128]{2,1,0:T(4,128)S(1)} %collective-permute-done.10.refs_2_, ...), custom_call_target="tpu_custom_call" | custom-call | flops 131072 | bytes 524288 | tf_op jit(solution)/shard_map/clip/pallas_call | solution.py:349
  (8 shorter events, 0.0 us)
Async XLA Ops:
  0.6 5.9 %copy-start = (bf16[1,512,1024]{2,1,0:T(8,128)(2,1)S(1)}, bf16[1,512,1024]{2,1,0:T(8,128)(2,1)}, u32[]{:S(2)}) copy-start(bf16[1,512,1024]{2,1,0:T(8,128)(2,1)} %left_ref.3) | copy-start | bytes 3145732
  0.6 5.9 %copy-start.1 = (bf16[1,512,1024]{2,1,0:T(8,128)(2,1)S(1)}, bf16[1,512,1024]{2,1,0:T(8,128)(2,1)}, u32[]{:S(2)}) copy-start(bf16[1,512,1024]{2,1,0:T(8,128)(2,1)} %right_ref.3) | copy-start | bytes 3145732
  3.3 7.0 %collective-permute-start = (bf16[16,2,2,16,128]{4,3,2,1,0:T(8,128)(2,1)}, bf16[16,2,2,16,128]{4,3,2,1,0:T(8,128)(2,1)S(1)}, u32[]{:S(2)}, u32[]{:S(2)}) collective-permute-start(bf16[16,2,2,16,128]{4,3,2,1,0:T(8,128)(2,1)} %get-tuple-element.24), channel_id=1, source_target_pairs={{0,8},{8,0},{16,24},{24,16},{1,9},{9,1},{17,25},{25,17},{2,10},{10... | collective-permute-start | bytes 786440 | tf_op jit(solution)/shard_map/ppermute | solution.py:290
  3.9 10.0 %collective-permute-start.1 = (bf16[16,2,2,16,128]{4,3,2,1,0:T(8,128)(2,1)}, bf16[16,2,2,16,128]{4,3,2,1,0:T(8,128)(2,1)S(1)}, u32[]{:S(2)}, u32[]{:S(2)}) collective-permute-start(bf16[16,2,2,16,128]{4,3,2,1,0:T(8,128)(2,1)} %get-tuple-element.25), channel_id=1, source_target_pairs={{0,16},{8,24},{16,0},{24,8},{1,17},{9,25},{17,1},{25,9},{2,18},{10... | collective-permute-start | bytes 786440 | tf_op jit(solution)/shard_map/ppermute | solution.py:290
  6.4 12.6 %copy-start.2 = (bf16[64,2048]{1,0:T(8,128)(2,1)S(1)}, bf16[64,2048]{1,0:T(8,128)(2,1)}, u32[]{:S(2)}) copy-start(bf16[64,2048]{1,0:T(8,128)(2,1)} %filt_ref.1) | copy-start | bytes 786436
  6.4 12.6 %copy-start.3 = (bf16[16,2,2,16,128]{4,3,2,1,0:T(8,128)(2,1)S(1)}, bf16[16,2,2,16,128]{4,3,2,1,0:T(8,128)(2,1)}, u32[]{:S(2)}) copy-start(bf16[16,2,2,16,128]{4,3,2,1,0:T(8,128)(2,1)} %get-tuple-element.23.refs_0_) | copy-start | bytes 786436
  6.5 12.6 %collective-permute-start.2 = (bf16[16,2,2,16,128]{4,3,2,1,0:T(8,128)(2,1)}, bf16[16,2,2,16,128]{4,3,2,1,0:T(8,128)(2,1)S(1)}, u32[]{:S(2)}, u32[]{:S(2)}) collective-permute-start(bf16[16,2,2,16,128]{4,3,2,1,0:T(8,128)(2,1)} %get-tuple-element.26), channel_id=1, source_target_pairs={{0,24},{8,16},{16,8},{24,0},{1,25},{9,17},{17,9},{25,1},{2,26},{10... | collective-permute-start | bytes 786440 | tf_op jit(solution)/shard_map/ppermute | solution.py:290
  8.2 18.3 %collective-permute-start.6 = (bf16[16,2,2,16,128]{4,3,2,1,0:T(8,128)(2,1)S(1)}, bf16[16,2,2,16,128]{4,3,2,1,0:T(8,128)(2,1)S(1)}, u32[]{:S(2)}, u32[]{:S(2)}) collective-permute-start(bf16[16,2,2,16,128]{4,3,2,1,0:T(8,128)(2,1)S(1)} %get-tuple-element.34), channel_id=1, source_target_pairs={{0,8},{8,0},{16,24},{24,16},{1,9},{9,1},{17,25},{25,17},{2,10},{10... | collective-permute-start | bytes 786440 | tf_op jit(solution)/shard_map/ppermute | solution.py:290
  8.4 18.1 %collective-permute-start.7 = (bf16[16,2,2,16,128]{4,3,2,1,0:T(8,128)(2,1)S(1)}, bf16[16,2,2,16,128]{4,3,2,1,0:T(8,128)(2,1)S(1)}, u32[]{:S(2)}, u32[]{:S(2)}) collective-permute-start(bf16[16,2,2,16,128]{4,3,2,1,0:T(8,128)(2,1)S(1)} %get-tuple-element.35), channel_id=1, source_target_pairs={{0,16},{8,24},{16,0},{24,8},{1,17},{9,25},{17,1},{25,9},{2,18},{10... | collective-permute-start | bytes 786440 | tf_op jit(solution)/shard_map/ppermute | solution.py:290
  10.4 19.8 %collective-permute-start.8 = (bf16[16,2,2,16,128]{4,3,2,1,0:T(8,128)(2,1)S(1)}, bf16[16,2,2,16,128]{4,3,2,1,0:T(8,128)(2,1)S(1)}, u32[]{:S(2)}, u32[]{:S(2)}) collective-permute-start(bf16[16,2,2,16,128]{4,3,2,1,0:T(8,128)(2,1)S(1)} %get-tuple-element.36), channel_id=1, source_target_pairs={{0,24},{8,16},{16,8},{24,0},{1,25},{9,17},{17,9},{25,1},{2,26},{10... | collective-permute-start | bytes 786440 | tf_op jit(solution)/shard_map/ppermute | solution.py:290
  24.4 14.0 %collective-permute-start.3 = (bf16[16,2,2,16,128]{4,3,2,1,0:T(8,128)(2,1)S(1)}, bf16[16,2,2,16,128]{4,3,2,1,0:T(8,128)(2,1)S(1)}, u32[]{:S(2)}, u32[]{:S(2)}) collective-permute-start(bf16[16,2,2,16,128]{4,3,2,1,0:T(8,128)(2,1)S(1)} %get-tuple-element.28), channel_id=1, source_target_pairs={{0,8},{8,0},{16,24},{24,16},{1,9},{9,1},{17,25},{25,17},{2,10},{10... | collective-permute-start | bytes 786440 | tf_op jit(solution)/shard_map/ppermute | solution.py:290
  24.6 19.9 %collective-permute-start.4 = (bf16[16,2,2,16,128]{4,3,2,1,0:T(8,128)(2,1)}, bf16[16,2,2,16,128]{4,3,2,1,0:T(8,128)(2,1)S(1)}, u32[]{:S(2)}, u32[]{:S(2)}) collective-permute-start(bf16[16,2,2,16,128]{4,3,2,1,0:T(8,128)(2,1)} %get-tuple-element.29), channel_id=1, source_target_pairs={{0,16},{8,24},{16,0},{24,8},{1,17},{9,25},{17,1},{25,9},{2,18},{10... | collective-permute-start | bytes 786440 | tf_op jit(solution)/shard_map/ppermute | solution.py:290
  26.6 17.9 %collective-permute-start.5 = (bf16[16,2,2,16,128]{4,3,2,1,0:T(8,128)(2,1)S(1)}, bf16[16,2,2,16,128]{4,3,2,1,0:T(8,128)(2,1)S(1)}, u32[]{:S(2)}, u32[]{:S(2)}) collective-permute-start(bf16[16,2,2,16,128]{4,3,2,1,0:T(8,128)(2,1)S(1)} %get-tuple-element.30), channel_id=1, source_target_pairs={{0,24},{8,16},{16,8},{24,0},{1,25},{9,17},{17,9},{25,1},{2,26},{10... | collective-permute-start | bytes 786440 | tf_op jit(solution)/shard_map/ppermute | solution.py:290
  36.1 15.5 %collective-permute-start.9 = (f32[16,4,128]{2,1,0:T(4,128)}, f32[16,4,128]{2,1,0:T(4,128)S(1)}, u32[]{:S(2)}, u32[]{:S(2)}) collective-permute-start(f32[16,4,128]{2,1,0:T(4,128)} %get-tuple-element.39), channel_id=1, source_target_pairs={{0,8},{8,0},{16,24},{24,16},{1,9},{9,1},{17,25},{25,17},{2,10},{10... | collective-permute-start | bytes 98312 | tf_op jit(solution)/shard_map/ppermute | solution.py:290
  36.5 15.2 %collective-permute-start.10 = (f32[16,4,128]{2,1,0:T(4,128)}, f32[16,4,128]{2,1,0:T(4,128)S(1)}, u32[]{:S(2)}, u32[]{:S(2)}) collective-permute-start(f32[16,4,128]{2,1,0:T(4,128)} %get-tuple-element.40), channel_id=1, source_target_pairs={{0,16},{8,24},{16,0},{24,8},{1,17},{9,25},{17,1},{25,9},{2,18},{10... | collective-permute-start | bytes 98312 | tf_op jit(solution)/shard_map/ppermute | solution.py:290
  38.4 13.2 %collective-permute-start.11 = (f32[16,4,128]{2,1,0:T(4,128)}, f32[16,4,128]{2,1,0:T(4,128)S(1)}, u32[]{:S(2)}, u32[]{:S(2)}) collective-permute-start(f32[16,4,128]{2,1,0:T(4,128)} %get-tuple-element.41), channel_id=1, source_target_pairs={{0,24},{8,16},{16,8},{24,0},{1,25},{9,17},{17,9},{25,1},{2,26},{10... | collective-permute-start | bytes 98312 | tf_op jit(solution)/shard_map/ppermute | solution.py:290
  38.4 13.2 %all-to-all-start = ((f32[32,1,128]{2,1,0:T(1,128)}), f32[32,1,128]{2,1,0:T(1,128)S(1)}, u32[]{:S(2)}, u32[]{:S(2)}) async-start(f32[32,1,128]{2,1,0:T(1,128)} %get-tuple-element.37), calls=%async_computation | async-start | bytes 32768 | tf_op jit(solution)/shard_map/all_to_all | solution.py:327

commit v5 on v4

--- a/solution.py
+++ b/solution.py
@@ -15,10 +15,10 @@
 BF16, F32 = jnp.bfloat16, jnp.float32
 
 
-def gate_kernel(pos_ref, left_ref, right_ref, *refs, reverse):
+def gate_kernel(pos_ref, left_ref, right_ref, *refs, reverse, chunks):
     *outs, left, right, out, in_sem, out_sem = refs
     local = left.shape[0] // LANES
-    per_device = outs[0].shape[0]
+    each = outs[0].shape[0]
     copies = []
     for i in range(local):
         here = pl.ds(i * LANES, LANES)
@@ -44,12 +44,12 @@
             value = jnp.dot(flip, value, preferred_element_type=F32).astype(BF16)
         value = value.T
         out[i % 2, i // 2] = value.reshape(out.shape[2:])
-        for k, target in enumerate(outs):
-            first = jnp.bitwise_xor(pos_ref[0], k) * per_device
+        for n, target in enumerate(outs):
+            first = (jnp.bitwise_xor(pos_ref[0], n // chunks) * chunks + n % chunks) * each
             send = pltpu.make_async_copy(
-                out.at[i % 2, i // 2, pl.ds(first, per_device)],
+                out.at[i % 2, i // 2, pl.ds(first, each)],
                 target.at[:, i % 2, i // 2],
-                out_sem.at[i, k],
+                out_sem.at[i, n],
             )
             send.start()
             sends.append(send)
@@ -118,18 +118,15 @@
             target[half, pl.ds(at, count)] = source[f, half].reshape(count, LANES)
 
 
-def conv_kernel(pos_ref, filt_ref, *refs, owners, unroll):
-    ins, outs, refs = refs[:owners], refs[owners : 2 * owners], refs[2 * owners :]
-    taps, refs = refs[0], refs[1:]
-    toeps, pads, accs = refs[:unroll], refs[unroll : 2 * unroll], refs[2 * unroll :]
+def reverse_taps(owner, filt_ref, taps):
     per_device, blocks = taps.shape[0], taps.shape[1] - 1
-    rows = pads[0].shape[1]
     groups = filt_ref.shape[0]
     picks = max(per_device, 8)
     row_id = lax.broadcasted_iota(jnp.int32, (picks, groups), 0)
     col_id = lax.broadcasted_iota(jnp.int32, (picks, groups), 1)
-    pick = (col_id == row_id + pos_ref[0] * per_device).astype(BF16)
-    mine = jnp.dot(pick, filt_ref[...], preferred_element_type=F32).astype(BF16)
+    pick = (col_id == row_id + owner * per_device).astype(BF16)
+    width = min((blocks + 1) * LANES, filt_ref.shape[1])
+    mine = jnp.dot(pick, filt_ref[:, :width], preferred_element_type=F32).astype(BF16)
     empty = jnp.zeros((picks, LANES), BF16)
     mine = jnp.concatenate([empty, mine, empty], axis=1)
     row_id = lax.broadcasted_iota(jnp.int32, (2 * LANES, LANES), 0)
@@ -140,29 +137,45 @@
         back = jnp.dot(near, flip, preferred_element_type=F32)
         for f in range(per_device):
             taps[f, block] = back[f : f + 1]
-    for toep in toeps:
-        toep[0] = jnp.zeros((LANES, LANES), BF16)
+
+
+def build_blocks(taps, f, toep):
     row_id = lax.broadcasted_iota(jnp.int32, (LANES, LANES), 0)
     col_id = lax.broadcasted_iota(jnp.int32, (LANES, LANES), 1)
     upper = col_id >= row_id
+    before = None
+    for block in range(taps.shape[1]):
+        tap = jnp.broadcast_to(taps[f, block], (LANES, LANES))
+        rolled = pltpu.roll(tap, 0, 1, stride=1, stride_axis=0)
+        if block:
+            toep[block] = jnp.where(upper, before, rolled).astype(BF16)
+        before = rolled
+
+
+def weights(toep, pair):
+    at = 2 * pair + 1
+    top = jnp.concatenate([toep[at], toep[at - 1]], axis=1)
+    low = jnp.concatenate([toep[at + 1], toep[at]], axis=1)
+    return jnp.concatenate([top, low], axis=0)
+
+
+def conv_kernel(pos_ref, filt_ref, *refs, owners, unroll):
+    ins, outs, refs = refs[:owners], refs[owners : 2 * owners], refs[2 * owners :]
+    taps, refs = refs[0], refs[1:]
+    toeps, pads, accs = refs[:unroll], refs[unroll : 2 * unroll], refs[2 * unroll :]
+    per_device, blocks = taps.shape[0], taps.shape[1] - 1
+    rows = pads[0].shape[1]
+    reverse_taps(pos_ref[0], filt_ref, taps)
+    for toep in toeps:
+        toep[0] = jnp.zeros((LANES, LANES), BF16)
 
     def one(f, toep, pad, out):
-        before = None
-        for block in range(blocks + 1):
-            tap = jnp.broadcast_to(taps[f, block], (LANES, LANES))
-            rolled = pltpu.roll(tap, 0, 1, stride=1, stride_axis=0)
-            if block:
-                toep[block] = jnp.where(upper, before, rolled).astype(BF16)
-            before = rolled
+        build_blocks(taps, f, toep)
         acc = jnp.zeros((rows, 2 * LANES), F32)
         for pair in range(blocks // 2):
             start = pair * GROUP
             left = jnp.concatenate([pad[0, start:], pad[1, start:]], axis=1)
-            at = 2 * pair + 1
-            top = jnp.concatenate([toep[at], toep[at - 1]], axis=1)
-            low = jnp.concatenate([toep[at + 1], toep[at]], axis=1)
-            right = jnp.concatenate([top, low], axis=0)
-            part = jnp.dot(left, right, preferred_element_type=F32)
+            part = jnp.dot(left, weights(toep, pair), preferred_element_type=F32)
             if start:
                 part = jnp.concatenate([part, jnp.zeros((start, 2 * LANES), F32)], axis=0)
             acc = acc + part
@@ -186,39 +199,45 @@
     lax.fori_loop(0, per_device // unroll, some, 0)
 
 
-def lag_kernel(pos_ref, *refs, owners, unroll, scale):
-    grads, prods, refs = refs[:owners], refs[owners : 2 * owners], refs[2 * owners + 1 :]
+def lag_sums(pad, flipped, rows, blocks):
+    row_id = lax.broadcasted_iota(jnp.int32, (LANES, LANES), 0)
+    col_id = lax.broadcasted_iota(jnp.int32, (LANES, LANES), 1)
+    wraps = col_id <= row_id
+    prod = jnp.concatenate([flipped[half, :rows].T for half in range(2)], axis=1)
+    after = jnp.zeros((LANES, LANES), F32)
+    sums = {}
+    for pair in reversed(range(blocks // 2)):
+        start = pair * GROUP
+        here, later = slice(start, start + rows), slice(start + GROUP, start + GROUP + rows)
+        even = jnp.concatenate([pad[0, here], pad[1, here]], axis=0)
+        odd = jnp.concatenate([pad[1, here], pad[0, later]], axis=0)
+        both = jnp.dot(prod, jnp.concatenate([even, odd], axis=1), preferred_element_type=F32)
+        for half in (1, 0):
+            rolled = pltpu.roll(
+                both[:, half * LANES : (half + 1) * LANES], 1, 1, stride=1, stride_axis=0
+            )
+            part = jnp.where(wraps, rolled, after)
+            sums[2 * pair + half] = jnp.sum(part, axis=0, keepdims=True)
+            after = rolled
+    return sums
+
+
+def lag_kernel(pos_ref, *refs, owners, unroll, scale, first, last):
+    grads, prods, refs = refs[:owners], refs[owners : 2 * owners], refs[2 * owners :]
+    olds, refs = (refs[: owners + 1], refs[owners + 1 :]) if first else ([], refs[1:])
     raws, sum_ref, refs = refs[:owners], refs[owners], refs[owners + 1 :]
     pads, flips, lags_v, sq_v = refs[:unroll], refs[unroll : 2 * unroll], refs[-2], refs[-1]
-    per_device, per_owner = raws[0].shape[:2]
+    per_owner = raws[0].shape[1]
     blocks = owners * per_owner
     rows = flips[0].shape[1]
     for pad in pads:
         pad[:, rows:] = jnp.zeros((2, rows, LANES), BF16)
-    sq_v[...] = jnp.zeros_like(sq_v)
-    row_id = lax.broadcasted_iota(jnp.int32, (LANES, LANES), 0)
-    col_id = lax.broadcasted_iota(jnp.int32, (LANES, LANES), 1)
-    wraps = col_id <= row_id
+    sq_v[...] = olds[-1][...] if olds else jnp.zeros_like(sq_v)
+    for old, target in zip(olds, raws):
+        target[:first] = old[...]
 
     def one(slot, pad, flipped):
-        prod = jnp.concatenate([flipped[half].T for half in range(2)], axis=1)
-        after = jnp.zeros((LANES, LANES), F32)
-        sums = {}
-        for pair in reversed(range(blocks // 2)):
-            start = pair * GROUP
-            here, later = slice(start, start + rows), slice(start + GROUP, start + GROUP + rows)
-            even = jnp.concatenate([pad[0, here], pad[1, here]], axis=0)
-            odd = jnp.concatenate([pad[1, here], pad[0, later]], axis=0)
-            both = jnp.dot(
-                prod, jnp.concatenate([even, odd], axis=1), preferred_element_type=F32
-            )
-            for half in (1, 0):
-                rolled = pltpu.roll(
-                    both[:, half * LANES : (half + 1) * LANES], 1, 1, stride=1, stride_axis=0
-                )
-                part = jnp.where(wraps, rolled, after)
-                sums[2 * pair + half] = jnp.sum(part, axis=0, keepdims=True)
-                after = rolled
+        sums = lag_sums(pad, flipped, rows, blocks)
         for owner in range(owners):
             lags = jnp.concatenate(
                 [sums[owner * per_owner + n] for n in range(per_owner)], axis=0
@@ -228,18 +247,22 @@
 
     def some(i, carry):
         for u in range(unroll):
-            spread_rows(pos_ref, grads, i * unroll + u, pads[u])
+            spread_rows(pos_ref, grads, first + i * unroll + u, pads[u])
             spread_rows(pos_ref, prods, i * unroll + u, flips[u])
         for u in range(unroll):
             one(u, pads[u], flips[u])
         for u in range(unroll):
             for k, target in enumerate(raws):
-                target[i * unroll + u] = lags_v[u, jnp.bitwise_xor(pos_ref[0], k)]
+                target[first + i * unroll + u] = lags_v[u, jnp.bitwise_xor(pos_ref[0], k)]
         return carry
 
-    lax.fori_loop(0, per_device // unroll, some, 0)
+    lax.fori_loop(0, prods[0].shape[0] // unroll, some, 0)
+    if not last:
+        sum_ref[...] = sq_v[...]
+        return
     squares = jnp.sum(sq_v[...], axis=0, keepdims=True)
-    sum_ref[...] = jnp.broadcast_to(squares[None], sum_ref.shape)
+    sum_ref[...] = jnp.zeros_like(sum_ref)
+    sum_ref[:, :1] = jnp.broadcast_to(squares[None], (sum_ref.shape[0], 1, LANES))
 
 
 def cost(flops, moved):
@@ -266,23 +289,25 @@
     piece = jax.ShapeDtypeStruct((per_device,) + tail, BF16)
     lag_piece = jax.ShapeDtypeStruct((per_device, blocks // owners, LANES), F32)
 
-    def gate(left, right, reverse, limit, name):
-        return pl.pallas_call(
-            functools.partial(gate_kernel, reverse=reverse),
+    def gate(left, right, reverse, chunks, limit, name):
+        part = jax.ShapeDtypeStruct((per_device // chunks,) + tail, BF16)
+        out = pl.pallas_call(
+            functools.partial(gate_kernel, reverse=reverse, chunks=chunks),
             in_specs=[smem] + [pl.BlockSpec(memory_space=pltpu.HBM)] * 2,
-            out_specs=[anywhere] * owners,
-            out_shape=[piece] * owners,
+            out_specs=[anywhere] * (owners * chunks),
+            out_shape=[part] * (owners * chunks),
             scratch_shapes=[
                 pltpu.VMEM((block_len, chans), BF16),
                 pltpu.VMEM((block_len, chans), BF16),
                 pltpu.VMEM((2, local // 2, groups, GROUP, LANES), BF16),
                 pltpu.SemaphoreType.DMA((local, 2)),
-                pltpu.SemaphoreType.DMA((local, owners)),
+                pltpu.SemaphoreType.DMA((local, owners * chunks)),
             ],
             cost_estimate=cost(block_len * chans, 3 * size),
             compiler_params=pltpu.CompilerParams(vmem_limit_bytes=limit << 20),
             name=name,
         )(pos, left, right)
+        return [out[n::chunks] for n in range(chunks)]
 
     def swap(values):
         out = [values[0]]
@@ -290,8 +315,10 @@
             out.append(lax.ppermute(values[k], "ctx", [(i, i ^ k) for i in range(owners)]))
         return out
 
-    grad_got = swap(gate(grad_out, out_gate, False, 56, "gate_grad"))
-    prod_got = swap(gate(q_branch, k_branch, True, 12, "gate_prod"))
+    chunks = 1
+    (grad_send,) = gate(grad_out, out_gate, False, 1, 56, "gate_grad")
+    grad_got = swap(grad_send)
+    prod_got = [swap(part) for part in gate(q_branch, k_branch, True, chunks, 12, "gate_prod")]
     unroll = math.gcd(4, per_device)
     conv = pl.pallas_call(
         functools.partial(conv_kernel, owners=owners, unroll=unroll),
@@ -308,22 +335,31 @@
     back = swap(conv)
     both = ("ctx", "ch")
     count = lax.axis_size(both)
-    unroll = math.gcd(8, per_device)
-    *raw, spread = pl.pallas_call(
-        functools.partial(lag_kernel, owners=owners, unroll=unroll, scale=scale),
-        in_specs=[smem] + [vmem] * (2 * owners) + [anywhere],
-        out_specs=[vmem] * (owners + 1),
-        out_shape=[lag_piece] * owners + [jax.ShapeDtypeStruct((count, 1, LANES), F32)],
-        scratch_shapes=[pltpu.VMEM((2, 2 * rows, LANES), BF16)] * unroll
-        + [pltpu.VMEM((2, rows, LANES), BF16)] * unroll
-        + [
-            pltpu.VMEM((unroll, owners, blocks // owners, LANES), F32),
-            pltpu.VMEM((blocks // owners, LANES), F32),
-        ],
-        cost_estimate=cost(per_device * 2 * rows * length * 2048, 2 * size + per_device * length * 4),
-        compiler_params=pltpu.CompilerParams(vmem_limit_bytes=16 << 20),
-        name="lags",
-    )(pos, *grad_got, *prod_got, conv[0])
+    each = per_device // chunks
+    unroll = math.gcd(8, each)
+    old = [conv[0]]
+    for n in range(chunks):
+        last = n == chunks - 1
+        done = jax.ShapeDtypeStruct(((n + 1) * each, blocks // owners, LANES), F32)
+        sums = jax.ShapeDtypeStruct((count, 8, LANES) if last else (blocks // owners, LANES), F32)
+        old = pl.pallas_call(
+            functools.partial(
+                lag_kernel, owners=owners, unroll=unroll, scale=scale, first=n * each, last=last
+            ),
+            in_specs=[smem] + [vmem] * (2 * owners) + ([vmem] * (owners + 1) if n else [anywhere]),
+            out_specs=[vmem] * (owners + 1),
+            out_shape=[done] * owners + [sums],
+            scratch_shapes=[pltpu.VMEM((2, 2 * rows, LANES), BF16)] * unroll
+            + [pltpu.VMEM((2, rows, LANES), BF16)] * unroll
+            + [
+                pltpu.VMEM((unroll, owners, blocks // owners, LANES), F32),
+                pltpu.VMEM((blocks // owners, LANES), F32),
+            ],
+            cost_estimate=cost(each * 2 * rows * length * 2048, 2 * size),
+            compiler_params=pltpu.CompilerParams(vmem_limit_bytes=16 << 20),
+            name="lags",
+        )(pos, *grad_got, *prod_got[n], *old)
+    *raw, spread = old
     total = lax.all_to_all(spread, both, 0, 0, tiled=True)
     raw = swap(raw)
     threshold = math.sqrt(WIDTH // GROUP * length)

time: 52.7 us -> 51.2 us (0.972)
  waiting for transfers between devices: 17.2 us -> 15.6 us
    all_to_all x1, waiting for transfers between devices: 5.02 us -> 2.13 us  [on_device(): total = lax.all_to_all(spread, both, 0, 0, tiled=True)]
    ppermute x12, waiting for transfers between devices: 12.2 us -> 13.5 us  [swap(): lax.ppermute(values[k], 'ctx', [(i, i ^ k) for i in range(owners)])]
  transfers between devices with their start and end apart: 13 -> 13, of which waited for: 4 -> 6; matrix products, arithmetic and copies ran while one was open for 0% -> 0% of each run, Pallas kernels for 29% -> 30%
where the time goes in v5:
time: 51.2 us; the launch traced here: 51 us
  Pallas kernels  18.9 us (37%)
  starting transfers between devices  15.7 us (31%)
  waiting for transfers between devices  15.6 us (30%)
  between operations  0.72 us (1%)
    ppermute x12, waiting for transfers between devices, swap(): lax.ppermute(values[k], 'ctx', [(i, i ^ k) for i in range(owners)])  13.5 us
    ppermute x12, starting transfers between devices, swap(): lax.ppermute(values[k], 'ctx', [(i, i ^ k) for i in range(owners)])  9.52 us
    all_to_all x1, starting transfers between devices, on_device(): total = lax.all_to_all(spread, both, 0, 0, tiled=True)  6.23 us
    pallas_call x1, Pallas kernels, on_device(): pl.pallas_call(functools.partial(lag_kernel, owners=owners, unroll=unroll...  5.99 us
    pallas_call x1, Pallas kernels, on_device(): pl.pallas_call(functools.partial(conv_kernel, owners=owners, unroll=unrol...  5.55 us
    pallas_call x2, Pallas kernels, gate(): pl.pallas_call(functools.partial(gate_kernel, reverse=reverse, chunks=chu...  4.37 us
    all_to_all x1, waiting for transfers between devices, on_device(): total = lax.all_to_all(spread, both, 0, 0, tiled=True)  2.13 us
    pallas_call x1, Pallas kernels, on_device(): pl.pallas_call(ungate_kernel, in_specs=[smem] + [anywhere] * (2 + owners)...  2.07 us
  transfers between devices with their start and end apart: 13, of which 6 were waited for; matrix products, arithmetic and copies ran while one was open for 0% of the time, Pallas kernels for 30%

profile of v5, /device:TPU:0, one launch (start us, length us, event | category | flops | bytes accessed | tf_op | source)
XLA Modules:
  0.0 51.0 jit_solution(15969621733046399622)
XLA Ops:
  0.7 2.7 %gate_grad.1 = (bf16[16,2,2,16,128]{4,3,2,1,0:T(8,128)(2,1)}, bf16[16,2,2,16,128]{4,3,2,1,0:T(8,128)(2,1)}, bf16[16,2,2,16,128]{4,3,2,1,0:T(8,128)(2,1)}, bf16[16,2,2,16,128]{4,3,2,1,0:T(8,128)(2,1)}) custom-call(s32[1]{0:T(128)} %bitcast.pos_ref, bf16[1,512,1024]{2,1,0:T(8,128)(2,1)} %left_ref.2, bf16[1,512,1024]{2,1,0:T(8,128)(2,1)} %right_ref.2), custom_call_target="tpu_custom_call" | custom-call | flops 524288 | bytes 3145728 | tf_op jit(solution)/shard_map/gate_grad/pallas_call | solution.py:294
  3.3 0.5 %collective-permute-start = (bf16[16,2,2,16,128]{4,3,2,1,0:T(8,128)(2,1)}, bf16[16,2,2,16,128]{4,3,2,1,0:T(8,128)(2,1)S(1)}, u32[]{:S(2)}, u32[]{:S(2)}) collective-permute-start(bf16[16,2,2,16,128]{4,3,2,1,0:T(8,128)(2,1)} %get-tuple-element.24), channel_id=1, source_target_pairs={{0,8},{8,0},{16,24},{24,16},{1,9},{9,1},{17,25},{25,17},{2,10},{10... | collective-permute-start | bytes 786440 | tf_op jit(solution)/shard_map/ppermute | solution.py:315
  3.9 2.6 %collective-permute-start.1 = (bf16[16,2,2,16,128]{4,3,2,1,0:T(8,128)(2,1)}, bf16[16,2,2,16,128]{4,3,2,1,0:T(8,128)(2,1)S(1)}, u32[]{:S(2)}, u32[]{:S(2)}) collective-permute-start(bf16[16,2,2,16,128]{4,3,2,1,0:T(8,128)(2,1)} %get-tuple-element.25), channel_id=1, source_target_pairs={{0,16},{8,24},{16,0},{24,8},{1,17},{9,25},{17,1},{25,9},{2,18},{10... | collective-permute-start | bytes 786440 | tf_op jit(solution)/shard_map/ppermute | solution.py:315
  6.5 0.1 collective-permute-start.2
  6.5 1.7 %gate_prod.1 = (bf16[16,2,2,16,128]{4,3,2,1,0:T(8,128)(2,1)S(1)}, bf16[16,2,2,16,128]{4,3,2,1,0:T(8,128)(2,1)S(1)}, bf16[16,2,2,16,128]{4,3,2,1,0:T(8,128)(2,1)S(1)}, bf16[16,2,2,16,128]{4,3,2,1,0:T(8,128)(2,1)S(1)}) custom-call(s32[1]{0:T(128)} %bitcast.pos_ref, bf16[1,512,1024]{2,1,0:T(8,128)(2,1)S(1)} %copy-done, bf16[1,512,1024]{2,1,0:T(8,128)(2,1)S(1)} %copy-done.1), custom_call_target="tpu_custom_call" | custom-call | flops 524288 | bytes 3145728 | tf_op jit(solution)/shard_map/gate_prod/pallas_call | solution.py:294
  8.2 0.2 collective-permute-start.6
  8.4 1.9 %collective-permute-start.7 = (bf16[16,2,2,16,128]{4,3,2,1,0:T(8,128)(2,1)S(1)}, bf16[16,2,2,16,128]{4,3,2,1,0:T(8,128)(2,1)S(1)}, u32[]{:S(2)}, u32[]{:S(2)}) collective-permute-start(bf16[16,2,2,16,128]{4,3,2,1,0:T(8,128)(2,1)S(1)} %get-tuple-element.35), channel_id=1, source_target_pairs={{0,16},{8,24},{16,0},{24,8},{1,17},{9,25},{17,1},{25,9},{2,18},{10... | collective-permute-start | bytes 786440 | tf_op jit(solution)/shard_map/ppermute | solution.py:315
  10.4 0.0 collective-permute-done.refs_1_
  10.4 0.0 collective-permute-start.8
  10.4 3.4 %collective-permute-done.1.refs_2_ = bf16[16,2,2,16,128]{4,3,2,1,0:T(8,128)(2,1)S(1)} collective-permute-done((bf16[16,2,2,16,128]{4,3,2,1,0:T(8,128)(2,1)}, bf16[16,2,2,16,128]{4,3,2,1,0:T(8,128)(2,1)S(1)}, u32[]{:S(2)}, u32[]{:S(2)}) %collective-permute-start.1) | collective-permute-done | bytes 262176 | tf_op jit(solution)/shard_map/ppermute | solution.py:315
  13.8 5.2 %collective-permute-done.2.refs_3_ = bf16[16,2,2,16,128]{4,3,2,1,0:T(8,128)(2,1)S(1)} collective-permute-done((bf16[16,2,2,16,128]{4,3,2,1,0:T(8,128)(2,1)}, bf16[16,2,2,16,128]{4,3,2,1,0:T(8,128)(2,1)S(1)}, u32[]{:S(2)}, u32[]{:S(2)}) %collective-permute-start.2) | collective-permute-done | bytes 262176 | tf_op jit(solution)/shard_map/ppermute | solution.py:315
  19.0 5.6 %conv.1 = (bf16[16,2,2,16,128]{4,3,2,1,0:T(8,128)(2,1)S(1)}, bf16[16,2,2,16,128]{4,3,2,1,0:T(8,128)(2,1)}, bf16[16,2,2,16,128]{4,3,2,1,0:T(8,128)(2,1)}, bf16[16,2,2,16,128]{4,3,2,1,0:T(8,128)(2,1)}) custom-call(s32[1]{0:T(128)} %bitcast.pos_ref, bf16[64,2048]{1,0:T(8,128)(2,1)S(1)} %copy-done.2, bf16[16,2,2,16,128]{4,3,2,1,0:T(8,128)(2,1)S(1)} %copy-done.3, ...), custom_call_target="tpu_custom_call" | custom-call | flops 17179869184 | bytes 2359296 | tf_op jit(solution)/shard_map/conv/pallas_call | solution.py:323
  24.6 0.2 collective-permute-start.3
  24.8 2.0 %collective-permute-start.4 = (bf16[16,2,2,16,128]{4,3,2,1,0:T(8,128)(2,1)}, bf16[16,2,2,16,128]{4,3,2,1,0:T(8,128)(2,1)S(1)}, u32[]{:S(2)}, u32[]{:S(2)}) collective-permute-start(bf16[16,2,2,16,128]{4,3,2,1,0:T(8,128)(2,1)} %get-tuple-element.29), channel_id=1, source_target_pairs={{0,16},{8,24},{16,0},{24,8},{1,17},{9,25},{17,1},{25,9},{2,18},{10... | collective-permute-start | bytes 786440 | tf_op jit(solution)/shard_map/ppermute | solution.py:315
  26.8 0.0 collective-permute-done.6.refs_5_
  26.8 0.0 collective-permute-start.5
  26.8 0.0 collective-permute-done.7.refs_6_
  26.8 3.4 %collective-permute-done.8.refs_7_ = bf16[16,2,2,16,128]{4,3,2,1,0:T(8,128)(2,1)S(1)} collective-permute-done((bf16[16,2,2,16,128]{4,3,2,1,0:T(8,128)(2,1)S(1)}, bf16[16,2,2,16,128]{4,3,2,1,0:T(8,128)(2,1)S(1)}, u32[]{:S(2)}, u32[]{:S(2)}) %collective-permute-start.8) | collective-permute-done | bytes 262176 | tf_op jit(solution)/shard_map/ppermute | solution.py:315
  30.1 6.0 %lags.1 = (f32[16,4,128]{2,1,0:T(4,128)S(1)}, f32[16,4,128]{2,1,0:T(4,128)S(1)}, f32[16,4,128]{2,1,0:T(4,128)S(1)}, f32[16,4,128]{2,1,0:T(4,128)S(1)}, f32[32,8,128]{2,1,0:T(8,128)}) custom-call(s32[1]{0:T(128)} %bitcast.pos_ref, bf16[16,2,2,16,128]{4,3,2,1,0:T(8,128)(2,1)S(1)} %copy-done.3, bf16[16,2,2,16,128]{4,3,2,1,0:T(8,128)(2,1)S(1)} %collective-permute-done.refs_1_, ...), custom_call_target="tpu_custom_call" | custom-call | flops 17179869184 | bytes 2097152 | tf_op jit(solution)/shard_map/lags/pallas_call | solution.py:345
  36.1 6.2 %all-to-all-start = ((f32[32,8,128]{2,1,0:T(8,128)}), f32[32,8,128]{2,1,0:T(8,128)S(1)}, u32[]{:S(2)}, u32[]{:S(2)}) async-start(f32[32,8,128]{2,1,0:T(8,128)} %get-tuple-element.37), calls=%async_computation | async-start | bytes 262144 | tf_op jit(solution)/shard_map/all_to_all | solution.py:363
  42.4 0.3 collective-permute-start.9
  42.7 1.7 %collective-permute-start.10 = (f32[16,4,128]{2,1,0:T(4,128)S(1)}, f32[16,4,128]{2,1,0:T(4,128)S(1)}, u32[]{:S(2)}, u32[]{:S(2)}) collective-permute-start(f32[16,4,128]{2,1,0:T(4,128)S(1)} %get-tuple-element.40), channel_id=1, source_target_pairs={{0,16},{8,24},{16,0},{24,8},{1,17},{9,25},{17,1},{25,9},{2,18},{10... | collective-permute-start | bytes 98312 | tf_op jit(solution)/shard_map/ppermute | solution.py:315
  44.4 0.0 collective-permute-done.3.refs_1_
  44.4 0.0 collective-permute-start.11
  44.4 0.0 collective-permute-done.4.refs_2_
  44.4 0.0 collective-permute-done.5.refs_3_
  44.4 2.1 %ungate.1 = (bf16[1,512,1024]{2,1,0:T(8,128)(2,1)}, bf16[1,512,1024]{2,1,0:T(8,128)(2,1)}, f32[8,128]{1,0:T(8,128)S(1)}) custom-call(s32[1]{0:T(128)} %bitcast.pos_ref, bf16[1,512,1024]{2,1,0:T(8,128)(2,1)S(1)} %copy-done, bf16[1,512,1024]{2,1,0:T(8,128)(2,1)S(1)} %copy-done.1, bf16[16,2,2,16,128]{4,3,2,1,0:T(8,128)(2,1)S(1)} %get-tuple-element.27.refs_0_.refs_8_, ...), custom_call_target="tpu_custom_call" | custom-call | flops 1048576 | bytes 5242880 | tf_op jit(solution)/shard_map/ungate/pallas_call | solution.py:366
  46.5 0.0 collective-permute-done.9.refs_1_
  46.5 0.2 collective-permute-done.10.refs_2_
  46.7 1.3 %collective-permute-done.11.refs_3_ = f32[16,4,128]{2,1,0:T(4,128)S(1)} collective-permute-done((f32[16,4,128]{2,1,0:T(4,128)S(1)}, f32[16,4,128]{2,1,0:T(4,128)S(1)}, u32[]{:S(2)}, u32[]{:S(2)}) %collective-permute-start.11) | collective-permute-done | bytes 32800 | tf_op jit(solution)/shard_map/ppermute | solution.py:315
  48.0 2.1 %all-to-all-done.total_ref = f32[32,8,128]{2,1,0:T(8,128)S(1)} async-done(((f32[32,8,128]{2,1,0:T(8,128)}), f32[32,8,128]{2,1,0:T(8,128)S(1)}, u32[]{:S(2)}, u32[]{:S(2)}) %all-to-all-start) | async-done | bytes 131104 | tf_op jit(solution)/shard_map/all_to_all | solution.py:363
  50.1 0.9 %clip.1 = f32[64,512]{1,0:T(8,128)} custom-call(s32[1]{0:T(128)} %bitcast.pos_ref, f32[32,8,128]{2,1,0:T(8,128)S(1)} %all-to-all-done.total_ref, f32[16,4,128]{2,1,0:T(4,128)S(1)} %get-tuple-element.38.refs_0_, f32[16,4,128]{2,1,0:T(4,128)S(1)} %collective-permute-done.9.refs_1_, f32[16,4,128]{2,1,0:T(4,128)S(1)} %collective-permute-done.10.refs_2_, ...), custom_call_target="tpu_custom_call" | custom-call | flops 131072 | bytes 524288 | tf_op jit(solution)/shard_map/clip/pallas_call | solution.py:385
  (8 shorter events, 0.0 us)
Async XLA Ops:
  0.6 5.9 %copy-start = (bf16[1,512,1024]{2,1,0:T(8,128)(2,1)S(1)}, bf16[1,512,1024]{2,1,0:T(8,128)(2,1)}, u32[]{:S(2)}) copy-start(bf16[1,512,1024]{2,1,0:T(8,128)(2,1)} %left_ref.3) | copy-start | bytes 3145732
  0.6 5.9 %copy-start.1 = (bf16[1,512,1024]{2,1,0:T(8,128)(2,1)S(1)}, bf16[1,512,1024]{2,1,0:T(8,128)(2,1)}, u32[]{:S(2)}) copy-start(bf16[1,512,1024]{2,1,0:T(8,128)(2,1)} %right_ref.3) | copy-start | bytes 3145732
  3.3 7.0 %collective-permute-start = (bf16[16,2,2,16,128]{4,3,2,1,0:T(8,128)(2,1)}, bf16[16,2,2,16,128]{4,3,2,1,0:T(8,128)(2,1)S(1)}, u32[]{:S(2)}, u32[]{:S(2)}) collective-permute-start(bf16[16,2,2,16,128]{4,3,2,1,0:T(8,128)(2,1)} %get-tuple-element.24), channel_id=1, source_target_pairs={{0,8},{8,0},{16,24},{24,16},{1,9},{9,1},{17,25},{25,17},{2,10},{10... | collective-permute-start | bytes 786440 | tf_op jit(solution)/shard_map/ppermute | solution.py:315
  3.9 10.0 %collective-permute-start.1 = (bf16[16,2,2,16,128]{4,3,2,1,0:T(8,128)(2,1)}, bf16[16,2,2,16,128]{4,3,2,1,0:T(8,128)(2,1)S(1)}, u32[]{:S(2)}, u32[]{:S(2)}) collective-permute-start(bf16[16,2,2,16,128]{4,3,2,1,0:T(8,128)(2,1)} %get-tuple-element.25), channel_id=1, source_target_pairs={{0,16},{8,24},{16,0},{24,8},{1,17},{9,25},{17,1},{25,9},{2,18},{10... | collective-permute-start | bytes 786440 | tf_op jit(solution)/shard_map/ppermute | solution.py:315
  6.4 12.6 %copy-start.2 = (bf16[64,2048]{1,0:T(8,128)(2,1)S(1)}, bf16[64,2048]{1,0:T(8,128)(2,1)}, u32[]{:S(2)}) copy-start(bf16[64,2048]{1,0:T(8,128)(2,1)} %filt_ref.1) | copy-start | bytes 786436
  6.4 12.6 %copy-start.3 = (bf16[16,2,2,16,128]{4,3,2,1,0:T(8,128)(2,1)S(1)}, bf16[16,2,2,16,128]{4,3,2,1,0:T(8,128)(2,1)}, u32[]{:S(2)}) copy-start(bf16[16,2,2,16,128]{4,3,2,1,0:T(8,128)(2,1)} %get-tuple-element.23.refs_0_) | copy-start | bytes 786436
  6.5 12.6 %collective-permute-start.2 = (bf16[16,2,2,16,128]{4,3,2,1,0:T(8,128)(2,1)}, bf16[16,2,2,16,128]{4,3,2,1,0:T(8,128)(2,1)S(1)}, u32[]{:S(2)}, u32[]{:S(2)}) collective-permute-start(bf16[16,2,2,16,128]{4,3,2,1,0:T(8,128)(2,1)} %get-tuple-element.26), channel_id=1, source_target_pairs={{0,24},{8,16},{16,8},{24,0},{1,25},{9,17},{17,9},{25,1},{2,26},{10... | collective-permute-start | bytes 786440 | tf_op jit(solution)/shard_map/ppermute | solution.py:315
  8.2 18.5 %collective-permute-start.6 = (bf16[16,2,2,16,128]{4,3,2,1,0:T(8,128)(2,1)S(1)}, bf16[16,2,2,16,128]{4,3,2,1,0:T(8,128)(2,1)S(1)}, u32[]{:S(2)}, u32[]{:S(2)}) collective-permute-start(bf16[16,2,2,16,128]{4,3,2,1,0:T(8,128)(2,1)S(1)} %get-tuple-element.34), channel_id=1, source_target_pairs={{0,8},{8,0},{16,24},{24,16},{1,9},{9,1},{17,25},{25,17},{2,10},{10... | collective-permute-start | bytes 786440 | tf_op jit(solution)/shard_map/ppermute | solution.py:315
  8.4 18.3 %collective-permute-start.7 = (bf16[16,2,2,16,128]{4,3,2,1,0:T(8,128)(2,1)S(1)}, bf16[16,2,2,16,128]{4,3,2,1,0:T(8,128)(2,1)S(1)}, u32[]{:S(2)}, u32[]{:S(2)}) collective-permute-start(bf16[16,2,2,16,128]{4,3,2,1,0:T(8,128)(2,1)S(1)} %get-tuple-element.35), channel_id=1, source_target_pairs={{0,16},{8,24},{16,0},{24,8},{1,17},{9,25},{17,1},{25,9},{2,18},{10... | collective-permute-start | bytes 786440 | tf_op jit(solution)/shard_map/ppermute | solution.py:315
  10.4 19.8 %collective-permute-start.8 = (bf16[16,2,2,16,128]{4,3,2,1,0:T(8,128)(2,1)S(1)}, bf16[16,2,2,16,128]{4,3,2,1,0:T(8,128)(2,1)S(1)}, u32[]{:S(2)}, u32[]{:S(2)}) collective-permute-start(bf16[16,2,2,16,128]{4,3,2,1,0:T(8,128)(2,1)S(1)} %get-tuple-element.36), channel_id=1, source_target_pairs={{0,24},{8,16},{16,8},{24,0},{1,25},{9,17},{17,9},{25,1},{2,26},{10... | collective-permute-start | bytes 786440 | tf_op jit(solution)/shard_map/ppermute | solution.py:315
  24.6 19.8 %collective-permute-start.3 = (bf16[16,2,2,16,128]{4,3,2,1,0:T(8,128)(2,1)}, bf16[16,2,2,16,128]{4,3,2,1,0:T(8,128)(2,1)S(1)}, u32[]{:S(2)}, u32[]{:S(2)}) collective-permute-start(bf16[16,2,2,16,128]{4,3,2,1,0:T(8,128)(2,1)} %get-tuple-element.28), channel_id=1, source_target_pairs={{0,8},{8,0},{16,24},{24,16},{1,9},{9,1},{17,25},{25,17},{2,10},{10... | collective-permute-start | bytes 786440 | tf_op jit(solution)/shard_map/ppermute | solution.py:315
  24.8 19.6 %collective-permute-start.4 = (bf16[16,2,2,16,128]{4,3,2,1,0:T(8,128)(2,1)}, bf16[16,2,2,16,128]{4,3,2,1,0:T(8,128)(2,1)S(1)}, u32[]{:S(2)}, u32[]{:S(2)}) collective-permute-start(bf16[16,2,2,16,128]{4,3,2,1,0:T(8,128)(2,1)} %get-tuple-element.29), channel_id=1, source_target_pairs={{0,16},{8,24},{16,0},{24,8},{1,17},{9,25},{17,1},{25,9},{2,18},{10... | collective-permute-start | bytes 786440 | tf_op jit(solution)/shard_map/ppermute | solution.py:315
  26.8 17.6 %collective-permute-start.5 = (bf16[16,2,2,16,128]{4,3,2,1,0:T(8,128)(2,1)}, bf16[16,2,2,16,128]{4,3,2,1,0:T(8,128)(2,1)S(1)}, u32[]{:S(2)}, u32[]{:S(2)}) collective-permute-start(bf16[16,2,2,16,128]{4,3,2,1,0:T(8,128)(2,1)} %get-tuple-element.30), channel_id=1, source_target_pairs={{0,24},{8,16},{16,8},{24,0},{1,25},{9,17},{17,9},{25,1},{2,26},{10... | collective-permute-start | bytes 786440 | tf_op jit(solution)/shard_map/ppermute | solution.py:315
  36.1 14.0 %all-to-all-start = ((f32[32,8,128]{2,1,0:T(8,128)}), f32[32,8,128]{2,1,0:T(8,128)S(1)}, u32[]{:S(2)}, u32[]{:S(2)}) async-start(f32[32,8,128]{2,1,0:T(8,128)} %get-tuple-element.37), calls=%async_computation | async-start | bytes 262144 | tf_op jit(solution)/shard_map/all_to_all | solution.py:363
  42.4 4.1 %collective-permute-start.9 = (f32[16,4,128]{2,1,0:T(4,128)S(1)}, f32[16,4,128]{2,1,0:T(4,128)S(1)}, u32[]{:S(2)}, u32[]{:S(2)}) collective-permute-start(f32[16,4,128]{2,1,0:T(4,128)S(1)} %get-tuple-element.39), channel_id=1, source_target_pairs={{0,8},{8,0},{16,24},{24,16},{1,9},{9,1},{17,25},{25,17},{2,10},{10... | collective-permute-start | bytes 98312 | tf_op jit(solution)/shard_map/ppermute | solution.py:315
  42.7 4.0 %collective-permute-start.10 = (f32[16,4,128]{2,1,0:T(4,128)S(1)}, f32[16,4,128]{2,1,0:T(4,128)S(1)}, u32[]{:S(2)}, u32[]{:S(2)}) collective-permute-start(f32[16,4,128]{2,1,0:T(4,128)S(1)} %get-tuple-element.40), channel_id=1, source_target_pairs={{0,16},{8,24},{16,0},{24,8},{1,17},{9,25},{17,1},{25,9},{2,18},{10... | collective-permute-start | bytes 98312 | tf_op jit(solution)/shard_map/ppermute | solution.py:315
  44.4 3.6 %collective-permute-start.11 = (f32[16,4,128]{2,1,0:T(4,128)S(1)}, f32[16,4,128]{2,1,0:T(4,128)S(1)}, u32[]{:S(2)}, u32[]{:S(2)}) collective-permute-start(f32[16,4,128]{2,1,0:T(4,128)S(1)} %get-tuple-element.41), channel_id=1, source_target_pairs={{0,24},{8,16},{16,8},{24,0},{1,25},{9,17},{17,9},{25,1},{2,26},{10... | collective-permute-start | bytes 98312 | tf_op jit(solution)/shard_map/ppermute | solution.py:315

commit v6 on v5

--- a/solution.py
+++ b/solution.py
@@ -315,10 +315,15 @@
             out.append(lax.ppermute(values[k], "ctx", [(i, i ^ k) for i in range(owners)]))
         return out
 
-    chunks = 1
+    chunks = 2 if per_device % 16 == 0 else 1
     (grad_send,) = gate(grad_out, out_gate, False, 1, 56, "gate_grad")
     grad_got = swap(grad_send)
-    prod_got = [swap(part) for part in gate(q_branch, k_branch, True, chunks, 12, "gate_prod")]
+    prod_send = gate(q_branch, k_branch, True, chunks, 12, "gate_prod")
+    prod_got = []
+    for part in prod_send:
+        if prod_got:
+            part, prod_got[-1][1] = lax.optimization_barrier((part, prod_got[-1][1]))
+        prod_got.append(swap(part))
     unroll = math.gcd(4, per_device)
     conv = pl.pallas_call(
         functools.partial(conv_kernel, owners=owners, unroll=unroll),

time: 51.2 us -> 48.6 us (0.949)
  waiting for transfers between devices: 15.6 us -> 8.92 us
  starting transfers between devices: 15.7 us -> 19.5 us
    ppermute x12 -> x15, waiting for transfers between devices: 13.5 us -> 6.8 us  [swap(): lax.ppermute(values[k], 'ctx', [(i, i ^ k) for i in range(owners)])]
    ppermute x12 -> x15, starting transfers between devices: 9.52 us -> 14.1 us  [swap(): lax.ppermute(values[k], 'ctx', [(i, i ^ k) for i in range(owners)])]
    all_to_all x1, starting transfers between devices: 6.23 us -> 5.37 us  [on_device(): total = lax.all_to_all(spread, both, 0, 0, tiled=True)]
    pallas_call x1 -> x2, Pallas kernels: 5.99 us -> 6.05 us  [on_device(): pl.pallas_call(functools.partial(lag_kernel, owners=owners, unroll=unroll...]
  transfers between devices with their start and end apart: 13 -> 16, of which waited for: 6 -> 5; matrix products, arithmetic and copies ran while one was open for 0% -> 0% of each run, Pallas kernels for 30% -> 32%
where the time goes in v6:
time: 48.6 us; the launch traced here: 48.4 us
  starting transfers between devices  19.5 us (40%)
  Pallas kernels  19.3 us (40%)
  waiting for transfers between devices  8.92 us (18%)
  between operations  0.73 us (2%)
    ppermute x15, starting transfers between devices, swap(): lax.ppermute(values[k], 'ctx', [(i, i ^ k) for i in range(owners)])  14.1 us
    ppermute x15, waiting for transfers between devices, swap(): lax.ppermute(values[k], 'ctx', [(i, i ^ k) for i in range(owners)])  6.8 us
    pallas_call x2, Pallas kernels, on_device(): pl.pallas_call(functools.partial(lag_kernel, owners=owners, unroll=unroll...  6.05 us
    pallas_call x1, Pallas kernels, on_device(): pl.pallas_call(functools.partial(conv_kernel, owners=owners, unroll=unrol...  5.56 us
    all_to_all x1, starting transfers between devices, on_device(): total = lax.all_to_all(spread, both, 0, 0, tiled=True)  5.37 us
    pallas_call x2, Pallas kernels, gate(): pl.pallas_call(functools.partial(gate_kernel, reverse=reverse, chunks=chu...  4.66 us
    all_to_all x1, waiting for transfers between devices, on_device(): total = lax.all_to_all(spread, both, 0, 0, tiled=True)  2.13 us
    pallas_call x1, Pallas kernels, on_device(): pl.pallas_call(ungate_kernel, in_specs=[smem] + [anywhere] * (2 + owners)...  2.07 us
  transfers between devices with their start and end apart: 16, of which 5 were waited for; matrix products, arithmetic and copies ran while one was open for 0% of the time, Pallas kernels for 32%

profile of v6, /device:TPU:0, one launch (start us, length us, event | category | flops | bytes accessed | tf_op | source)
XLA Modules:
  0.0 48.4 jit_solution(2779379184572878215)
XLA Ops:
  0.7 2.7 %gate_grad.1 = (bf16[16,2,2,16,128]{4,3,2,1,0:T(8,128)(2,1)}, bf16[16,2,2,16,128]{4,3,2,1,0:T(8,128)(2,1)}, bf16[16,2,2,16,128]{4,3,2,1,0:T(8,128)(2,1)}, bf16[16,2,2,16,128]{4,3,2,1,0:T(8,128)(2,1)}) custom-call(s32[1]{0:T(128)} %bitcast.pos_ref, bf16[1,512,1024]{2,1,0:T(8,128)(2,1)} %left_ref.2, bf16[1,512,1024]{2,1,0:T(8,128)(2,1)} %right_ref.2), custom_call_target="tpu_custom_call" | custom-call | flops 524288 | bytes 3145728 | tf_op jit(solution)/shard_map/gate_grad/pallas_call | solution.py:294
  3.3 0.5 %collective-permute-start = (bf16[16,2,2,16,128]{4,3,2,1,0:T(8,128)(2,1)}, bf16[16,2,2,16,128]{4,3,2,1,0:T(8,128)(2,1)S(1)}, u32[]{:S(2)}, u32[]{:S(2)}) collective-permute-start(bf16[16,2,2,16,128]{4,3,2,1,0:T(8,128)(2,1)} %get-tuple-element.38), channel_id=1, source_target_pairs={{0,8},{8,0},{16,24},{24,16},{1,9},{9,1},{17,25},{25,17},{2,10},{10... | collective-permute-start | bytes 786440 | tf_op jit(solution)/shard_map/ppermute | solution.py:315
  3.9 2.6 %collective-permute-start.1 = (bf16[16,2,2,16,128]{4,3,2,1,0:T(8,128)(2,1)}, bf16[16,2,2,16,128]{4,3,2,1,0:T(8,128)(2,1)S(1)}, u32[]{:S(2)}, u32[]{:S(2)}) collective-permute-start(bf16[16,2,2,16,128]{4,3,2,1,0:T(8,128)(2,1)} %get-tuple-element.39), channel_id=1, source_target_pairs={{0,16},{8,24},{16,0},{24,8},{1,17},{9,25},{17,1},{25,9},{2,18},{10... | collective-permute-start | bytes 786440 | tf_op jit(solution)/shard_map/ppermute | solution.py:315
  6.5 0.1 collective-permute-start.2
  6.5 2.0 %gate_prod.1 = (bf16[8,2,2,16,128]{4,3,2,1,0:T(8,128)(2,1)S(1)}, bf16[8,2,2,16,128]{4,3,2,1,0:T(8,128)(2,1)S(1)}, bf16[8,2,2,16,128]{4,3,2,1,0:T(8,128)(2,1)S(1)...) custom-call(s32[1]{0:T(128)} %bitcast.pos_ref, ...), custom_call_target="tpu_custom_call" | custom-call | flops 524288 | bytes 3145728 | tf_op jit(solution)/shard_map/gate_prod/pallas_call | solution.py:294
  8.5 0.2 collective-permute-start.6
  8.7 1.9 %collective-permute-start.10 = (bf16[8,2,2,16,128]{4,3,2,1,0:T(8,128)(2,1)S(1)}, bf16[8,2,2,16,128]{4,3,2,1,0:T(8,128)(2,1)S(1)}, u32[]{:S(2)}, u32[]{:S(2)}) collective-permute-start(bf16[8,2,2,16,128]{4,3,2,1,0:T(8,128)(2,1)S(1)} %get-tuple-element.58), channel_id=1, source_target_pairs={{0,16},{8,24},{16,0},{24,8},{1,17},{9,25},{17,1},{25,9},{2,18},{10... | collective-permute-start | bytes 393224 | tf_op jit(solution)/shard_map/ppermute | solution.py:315
  10.7 0.0 collective-permute-done.6.refs_5_
  10.7 0.9 %collective-permute-start.11 = (bf16[8,2,2,16,128]{4,3,2,1,0:T(8,128)(2,1)S(1)}, bf16[8,2,2,16,128]{4,3,2,1,0:T(8,128)(2,1)S(1)}, u32[]{:S(2)}, u32[]{:S(2)}) collective-permute-start(bf16[8,2,2,16,128]{4,3,2,1,0:T(8,128)(2,1)S(1)} %get-tuple-element.59), channel_id=1, source_target_pairs={{0,24},{8,16},{16,8},{24,0},{1,25},{9,17},{17,9},{25,1},{2,26},{10... | collective-permute-start | bytes 393224 | tf_op jit(solution)/shard_map/ppermute | solution.py:315
  11.6 0.0 collective-permute-done.refs_1_
  11.6 0.2 collective-permute-start.7
  11.8 2.0 %collective-permute-done.1.refs_2_ = bf16[16,2,2,16,128]{4,3,2,1,0:T(8,128)(2,1)S(1)} collective-permute-done((bf16[16,2,2,16,128]{4,3,2,1,0:T(8,128)(2,1)}, bf16[16,2,2,16,128]{4,3,2,1,0:T(8,128)(2,1)S(1)}, u32[]{:S(2)}, u32[]{:S(2)}) %collective-permute-start.1) | collective-permute-done | bytes 262176 | tf_op jit(solution)/shard_map/ppermute | solution.py:315
  13.8 1.9 %collective-permute-start.8 = (bf16[8,2,2,16,128]{4,3,2,1,0:T(8,128)(2,1)S(1)}, bf16[8,2,2,16,128]{4,3,2,1,0:T(8,128)(2,1)S(1)}, u32[]{:S(2)}, u32[]{:S(2)}) collective-permute-start(bf16[8,2,2,16,128]{4,3,2,1,0:T(8,128)(2,1)S(1)} %get-tuple-element.54), channel_id=1, source_target_pairs={{0,16},{8,24},{16,0},{24,8},{1,17},{9,25},{17,1},{25,9},{2,18},{10... | collective-permute-start | bytes 393224 | tf_op jit(solution)/shard_map/ppermute | solution.py:315
  15.8 3.2 %collective-permute-done.2.refs_3_ = bf16[16,2,2,16,128]{4,3,2,1,0:T(8,128)(2,1)S(1)} collective-permute-done((bf16[16,2,2,16,128]{4,3,2,1,0:T(8,128)(2,1)}, bf16[16,2,2,16,128]{4,3,2,1,0:T(8,128)(2,1)S(1)}, u32[]{:S(2)}, u32[]{:S(2)}) %collective-permute-start.2) | collective-permute-done | bytes 262176 | tf_op jit(solution)/shard_map/ppermute | solution.py:315
  19.0 1.8 %collective-permute-start.9 = (bf16[8,2,2,16,128]{4,3,2,1,0:T(8,128)(2,1)S(1)}, bf16[8,2,2,16,128]{4,3,2,1,0:T(8,128)(2,1)S(1)}, u32[]{:S(2)}, u32[]{:S(2)}) collective-permute-start(bf16[8,2,2,16,128]{4,3,2,1,0:T(8,128)(2,1)S(1)} %get-tuple-element.55), channel_id=1, source_target_pairs={{0,24},{8,16},{16,8},{24,0},{1,25},{9,17},{17,9},{25,1},{2,26},{10... | collective-permute-start | bytes 393224 | tf_op jit(solution)/shard_map/ppermute | solution.py:315
  20.8 5.6 %conv.1 = (bf16[16,2,2,16,128]{4,3,2,1,0:T(8,128)(2,1)S(1)}, bf16[16,2,2,16,128]{4,3,2,1,0:T(8,128)(2,1)}, bf16[16,2,2,16,128]{4,3,2,1,0:T(8,128)(2,1)}, bf16[16,2,2,16,128]{4,3,2,1,0:T(8,128)(2,1)}) custom-call(s32[1]{0:T(128)} %bitcast.pos_ref, bf16[64,2048]{1,0:T(8,128)(2,1)S(1)} %copy-done.2, bf16[16,2,2,16,128]{4,3,2,1,0:T(8,128)(2,1)S(1)} %copy-done.3, ...), custom_call_target="tpu_custom_call" | custom-call | flops 17179869184 | bytes 2359296 | tf_op jit(solution)/shard_map/conv/pallas_call | solution.py:328
  26.4 0.0 collective-permute-done.10.refs_6_
  26.4 0.0 collective-permute-start.3
  26.4 0.4 collective-permute-start.4
  26.8 2.7 %lags.2 = (f32[8,4,128]{2,1,0:T(4,128)S(1)}, f32[8,4,128]{2,1,0:T(4,128)S(1)}, f32[8,4,128]{2,1,0:T(4,128)S(1)}, f32[8,4,128]{2,1,0:T(4,128)S(1)}, f32[4,128]{1,0:T(4,128)S(1)}) custom-call(s32[1]{0:T(128)} %bitcast.pos_ref, bf16[16,2,2,16,128]{4,3,2,1,0:T(8,128)(2,1)S(1)} %copy-done.3, bf16[16,2,2,16,128]{4,3,2,1,0:T(8,128)(2,1)S(1)} %collective-permute-done.refs_1_, ...), custom_call_target="tpu_custom_call" | custom-call | flops 8589934592 | bytes 2097152 | tf_op jit(solution)/shard_map/lags/pallas_call | solution.py:350
  29.5 1.5 %collective-permute-start.5 = (bf16[16,2,2,16,128]{4,3,2,1,0:T(8,128)(2,1)}, bf16[16,2,2,16,128]{4,3,2,1,0:T(8,128)(2,1)S(1)}, u32[]{:S(2)}, u32[]{:S(2)}) collective-permute-start(bf16[16,2,2,16,128]{4,3,2,1,0:T(8,128)(2,1)} %get-tuple-element.44), channel_id=1, source_target_pairs={{0,24},{8,16},{16,8},{24,0},{1,25},{9,17},{17,9},{25,1},{2,26},{10... | collective-permute-start | bytes 786440 | tf_op jit(solution)/shard_map/ppermute | solution.py:315
  31.0 3.4 %lags.3 = (f32[16,4,128]{2,1,0:T(4,128)S(1)}, f32[16,4,128]{2,1,0:T(4,128)S(1)}, f32[16,4,128]{2,1,0:T(4,128)S(1)}, f32[16,4,128]{2,1,0:T(4,128)S(1)}, f32[32,8,128]{2,1,0:T(8,128)}) custom-call(s32[1]{0:T(128)} %bitcast.pos_ref, bf16[16,2,2,16,128]{4,3,2,1,0:T(8,128)(2,1)S(1)} %copy-done.3, bf16[16,2,2,16,128]{4,3,2,1,0:T(8,128)(2,1)S(1)} %collective-permute-done.refs_1_, ...), custom_call_target="tpu_custom_call" | custom-call | flops 8589934592 | bytes 2097152 | tf_op jit(solution)/shard_map/lags/pallas_call | solution.py:350
  34.4 5.4 %all-to-all-start = ((f32[32,8,128]{2,1,0:T(8,128)}), f32[32,8,128]{2,1,0:T(8,128)S(1)}, u32[]{:S(2)}, u32[]{:S(2)}) async-start(f32[32,8,128]{2,1,0:T(8,128)} %get-tuple-element.65), calls=%async_computation | async-start | bytes 262144 | tf_op jit(solution)/shard_map/all_to_all | solution.py:368
  39.8 0.3 collective-permute-start.12
  40.1 1.7 %collective-permute-start.13 = (f32[16,4,128]{2,1,0:T(4,128)S(1)}, f32[16,4,128]{2,1,0:T(4,128)S(1)}, u32[]{:S(2)}, u32[]{:S(2)}) collective-permute-start(f32[16,4,128]{2,1,0:T(4,128)S(1)} %get-tuple-element.68), channel_id=1, source_target_pairs={{0,16},{8,24},{16,0},{24,8},{1,17},{9,25},{17,1},{25,9},{2,18},{10... | collective-permute-start | bytes 98312 | tf_op jit(solution)/shard_map/ppermute | solution.py:315
  41.8 0.0 collective-permute-done.5.refs_3_
  41.8 2.1 %ungate.1 = (bf16[1,512,1024]{2,1,0:T(8,128)(2,1)}, bf16[1,512,1024]{2,1,0:T(8,128)(2,1)}, f32[8,128]{1,0:T(8,128)S(1)}) custom-call(s32[1]{0:T(128)} %bitcast.pos_ref, bf16[1,512,1024]{2,1,0:T(8,128)(2,1)S(1)} %copy-done, bf16[1,512,1024]{2,1,0:T(8,128)(2,1)S(1)} %copy-done.1, bf16[16,2,2,16,128]{4,3,2,1,0:T(8,128)(2,1)S(1)} %get-tuple-element.41.refs_0_.refs_8_, ...), custom_call_target="tpu_custom_call" | custom-call | flops 1048576 | bytes 5242880 | tf_op jit(solution)/shard_map/ungate/pallas_call | solution.py:371
  43.9 0.0 collective-permute-done.12.refs_1_
  43.9 0.2 collective-permute-done.13.refs_2_
  44.0 1.3 %collective-permute-done.14.refs_3_ = f32[16,4,128]{2,1,0:T(4,128)S(1)} collective-permute-done((f32[16,4,128]{2,1,0:T(4,128)S(1)}, f32[16,4,128]{2,1,0:T(4,128)S(1)}, u32[]{:S(2)}, u32[]{:S(2)}) %collective-permute-start.14) | collective-permute-done | bytes 32800 | tf_op jit(solution)/shard_map/ppermute | solution.py:315
  45.4 2.1 %all-to-all-done.total_ref = f32[32,8,128]{2,1,0:T(8,128)S(1)} async-done(((f32[32,8,128]{2,1,0:T(8,128)}), f32[32,8,128]{2,1,0:T(8,128)S(1)}, u32[]{:S(2)}, u32[]{:S(2)}) %all-to-all-start) | async-done | bytes 131104 | tf_op jit(solution)/shard_map/all_to_all | solution.py:368
  47.5 0.9 %clip.1 = f32[64,512]{1,0:T(8,128)} custom-call(s32[1]{0:T(128)} %bitcast.pos_ref, f32[32,8,128]{2,1,0:T(8,128)S(1)} %all-to-all-done.total_ref, f32[16,4,128]{2,1,0:T(4,128)S(1)} %get-tuple-element.66.refs_0_, f32[16,4,128]{2,1,0:T(4,128)S(1)} %collective-permute-done.12.refs_1_, f32[16,4,128]{2,1,0:T(4,128)S(1)} %collective-permute-done.13.refs_2_, ...), custom_call_target="tpu_custom_call" | custom-call | flops 131072 | bytes 524288 | tf_op jit(solution)/shard_map/clip/pallas_call | solution.py:390
  (15 shorter events, 0.0 us)
Async XLA Ops:
  0.6 5.9 %copy-start = (bf16[1,512,1024]{2,1,0:T(8,128)(2,1)S(1)}, bf16[1,512,1024]{2,1,0:T(8,128)(2,1)}, u32[]{:S(2)}) copy-start(bf16[1,512,1024]{2,1,0:T(8,128)(2,1)} %left_ref.3) | copy-start | bytes 3145732
  0.6 5.9 %copy-start.1 = (bf16[1,512,1024]{2,1,0:T(8,128)(2,1)S(1)}, bf16[1,512,1024]{2,1,0:T(8,128)(2,1)}, u32[]{:S(2)}) copy-start(bf16[1,512,1024]{2,1,0:T(8,128)(2,1)} %right_ref.3) | copy-start | bytes 3145732
  3.3 8.3 %collective-permute-start = (bf16[16,2,2,16,128]{4,3,2,1,0:T(8,128)(2,1)}, bf16[16,2,2,16,128]{4,3,2,1,0:T(8,128)(2,1)S(1)}, u32[]{:S(2)}, u32[]{:S(2)}) collective-permute-start(bf16[16,2,2,16,128]{4,3,2,1,0:T(8,128)(2,1)} %get-tuple-element.38), channel_id=1, source_target_pairs={{0,8},{8,0},{16,24},{24,16},{1,9},{9,1},{17,25},{25,17},{2,10},{10... | collective-permute-start | bytes 786440 | tf_op jit(solution)/shard_map/ppermute | solution.py:315
  3.9 10.0 %collective-permute-start.1 = (bf16[16,2,2,16,128]{4,3,2,1,0:T(8,128)(2,1)}, bf16[16,2,2,16,128]{4,3,2,1,0:T(8,128)(2,1)S(1)}, u32[]{:S(2)}, u32[]{:S(2)}) collective-permute-start(bf16[16,2,2,16,128]{4,3,2,1,0:T(8,128)(2,1)} %get-tuple-element.39), channel_id=1, source_target_pairs={{0,16},{8,24},{16,0},{24,8},{1,17},{9,25},{17,1},{25,9},{2,18},{10... | collective-permute-start | bytes 786440 | tf_op jit(solution)/shard_map/ppermute | solution.py:315
  6.4 14.4 %copy-start.2 = (bf16[64,2048]{1,0:T(8,128)(2,1)S(1)}, bf16[64,2048]{1,0:T(8,128)(2,1)}, u32[]{:S(2)}) copy-start(bf16[64,2048]{1,0:T(8,128)(2,1)} %filt_ref.1) | copy-start | bytes 786436
  6.4 14.4 %copy-start.3 = (bf16[16,2,2,16,128]{4,3,2,1,0:T(8,128)(2,1)S(1)}, bf16[16,2,2,16,128]{4,3,2,1,0:T(8,128)(2,1)}, u32[]{:S(2)}) copy-start(bf16[16,2,2,16,128]{4,3,2,1,0:T(8,128)(2,1)} %get-tuple-element.37.refs_0_) | copy-start | bytes 786436
  6.5 12.6 %collective-permute-start.2 = (bf16[16,2,2,16,128]{4,3,2,1,0:T(8,128)(2,1)}, bf16[16,2,2,16,128]{4,3,2,1,0:T(8,128)(2,1)S(1)}, u32[]{:S(2)}, u32[]{:S(2)}) collective-permute-start(bf16[16,2,2,16,128]{4,3,2,1,0:T(8,128)(2,1)} %get-tuple-element.40), channel_id=1, source_target_pairs={{0,24},{8,16},{16,8},{24,0},{1,25},{9,17},{17,9},{25,1},{2,26},{10... | collective-permute-start | bytes 786440 | tf_op jit(solution)/shard_map/ppermute | solution.py:315
  8.5 2.1 %collective-permute-start.6 = (bf16[8,2,2,16,128]{4,3,2,1,0:T(8,128)(2,1)S(1)}, bf16[8,2,2,16,128]{4,3,2,1,0:T(8,128)(2,1)S(1)}, u32[]{:S(2)}, u32[]{:S(2)}) collective-permute-start(bf16[8,2,2,16,128]{4,3,2,1,0:T(8,128)(2,1)S(1)} %get-tuple-element.51), channel_id=1, source_target_pairs={{0,8},{8,0},{16,24},{24,16},{1,9},{9,1},{17,25},{25,17},{2,10},{10... | collective-permute-start | bytes 393224 | tf_op jit(solution)/shard_map/ppermute | solution.py:315
  8.7 17.6 %collective-permute-start.10 = (bf16[8,2,2,16,128]{4,3,2,1,0:T(8,128)(2,1)S(1)}, bf16[8,2,2,16,128]{4,3,2,1,0:T(8,128)(2,1)S(1)}, u32[]{:S(2)}, u32[]{:S(2)}) collective-permute-start(bf16[8,2,2,16,128]{4,3,2,1,0:T(8,128)(2,1)S(1)} %get-tuple-element.58), channel_id=1, source_target_pairs={{0,16},{8,24},{16,0},{24,8},{1,17},{9,25},{17,1},{25,9},{2,18},{10... | collective-permute-start | bytes 393224 | tf_op jit(solution)/shard_map/ppermute | solution.py:315
  10.7 15.7 %collective-permute-start.11 = (bf16[8,2,2,16,128]{4,3,2,1,0:T(8,128)(2,1)S(1)}, bf16[8,2,2,16,128]{4,3,2,1,0:T(8,128)(2,1)S(1)}, u32[]{:S(2)}, u32[]{:S(2)}) collective-permute-start(bf16[8,2,2,16,128]{4,3,2,1,0:T(8,128)(2,1)S(1)} %get-tuple-element.59), channel_id=1, source_target_pairs={{0,24},{8,16},{16,8},{24,0},{1,25},{9,17},{17,9},{25,1},{2,26},{10... | collective-permute-start | bytes 393224 | tf_op jit(solution)/shard_map/ppermute | solution.py:315
  11.6 17.8 %collective-permute-start.7 = (bf16[8,2,2,16,128]{4,3,2,1,0:T(8,128)(2,1)S(1)}, bf16[8,2,2,16,128]{4,3,2,1,0:T(8,128)(2,1)S(1)}, u32[]{:S(2)}, u32[]{:S(2)}) collective-permute-start(bf16[8,2,2,16,128]{4,3,2,1,0:T(8,128)(2,1)S(1)} %get-tuple-element.53), channel_id=1, source_target_pairs={{0,8},{8,0},{16,24},{24,16},{1,9},{9,1},{17,25},{25,17},{2,10},{10... | collective-permute-start | bytes 393224 | tf_op jit(solution)/shard_map/ppermute | solution.py:315
  13.8 17.2 %collective-permute-start.8 = (bf16[8,2,2,16,128]{4,3,2,1,0:T(8,128)(2,1)S(1)}, bf16[8,2,2,16,128]{4,3,2,1,0:T(8,128)(2,1)S(1)}, u32[]{:S(2)}, u32[]{:S(2)}) collective-permute-start(bf16[8,2,2,16,128]{4,3,2,1,0:T(8,128)(2,1)S(1)} %get-tuple-element.54), channel_id=1, source_target_pairs={{0,16},{8,24},{16,0},{24,8},{1,17},{9,25},{17,1},{25,9},{2,18},{10... | collective-permute-start | bytes 393224 | tf_op jit(solution)/shard_map/ppermute | solution.py:315
  19.0 12.0 %collective-permute-start.9 = (bf16[8,2,2,16,128]{4,3,2,1,0:T(8,128)(2,1)S(1)}, bf16[8,2,2,16,128]{4,3,2,1,0:T(8,128)(2,1)S(1)}, u32[]{:S(2)}, u32[]{:S(2)}) collective-permute-start(bf16[8,2,2,16,128]{4,3,2,1,0:T(8,128)(2,1)S(1)} %get-tuple-element.55), channel_id=1, source_target_pairs={{0,24},{8,16},{16,8},{24,0},{1,25},{9,17},{17,9},{25,1},{2,26},{10... | collective-permute-start | bytes 393224 | tf_op jit(solution)/shard_map/ppermute | solution.py:315
  26.4 15.4 %collective-permute-start.3 = (bf16[16,2,2,16,128]{4,3,2,1,0:T(8,128)(2,1)}, bf16[16,2,2,16,128]{4,3,2,1,0:T(8,128)(2,1)S(1)}, u32[]{:S(2)}, u32[]{:S(2)}) collective-permute-start(bf16[16,2,2,16,128]{4,3,2,1,0:T(8,128)(2,1)} %get-tuple-element.42), channel_id=1, source_target_pairs={{0,8},{8,0},{16,24},{24,16},{1,9},{9,1},{17,25},{25,17},{2,10},{10... | collective-permute-start | bytes 786440 | tf_op jit(solution)/shard_map/ppermute | solution.py:315
  26.4 15.4 %collective-permute-start.4 = (bf16[16,2,2,16,128]{4,3,2,1,0:T(8,128)(2,1)}, bf16[16,2,2,16,128]{4,3,2,1,0:T(8,128)(2,1)S(1)}, u32[]{:S(2)}, u32[]{:S(2)}) collective-permute-start(bf16[16,2,2,16,128]{4,3,2,1,0:T(8,128)(2,1)} %get-tuple-element.43), channel_id=1, source_target_pairs={{0,16},{8,24},{16,0},{24,8},{1,17},{9,25},{17,1},{25,9},{2,18},{10... | collective-permute-start | bytes 786440 | tf_op jit(solution)/shard_map/ppermute | solution.py:315
  29.5 12.3 %collective-permute-start.5 = (bf16[16,2,2,16,128]{4,3,2,1,0:T(8,128)(2,1)}, bf16[16,2,2,16,128]{4,3,2,1,0:T(8,128)(2,1)S(1)}, u32[]{:S(2)}, u32[]{:S(2)}) collective-permute-start(bf16[16,2,2,16,128]{4,3,2,1,0:T(8,128)(2,1)} %get-tuple-element.44), channel_id=1, source_target_pairs={{0,24},{8,16},{16,8},{24,0},{1,25},{9,17},{17,9},{25,1},{2,26},{10... | collective-permute-start | bytes 786440 | tf_op jit(solution)/shard_map/ppermute | solution.py:315
  34.4 13.1 %all-to-all-start = ((f32[32,8,128]{2,1,0:T(8,128)}), f32[32,8,128]{2,1,0:T(8,128)S(1)}, u32[]{:S(2)}, u32[]{:S(2)}) async-start(f32[32,8,128]{2,1,0:T(8,128)} %get-tuple-element.65), calls=%async_computation | async-start | bytes 262144 | tf_op jit(solution)/shard_map/all_to_all | solution.py:368
  39.8 4.1 %collective-permute-start.12 = (f32[16,4,128]{2,1,0:T(4,128)S(1)}, f32[16,4,128]{2,1,0:T(4,128)S(1)}, u32[]{:S(2)}, u32[]{:S(2)}) collective-permute-start(f32[16,4,128]{2,1,0:T(4,128)S(1)} %get-tuple-element.67), channel_id=1, source_target_pairs={{0,8},{8,0},{16,24},{24,16},{1,9},{9,1},{17,25},{25,17},{2,10},{10... | collective-permute-start | bytes 98312 | tf_op jit(solution)/shard_map/ppermute | solution.py:315
  40.1 4.0 %collective-permute-start.13 = (f32[16,4,128]{2,1,0:T(4,128)S(1)}, f32[16,4,128]{2,1,0:T(4,128)S(1)}, u32[]{:S(2)}, u32[]{:S(2)}) collective-permute-start(f32[16,4,128]{2,1,0:T(4,128)S(1)} %get-tuple-element.68), channel_id=1, source_target_pairs={{0,16},{8,24},{16,0},{24,8},{1,17},{9,25},{17,1},{25,9},{2,18},{10... | collective-permute-start | bytes 98312 | tf_op jit(solution)/shard_map/ppermute | solution.py:315
  41.8 3.6 %collective-permute-start.14 = (f32[16,4,128]{2,1,0:T(4,128)S(1)}, f32[16,4,128]{2,1,0:T(4,128)S(1)}, u32[]{:S(2)}, u32[]{:S(2)}) collective-permute-start(f32[16,4,128]{2,1,0:T(4,128)S(1)} %get-tuple-element.69), channel_id=1, source_target_pairs={{0,24},{8,16},{16,8},{24,0},{1,25},{9,17},{17,9},{25,1},{2,26},{10... | collective-permute-start | bytes 98312 | tf_op jit(solution)/shard_map/ppermute | solution.py:315

commit v7 on v6

--- a/solution.py
+++ b/solution.py
@@ -15,10 +15,11 @@
 BF16, F32 = jnp.bfloat16, jnp.float32
 
 
-def gate_kernel(pos_ref, left_ref, right_ref, *refs, reverse, chunks):
-    *outs, left, right, out, in_sem, out_sem = refs
+def gate_kernel(pos_ref, left_ref, right_ref, *refs, reverse, sizes):
+    _, *outs, mark_ref, left, right, out, in_sem, out_sem = refs
+    mark_ref[...] = jnp.zeros_like(mark_ref)
     local = left.shape[0] // LANES
-    each = outs[0].shape[0]
+    per_device = sum(sizes)
     copies = []
     for i in range(local):
         here = pl.ds(i * LANES, LANES)
@@ -45,9 +46,10 @@
         value = value.T
         out[i % 2, i // 2] = value.reshape(out.shape[2:])
         for n, target in enumerate(outs):
-            first = (jnp.bitwise_xor(pos_ref[0], n // chunks) * chunks + n % chunks) * each
+            k, chunk = divmod(n, len(sizes))
+            first = jnp.bitwise_xor(pos_ref[0], k) * per_device + sum(sizes[:chunk])
             send = pltpu.make_async_copy(
-                out.at[i % 2, i // 2, pl.ds(first, each)],
+                out.at[i % 2, i // 2, pl.ds(first, sizes[chunk])],
                 target.at[:, i % 2, i // 2],
                 out_sem.at[i, n],
             )
@@ -159,18 +161,29 @@
     return jnp.concatenate([top, low], axis=0)
 
 
-def conv_kernel(pos_ref, filt_ref, *refs, owners, unroll):
+def blocks_kernel(pos_ref, filt_ref, *refs):
+    _, *toeps, taps = refs
+    unroll = len(toeps)
+    reverse_taps(pos_ref[0], filt_ref, taps)
+
+    def some(i, carry):
+        for u in range(unroll):
+            toep = toeps[u].at[i]
+            toep[0] = jnp.zeros((LANES, LANES), BF16)
+            build_blocks(taps, i * unroll + u, toep)
+        return carry
+
+    lax.fori_loop(0, toeps[0].shape[0], some, 0)
+
+
+def conv_kernel(pos_ref, *refs, owners, unroll):
+    toeps, refs = refs[:unroll], refs[unroll:]
     ins, outs, refs = refs[:owners], refs[owners : 2 * owners], refs[2 * owners :]
-    taps, refs = refs[0], refs[1:]
-    toeps, pads, accs = refs[:unroll], refs[unroll : 2 * unroll], refs[2 * unroll :]
-    per_device, blocks = taps.shape[0], taps.shape[1] - 1
+    pads, accs = refs[:unroll], refs[unroll:]
+    per_device, blocks = ins[0].shape[0], toeps[0].shape[1] - 1
     rows = pads[0].shape[1]
-    reverse_taps(pos_ref[0], filt_ref, taps)
-    for toep in toeps:
-        toep[0] = jnp.zeros((LANES, LANES), BF16)
-
-    def one(f, toep, pad, out):
-        build_blocks(taps, f, toep)
+
+    def one(toep, pad, out):
         acc = jnp.zeros((rows, 2 * LANES), F32)
         for pair in range(blocks // 2):
             start = pair * GROUP
@@ -186,7 +199,7 @@
         for u in range(unroll):
             spread_rows(pos_ref, ins, i * unroll + u, pads[u])
         for u in range(unroll):
-            one(i * unroll + u, toeps[u], pads[u], accs[u])
+            one(toeps[u].at[i], pads[u], accs[u])
         for u in range(unroll):
             for k, target in enumerate(outs):
                 count = target.shape[2] * GROUP
@@ -233,8 +246,6 @@
     for pad in pads:
         pad[:, rows:] = jnp.zeros((2, rows, LANES), BF16)
     sq_v[...] = olds[-1][...] if olds else jnp.zeros_like(sq_v)
-    for old, target in zip(olds, raws):
-        target[:first] = old[...]
 
     def one(slot, pad, flipped):
         sums = lag_sums(pad, flipped, rows, blocks)
@@ -289,25 +300,25 @@
     piece = jax.ShapeDtypeStruct((per_device,) + tail, BF16)
     lag_piece = jax.ShapeDtypeStruct((per_device, blocks // owners, LANES), F32)
 
-    def gate(left, right, reverse, chunks, limit, name):
-        part = jax.ShapeDtypeStruct((per_device // chunks,) + tail, BF16)
+    def gate(left, right, after, reverse, sizes, limit, name):
+        parts = [jax.ShapeDtypeStruct((n,) + tail, BF16) for n in sizes]
         out = pl.pallas_call(
-            functools.partial(gate_kernel, reverse=reverse, chunks=chunks),
-            in_specs=[smem] + [pl.BlockSpec(memory_space=pltpu.HBM)] * 2,
-            out_specs=[anywhere] * (owners * chunks),
-            out_shape=[part] * (owners * chunks),
+            functools.partial(gate_kernel, reverse=reverse, sizes=sizes),
+            in_specs=[smem] + [anywhere] * 2 + [vmem],
+            out_specs=[anywhere] * (owners * len(sizes)) + [vmem],
+            out_shape=parts * owners + [jax.ShapeDtypeStruct((8, LANES), F32)],
             scratch_shapes=[
                 pltpu.VMEM((block_len, chans), BF16),
                 pltpu.VMEM((block_len, chans), BF16),
                 pltpu.VMEM((2, local // 2, groups, GROUP, LANES), BF16),
                 pltpu.SemaphoreType.DMA((local, 2)),
-                pltpu.SemaphoreType.DMA((local, owners * chunks)),
+                pltpu.SemaphoreType.DMA((local, owners * len(sizes))),
             ],
             cost_estimate=cost(block_len * chans, 3 * size),
             compiler_params=pltpu.CompilerParams(vmem_limit_bytes=limit << 20),
             name=name,
-        )(pos, left, right)
-        return [out[n::chunks] for n in range(chunks)]
+        )(pos, left, right, after)
+        return [out[n : -1 : len(sizes)] for n in range(len(sizes))], out[-1]
 
     def swap(values):
         out = [values[0]]
@@ -315,45 +326,55 @@
             out.append(lax.ppermute(values[k], "ctx", [(i, i ^ k) for i in range(owners)]))
         return out
 
-    chunks = 2 if per_device % 16 == 0 else 1
-    (grad_send,) = gate(grad_out, out_gate, False, 1, 56, "gate_grad")
+    sizes = (8, 4, 4) if per_device == 16 else (per_device,)
+    mark = jnp.zeros((8, LANES), F32)
+    (grad_send,), mark = gate(grad_out, out_gate, mark, False, (per_device,), 56, "gate_grad")
     grad_got = swap(grad_send)
-    prod_send = gate(q_branch, k_branch, True, chunks, 12, "gate_prod")
+    prod_send, mark = gate(q_branch, k_branch, mark, True, sizes, 12, "gate_prod")
     prod_got = []
     for part in prod_send:
         if prod_got:
             part, prod_got[-1][1] = lax.optimization_barrier((part, prod_got[-1][1]))
         prod_got.append(swap(part))
     unroll = math.gcd(4, per_device)
+    toeps = pl.pallas_call(
+        blocks_kernel,
+        in_specs=[smem, vmem, vmem],
+        out_specs=[vmem] * unroll,
+        out_shape=[
+            jax.ShapeDtypeStruct((per_device // unroll, blocks + 1, LANES, LANES), BF16)
+        ] * unroll,
+        scratch_shapes=[pltpu.VMEM((per_device, blocks + 1, 1, LANES), F32)],
+        cost_estimate=cost(1, 1),
+        compiler_params=pltpu.CompilerParams(vmem_limit_bytes=16 << 20),
+        name="blocks",
+    )(pos, filters, mark)
     conv = pl.pallas_call(
         functools.partial(conv_kernel, owners=owners, unroll=unroll),
-        in_specs=[smem] + [vmem] * (1 + owners),
+        in_specs=[smem] + [vmem] * (unroll + owners),
         out_specs=[vmem] * owners,
         out_shape=[piece] * owners,
-        scratch_shapes=[pltpu.VMEM((per_device, blocks + 1, 1, LANES), F32)]
-        + [pltpu.VMEM((blocks + 1, LANES, LANES), BF16)] * unroll
-        + [pltpu.VMEM((2, rows, LANES), BF16)] * (2 * unroll),
+        scratch_shapes=[pltpu.VMEM((2, rows, LANES), BF16)] * (2 * unroll),
         cost_estimate=cost(per_device * rows * length * 4096, 2 * size + groups * length * 2),
         compiler_params=pltpu.CompilerParams(vmem_limit_bytes=16 << 20),
         name="conv",
-    )(pos, filters, *grad_got)
+    )(pos, *toeps, *grad_got)
     back = swap(conv)
     both = ("ctx", "ch")
     count = lax.axis_size(both)
-    each = per_device // chunks
-    unroll = math.gcd(8, each)
     old = [conv[0]]
-    for n in range(chunks):
-        last = n == chunks - 1
-        done = jax.ShapeDtypeStruct(((n + 1) * each, blocks // owners, LANES), F32)
+    for n, each in enumerate(sizes):
+        last = n == len(sizes) - 1
+        unroll = math.gcd(8, each)
         sums = jax.ShapeDtypeStruct((count, 8, LANES) if last else (blocks // owners, LANES), F32)
         old = pl.pallas_call(
             functools.partial(
-                lag_kernel, owners=owners, unroll=unroll, scale=scale, first=n * each, last=last
+                lag_kernel, owners=owners, unroll=unroll, scale=scale, first=sum(sizes[:n]), last=last
             ),
             in_specs=[smem] + [vmem] * (2 * owners) + ([vmem] * (owners + 1) if n else [anywhere]),
             out_specs=[vmem] * (owners + 1),
-            out_shape=[done] * owners + [sums],
+            out_shape=[lag_piece] * owners + [sums],
+            input_output_aliases={2 * owners + 1 + k: k for k in range(owners)} if n else {},
             scratch_shapes=[pltpu.VMEM((2, 2 * rows, LANES), BF16)] * unroll
             + [pltpu.VMEM((2, rows, LANES), BF16)] * unroll
             + [

time: 48.6 us -> 50.9 us (1.047)
  Pallas kernels: 19.3 us -> 22.7 us
  waiting for transfers between devices: 8.92 us -> 5.93 us
  local copies, waits for them, and re-layouts: 0.02 us -> 1.29 us
    pallas_call x2 -> x3, Pallas kernels: 4.66 us -> 9.25 us  [the longest x2 6.21 us: gate(): pl.pallas_call(functools.partial(gate_kernel, reverse=reverse, sizes=size...]
    ppermute x15 -> x18, waiting for transfers between devices: 6.8 us -> 3.8 us  [swap(): lax.ppermute(values[k], 'ctx', [(i, i ^ k) for i in range(owners)])]
    pallas_call x1, Pallas kernels: 5.56 us -> 4.11 us  [on_device(): pl.pallas_call(functools.partial(conv_kernel, owners=owners, unroll=unrol...]
    unnamed x8 -> x10, local copies, waits for them, and re-layouts: 0.02 us -> 0.7 us
    broadcast_in_dim x0 -> x1, local copies, waits for them, and re-layouts: none -> 0.6 us  [on_device(): mark = jnp.zeros((8, LANES), F32)]
    ppermute x15 -> x18, starting transfers between devices: 14.1 us -> 14.6 us  [swap(): lax.ppermute(values[k], 'ctx', [(i, i ^ k) for i in range(owners)])]
    pallas_call x2 -> x3, Pallas kernels: 6.05 us -> 6.37 us  [on_device(): pl.pallas_call(functools.partial(lag_kernel, owners=owners, unroll=unroll...]
  transfers between devices with their start and end apart: 16 -> 19, of which waited for: 5 -> 5; matrix products, arithmetic and copies ran while one was open for 0% -> 0% of each run, Pallas kernels for 32% -> 35%
where the time goes in v7:
time: 50.9 us; the launch traced here: 50.6 us
  Pallas kernels  22.7 us (45%)
  starting transfers between devices  19.9 us (39%)
  waiting for transfers between devices  5.93 us (12%)
  local copies, waits for them, and re-layouts  1.29 us (3%)
  between operations  0.78 us (2%)
    ppermute x18, starting transfers between devices, swap(): lax.ppermute(values[k], 'ctx', [(i, i ^ k) for i in range(owners)])  14.6 us
    pallas_call x3, Pallas kernels, on_device(): pl.pallas_call(functools.partial(lag_kernel, owners=owners, unroll=unroll...  6.37 us
    pallas_call x2, Pallas kernels, gate(): pl.pallas_call(functools.partial(gate_kernel, reverse=reverse, sizes=size...  6.21 us
    all_to_all x1, starting transfers between devices, on_device(): total = lax.all_to_all(spread, both, 0, 0, tiled=True)  5.3 us
    pallas_call x1, Pallas kernels, on_device(): pl.pallas_call(functools.partial(conv_kernel, owners=owners, unroll=unrol...  4.11 us
    ppermute x18, waiting for transfers between devices, swap(): lax.ppermute(values[k], 'ctx', [(i, i ^ k) for i in range(owners)])  3.8 us
    pallas_call x1, Pallas kernels, on_device(): pl.pallas_call(blocks_kernel, in_specs=[smem, vmem, vmem], out_specs=[vme...  3.04 us
    all_to_all x1, waiting for transfers between devices, on_device(): total = lax.all_to_all(spread, both, 0, 0, tiled=True)  2.13 us
  transfers between devices with their start and end apart: 19, of which 5 were waited for; matrix products, arithmetic and copies ran while one was open for 0% of the time, Pallas kernels for 35%

profile of v7, /device:TPU:0, one launch (start us, length us, event | category | flops | bytes accessed | tf_op | source)
XLA Modules:
  0.0 50.6 jit_solution(3409543238170093578)
XLA Ops:
  0.7 0.6 %broadcast_in_dim.3.refs_0_ = f32[8,128]{1,0:T(8,128)} broadcast(f32[]{:T(128)} %constant.6.clone.1), dimensions={} | broadcast | bytes 4100 | tf_op jit(solution)/shard_map/broadcast_in_dim | solution.py:330
  1.3 3.9 %gate_grad.1 = (bf16[16,2,2,16,128]{4,3,2,1,0:T(8,128)(2,1)}, bf16[16,2,2,16,128]{4,3,2,1,0:T(8,128)(2,1)}, bf16[16,2,2,16,128]{4,3,2,1,0:T(8,128)(2,1)}, bf16[16,2,2,16,128]{4,3,2,1,0:T(8,128)(2,1)}, f32[8,128]{1,0:T(8,128)}) custom-call(s32[1]{0:T(128)} %bitcast.pos_ref, bf16[1,512,1024]{2,1,0:T(8,128)(2,1)} %left_ref.2, bf16[1,512,1024]{2,1,0:T(8,128)(2,1)} %right_ref.2, ...), custom_call_target="tpu_custom_call" | custom-call | flops 524288 | bytes 3145728 | tf_op jit(solution)/shard_map/gate_grad/pallas_call | solution.py:305
  5.2 0.5 %collective-permute-start = (bf16[16,2,2,16,128]{4,3,2,1,0:T(8,128)(2,1)}, bf16[16,2,2,16,128]{4,3,2,1,0:T(8,128)(2,1)S(1)}, u32[]{:S(2)}, u32[]{:S(2)}) collective-permute-start(bf16[16,2,2,16,128]{4,3,2,1,0:T(8,128)(2,1)} %get-tuple-element.64), channel_id=1, source_target_pairs={{0,8},{8,0},{16,24},{24,16},{1,9},{9,1},{17,25},{25,17},{2,10},{10... | collective-permute-start | bytes 786440 | tf_op jit(solution)/shard_map/ppermute | solution.py:326
  5.7 2.6 %collective-permute-start.1 = (bf16[16,2,2,16,128]{4,3,2,1,0:T(8,128)(2,1)}, bf16[16,2,2,16,128]{4,3,2,1,0:T(8,128)(2,1)S(1)}, u32[]{:S(2)}, u32[]{:S(2)}) collective-permute-start(bf16[16,2,2,16,128]{4,3,2,1,0:T(8,128)(2,1)} %get-tuple-element.65), channel_id=1, source_target_pairs={{0,16},{8,24},{16,0},{24,8},{1,17},{9,25},{17,1},{25,9},{2,18},{10... | collective-permute-start | bytes 786440 | tf_op jit(solution)/shard_map/ppermute | solution.py:326
  8.4 0.7 %copy-done.3 = f32[8,128]{1,0:T(8,128)S(1)} copy-done((f32[8,128]{1,0:T(8,128)S(1)}, f32[8,128]{1,0:T(8,128)}, u32[]{:S(2)}) %copy-start.3) | copy-done | bytes 4120
  9.0 2.3 %gate_prod.1 = (bf16[8,2,2,16,128]{4,3,2,1,0:T(8,128)(2,1)S(1)}, bf16[4,2,2,16,128]{4,3,2,1,0:T(8,128)(2,1)S(1)}, bf16[4,2,2,16,128]{4,3,2,1,0:T(8,128)(2,1)S(1)...) custom-call(s32[1]{0:T(128)} %bitcast.pos_ref, ...), custom_call_target="tpu_custom_call" | custom-call | flops 524288 | bytes 3145728 | tf_op jit(solution)/shard_map/gate_prod/pallas_call | solution.py:305
  11.4 0.2 collective-permute-start.6
  11.6 1.2 %collective-permute-done.6.refs_5_ = bf16[8,2,2,16,128]{4,3,2,1,0:T(8,128)(2,1)S(1)} collective-permute-done((bf16[8,2,2,16,128]{4,3,2,1,0:T(8,128)(2,1)S(1)}, bf16[8,2,2,16,128]{4,3,2,1,0:T(8,128)(2,1)S(1)}, u32[]{:S(2)}, u32[]{:S(2)}) %collective-permute-start.6) | collective-permute-done | bytes 131104 | tf_op jit(solution)/shard_map/ppermute | solution.py:326
  12.8 0.1 collective-permute-start.7
  12.9 1.9 %collective-permute-start.13 = (bf16[8,2,2,16,128]{4,3,2,1,0:T(8,128)(2,1)S(1)}, bf16[8,2,2,16,128]{4,3,2,1,0:T(8,128)(2,1)S(1)}, u32[]{:S(2)}, u32[]{:S(2)}) collective-permute-start(bf16[8,2,2,16,128]{4,3,2,1,0:T(8,128)(2,1)S(1)} %get-tuple-element.93), channel_id=1, source_target_pairs={{0,16},{8,24},{16,0},{24,8},{1,17},{9,25},{17,1},{25,9},{2,18},{10... | collective-permute-start | bytes 393224 | tf_op jit(solution)/shard_map/ppermute | solution.py:326
  14.8 3.0 %blocks.1 = (bf16[4,17,128,128]{3,2,1,0:T(8,128)(2,1)S(1)}, bf16[4,17,128,128]{3,2,1,0:T(8,128)(2,1)S(1)}, bf16[4,17,128,128]{3,2,1,0:T(8,128)(2,1)S(1)}, bf16[4,17,128,128]{3,2,1,0:T(8,128)(2,1)S(1)}) custom-call(s32[1]{0:T(128)} %bitcast.pos_ref, bf16[64,2048]{1,0:T(8,128)(2,1)S(1)} %copy-done.2, f32[8,128]{1,0:T(8,128)S(1)} %get-tuple-element.58.refs_0_), custom_call_target="tpu_custom_call" | custom-call | flops 1 | bytes 1 | tf_op jit(solution)/shard_map/blocks/pallas_call | solution.py:340
  17.9 0.1 collective-permute-start.14
  18.0 1.5 %collective-permute-start.11 = (bf16[4,2,2,16,128]{4,3,2,1,0:T(8,128)(2,1)S(1)}, bf16[4,2,2,16,128]{4,3,2,1,0:T(8,128)(2,1)S(1)}, u32[]{:S(2)}, u32[]{:S(2)}) collective-permute-start(bf16[4,2,2,16,128]{4,3,2,1,0:T(8,128)(2,1)S(1)} %get-tuple-element.89), channel_id=1, source_target_pairs={{0,16},{8,24},{16,0},{24,8},{1,17},{9,25},{17,1},{25,9},{2,18},{10... | collective-permute-start | bytes 196616 | tf_op jit(solution)/shard_map/ppermute | solution.py:326
  19.5 0.3 collective-permute-start.12
  19.8 1.0 %collective-permute-done.2.refs_7_.refs_3_ = bf16[16,2,2,16,128]{4,3,2,1,0:T(8,128)(2,1)S(1)} collective-permute-done((bf16[16,2,2,16,128]{4,3,2,1,0:T(8,128)(2,1)}, bf16[16,2,2,16,128]{4,3,2,1,0:T(8,128)(2,1)S(1)}, u32[]{:S(2)}, u32[]{:S(2)}) %collective-permute-start.2) | collective-permute-done | bytes 262176 | tf_op jit(solution)/shard_map/ppermute | solution.py:326
  20.8 0.2 collective-permute-start.8
  21.1 4.1 %conv.1 = (bf16[16,2,2,16,128]{4,3,2,1,0:T(8,128)(2,1)S(1)}, bf16[16,2,2,16,128]{4,3,2,1,0:T(8,128)(2,1)}, bf16[16,2,2,16,128]{4,3,2,1,0:T(8,128)(2,1)}, bf16[16,2,2,16,128]{4,3,2,1,0:T(8,128)(2,1)}) custom-call(s32[1]{0:T(128)} %bitcast.pos_ref, bf16[4,17,128,128]{3,2,1,0:T(8,128)(2,1)S(1)} %get-tuple-element.59.refs_0_, ...), custom_call_target="tpu_custom_call" | custom-call | flops 17179869184 | bytes 2359296 | tf_op jit(solution)/shard_map/conv/pallas_call | solution.py:352
  25.2 2.0 %collective-permute-start.9 = (bf16[4,2,2,16,128]{4,3,2,1,0:T(8,128)(2,1)S(1)}, bf16[4,2,2,16,128]{4,3,2,1,0:T(8,128)(2,1)S(1)}, u32[]{:S(2)}, u32[]{:S(2)}) collective-permute-start(bf16[4,2,2,16,128]{4,3,2,1,0:T(8,128)(2,1)S(1)} %get-tuple-element.85), channel_id=1, source_target_pairs={{0,16},{8,24},{16,0},{24,8},{1,17},{9,25},{17,1},{25,9},{2,18},{10... | collective-permute-start | bytes 196616 | tf_op jit(solution)/shard_map/ppermute | solution.py:326
  27.2 1.1 %collective-permute-start.10 = (bf16[4,2,2,16,128]{4,3,2,1,0:T(8,128)(2,1)S(1)}, bf16[4,2,2,16,128]{4,3,2,1,0:T(8,128)(2,1)S(1)}, u32[]{:S(2)}, u32[]{:S(2)}) collective-permute-start(bf16[4,2,2,16,128]{4,3,2,1,0:T(8,128)(2,1)S(1)} %get-tuple-element.86), channel_id=1, source_target_pairs={{0,24},{8,16},{16,8},{24,0},{1,25},{9,17},{17,9},{25,1},{2,26},{10... | collective-permute-start | bytes 196616 | tf_op jit(solution)/shard_map/ppermute | solution.py:326
  28.3 2.7 %lags.3 = (f32[16,4,128]{2,1,0:T(4,128)S(1)}, f32[16,4,128]{2,1,0:T(4,128)S(1)}, f32[16,4,128]{2,1,0:T(4,128)S(1)}, f32[16,4,128]{2,1,0:T(4,128)S(1)}, f32[4,128]{1,0:T(4,128)S(1)}) custom-call(s32[1]{0:T(128)} %bitcast.pos_ref, bf16[16,2,2,16,128]{4,3,2,1,0:T(8,128)(2,1)S(1)} %copy-done.4, ...), custom_call_target="tpu_custom_call" | custom-call | flops 8589934592 | bytes 2097152 | tf_op jit(solution)/shard_map/lags/pallas_call | solution.py:370
  31.0 1.1 %collective-permute-start.4 = (bf16[16,2,2,16,128]{4,3,2,1,0:T(8,128)(2,1)}, bf16[16,2,2,16,128]{4,3,2,1,0:T(8,128)(2,1)S(1)}, u32[]{:S(2)}, u32[]{:S(2)}) collective-permute-start(bf16[16,2,2,16,128]{4,3,2,1,0:T(8,128)(2,1)} %get-tuple-element.69), channel_id=1, source_target_pairs={{0,16},{8,24},{16,0},{24,8},{1,17},{9,25},{17,1},{25,9},{2,18},{10... | collective-permute-start | bytes 786440 | tf_op jit(solution)/shard_map/ppermute | solution.py:326
  32.1 1.5 %lags.4 = (f32[16,4,128]{2,1,0:T(4,128)S(1)}, f32[16,4,128]{2,1,0:T(4,128)S(1)}, f32[16,4,128]{2,1,0:T(4,128)S(1)}, f32[16,4,128]{2,1,0:T(4,128)S(1)}, f32[4,128]{1,0:T(4,128)S(1)}) custom-call(s32[1]{0:T(128)} %bitcast.pos_ref, ...), custom_call_target="tpu_custom_call", output_to_operand_aliasing={{0}: (9, {}), {1}: (10, {}), {2}: (11, {}), {3}: (12, {})} | custom-call | flops 4294967296 | bytes 2097152 | tf_op jit(solution)/shard_map/lags/pallas_call | solution.py:370
  33.6 0.8 %collective-permute-start.5 = (bf16[16,2,2,16,128]{4,3,2,1,0:T(8,128)(2,1)}, bf16[16,2,2,16,128]{4,3,2,1,0:T(8,128)(2,1)S(1)}, u32[]{:S(2)}, u32[]{:S(2)}) collective-permute-start(bf16[16,2,2,16,128]{4,3,2,1,0:T(8,128)(2,1)} %get-tuple-element.70), channel_id=1, source_target_pairs={{0,24},{8,16},{16,8},{24,0},{1,25},{9,17},{17,9},{25,1},{2,26},{10... | collective-permute-start | bytes 786440 | tf_op jit(solution)/shard_map/ppermute | solution.py:326
  34.5 2.2 %lags.5 = (f32[16,4,128]{2,1,0:T(4,128)S(1)}, f32[16,4,128]{2,1,0:T(4,128)S(1)}, f32[16,4,128]{2,1,0:T(4,128)S(1)}, f32[16,4,128]{2,1,0:T(4,128)S(1)}, f32[32,8,128]{2,1,0:T(8,128)}) custom-call(s32[1]{0:T(128)} %bitcast.pos_ref, ...), custom_call_target="tpu_custom_call", output_to_operand_aliasing={{0}: (9, {}), {1}: (10, {}), {2}: (11, {}), {3}: (12, {})} | custom-call | flops 4294967296 | bytes 2097152 | tf_op jit(solution)/shard_map/lags/pallas_call | solution.py:370
  36.7 5.3 %all-to-all-start = ((f32[32,8,128]{2,1,0:T(8,128)}), f32[32,8,128]{2,1,0:T(8,128)S(1)}, u32[]{:S(2)}, u32[]{:S(2)}) async-start(f32[32,8,128]{2,1,0:T(8,128)} %get-tuple-element.105), calls=%async_computation | async-start | bytes 262144 | tf_op jit(solution)/shard_map/all_to_all | solution.py:389
  42.0 0.3 collective-permute-start.15
  42.3 1.7 %collective-permute-start.16 = (f32[16,4,128]{2,1,0:T(4,128)S(1)}, f32[16,4,128]{2,1,0:T(4,128)S(1)}, u32[]{:S(2)}, u32[]{:S(2)}) collective-permute-start(f32[16,4,128]{2,1,0:T(4,128)S(1)} %get-tuple-element.108), channel_id=1, source_target_pairs={{0,16},{8,24},{16,0},{24,8},{1,17},{9,25},{17,1},{25,9},{2,18},{10... | collective-permute-start | bytes 98312 | tf_op jit(solution)/shard_map/ppermute | solution.py:326
  44.0 1.1 %collective-permute-done.5.refs_3_ = bf16[16,2,2,16,128]{4,3,2,1,0:T(8,128)(2,1)S(1)} collective-permute-done((bf16[16,2,2,16,128]{4,3,2,1,0:T(8,128)(2,1)}, bf16[16,2,2,16,128]{4,3,2,1,0:T(8,128)(2,1)S(1)}, u32[]{:S(2)}, u32[]{:S(2)}) %collective-permute-start.5) | collective-permute-done | bytes 262176 | tf_op jit(solution)/shard_map/ppermute | solution.py:326
  45.1 2.1 %ungate.1 = (bf16[1,512,1024]{2,1,0:T(8,128)(2,1)}, bf16[1,512,1024]{2,1,0:T(8,128)(2,1)}, f32[8,128]{1,0:T(8,128)S(1)}) custom-call(s32[1]{0:T(128)} %bitcast.pos_ref, bf16[1,512,1024]{2,1,0:T(8,128)(2,1)S(1)} %copy-done, bf16[1,512,1024]{2,1,0:T(8,128)(2,1)S(1)} %copy-done.1, bf16[16,2,2,16,128]{4,3,2,1,0:T(8,128)(2,1)S(1)} %get-tuple-element.67.refs_0_.refs_8_, ...), custom_call_target="tpu_custom_call" | custom-call | flops 1048576 | bytes 5242880 | tf_op jit(solution)/shard_map/ungate/pallas_call | solution.py:392
  47.2 0.4 collective-permute-done.17.refs_3_
  47.6 2.1 %all-to-all-done.total_ref = f32[32,8,128]{2,1,0:T(8,128)S(1)} async-done(((f32[32,8,128]{2,1,0:T(8,128)}), f32[32,8,128]{2,1,0:T(8,128)S(1)}, u32[]{:S(2)}, u32[]{:S(2)}) %all-to-all-start) | async-done | bytes 131104 | tf_op jit(solution)/shard_map/all_to_all | solution.py:389
  49.7 0.9 %clip.1 = f32[64,512]{1,0:T(8,128)} custom-call(s32[1]{0:T(128)} %bitcast.pos_ref, f32[32,8,128]{2,1,0:T(8,128)S(1)} %all-to-all-done.total_ref, f32[16,4,128]{2,1,0:T(4,128)S(1)} %get-tuple-element.106.refs_0_, f32[16,4,128]{2,1,0:T(4,128)S(1)} %collective-permute-done.15.refs_1_, f32[16,4,128]{2,1,0:T(4,128)S(1)} %collective-permute-done.16.refs_2_, ...), custom_call_target="tpu_custom_call" | custom-call | flops 131072 | bytes 524288 | tf_op jit(solution)/shard_map/clip/pallas_call | solution.py:411
  (26 shorter events, 0.2 us)
Async XLA Ops:
  0.6 7.7 %copy-start.1 = (bf16[1,512,1024]{2,1,0:T(8,128)(2,1)S(1)}, bf16[1,512,1024]{2,1,0:T(8,128)(2,1)}, u32[]{:S(2)}) copy-start(bf16[1,512,1024]{2,1,0:T(8,128)(2,1)} %k_ref.1) | copy-start | bytes 3145732
  0.6 7.7 %copy-start = (bf16[1,512,1024]{2,1,0:T(8,128)(2,1)S(1)}, bf16[1,512,1024]{2,1,0:T(8,128)(2,1)}, u32[]{:S(2)}) copy-start(bf16[1,512,1024]{2,1,0:T(8,128)(2,1)} %q_ref.1) | copy-start | bytes 3145732
  0.7 14.2 %copy-start.2 = (bf16[64,2048]{1,0:T(8,128)(2,1)S(1)}, bf16[64,2048]{1,0:T(8,128)(2,1)}, u32[]{:S(2)}) copy-start(bf16[64,2048]{1,0:T(8,128)(2,1)} %filt_ref.1) | copy-start | bytes 786436
  5.2 12.8 %collective-permute-start = (bf16[16,2,2,16,128]{4,3,2,1,0:T(8,128)(2,1)}, bf16[16,2,2,16,128]{4,3,2,1,0:T(8,128)(2,1)S(1)}, u32[]{:S(2)}, u32[]{:S(2)}) collective-permute-start(bf16[16,2,2,16,128]{4,3,2,1,0:T(8,128)(2,1)} %get-tuple-element.64), channel_id=1, source_target_pairs={{0,8},{8,0},{16,24},{24,16},{1,9},{9,1},{17,25},{25,17},{2,10},{10... | collective-permute-start | bytes 786440 | tf_op jit(solution)/shard_map/ppermute | solution.py:326
  5.7 13.8 %collective-permute-start.1 = (bf16[16,2,2,16,128]{4,3,2,1,0:T(8,128)(2,1)}, bf16[16,2,2,16,128]{4,3,2,1,0:T(8,128)(2,1)S(1)}, u32[]{:S(2)}, u32[]{:S(2)}) collective-permute-start(bf16[16,2,2,16,128]{4,3,2,1,0:T(8,128)(2,1)} %get-tuple-element.65), channel_id=1, source_target_pairs={{0,16},{8,24},{16,0},{24,8},{1,17},{9,25},{17,1},{25,9},{2,18},{10... | collective-permute-start | bytes 786440 | tf_op jit(solution)/shard_map/ppermute | solution.py:326
  8.3 12.6 %collective-permute-start.2 = (bf16[16,2,2,16,128]{4,3,2,1,0:T(8,128)(2,1)}, bf16[16,2,2,16,128]{4,3,2,1,0:T(8,128)(2,1)S(1)}, u32[]{:S(2)}, u32[]{:S(2)}) collective-permute-start(bf16[16,2,2,16,128]{4,3,2,1,0:T(8,128)(2,1)} %get-tuple-element.66), channel_id=1, source_target_pairs={{0,24},{8,16},{16,8},{24,0},{1,25},{9,17},{17,9},{25,1},{2,26},{10... | collective-permute-start | bytes 786440 | tf_op jit(solution)/shard_map/ppermute | solution.py:326
  8.4 0.7 %copy-start.3 = (f32[8,128]{1,0:T(8,128)S(1)}, f32[8,128]{1,0:T(8,128)}, u32[]{:S(2)}) copy-start(f32[8,128]{1,0:T(8,128)} %get-tuple-element.57.refs_0_) | copy-start | bytes 12292
  9.0 12.1 %copy-start.4 = (bf16[16,2,2,16,128]{4,3,2,1,0:T(8,128)(2,1)S(1)}, bf16[16,2,2,16,128]{4,3,2,1,0:T(8,128)(2,1)}, u32[]{:S(2)}) copy-start(bf16[16,2,2,16,128]{4,3,2,1,0:T(8,128)(2,1)} %get-tuple-element.63.refs_4_.refs_0_) | copy-start | bytes 786436
  11.4 1.4 %collective-permute-start.6 = (bf16[8,2,2,16,128]{4,3,2,1,0:T(8,128)(2,1)S(1)}, bf16[8,2,2,16,128]{4,3,2,1,0:T(8,128)(2,1)S(1)}, u32[]{:S(2)}, u32[]{:S(2)}) collective-permute-start(bf16[8,2,2,16,128]{4,3,2,1,0:T(8,128)(2,1)S(1)} %get-tuple-element.81), channel_id=1, source_target_pairs={{0,8},{8,0},{16,24},{24,16},{1,9},{9,1},{17,25},{25,17},{2,10},{10... | collective-permute-start | bytes 393224 | tf_op jit(solution)/shard_map/ppermute | solution.py:326
  12.8 5.1 %collective-permute-start.7 = (bf16[4,2,2,16,128]{4,3,2,1,0:T(8,128)(2,1)S(1)}, bf16[4,2,2,16,128]{4,3,2,1,0:T(8,128)(2,1)S(1)}, u32[]{:S(2)}, u32[]{:S(2)}) collective-permute-start(bf16[4,2,2,16,128]{4,3,2,1,0:T(8,128)(2,1)S(1)} %get-tuple-element.82), channel_id=1, source_target_pairs={{0,8},{8,0},{16,24},{24,16},{1,9},{9,1},{17,25},{25,17},{2,10},{10... | collective-permute-start | bytes 196616 | tf_op jit(solution)/shard_map/ppermute | solution.py:326
  12.9 12.3 %collective-permute-start.13 = (bf16[8,2,2,16,128]{4,3,2,1,0:T(8,128)(2,1)S(1)}, bf16[8,2,2,16,128]{4,3,2,1,0:T(8,128)(2,1)S(1)}, u32[]{:S(2)}, u32[]{:S(2)}) collective-permute-start(bf16[8,2,2,16,128]{4,3,2,1,0:T(8,128)(2,1)S(1)} %get-tuple-element.93), channel_id=1, source_target_pairs={{0,16},{8,24},{16,0},{24,8},{1,17},{9,25},{17,1},{25,9},{2,18},{10... | collective-permute-start | bytes 393224 | tf_op jit(solution)/shard_map/ppermute | solution.py:326
  17.9 9.3 %collective-permute-start.14 = (bf16[8,2,2,16,128]{4,3,2,1,0:T(8,128)(2,1)S(1)}, bf16[8,2,2,16,128]{4,3,2,1,0:T(8,128)(2,1)S(1)}, u32[]{:S(2)}, u32[]{:S(2)}) collective-permute-start(bf16[8,2,2,16,128]{4,3,2,1,0:T(8,128)(2,1)S(1)} %get-tuple-element.94), channel_id=1, source_target_pairs={{0,24},{8,16},{16,8},{24,0},{1,25},{9,17},{17,9},{25,1},{2,26},{10... | collective-permute-start | bytes 393224 | tf_op jit(solution)/shard_map/ppermute | solution.py:326
  18.0 12.9 %collective-permute-start.11 = (bf16[4,2,2,16,128]{4,3,2,1,0:T(8,128)(2,1)S(1)}, bf16[4,2,2,16,128]{4,3,2,1,0:T(8,128)(2,1)S(1)}, u32[]{:S(2)}, u32[]{:S(2)}) collective-permute-start(bf16[4,2,2,16,128]{4,3,2,1,0:T(8,128)(2,1)S(1)} %get-tuple-element.89), channel_id=1, source_target_pairs={{0,16},{8,24},{16,0},{24,8},{1,17},{9,25},{17,1},{25,9},{2,18},{10... | collective-permute-start | bytes 196616 | tf_op jit(solution)/shard_map/ppermute | solution.py:326
  19.5 11.5 %collective-permute-start.12 = (bf16[4,2,2,16,128]{4,3,2,1,0:T(8,128)(2,1)S(1)}, bf16[4,2,2,16,128]{4,3,2,1,0:T(8,128)(2,1)S(1)}, u32[]{:S(2)}, u32[]{:S(2)}) collective-permute-start(bf16[4,2,2,16,128]{4,3,2,1,0:T(8,128)(2,1)S(1)} %get-tuple-element.90), channel_id=1, source_target_pairs={{0,24},{8,16},{16,8},{24,0},{1,25},{9,17},{17,9},{25,1},{2,26},{10... | collective-permute-start | bytes 196616 | tf_op jit(solution)/shard_map/ppermute | solution.py:326
  20.8 12.8 %collective-permute-start.8 = (bf16[4,2,2,16,128]{4,3,2,1,0:T(8,128)(2,1)S(1)}, bf16[4,2,2,16,128]{4,3,2,1,0:T(8,128)(2,1)S(1)}, u32[]{:S(2)}, u32[]{:S(2)}) collective-permute-start(bf16[4,2,2,16,128]{4,3,2,1,0:T(8,128)(2,1)S(1)} %get-tuple-element.84), channel_id=1, source_target_pairs={{0,8},{8,0},{16,24},{24,16},{1,9},{9,1},{17,25},{25,17},{2,10},{10... | collective-permute-start | bytes 196616 | tf_op jit(solution)/shard_map/ppermute | solution.py:326
  25.2 9.3 %collective-permute-start.9 = (bf16[4,2,2,16,128]{4,3,2,1,0:T(8,128)(2,1)S(1)}, bf16[4,2,2,16,128]{4,3,2,1,0:T(8,128)(2,1)S(1)}, u32[]{:S(2)}, u32[]{:S(2)}) collective-permute-start(bf16[4,2,2,16,128]{4,3,2,1,0:T(8,128)(2,1)S(1)} %get-tuple-element.85), channel_id=1, source_target_pairs={{0,16},{8,24},{16,0},{24,8},{1,17},{9,25},{17,1},{25,9},{2,18},{10... | collective-permute-start | bytes 196616 | tf_op jit(solution)/shard_map/ppermute | solution.py:326
  27.2 7.3 %collective-permute-start.10 = (bf16[4,2,2,16,128]{4,3,2,1,0:T(8,128)(2,1)S(1)}, bf16[4,2,2,16,128]{4,3,2,1,0:T(8,128)(2,1)S(1)}, u32[]{:S(2)}, u32[]{:S(2)}) collective-permute-start(bf16[4,2,2,16,128]{4,3,2,1,0:T(8,128)(2,1)S(1)} %get-tuple-element.86), channel_id=1, source_target_pairs={{0,24},{8,16},{16,8},{24,0},{1,25},{9,17},{17,9},{25,1},{2,26},{10... | collective-permute-start | bytes 196616 | tf_op jit(solution)/shard_map/ppermute | solution.py:326
  30.9 13.0 %collective-permute-start.3 = (bf16[16,2,2,16,128]{4,3,2,1,0:T(8,128)(2,1)}, bf16[16,2,2,16,128]{4,3,2,1,0:T(8,128)(2,1)S(1)}, u32[]{:S(2)}, u32[]{:S(2)}) collective-permute-start(bf16[16,2,2,16,128]{4,3,2,1,0:T(8,128)(2,1)} %get-tuple-element.68), channel_id=1, source_target_pairs={{0,8},{8,0},{16,24},{24,16},{1,9},{9,1},{17,25},{25,17},{2,10},{10... | collective-permute-start | bytes 786440 | tf_op jit(solution)/shard_map/ppermute | solution.py:326
  31.0 13.0 %collective-permute-start.4 = (bf16[16,2,2,16,128]{4,3,2,1,0:T(8,128)(2,1)}, bf16[16,2,2,16,128]{4,3,2,1,0:T(8,128)(2,1)S(1)}, u32[]{:S(2)}, u32[]{:S(2)}) collective-permute-start(bf16[16,2,2,16,128]{4,3,2,1,0:T(8,128)(2,1)} %get-tuple-element.69), channel_id=1, source_target_pairs={{0,16},{8,24},{16,0},{24,8},{1,17},{9,25},{17,1},{25,9},{2,18},{10... | collective-permute-start | bytes 786440 | tf_op jit(solution)/shard_map/ppermute | solution.py:326
  33.6 11.5 %collective-permute-start.5 = (bf16[16,2,2,16,128]{4,3,2,1,0:T(8,128)(2,1)}, bf16[16,2,2,16,128]{4,3,2,1,0:T(8,128)(2,1)S(1)}, u32[]{:S(2)}, u32[]{:S(2)}) collective-permute-start(bf16[16,2,2,16,128]{4,3,2,1,0:T(8,128)(2,1)} %get-tuple-element.70), channel_id=1, source_target_pairs={{0,24},{8,16},{16,8},{24,0},{1,25},{9,17},{17,9},{25,1},{2,26},{10... | collective-permute-start | bytes 786440 | tf_op jit(solution)/shard_map/ppermute | solution.py:326
  36.7 13.1 %all-to-all-start = ((f32[32,8,128]{2,1,0:T(8,128)}), f32[32,8,128]{2,1,0:T(8,128)S(1)}, u32[]{:S(2)}, u32[]{:S(2)}) async-start(f32[32,8,128]{2,1,0:T(8,128)} %get-tuple-element.105), calls=%async_computation | async-start | bytes 262144 | tf_op jit(solution)/shard_map/all_to_all | solution.py:389
  42.0 5.2 %collective-permute-start.15 = (f32[16,4,128]{2,1,0:T(4,128)S(1)}, f32[16,4,128]{2,1,0:T(4,128)S(1)}, u32[]{:S(2)}, u32[]{:S(2)}) collective-permute-start(f32[16,4,128]{2,1,0:T(4,128)S(1)} %get-tuple-element.107), channel_id=1, source_target_pairs={{0,8},{8,0},{16,24},{24,16},{1,9},{9,1},{17,25},{25,17},{2,10},{10... | collective-permute-start | bytes 98312 | tf_op jit(solution)/shard_map/ppermute | solution.py:326
  42.3 4.9 %collective-permute-start.16 = (f32[16,4,128]{2,1,0:T(4,128)S(1)}, f32[16,4,128]{2,1,0:T(4,128)S(1)}, u32[]{:S(2)}, u32[]{:S(2)}) collective-permute-start(f32[16,4,128]{2,1,0:T(4,128)S(1)} %get-tuple-element.108), channel_id=1, source_target_pairs={{0,16},{8,24},{16,0},{24,8},{1,17},{9,25},{17,1},{25,9},{2,18},{10... | collective-permute-start | bytes 98312 | tf_op jit(solution)/shard_map/ppermute | solution.py:326
  44.0 3.6 %collective-permute-start.17 = (f32[16,4,128]{2,1,0:T(4,128)S(1)}, f32[16,4,128]{2,1,0:T(4,128)S(1)}, u32[]{:S(2)}, u32[]{:S(2)}) collective-permute-start(f32[16,4,128]{2,1,0:T(4,128)S(1)} %get-tuple-element.109), channel_id=1, source_target_pairs={{0,24},{8,16},{16,8},{24,0},{1,25},{9,17},{17,9},{25,1},{2,26},{10... | collective-permute-start | bytes 98312 | tf_op jit(solution)/shard_map/ppermute | solution.py:326

commit v8 on v7

--- a/solution.py
+++ b/solution.py
@@ -15,9 +15,8 @@
 BF16, F32 = jnp.bfloat16, jnp.float32
 
 
-def gate_kernel(pos_ref, left_ref, right_ref, *refs, reverse, sizes):
-    _, *outs, mark_ref, left, right, out, in_sem, out_sem = refs
-    mark_ref[...] = jnp.zeros_like(mark_ref)
+def gate_kernel(pos_ref, left_ref, right_ref, *refs, reverse, sizes, ordered):
+    *outs, left, right, out, in_sem, out_sem = refs[ordered:]
     local = left.shape[0] // LANES
     per_device = sum(sizes)
     copies = []
@@ -162,7 +161,7 @@
 
 
 def blocks_kernel(pos_ref, filt_ref, *refs):
-    _, *toeps, taps = refs
+    *toeps, taps = refs
     unroll = len(toeps)
     reverse_taps(pos_ref[0], filt_ref, taps)
 
@@ -303,10 +302,10 @@
     def gate(left, right, after, reverse, sizes, limit, name):
         parts = [jax.ShapeDtypeStruct((n,) + tail, BF16) for n in sizes]
         out = pl.pallas_call(
-            functools.partial(gate_kernel, reverse=reverse, sizes=sizes),
-            in_specs=[smem] + [anywhere] * 2 + [vmem],
-            out_specs=[anywhere] * (owners * len(sizes)) + [vmem],
-            out_shape=parts * owners + [jax.ShapeDtypeStruct((8, LANES), F32)],
+            functools.partial(gate_kernel, reverse=reverse, sizes=sizes, ordered=len(after)),
+            in_specs=[smem] + [pl.BlockSpec(memory_space=pltpu.HBM)] * 2 + [vmem] * len(after),
+            out_specs=[anywhere] * (owners * len(sizes)),
+            out_shape=parts * owners,
             scratch_shapes=[
                 pltpu.VMEM((block_len, chans), BF16),
                 pltpu.VMEM((block_len, chans), BF16),
@@ -317,8 +316,8 @@
             cost_estimate=cost(block_len * chans, 3 * size),
             compiler_params=pltpu.CompilerParams(vmem_limit_bytes=limit << 20),
             name=name,
-        )(pos, left, right, after)
-        return [out[n : -1 : len(sizes)] for n in range(len(sizes))], out[-1]
+        )(pos, left, right, *after)
+        return [out[n :: len(sizes)] for n in range(len(sizes))]
 
     def swap(values):
         out = [values[0]]
@@ -326,11 +325,10 @@
             out.append(lax.ppermute(values[k], "ctx", [(i, i ^ k) for i in range(owners)]))
         return out
 
-    sizes = (8, 4, 4) if per_device == 16 else (per_device,)
-    mark = jnp.zeros((8, LANES), F32)
-    (grad_send,), mark = gate(grad_out, out_gate, mark, False, (per_device,), 56, "gate_grad")
+    sizes = (8, 8) if per_device == 16 else (per_device,)
+    (grad_send,) = gate(grad_out, out_gate, (), False, (per_device,), 56, "gate_grad")
     grad_got = swap(grad_send)
-    prod_send, mark = gate(q_branch, k_branch, mark, True, sizes, 12, "gate_prod")
+    prod_send = gate(q_branch, k_branch, grad_send[:1], True, sizes, 12, "gate_prod")
     prod_got = []
     for part in prod_send:
         if prod_got:
@@ -339,7 +337,7 @@
     unroll = math.gcd(4, per_device)
     toeps = pl.pallas_call(
         blocks_kernel,
-        in_specs=[smem, vmem, vmem],
+        in_specs=[smem, vmem],
         out_specs=[vmem] * unroll,
         out_shape=[
             jax.ShapeDtypeStruct((per_device // unroll, blocks + 1, LANES, LANES), BF16)
@@ -348,7 +346,7 @@
         cost_estimate=cost(1, 1),
         compiler_params=pltpu.CompilerParams(vmem_limit_bytes=16 << 20),
         name="blocks",
-    )(pos, filters, mark)
+    )(pos, filters)
     conv = pl.pallas_call(
         functools.partial(conv_kernel, owners=owners, unroll=unroll),
         in_specs=[smem] + [vmem] * (unroll + owners),

time: 50.9 us -> 48.6 us (0.955)
  Pallas kernels: 22.7 us -> 20.9 us
    pallas_call x2, Pallas kernels: 6.21 us -> 4.66 us  [gate(): pl.pallas_call(functools.partial(gate_kernel, reverse=reverse, sizes=size...]
    ppermute x18 -> x15, starting transfers between devices: 14.6 us -> 13.2 us  [swap(): lax.ppermute(values[k], 'ctx', [(i, i ^ k) for i in range(owners)])]
    all_to_all x1, starting transfers between devices: 5.3 us -> 6.23 us  [on_device(): total = lax.all_to_all(spread, both, 0, 0, tiled=True)]
    broadcast_in_dim x1 -> x0, local copies, waits for them, and re-layouts: 0.6 us -> none  [on_device(): mark = jnp.zeros((8, LANES), F32)]
    ppermute x18 -> x15, waiting for transfers between devices: 3.8 us -> 4.21 us  [swap(): lax.ppermute(values[k], 'ctx', [(i, i ^ k) for i in range(owners)])]
    pallas_call x3 -> x2, Pallas kernels: 6.37 us -> 6.04 us  [on_device(): pl.pallas_call(functools.partial(lag_kernel, owners=owners, unroll=unroll...]
  transfers between devices with their start and end apart: 19 -> 16, of which waited for: 5 -> 5; matrix products, arithmetic and copies ran while one was open for 0% -> 0% of each run, Pallas kernels for 35% -> 36%
where the time goes in v8:
time: 48.6 us; the launch traced here: 48.4 us
  Pallas kernels  20.9 us (43%)
  starting transfers between devices  19.5 us (40%)
  waiting for transfers between devices  6.33 us (13%)
  local copies, waits for them, and re-layouts  0.97 us (2%)
  between operations  0.76 us (2%)
    ppermute x15, starting transfers between devices, swap(): lax.ppermute(values[k], 'ctx', [(i, i ^ k) for i in range(owners)])  13.2 us
    all_to_all x1, starting transfers between devices, on_device(): total = lax.all_to_all(spread, both, 0, 0, tiled=True)  6.23 us
    pallas_call x2, Pallas kernels, on_device(): pl.pallas_call(functools.partial(lag_kernel, owners=owners, unroll=unroll...  6.04 us
    pallas_call x2, Pallas kernels, gate(): pl.pallas_call(functools.partial(gate_kernel, reverse=reverse, sizes=size...  4.66 us
    ppermute x15, waiting for transfers between devices, swap(): lax.ppermute(values[k], 'ctx', [(i, i ^ k) for i in range(owners)])  4.21 us
    pallas_call x1, Pallas kernels, on_device(): pl.pallas_call(functools.partial(conv_kernel, owners=owners, unroll=unrol...  4.14 us
    pallas_call x1, Pallas kernels, on_device(): pl.pallas_call(blocks_kernel, in_specs=[smem, vmem], out_specs=[vmem] * u...  3.04 us
    all_to_all x1, waiting for transfers between devices, on_device(): total = lax.all_to_all(spread, both, 0, 0, tiled=True)  2.13 us
  transfers between devices with their start and end apart: 16, of which 5 were waited for; matrix products, arithmetic and copies ran while one was open for 0% of the time, Pallas kernels for 36%

profile of v8, /device:TPU:0, one launch (start us, length us, event | category | flops | bytes accessed | tf_op | source)
XLA Modules:
  0.0 48.4 jit_solution(10572546743122719790)
XLA Ops:
  0.7 2.7 %gate_grad.1 = (bf16[16,2,2,16,128]{4,3,2,1,0:T(8,128)(2,1)}, bf16[16,2,2,16,128]{4,3,2,1,0:T(8,128)(2,1)}, bf16[16,2,2,16,128]{4,3,2,1,0:T(8,128)(2,1)}, bf16[16,2,2,16,128]{4,3,2,1,0:T(8,128)(2,1)}) custom-call(s32[1]{0:T(128)} %bitcast.pos_ref, bf16[1,512,1024]{2,1,0:T(8,128)(2,1)} %left_ref.2, bf16[1,512,1024]{2,1,0:T(8,128)(2,1)} %right_ref.2), custom_call_target="tpu_custom_call" | custom-call | flops 524288 | bytes 3145728 | tf_op jit(solution)/shard_map/gate_grad/pallas_call | solution.py:304
  3.3 0.5 %collective-permute-start = (bf16[16,2,2,16,128]{4,3,2,1,0:T(8,128)(2,1)}, bf16[16,2,2,16,128]{4,3,2,1,0:T(8,128)(2,1)S(1)}, u32[]{:S(2)}, u32[]{:S(2)}) collective-permute-start(bf16[16,2,2,16,128]{4,3,2,1,0:T(8,128)(2,1)} %get-tuple-element.46), channel_id=1, source_target_pairs={{0,8},{8,0},{16,24},{24,16},{1,9},{9,1},{17,25},{25,17},{2,10},{10... | collective-permute-start | bytes 786440 | tf_op jit(solution)/shard_map/ppermute | solution.py:325
  3.8 2.6 %collective-permute-start.1 = (bf16[16,2,2,16,128]{4,3,2,1,0:T(8,128)(2,1)}, bf16[16,2,2,16,128]{4,3,2,1,0:T(8,128)(2,1)S(1)}, u32[]{:S(2)}, u32[]{:S(2)}) collective-permute-start(bf16[16,2,2,16,128]{4,3,2,1,0:T(8,128)(2,1)} %get-tuple-element.47), channel_id=1, source_target_pairs={{0,16},{8,24},{16,0},{24,8},{1,17},{9,25},{17,1},{25,9},{2,18},{10... | collective-permute-start | bytes 786440 | tf_op jit(solution)/shard_map/ppermute | solution.py:325
  6.4 0.1 collective-permute-start.2
  6.5 0.9 %copy-done.2 = bf16[16,2,2,16,128]{4,3,2,1,0:T(8,128)(2,1)S(1)} copy-done((bf16[16,2,2,16,128]{4,3,2,1,0:T(8,128)(2,1)S(1)}, bf16[16,2,2,16,128]{4,3,2,1,0:T(8,128)(2,1)}, u32[]{:S(2)}) %copy-start.2) | copy-done | bytes 262168
  7.5 2.0 %gate_prod.1 = (bf16[8,2,2,16,128]{4,3,2,1,0:T(8,128)(2,1)S(1)}, bf16[8,2,2,16,128]{4,3,2,1,0:T(8,128)(2,1)S(1)}, bf16[8,2,2,16,128]{4,3,2,1,0:T(8,128)(2,1)S(1)...) custom-call(s32[1]{0:T(128)} %bitcast.pos_ref, ...), custom_call_target="tpu_custom_call" | custom-call | flops 524288 | bytes 3145728 | tf_op jit(solution)/shard_map/gate_prod/pallas_call | solution.py:304
  9.5 0.2 collective-permute-start.6
  9.7 1.9 %collective-permute-start.10 = (bf16[8,2,2,16,128]{4,3,2,1,0:T(8,128)(2,1)S(1)}, bf16[8,2,2,16,128]{4,3,2,1,0:T(8,128)(2,1)S(1)}, u32[]{:S(2)}, u32[]{:S(2)}) collective-permute-start(bf16[8,2,2,16,128]{4,3,2,1,0:T(8,128)(2,1)S(1)} %get-tuple-element.66), channel_id=1, source_target_pairs={{0,16},{8,24},{16,0},{24,8},{1,17},{9,25},{17,1},{25,9},{2,18},{10... | collective-permute-start | bytes 393224 | tf_op jit(solution)/shard_map/ppermute | solution.py:325
  11.6 3.0 %blocks.1 = (bf16[4,17,128,128]{3,2,1,0:T(8,128)(2,1)S(1)}, bf16[4,17,128,128]{3,2,1,0:T(8,128)(2,1)S(1)}, bf16[4,17,128,128]{3,2,1,0:T(8,128)(2,1)S(1)}, bf16[4,17,128,128]{3,2,1,0:T(8,128)(2,1)S(1)}) custom-call(s32[1]{0:T(128)} %bitcast.pos_ref, bf16[64,2048]{1,0:T(8,128)(2,1)S(1)} %copy-done.4), custom_call_target="tpu_custom_call" | custom-call | flops 1 | bytes 1 | tf_op jit(solution)/shard_map/blocks/pallas_call | solution.py:338
  14.7 0.1 collective-permute-start.11
  14.7 0.0 collective-permute-done.refs_5_.refs_1_
  14.8 0.2 collective-permute-start.7
  15.0 1.9 %collective-permute-start.8 = (bf16[8,2,2,16,128]{4,3,2,1,0:T(8,128)(2,1)S(1)}, bf16[8,2,2,16,128]{4,3,2,1,0:T(8,128)(2,1)S(1)}, u32[]{:S(2)}, u32[]{:S(2)}) collective-permute-start(bf16[8,2,2,16,128]{4,3,2,1,0:T(8,128)(2,1)S(1)} %get-tuple-element.62), channel_id=1, source_target_pairs={{0,16},{8,24},{16,0},{24,8},{1,17},{9,25},{17,1},{25,9},{2,18},{10... | collective-permute-start | bytes 393224 | tf_op jit(solution)/shard_map/ppermute | solution.py:325
  16.9 2.1 %collective-permute-done.2.refs_7_.refs_3_ = bf16[16,2,2,16,128]{4,3,2,1,0:T(8,128)(2,1)S(1)} collective-permute-done((bf16[16,2,2,16,128]{4,3,2,1,0:T(8,128)(2,1)}, bf16[16,2,2,16,128]{4,3,2,1,0:T(8,128)(2,1)S(1)}, u32[]{:S(2)}, u32[]{:S(2)}) %collective-permute-start.2) | collective-permute-done | bytes 262176 | tf_op jit(solution)/shard_map/ppermute | solution.py:325
  19.0 1.8 %collective-permute-start.9 = (bf16[8,2,2,16,128]{4,3,2,1,0:T(8,128)(2,1)S(1)}, bf16[8,2,2,16,128]{4,3,2,1,0:T(8,128)(2,1)S(1)}, u32[]{:S(2)}, u32[]{:S(2)}) collective-permute-start(bf16[8,2,2,16,128]{4,3,2,1,0:T(8,128)(2,1)S(1)} %get-tuple-element.63), channel_id=1, source_target_pairs={{0,24},{8,16},{16,8},{24,0},{1,25},{9,17},{17,9},{25,1},{2,26},{10... | collective-permute-start | bytes 393224 | tf_op jit(solution)/shard_map/ppermute | solution.py:325
  20.8 4.1 %conv.1 = (bf16[16,2,2,16,128]{4,3,2,1,0:T(8,128)(2,1)S(1)}, bf16[16,2,2,16,128]{4,3,2,1,0:T(8,128)(2,1)}, bf16[16,2,2,16,128]{4,3,2,1,0:T(8,128)(2,1)}, bf16[16,2,2,16,128]{4,3,2,1,0:T(8,128)(2,1)}) custom-call(s32[1]{0:T(128)} %bitcast.pos_ref, bf16[4,17,128,128]{3,2,1,0:T(8,128)(2,1)S(1)} %get-tuple-element.41.refs_0_, ...), custom_call_target="tpu_custom_call" | custom-call | flops 17179869184 | bytes 2359296 | tf_op jit(solution)/shard_map/conv/pallas_call | solution.py:350
  24.9 0.0 collective-permute-done.10.refs_6_
  25.0 0.0 collective-permute-start.3
  25.0 0.0 collective-permute-done.11.refs_7_
  25.0 1.1 %collective-permute-start.4 = (bf16[16,2,2,16,128]{4,3,2,1,0:T(8,128)(2,1)}, bf16[16,2,2,16,128]{4,3,2,1,0:T(8,128)(2,1)S(1)}, u32[]{:S(2)}, u32[]{:S(2)}) collective-permute-start(bf16[16,2,2,16,128]{4,3,2,1,0:T(8,128)(2,1)} %get-tuple-element.51), channel_id=1, source_target_pairs={{0,16},{8,24},{16,0},{24,8},{1,17},{9,25},{17,1},{25,9},{2,18},{10... | collective-permute-start | bytes 786440 | tf_op jit(solution)/shard_map/ppermute | solution.py:325
  26.1 2.7 %lags.2 = (f32[16,4,128]{2,1,0:T(4,128)S(1)}, f32[16,4,128]{2,1,0:T(4,128)S(1)}, f32[16,4,128]{2,1,0:T(4,128)S(1)}, f32[16,4,128]{2,1,0:T(4,128)S(1)}, f32[4,128]{1,0:T(4,128)S(1)}) custom-call(s32[1]{0:T(128)} %bitcast.pos_ref, bf16[16,2,2,16,128]{4,3,2,1,0:T(8,128)(2,1)S(1)} %copy-done.3, ...), custom_call_target="tpu_custom_call" | custom-call | flops 8589934592 | bytes 2097152 | tf_op jit(solution)/shard_map/lags/pallas_call | solution.py:368
  28.8 0.8 %collective-permute-start.5 = (bf16[16,2,2,16,128]{4,3,2,1,0:T(8,128)(2,1)}, bf16[16,2,2,16,128]{4,3,2,1,0:T(8,128)(2,1)S(1)}, u32[]{:S(2)}, u32[]{:S(2)}) collective-permute-start(bf16[16,2,2,16,128]{4,3,2,1,0:T(8,128)(2,1)} %get-tuple-element.52), channel_id=1, source_target_pairs={{0,24},{8,16},{16,8},{24,0},{1,25},{9,17},{17,9},{25,1},{2,26},{10... | collective-permute-start | bytes 786440 | tf_op jit(solution)/shard_map/ppermute | solution.py:325
  29.6 0.6 %collective-permute-done.9.refs_7_ = bf16[8,2,2,16,128]{4,3,2,1,0:T(8,128)(2,1)S(1)} collective-permute-done((bf16[8,2,2,16,128]{4,3,2,1,0:T(8,128)(2,1)S(1)}, bf16[8,2,2,16,128]{4,3,2,1,0:T(8,128)(2,1)S(1)}, u32[]{:S(2)}, u32[]{:S(2)}) %collective-permute-start.9) | collective-permute-done | bytes 131104 | tf_op jit(solution)/shard_map/ppermute | solution.py:325
  30.1 3.4 %lags.3 = (f32[16,4,128]{2,1,0:T(4,128)S(1)}, f32[16,4,128]{2,1,0:T(4,128)S(1)}, f32[16,4,128]{2,1,0:T(4,128)S(1)}, f32[16,4,128]{2,1,0:T(4,128)S(1)}, f32[32,8,128]{2,1,0:T(8,128)}) custom-call(s32[1]{0:T(128)} %bitcast.pos_ref, ...), custom_call_target="tpu_custom_call", output_to_operand_aliasing={{0}: (9, {}), {1}: (10, {}), {2}: (11, {}), {3}: (12, {})} | custom-call | flops 8589934592 | bytes 2097152 | tf_op jit(solution)/shard_map/lags/pallas_call | solution.py:368
  33.5 6.2 %all-to-all-start = ((f32[32,8,128]{2,1,0:T(8,128)}), f32[32,8,128]{2,1,0:T(8,128)S(1)}, u32[]{:S(2)}, u32[]{:S(2)}) async-start(f32[32,8,128]{2,1,0:T(8,128)} %get-tuple-element.73), calls=%async_computation | async-start | bytes 262144 | tf_op jit(solution)/shard_map/all_to_all | solution.py:387
  39.7 0.3 collective-permute-start.12
  40.1 1.7 %collective-permute-start.13 = (f32[16,4,128]{2,1,0:T(4,128)S(1)}, f32[16,4,128]{2,1,0:T(4,128)S(1)}, u32[]{:S(2)}, u32[]{:S(2)}) collective-permute-start(f32[16,4,128]{2,1,0:T(4,128)S(1)} %get-tuple-element.76), channel_id=1, source_target_pairs={{0,16},{8,24},{16,0},{24,8},{1,17},{9,25},{17,1},{25,9},{2,18},{10... | collective-permute-start | bytes 98312 | tf_op jit(solution)/shard_map/ppermute | solution.py:325
  41.8 2.1 %ungate.1 = (bf16[1,512,1024]{2,1,0:T(8,128)(2,1)}, bf16[1,512,1024]{2,1,0:T(8,128)(2,1)}, f32[8,128]{1,0:T(8,128)S(1)}) custom-call(s32[1]{0:T(128)} %bitcast.pos_ref, bf16[1,512,1024]{2,1,0:T(8,128)(2,1)S(1)} %copy-done, bf16[1,512,1024]{2,1,0:T(8,128)(2,1)S(1)} %copy-done.1, bf16[16,2,2,16,128]{4,3,2,1,0:T(8,128)(2,1)S(1)} %get-tuple-element.49.refs_0_.refs_8_, ...), custom_call_target="tpu_custom_call" | custom-call | flops 1048576 | bytes 5242880 | tf_op jit(solution)/shard_map/ungate/pallas_call | solution.py:390
  43.8 0.2 collective-permute-done.13.refs_2_
  44.0 1.3 %collective-permute-done.14.refs_3_ = f32[16,4,128]{2,1,0:T(4,128)S(1)} collective-permute-done((f32[16,4,128]{2,1,0:T(4,128)S(1)}, f32[16,4,128]{2,1,0:T(4,128)S(1)}, u32[]{:S(2)}, u32[]{:S(2)}) %collective-permute-start.14) | collective-permute-done | bytes 32800 | tf_op jit(solution)/shard_map/ppermute | solution.py:325
  45.3 2.1 %all-to-all-done.total_ref = f32[32,8,128]{2,1,0:T(8,128)S(1)} async-done(((f32[32,8,128]{2,1,0:T(8,128)}), f32[32,8,128]{2,1,0:T(8,128)S(1)}, u32[]{:S(2)}, u32[]{:S(2)}) %all-to-all-start) | async-done | bytes 131104 | tf_op jit(solution)/shard_map/all_to_all | solution.py:387
  47.5 0.9 %clip.1 = f32[64,512]{1,0:T(8,128)} custom-call(s32[1]{0:T(128)} %bitcast.pos_ref, f32[32,8,128]{2,1,0:T(8,128)S(1)} %all-to-all-done.total_ref, f32[16,4,128]{2,1,0:T(4,128)S(1)} %get-tuple-element.74.refs_0_, f32[16,4,128]{2,1,0:T(4,128)S(1)} %collective-permute-done.12.refs_1_, f32[16,4,128]{2,1,0:T(4,128)S(1)} %collective-permute-done.13.refs_2_, ...), custom_call_target="tpu_custom_call" | custom-call | flops 131072 | bytes 524288 | tf_op jit(solution)/shard_map/clip/pallas_call | solution.py:409
  (18 shorter events, 0.0 us)
Async XLA Ops:
  0.6 5.9 %copy-start = (bf16[1,512,1024]{2,1,0:T(8,128)(2,1)S(1)}, bf16[1,512,1024]{2,1,0:T(8,128)(2,1)}, u32[]{:S(2)}) copy-start(bf16[1,512,1024]{2,1,0:T(8,128)(2,1)} %left_ref.3) | copy-start | bytes 3145732
  0.6 5.9 %copy-start.1 = (bf16[1,512,1024]{2,1,0:T(8,128)(2,1)S(1)}, bf16[1,512,1024]{2,1,0:T(8,128)(2,1)}, u32[]{:S(2)}) copy-start(bf16[1,512,1024]{2,1,0:T(8,128)(2,1)} %right_ref.3) | copy-start | bytes 3145732
  3.3 11.4 %collective-permute-start = (bf16[16,2,2,16,128]{4,3,2,1,0:T(8,128)(2,1)}, bf16[16,2,2,16,128]{4,3,2,1,0:T(8,128)(2,1)S(1)}, u32[]{:S(2)}, u32[]{:S(2)}) collective-permute-start(bf16[16,2,2,16,128]{4,3,2,1,0:T(8,128)(2,1)} %get-tuple-element.46), channel_id=1, source_target_pairs={{0,8},{8,0},{16,24},{24,16},{1,9},{9,1},{17,25},{25,17},{2,10},{10... | collective-permute-start | bytes 786440 | tf_op jit(solution)/shard_map/ppermute | solution.py:325
  3.8 11.1 %collective-permute-start.1 = (bf16[16,2,2,16,128]{4,3,2,1,0:T(8,128)(2,1)}, bf16[16,2,2,16,128]{4,3,2,1,0:T(8,128)(2,1)S(1)}, u32[]{:S(2)}, u32[]{:S(2)}) collective-permute-start(bf16[16,2,2,16,128]{4,3,2,1,0:T(8,128)(2,1)} %get-tuple-element.47), channel_id=1, source_target_pairs={{0,16},{8,24},{16,0},{24,8},{1,17},{9,25},{17,1},{25,9},{2,18},{10... | collective-permute-start | bytes 786440 | tf_op jit(solution)/shard_map/ppermute | solution.py:325
  6.4 12.6 %collective-permute-start.2 = (bf16[16,2,2,16,128]{4,3,2,1,0:T(8,128)(2,1)}, bf16[16,2,2,16,128]{4,3,2,1,0:T(8,128)(2,1)S(1)}, u32[]{:S(2)}, u32[]{:S(2)}) collective-permute-start(bf16[16,2,2,16,128]{4,3,2,1,0:T(8,128)(2,1)} %get-tuple-element.48), channel_id=1, source_target_pairs={{0,24},{8,16},{16,8},{24,0},{1,25},{9,17},{17,9},{25,1},{2,26},{10... | collective-permute-start | bytes 786440 | tf_op jit(solution)/shard_map/ppermute | solution.py:325
  6.5 1.0 %copy-start.2 = (bf16[16,2,2,16,128]{4,3,2,1,0:T(8,128)(2,1)S(1)}, bf16[16,2,2,16,128]{4,3,2,1,0:T(8,128)(2,1)}, u32[]{:S(2)}) copy-start(bf16[16,2,2,16,128]{4,3,2,1,0:T(8,128)(2,1)} %get-tuple-element.45.refs_4_.refs_0_) | copy-start | bytes 786436
  7.5 4.1 %copy-start.4 = (bf16[64,2048]{1,0:T(8,128)(2,1)S(1)}, bf16[64,2048]{1,0:T(8,128)(2,1)}, u32[]{:S(2)}) copy-start(bf16[64,2048]{1,0:T(8,128)(2,1)} %filt_ref.1) | copy-start | bytes 786436
  7.5 13.3 %copy-start.3 = (bf16[16,2,2,16,128]{4,3,2,1,0:T(8,128)(2,1)S(1)}, bf16[16,2,2,16,128]{4,3,2,1,0:T(8,128)(2,1)}, u32[]{:S(2)}) copy-start(bf16[16,2,2,16,128]{4,3,2,1,0:T(8,128)(2,1)} %get-tuple-element.45.refs_4_.refs_0_) | copy-start | bytes 786436
  9.5 5.2 %collective-permute-start.6 = (bf16[8,2,2,16,128]{4,3,2,1,0:T(8,128)(2,1)S(1)}, bf16[8,2,2,16,128]{4,3,2,1,0:T(8,128)(2,1)S(1)}, u32[]{:S(2)}, u32[]{:S(2)}) collective-permute-start(bf16[8,2,2,16,128]{4,3,2,1,0:T(8,128)(2,1)S(1)} %get-tuple-element.59), channel_id=1, source_target_pairs={{0,8},{8,0},{16,24},{24,16},{1,9},{9,1},{17,25},{25,17},{2,10},{10... | collective-permute-start | bytes 393224 | tf_op jit(solution)/shard_map/ppermute | solution.py:325
  9.7 15.3 %collective-permute-start.10 = (bf16[8,2,2,16,128]{4,3,2,1,0:T(8,128)(2,1)S(1)}, bf16[8,2,2,16,128]{4,3,2,1,0:T(8,128)(2,1)S(1)}, u32[]{:S(2)}, u32[]{:S(2)}) collective-permute-start(bf16[8,2,2,16,128]{4,3,2,1,0:T(8,128)(2,1)S(1)} %get-tuple-element.66), channel_id=1, source_target_pairs={{0,16},{8,24},{16,0},{24,8},{1,17},{9,25},{17,1},{25,9},{2,18},{10... | collective-permute-start | bytes 393224 | tf_op jit(solution)/shard_map/ppermute | solution.py:325
  14.7 10.3 %collective-permute-start.11 = (bf16[8,2,2,16,128]{4,3,2,1,0:T(8,128)(2,1)S(1)}, bf16[8,2,2,16,128]{4,3,2,1,0:T(8,128)(2,1)S(1)}, u32[]{:S(2)}, u32[]{:S(2)}) collective-permute-start(bf16[8,2,2,16,128]{4,3,2,1,0:T(8,128)(2,1)S(1)} %get-tuple-element.67), channel_id=1, source_target_pairs={{0,24},{8,16},{16,8},{24,0},{1,25},{9,17},{17,9},{25,1},{2,26},{10... | collective-permute-start | bytes 393224 | tf_op jit(solution)/shard_map/ppermute | solution.py:325
  14.8 14.0 %collective-permute-start.7 = (bf16[8,2,2,16,128]{4,3,2,1,0:T(8,128)(2,1)S(1)}, bf16[8,2,2,16,128]{4,3,2,1,0:T(8,128)(2,1)S(1)}, u32[]{:S(2)}, u32[]{:S(2)}) collective-permute-start(bf16[8,2,2,16,128]{4,3,2,1,0:T(8,128)(2,1)S(1)} %get-tuple-element.61), channel_id=1, source_target_pairs={{0,8},{8,0},{16,24},{24,16},{1,9},{9,1},{17,25},{25,17},{2,10},{10... | collective-permute-start | bytes 393224 | tf_op jit(solution)/shard_map/ppermute | solution.py:325
  15.0 14.6 %collective-permute-start.8 = (bf16[8,2,2,16,128]{4,3,2,1,0:T(8,128)(2,1)S(1)}, bf16[8,2,2,16,128]{4,3,2,1,0:T(8,128)(2,1)S(1)}, u32[]{:S(2)}, u32[]{:S(2)}) collective-permute-start(bf16[8,2,2,16,128]{4,3,2,1,0:T(8,128)(2,1)S(1)} %get-tuple-element.62), channel_id=1, source_target_pairs={{0,16},{8,24},{16,0},{24,8},{1,17},{9,25},{17,1},{25,9},{2,18},{10... | collective-permute-start | bytes 393224 | tf_op jit(solution)/shard_map/ppermute | solution.py:325
  19.0 11.1 %collective-permute-start.9 = (bf16[8,2,2,16,128]{4,3,2,1,0:T(8,128)(2,1)S(1)}, bf16[8,2,2,16,128]{4,3,2,1,0:T(8,128)(2,1)S(1)}, u32[]{:S(2)}, u32[]{:S(2)}) collective-permute-start(bf16[8,2,2,16,128]{4,3,2,1,0:T(8,128)(2,1)S(1)} %get-tuple-element.63), channel_id=1, source_target_pairs={{0,24},{8,16},{16,8},{24,0},{1,25},{9,17},{17,9},{25,1},{2,26},{10... | collective-permute-start | bytes 393224 | tf_op jit(solution)/shard_map/ppermute | solution.py:325
  25.0 16.8 %collective-permute-start.3 = (bf16[16,2,2,16,128]{4,3,2,1,0:T(8,128)(2,1)}, bf16[16,2,2,16,128]{4,3,2,1,0:T(8,128)(2,1)S(1)}, u32[]{:S(2)}, u32[]{:S(2)}) collective-permute-start(bf16[16,2,2,16,128]{4,3,2,1,0:T(8,128)(2,1)} %get-tuple-element.50), channel_id=1, source_target_pairs={{0,8},{8,0},{16,24},{24,16},{1,9},{9,1},{17,25},{25,17},{2,10},{10... | collective-permute-start | bytes 786440 | tf_op jit(solution)/shard_map/ppermute | solution.py:325
  25.0 16.8 %collective-permute-start.4 = (bf16[16,2,2,16,128]{4,3,2,1,0:T(8,128)(2,1)}, bf16[16,2,2,16,128]{4,3,2,1,0:T(8,128)(2,1)S(1)}, u32[]{:S(2)}, u32[]{:S(2)}) collective-permute-start(bf16[16,2,2,16,128]{4,3,2,1,0:T(8,128)(2,1)} %get-tuple-element.51), channel_id=1, source_target_pairs={{0,16},{8,24},{16,0},{24,8},{1,17},{9,25},{17,1},{25,9},{2,18},{10... | collective-permute-start | bytes 786440 | tf_op jit(solution)/shard_map/ppermute | solution.py:325
  28.8 13.0 %collective-permute-start.5 = (bf16[16,2,2,16,128]{4,3,2,1,0:T(8,128)(2,1)}, bf16[16,2,2,16,128]{4,3,2,1,0:T(8,128)(2,1)S(1)}, u32[]{:S(2)}, u32[]{:S(2)}) collective-permute-start(bf16[16,2,2,16,128]{4,3,2,1,0:T(8,128)(2,1)} %get-tuple-element.52), channel_id=1, source_target_pairs={{0,24},{8,16},{16,8},{24,0},{1,25},{9,17},{17,9},{25,1},{2,26},{10... | collective-permute-start | bytes 786440 | tf_op jit(solution)/shard_map/ppermute | solution.py:325
  33.5 14.0 %all-to-all-start = ((f32[32,8,128]{2,1,0:T(8,128)}), f32[32,8,128]{2,1,0:T(8,128)S(1)}, u32[]{:S(2)}, u32[]{:S(2)}) async-start(f32[32,8,128]{2,1,0:T(8,128)} %get-tuple-element.73), calls=%async_computation | async-start | bytes 262144 | tf_op jit(solution)/shard_map/all_to_all | solution.py:387
  39.7 4.1 %collective-permute-start.12 = (f32[16,4,128]{2,1,0:T(4,128)S(1)}, f32[16,4,128]{2,1,0:T(4,128)S(1)}, u32[]{:S(2)}, u32[]{:S(2)}) collective-permute-start(f32[16,4,128]{2,1,0:T(4,128)S(1)} %get-tuple-element.75), channel_id=1, source_target_pairs={{0,8},{8,0},{16,24},{24,16},{1,9},{9,1},{17,25},{25,17},{2,10},{10... | collective-permute-start | bytes 98312 | tf_op jit(solution)/shard_map/ppermute | solution.py:325
  40.1 4.0 %collective-permute-start.13 = (f32[16,4,128]{2,1,0:T(4,128)S(1)}, f32[16,4,128]{2,1,0:T(4,128)S(1)}, u32[]{:S(2)}, u32[]{:S(2)}) collective-permute-start(f32[16,4,128]{2,1,0:T(4,128)S(1)} %get-tuple-element.76), channel_id=1, source_target_pairs={{0,16},{8,24},{16,0},{24,8},{1,17},{9,25},{17,1},{25,9},{2,18},{10... | collective-permute-start | bytes 98312 | tf_op jit(solution)/shard_map/ppermute | solution.py:325
  41.7 3.6 %collective-permute-start.14 = (f32[16,4,128]{2,1,0:T(4,128)S(1)}, f32[16,4,128]{2,1,0:T(4,128)S(1)}, u32[]{:S(2)}, u32[]{:S(2)}) collective-permute-start(f32[16,4,128]{2,1,0:T(4,128)S(1)} %get-tuple-element.77), channel_id=1, source_target_pairs={{0,24},{8,16},{16,8},{24,0},{1,25},{9,17},{17,9},{25,1},{2,26},{10... | collective-permute-start | bytes 98312 | tf_op jit(solution)/shard_map/ppermute | solution.py:325

commit v9 on v8

--- a/solution.py
+++ b/solution.py
@@ -178,7 +178,8 @@
 def conv_kernel(pos_ref, *refs, owners, unroll):
     toeps, refs = refs[:unroll], refs[unroll:]
     ins, outs, refs = refs[:owners], refs[owners : 2 * owners], refs[2 * owners :]
-    pads, accs = refs[:unroll], refs[unroll:]
+    pads, accs, refs = refs[:unroll], refs[unroll : 2 * unroll], refs[2 * unroll :]
+    outs_v, sem = refs[:owners], refs[owners]
     per_device, blocks = ins[0].shape[0], toeps[0].shape[1] - 1
     rows = pads[0].shape[1]
 
@@ -200,15 +201,20 @@
         for u in range(unroll):
             one(toeps[u].at[i], pads[u], accs[u])
         for u in range(unroll):
-            for k, target in enumerate(outs):
+            for k, target in enumerate(outs_v):
                 count = target.shape[2] * GROUP
                 at = pl.multiple_of(jnp.bitwise_xor(pos_ref[0], k) * count, count)
                 for half in range(2):
                     value = accs[u][half, pl.ds(at, count)]
                     target[i * unroll + u, half] = value.reshape(target.shape[2:])
+        here = pl.ds(i * unroll, unroll)
+        for k in range(owners):
+            pltpu.make_async_copy(outs_v[k].at[here], outs[k].at[here], sem.at[k]).start()
         return carry
 
     lax.fori_loop(0, per_device // unroll, some, 0)
+    for k in range(owners):
+        pltpu.make_async_copy(outs_v[k], outs[k], sem.at[k]).wait()
 
 
 def lag_sums(pad, flipped, rows, blocks):
@@ -325,7 +331,7 @@
             out.append(lax.ppermute(values[k], "ctx", [(i, i ^ k) for i in range(owners)]))
         return out
 
-    sizes = (8, 8) if per_device == 16 else (per_device,)
+    sizes = (8, 4, 4) if per_device == 16 else (per_device,)
     (grad_send,) = gate(grad_out, out_gate, (), False, (per_device,), 56, "gate_grad")
     grad_got = swap(grad_send)
     prod_send = gate(q_branch, k_branch, grad_send[:1], True, sizes, 12, "gate_prod")
@@ -350,9 +356,11 @@
     conv = pl.pallas_call(
         functools.partial(conv_kernel, owners=owners, unroll=unroll),
         in_specs=[smem] + [vmem] * (unroll + owners),
-        out_specs=[vmem] * owners,
+        out_specs=[anywhere] * owners,
         out_shape=[piece] * owners,
-        scratch_shapes=[pltpu.VMEM((2, rows, LANES), BF16)] * (2 * unroll),
+        scratch_shapes=[pltpu.VMEM((2, rows, LANES), BF16)] * (2 * unroll)
+        + [pltpu.VMEM(piece.shape, BF16)] * owners
+        + [pltpu.SemaphoreType.DMA((owners,))],
         cost_estimate=cost(per_device * rows * length * 4096, 2 * size + groups * length * 2),
         compiler_params=pltpu.CompilerParams(vmem_limit_bytes=16 << 20),
         name="conv",
@@ -364,7 +372,7 @@
     for n, each in enumerate(sizes):
         last = n == len(sizes) - 1
         unroll = math.gcd(8, each)
-        sums = jax.ShapeDtypeStruct((count, 8, LANES) if last else (blocks // owners, LANES), F32)
+        sums = jax.ShapeDtypeStruct((count, 4, LANES) if last else (blocks // owners, LANES), F32)
         old = pl.pallas_call(
             functools.partial(
                 lag_kernel, owners=owners, unroll=unroll, scale=scale, first=sum(sizes[:n]), last=last

time: 48.6 us -> 48.8 us (level)
  waiting for transfers between devices: 6.33 us -> 5.2 us
  Pallas kernels: 20.9 us -> 21.7 us
    ppermute x15 -> x18, starting transfers between devices: 13.2 us -> 14.4 us  [swap(): lax.ppermute(values[k], 'ctx', [(i, i ^ k) for i in range(owners)])]
    ppermute x15 -> x18, waiting for transfers between devices: 4.21 us -> 3.46 us  [swap(): lax.ppermute(values[k], 'ctx', [(i, i ^ k) for i in range(owners)])]
    all_to_all x1, starting transfers between devices: 6.23 us -> 5.58 us  [on_device(): total = lax.all_to_all(spread, both, 0, 0, tiled=True)]
    pallas_call x2 -> x3, Pallas kernels: 6.04 us -> 6.35 us  [on_device(): pl.pallas_call(functools.partial(lag_kernel, owners=owners, unroll=unroll...]
  transfers between devices with their start and end apart: 16 -> 19, of which waited for: 5 -> 5; matrix products, arithmetic and copies ran while one was open for 0% -> 0% of each run, Pallas kernels for 36% -> 37%
where the time goes in v9:
time: 48.8 us; the launch traced here: 48.6 us
  Pallas kernels  21.7 us (44%)
  starting transfers between devices  19.9 us (41%)
  waiting for transfers between devices  5.2 us (11%)
  local copies, waits for them, and re-layouts  0.97 us (2%)
  between operations  0.79 us (2%)
    ppermute x18, starting transfers between devices, swap(): lax.ppermute(values[k], 'ctx', [(i, i ^ k) for i in range(owners)])  14.4 us
    pallas_call x3, Pallas kernels, on_device(): pl.pallas_call(functools.partial(lag_kernel, owners=owners, unroll=unroll...  6.35 us
    all_to_all x1, starting transfers between devices, on_device(): total = lax.all_to_all(spread, both, 0, 0, tiled=True)  5.58 us
    pallas_call x2, Pallas kernels, gate(): pl.pallas_call(functools.partial(gate_kernel, reverse=reverse, sizes=size...  4.99 us
    pallas_call x1, Pallas kernels, on_device(): pl.pallas_call(functools.partial(conv_kernel, owners=owners, unroll=unrol...  4.36 us
    ppermute x18, waiting for transfers between devices, swap(): lax.ppermute(values[k], 'ctx', [(i, i ^ k) for i in range(owners)])  3.46 us
    pallas_call x1, Pallas kernels, on_device(): pl.pallas_call(blocks_kernel, in_specs=[smem, vmem], out_specs=[vmem] * u...  3.04 us
    pallas_call x1, Pallas kernels, on_device(): pl.pallas_call(ungate_kernel, in_specs=[smem] + [anywhere] * (2 + owners)...  2.06 us
  transfers between devices with their start and end apart: 19, of which 5 were waited for; matrix products, arithmetic and copies ran while one was open for 0% of the time, Pallas kernels for 37%

profile of v9, /device:TPU:0, one launch (start us, length us, event | category | flops | bytes accessed | tf_op | source)
XLA Modules:
  0.0 48.6 jit_solution(9609485209144195264)
XLA Ops:
  0.7 2.7 %gate_grad.1 = (bf16[16,2,2,16,128]{4,3,2,1,0:T(8,128)(2,1)}, bf16[16,2,2,16,128]{4,3,2,1,0:T(8,128)(2,1)}, bf16[16,2,2,16,128]{4,3,2,1,0:T(8,128)(2,1)}, bf16[16,2,2,16,128]{4,3,2,1,0:T(8,128)(2,1)}) custom-call(s32[1]{0:T(128)} %bitcast.pos_ref, bf16[1,512,1024]{2,1,0:T(8,128)(2,1)} %left_ref.2, bf16[1,512,1024]{2,1,0:T(8,128)(2,1)} %right_ref.2), custom_call_target="tpu_custom_call" | custom-call | flops 524288 | bytes 3145728 | tf_op jit(solution)/shard_map/gate_grad/pallas_call | solution.py:310
  3.3 0.5 %collective-permute-start = (bf16[16,2,2,16,128]{4,3,2,1,0:T(8,128)(2,1)}, bf16[16,2,2,16,128]{4,3,2,1,0:T(8,128)(2,1)S(1)}, u32[]{:S(2)}, u32[]{:S(2)}) collective-permute-start(bf16[16,2,2,16,128]{4,3,2,1,0:T(8,128)(2,1)} %get-tuple-element.60), channel_id=1, source_target_pairs={{0,8},{8,0},{16,24},{24,16},{1,9},{9,1},{17,25},{25,17},{2,10},{10... | collective-permute-start | bytes 786440 | tf_op jit(solution)/shard_map/ppermute | solution.py:331
  3.9 2.6 %collective-permute-start.1 = (bf16[16,2,2,16,128]{4,3,2,1,0:T(8,128)(2,1)}, bf16[16,2,2,16,128]{4,3,2,1,0:T(8,128)(2,1)S(1)}, u32[]{:S(2)}, u32[]{:S(2)}) collective-permute-start(bf16[16,2,2,16,128]{4,3,2,1,0:T(8,128)(2,1)} %get-tuple-element.61), channel_id=1, source_target_pairs={{0,16},{8,24},{16,0},{24,8},{1,17},{9,25},{17,1},{25,9},{2,18},{10... | collective-permute-start | bytes 786440 | tf_op jit(solution)/shard_map/ppermute | solution.py:331
  6.5 0.9 %copy-done.2 = bf16[16,2,2,16,128]{4,3,2,1,0:T(8,128)(2,1)S(1)} copy-done((bf16[16,2,2,16,128]{4,3,2,1,0:T(8,128)(2,1)S(1)}, bf16[16,2,2,16,128]{4,3,2,1,0:T(8,128)(2,1)}, u32[]{:S(2)}) %copy-start.2) | copy-done | bytes 262168
  7.5 2.3 %gate_prod.1 = (bf16[8,2,2,16,128]{4,3,2,1,0:T(8,128)(2,1)S(1)}, bf16[4,2,2,16,128]{4,3,2,1,0:T(8,128)(2,1)S(1)}, bf16[4,2,2,16,128]{4,3,2,1,0:T(8,128)(2,1)S(1)...) custom-call(s32[1]{0:T(128)} %bitcast.pos_ref, ...), custom_call_target="tpu_custom_call" | custom-call | flops 524288 | bytes 3145728 | tf_op jit(solution)/shard_map/gate_prod/pallas_call | solution.py:310
  9.8 0.2 collective-permute-start.6
  10.0 1.2 %collective-permute-done.6.refs_5_ = bf16[8,2,2,16,128]{4,3,2,1,0:T(8,128)(2,1)S(1)} collective-permute-done((bf16[8,2,2,16,128]{4,3,2,1,0:T(8,128)(2,1)S(1)}, bf16[8,2,2,16,128]{4,3,2,1,0:T(8,128)(2,1)S(1)}, u32[]{:S(2)}, u32[]{:S(2)}) %collective-permute-start.6) | collective-permute-done | bytes 131104 | tf_op jit(solution)/shard_map/ppermute | solution.py:331
  11.2 0.1 collective-permute-start.7
  11.4 1.9 %collective-permute-start.13 = (bf16[8,2,2,16,128]{4,3,2,1,0:T(8,128)(2,1)S(1)}, bf16[8,2,2,16,128]{4,3,2,1,0:T(8,128)(2,1)S(1)}, u32[]{:S(2)}, u32[]{:S(2)}) collective-permute-start(bf16[8,2,2,16,128]{4,3,2,1,0:T(8,128)(2,1)S(1)} %get-tuple-element.89), channel_id=1, source_target_pairs={{0,16},{8,24},{16,0},{24,8},{1,17},{9,25},{17,1},{25,9},{2,18},{10... | collective-permute-start | bytes 393224 | tf_op jit(solution)/shard_map/ppermute | solution.py:331
  13.3 3.0 %blocks.1 = (bf16[4,17,128,128]{3,2,1,0:T(8,128)(2,1)S(1)}, bf16[4,17,128,128]{3,2,1,0:T(8,128)(2,1)S(1)}, bf16[4,17,128,128]{3,2,1,0:T(8,128)(2,1)S(1)}, bf16[4,17,128,128]{3,2,1,0:T(8,128)(2,1)S(1)}) custom-call(s32[1]{0:T(128)} %bitcast.pos_ref, bf16[64,2048]{1,0:T(8,128)(2,1)S(1)} %copy-done.4), custom_call_target="tpu_custom_call" | custom-call | flops 1 | bytes 1 | tf_op jit(solution)/shard_map/blocks/pallas_call | solution.py:344
  16.4 0.1 collective-permute-start.14
  16.4 1.5 %collective-permute-start.11 = (bf16[4,2,2,16,128]{4,3,2,1,0:T(8,128)(2,1)S(1)}, bf16[4,2,2,16,128]{4,3,2,1,0:T(8,128)(2,1)S(1)}, u32[]{:S(2)}, u32[]{:S(2)}) collective-permute-start(bf16[4,2,2,16,128]{4,3,2,1,0:T(8,128)(2,1)S(1)} %get-tuple-element.85), channel_id=1, source_target_pairs={{0,16},{8,24},{16,0},{24,8},{1,17},{9,25},{17,1},{25,9},{2,18},{10... | collective-permute-start | bytes 196616 | tf_op jit(solution)/shard_map/ppermute | solution.py:331
  17.9 0.3 collective-permute-start.12
  18.2 0.8 %collective-permute-done.2.refs_7_.refs_3_ = bf16[16,2,2,16,128]{4,3,2,1,0:T(8,128)(2,1)S(1)} collective-permute-done((bf16[16,2,2,16,128]{4,3,2,1,0:T(8,128)(2,1)}, bf16[16,2,2,16,128]{4,3,2,1,0:T(8,128)(2,1)S(1)}, u32[]{:S(2)}, u32[]{:S(2)}) %collective-permute-start.2) | collective-permute-done | bytes 262176 | tf_op jit(solution)/shard_map/ppermute | solution.py:331
  19.0 0.2 collective-permute-start.8
  19.3 4.4 %conv.1 = (bf16[16,2,2,16,128]{4,3,2,1,0:T(8,128)(2,1)S(1)}, bf16[16,2,2,16,128]{4,3,2,1,0:T(8,128)(2,1)}, bf16[16,2,2,16,128]{4,3,2,1,0:T(8,128)(2,1)}, bf16[16,2,2,16,128]{4,3,2,1,0:T(8,128)(2,1)}) custom-call(s32[1]{0:T(128)} %bitcast.pos_ref, bf16[4,17,128,128]{3,2,1,0:T(8,128)(2,1)S(1)} %get-tuple-element.55.refs_0_, ...), custom_call_target="tpu_custom_call" | custom-call | flops 17179869184 | bytes 2359296 | tf_op jit(solution)/shard_map/conv/pallas_call | solution.py:356
  23.6 2.0 %collective-permute-start.9 = (bf16[4,2,2,16,128]{4,3,2,1,0:T(8,128)(2,1)S(1)}, bf16[4,2,2,16,128]{4,3,2,1,0:T(8,128)(2,1)S(1)}, u32[]{:S(2)}, u32[]{:S(2)}) collective-permute-start(bf16[4,2,2,16,128]{4,3,2,1,0:T(8,128)(2,1)S(1)} %get-tuple-element.81), channel_id=1, source_target_pairs={{0,16},{8,24},{16,0},{24,8},{1,17},{9,25},{17,1},{25,9},{2,18},{10... | collective-permute-start | bytes 196616 | tf_op jit(solution)/shard_map/ppermute | solution.py:331
  25.7 0.8 %collective-permute-start.10 = (bf16[4,2,2,16,128]{4,3,2,1,0:T(8,128)(2,1)S(1)}, bf16[4,2,2,16,128]{4,3,2,1,0:T(8,128)(2,1)S(1)}, u32[]{:S(2)}, u32[]{:S(2)}) collective-permute-start(bf16[4,2,2,16,128]{4,3,2,1,0:T(8,128)(2,1)S(1)} %get-tuple-element.82), channel_id=1, source_target_pairs={{0,24},{8,16},{16,8},{24,0},{1,25},{9,17},{17,9},{25,1},{2,26},{10... | collective-permute-start | bytes 196616 | tf_op jit(solution)/shard_map/ppermute | solution.py:331
  26.4 2.7 %lags.3 = (f32[16,4,128]{2,1,0:T(4,128)S(1)}, f32[16,4,128]{2,1,0:T(4,128)S(1)}, f32[16,4,128]{2,1,0:T(4,128)S(1)}, f32[16,4,128]{2,1,0:T(4,128)S(1)}, f32[4,128]{1,0:T(4,128)S(1)}) custom-call(s32[1]{0:T(128)} %bitcast.pos_ref, bf16[16,2,2,16,128]{4,3,2,1,0:T(8,128)(2,1)S(1)} %copy-done.3, ...), custom_call_target="tpu_custom_call" | custom-call | flops 8589934592 | bytes 2097152 | tf_op jit(solution)/shard_map/lags/pallas_call | solution.py:376
  29.1 0.1 collective-permute-start.3
  29.2 1.4 %collective-permute-start.4 = (bf16[16,2,2,16,128]{4,3,2,1,0:T(8,128)(2,1)}, bf16[16,2,2,16,128]{4,3,2,1,0:T(8,128)(2,1)S(1)}, u32[]{:S(2)}, u32[]{:S(2)}) collective-permute-start(bf16[16,2,2,16,128]{4,3,2,1,0:T(8,128)(2,1)} %get-tuple-element.65), channel_id=1, source_target_pairs={{0,16},{8,24},{16,0},{24,8},{1,17},{9,25},{17,1},{25,9},{2,18},{10... | collective-permute-start | bytes 786440 | tf_op jit(solution)/shard_map/ppermute | solution.py:331
  30.6 1.5 %lags.4 = (f32[16,4,128]{2,1,0:T(4,128)S(1)}, f32[16,4,128]{2,1,0:T(4,128)S(1)}, f32[16,4,128]{2,1,0:T(4,128)S(1)}, f32[16,4,128]{2,1,0:T(4,128)S(1)}, f32[4,128]{1,0:T(4,128)S(1)}) custom-call(s32[1]{0:T(128)} %bitcast.pos_ref, ...), custom_call_target="tpu_custom_call", output_to_operand_aliasing={{0}: (9, {}), {1}: (10, {}), {2}: (11, {}), {3}: (12, {})} | custom-call | flops 4294967296 | bytes 2097152 | tf_op jit(solution)/shard_map/lags/pallas_call | solution.py:376
  32.1 0.6 %collective-permute-start.5 = (bf16[16,2,2,16,128]{4,3,2,1,0:T(8,128)(2,1)}, bf16[16,2,2,16,128]{4,3,2,1,0:T(8,128)(2,1)S(1)}, u32[]{:S(2)}, u32[]{:S(2)}) collective-permute-start(bf16[16,2,2,16,128]{4,3,2,1,0:T(8,128)(2,1)} %get-tuple-element.66), channel_id=1, source_target_pairs={{0,24},{8,16},{16,8},{24,0},{1,25},{9,17},{17,9},{25,1},{2,26},{10... | collective-permute-start | bytes 786440 | tf_op jit(solution)/shard_map/ppermute | solution.py:331
  32.7 2.2 %lags.5 = (f32[16,4,128]{2,1,0:T(4,128)S(1)}, f32[16,4,128]{2,1,0:T(4,128)S(1)}, f32[16,4,128]{2,1,0:T(4,128)S(1)}, f32[16,4,128]{2,1,0:T(4,128)S(1)}, f32[32,4,128]{2,1,0:T(4,128)}) custom-call(s32[1]{0:T(128)} %bitcast.pos_ref, ...), custom_call_target="tpu_custom_call", output_to_operand_aliasing={{0}: (9, {}), {1}: (10, {}), {2}: (11, {}), {3}: (12, {})} | custom-call | flops 4294967296 | bytes 2097152 | tf_op jit(solution)/shard_map/lags/pallas_call | solution.py:376
  34.8 5.6 %all-to-all-start = ((f32[32,4,128]{2,1,0:T(4,128)}), f32[32,4,128]{2,1,0:T(4,128)S(1)}, u32[]{:S(2)}, u32[]{:S(2)}) async-start(f32[32,4,128]{2,1,0:T(4,128)} %get-tuple-element.101), calls=%async_computation | async-start | bytes 131072 | tf_op jit(solution)/shard_map/all_to_all | solution.py:395
  40.4 0.3 collective-permute-start.15
  40.7 1.7 %collective-permute-start.16 = (f32[16,4,128]{2,1,0:T(4,128)S(1)}, f32[16,4,128]{2,1,0:T(4,128)S(1)}, u32[]{:S(2)}, u32[]{:S(2)}) collective-permute-start(f32[16,4,128]{2,1,0:T(4,128)S(1)} %get-tuple-element.104), channel_id=1, source_target_pairs={{0,16},{8,24},{16,0},{24,8},{1,17},{9,25},{17,1},{25,9},{2,18},{10... | collective-permute-start | bytes 98312 | tf_op jit(solution)/shard_map/ppermute | solution.py:331
  42.4 0.9 %collective-permute-done.5.refs_3_ = bf16[16,2,2,16,128]{4,3,2,1,0:T(8,128)(2,1)S(1)} collective-permute-done((bf16[16,2,2,16,128]{4,3,2,1,0:T(8,128)(2,1)}, bf16[16,2,2,16,128]{4,3,2,1,0:T(8,128)(2,1)S(1)}, u32[]{:S(2)}, u32[]{:S(2)}) %collective-permute-start.5) | collective-permute-done | bytes 262176 | tf_op jit(solution)/shard_map/ppermute | solution.py:331
  43.3 2.1 %ungate.1 = (bf16[1,512,1024]{2,1,0:T(8,128)(2,1)}, bf16[1,512,1024]{2,1,0:T(8,128)(2,1)}, f32[8,128]{1,0:T(8,128)S(1)}) custom-call(s32[1]{0:T(128)} %bitcast.pos_ref, bf16[1,512,1024]{2,1,0:T(8,128)(2,1)S(1)} %copy-done, bf16[1,512,1024]{2,1,0:T(8,128)(2,1)S(1)} %copy-done.1, bf16[16,2,2,16,128]{4,3,2,1,0:T(8,128)(2,1)S(1)} %get-tuple-element.63.refs_0_.refs_8_, ...), custom_call_target="tpu_custom_call" | custom-call | flops 1048576 | bytes 5242880 | tf_op jit(solution)/shard_map/ungate/pallas_call | solution.py:398
  45.4 0.6 %collective-permute-done.17.refs_3_ = f32[16,4,128]{2,1,0:T(4,128)S(1)} collective-permute-done((f32[16,4,128]{2,1,0:T(4,128)S(1)}, f32[16,4,128]{2,1,0:T(4,128)S(1)}, u32[]{:S(2)}, u32[]{:S(2)}) %collective-permute-start.17) | collective-permute-done | bytes 32800 | tf_op jit(solution)/shard_map/ppermute | solution.py:331
  45.9 1.7 %all-to-all-done.total_ref = f32[32,4,128]{2,1,0:T(4,128)S(1)} async-done(((f32[32,4,128]{2,1,0:T(4,128)}), f32[32,4,128]{2,1,0:T(4,128)S(1)}, u32[]{:S(2)}, u32[]{:S(2)}) %all-to-all-start) | async-done | bytes 65568 | tf_op jit(solution)/shard_map/all_to_all | solution.py:395
  47.7 0.9 %clip.1 = f32[64,512]{1,0:T(8,128)} custom-call(s32[1]{0:T(128)} %bitcast.pos_ref, f32[32,4,128]{2,1,0:T(4,128)S(1)} %all-to-all-done.total_ref, f32[16,4,128]{2,1,0:T(4,128)S(1)} %get-tuple-element.102.refs_0_, f32[16,4,128]{2,1,0:T(4,128)S(1)} %collective-permute-done.15.refs_1_, f32[16,4,128]{2,1,0:T(4,128)S(1)} %collective-permute-done.16.refs_2_, ...), custom_call_target="tpu_custom_call" | custom-call | flops 131072 | bytes 524288 | tf_op jit(solution)/shard_map/clip/pallas_call | solution.py:417
  (25 shorter events, 0.1 us)
Async XLA Ops:
  0.6 5.9 %copy-start = (bf16[1,512,1024]{2,1,0:T(8,128)(2,1)S(1)}, bf16[1,512,1024]{2,1,0:T(8,128)(2,1)}, u32[]{:S(2)}) copy-start(bf16[1,512,1024]{2,1,0:T(8,128)(2,1)} %left_ref.3) | copy-start | bytes 3145732
  0.6 5.9 %copy-start.1 = (bf16[1,512,1024]{2,1,0:T(8,128)(2,1)S(1)}, bf16[1,512,1024]{2,1,0:T(8,128)(2,1)}, u32[]{:S(2)}) copy-start(bf16[1,512,1024]{2,1,0:T(8,128)(2,1)} %right_ref.3) | copy-start | bytes 3145732
  3.3 13.1 %collective-permute-start = (bf16[16,2,2,16,128]{4,3,2,1,0:T(8,128)(2,1)}, bf16[16,2,2,16,128]{4,3,2,1,0:T(8,128)(2,1)S(1)}, u32[]{:S(2)}, u32[]{:S(2)}) collective-permute-start(bf16[16,2,2,16,128]{4,3,2,1,0:T(8,128)(2,1)} %get-tuple-element.60), channel_id=1, source_target_pairs={{0,8},{8,0},{16,24},{24,16},{1,9},{9,1},{17,25},{25,17},{2,10},{10... | collective-permute-start | bytes 786440 | tf_op jit(solution)/shard_map/ppermute | solution.py:331
  3.9 14.1 %collective-permute-start.1 = (bf16[16,2,2,16,128]{4,3,2,1,0:T(8,128)(2,1)}, bf16[16,2,2,16,128]{4,3,2,1,0:T(8,128)(2,1)S(1)}, u32[]{:S(2)}, u32[]{:S(2)}) collective-permute-start(bf16[16,2,2,16,128]{4,3,2,1,0:T(8,128)(2,1)} %get-tuple-element.61), channel_id=1, source_target_pairs={{0,16},{8,24},{16,0},{24,8},{1,17},{9,25},{17,1},{25,9},{2,18},{10... | collective-permute-start | bytes 786440 | tf_op jit(solution)/shard_map/ppermute | solution.py:331
  6.5 12.6 %collective-permute-start.2 = (bf16[16,2,2,16,128]{4,3,2,1,0:T(8,128)(2,1)}, bf16[16,2,2,16,128]{4,3,2,1,0:T(8,128)(2,1)S(1)}, u32[]{:S(2)}, u32[]{:S(2)}) collective-permute-start(bf16[16,2,2,16,128]{4,3,2,1,0:T(8,128)(2,1)} %get-tuple-element.62), channel_id=1, source_target_pairs={{0,24},{8,16},{16,8},{24,0},{1,25},{9,17},{17,9},{25,1},{2,26},{10... | collective-permute-start | bytes 786440 | tf_op jit(solution)/shard_map/ppermute | solution.py:331
  6.5 1.0 %copy-start.2 = (bf16[16,2,2,16,128]{4,3,2,1,0:T(8,128)(2,1)S(1)}, bf16[16,2,2,16,128]{4,3,2,1,0:T(8,128)(2,1)}, u32[]{:S(2)}) copy-start(bf16[16,2,2,16,128]{4,3,2,1,0:T(8,128)(2,1)} %get-tuple-element.59.refs_4_.refs_0_) | copy-start | bytes 786436
  7.5 5.8 %copy-start.4 = (bf16[64,2048]{1,0:T(8,128)(2,1)S(1)}, bf16[64,2048]{1,0:T(8,128)(2,1)}, u32[]{:S(2)}) copy-start(bf16[64,2048]{1,0:T(8,128)(2,1)} %filt_ref.1) | copy-start | bytes 786436
  7.5 11.8 %copy-start.3 = (bf16[16,2,2,16,128]{4,3,2,1,0:T(8,128)(2,1)S(1)}, bf16[16,2,2,16,128]{4,3,2,1,0:T(8,128)(2,1)}, u32[]{:S(2)}) copy-start(bf16[16,2,2,16,128]{4,3,2,1,0:T(8,128)(2,1)} %get-tuple-element.59.refs_4_.refs_0_) | copy-start | bytes 786436
  9.8 1.4 %collective-permute-start.6 = (bf16[8,2,2,16,128]{4,3,2,1,0:T(8,128)(2,1)S(1)}, bf16[8,2,2,16,128]{4,3,2,1,0:T(8,128)(2,1)S(1)}, u32[]{:S(2)}, u32[]{:S(2)}) collective-permute-start(bf16[8,2,2,16,128]{4,3,2,1,0:T(8,128)(2,1)S(1)} %get-tuple-element.77), channel_id=1, source_target_pairs={{0,8},{8,0},{16,24},{24,16},{1,9},{9,1},{17,25},{25,17},{2,10},{10... | collective-permute-start | bytes 393224 | tf_op jit(solution)/shard_map/ppermute | solution.py:331
  11.2 5.1 %collective-permute-start.7 = (bf16[4,2,2,16,128]{4,3,2,1,0:T(8,128)(2,1)S(1)}, bf16[4,2,2,16,128]{4,3,2,1,0:T(8,128)(2,1)S(1)}, u32[]{:S(2)}, u32[]{:S(2)}) collective-permute-start(bf16[4,2,2,16,128]{4,3,2,1,0:T(8,128)(2,1)S(1)} %get-tuple-element.78), channel_id=1, source_target_pairs={{0,8},{8,0},{16,24},{24,16},{1,9},{9,1},{17,25},{25,17},{2,10},{10... | collective-permute-start | bytes 196616 | tf_op jit(solution)/shard_map/ppermute | solution.py:331
  11.4 12.3 %collective-permute-start.13 = (bf16[8,2,2,16,128]{4,3,2,1,0:T(8,128)(2,1)S(1)}, bf16[8,2,2,16,128]{4,3,2,1,0:T(8,128)(2,1)S(1)}, u32[]{:S(2)}, u32[]{:S(2)}) collective-permute-start(bf16[8,2,2,16,128]{4,3,2,1,0:T(8,128)(2,1)S(1)} %get-tuple-element.89), channel_id=1, source_target_pairs={{0,16},{8,24},{16,0},{24,8},{1,17},{9,25},{17,1},{25,9},{2,18},{10... | collective-permute-start | bytes 393224 | tf_op jit(solution)/shard_map/ppermute | solution.py:331
  16.4 9.3 %collective-permute-start.14 = (bf16[8,2,2,16,128]{4,3,2,1,0:T(8,128)(2,1)S(1)}, bf16[8,2,2,16,128]{4,3,2,1,0:T(8,128)(2,1)S(1)}, u32[]{:S(2)}, u32[]{:S(2)}) collective-permute-start(bf16[8,2,2,16,128]{4,3,2,1,0:T(8,128)(2,1)S(1)} %get-tuple-element.90), channel_id=1, source_target_pairs={{0,24},{8,16},{16,8},{24,0},{1,25},{9,17},{17,9},{25,1},{2,26},{10... | collective-permute-start | bytes 393224 | tf_op jit(solution)/shard_map/ppermute | solution.py:331
  16.4 12.7 %collective-permute-start.11 = (bf16[4,2,2,16,128]{4,3,2,1,0:T(8,128)(2,1)S(1)}, bf16[4,2,2,16,128]{4,3,2,1,0:T(8,128)(2,1)S(1)}, u32[]{:S(2)}, u32[]{:S(2)}) collective-permute-start(bf16[4,2,2,16,128]{4,3,2,1,0:T(8,128)(2,1)S(1)} %get-tuple-element.85), channel_id=1, source_target_pairs={{0,16},{8,24},{16,0},{24,8},{1,17},{9,25},{17,1},{25,9},{2,18},{10... | collective-permute-start | bytes 196616 | tf_op jit(solution)/shard_map/ppermute | solution.py:331
  17.9 11.3 %collective-permute-start.12 = (bf16[4,2,2,16,128]{4,3,2,1,0:T(8,128)(2,1)S(1)}, bf16[4,2,2,16,128]{4,3,2,1,0:T(8,128)(2,1)S(1)}, u32[]{:S(2)}, u32[]{:S(2)}) collective-permute-start(bf16[4,2,2,16,128]{4,3,2,1,0:T(8,128)(2,1)S(1)} %get-tuple-element.86), channel_id=1, source_target_pairs={{0,24},{8,16},{16,8},{24,0},{1,25},{9,17},{17,9},{25,1},{2,26},{10... | collective-permute-start | bytes 196616 | tf_op jit(solution)/shard_map/ppermute | solution.py:331
  19.0 13.1 %collective-permute-start.8 = (bf16[4,2,2,16,128]{4,3,2,1,0:T(8,128)(2,1)S(1)}, bf16[4,2,2,16,128]{4,3,2,1,0:T(8,128)(2,1)S(1)}, u32[]{:S(2)}, u32[]{:S(2)}) collective-permute-start(bf16[4,2,2,16,128]{4,3,2,1,0:T(8,128)(2,1)S(1)} %get-tuple-element.80), channel_id=1, source_target_pairs={{0,8},{8,0},{16,24},{24,16},{1,9},{9,1},{17,25},{25,17},{2,10},{10... | collective-permute-start | bytes 196616 | tf_op jit(solution)/shard_map/ppermute | solution.py:331
  23.6 9.0 %collective-permute-start.9 = (bf16[4,2,2,16,128]{4,3,2,1,0:T(8,128)(2,1)S(1)}, bf16[4,2,2,16,128]{4,3,2,1,0:T(8,128)(2,1)S(1)}, u32[]{:S(2)}, u32[]{:S(2)}) collective-permute-start(bf16[4,2,2,16,128]{4,3,2,1,0:T(8,128)(2,1)S(1)} %get-tuple-element.81), channel_id=1, source_target_pairs={{0,16},{8,24},{16,0},{24,8},{1,17},{9,25},{17,1},{25,9},{2,18},{10... | collective-permute-start | bytes 196616 | tf_op jit(solution)/shard_map/ppermute | solution.py:331
  25.7 7.0 %collective-permute-start.10 = (bf16[4,2,2,16,128]{4,3,2,1,0:T(8,128)(2,1)S(1)}, bf16[4,2,2,16,128]{4,3,2,1,0:T(8,128)(2,1)S(1)}, u32[]{:S(2)}, u32[]{:S(2)}) collective-permute-start(bf16[4,2,2,16,128]{4,3,2,1,0:T(8,128)(2,1)S(1)} %get-tuple-element.82), channel_id=1, source_target_pairs={{0,24},{8,16},{16,8},{24,0},{1,25},{9,17},{17,9},{25,1},{2,26},{10... | collective-permute-start | bytes 196616 | tf_op jit(solution)/shard_map/ppermute | solution.py:331
  29.1 13.3 %collective-permute-start.3 = (bf16[16,2,2,16,128]{4,3,2,1,0:T(8,128)(2,1)}, bf16[16,2,2,16,128]{4,3,2,1,0:T(8,128)(2,1)S(1)}, u32[]{:S(2)}, u32[]{:S(2)}) collective-permute-start(bf16[16,2,2,16,128]{4,3,2,1,0:T(8,128)(2,1)} %get-tuple-element.64), channel_id=1, source_target_pairs={{0,8},{8,0},{16,24},{24,16},{1,9},{9,1},{17,25},{25,17},{2,10},{10... | collective-permute-start | bytes 786440 | tf_op jit(solution)/shard_map/ppermute | solution.py:331
  29.2 13.2 %collective-permute-start.4 = (bf16[16,2,2,16,128]{4,3,2,1,0:T(8,128)(2,1)}, bf16[16,2,2,16,128]{4,3,2,1,0:T(8,128)(2,1)S(1)}, u32[]{:S(2)}, u32[]{:S(2)}) collective-permute-start(bf16[16,2,2,16,128]{4,3,2,1,0:T(8,128)(2,1)} %get-tuple-element.65), channel_id=1, source_target_pairs={{0,16},{8,24},{16,0},{24,8},{1,17},{9,25},{17,1},{25,9},{2,18},{10... | collective-permute-start | bytes 786440 | tf_op jit(solution)/shard_map/ppermute | solution.py:331
  32.1 11.2 %collective-permute-start.5 = (bf16[16,2,2,16,128]{4,3,2,1,0:T(8,128)(2,1)}, bf16[16,2,2,16,128]{4,3,2,1,0:T(8,128)(2,1)S(1)}, u32[]{:S(2)}, u32[]{:S(2)}) collective-permute-start(bf16[16,2,2,16,128]{4,3,2,1,0:T(8,128)(2,1)} %get-tuple-element.66), channel_id=1, source_target_pairs={{0,24},{8,16},{16,8},{24,0},{1,25},{9,17},{17,9},{25,1},{2,26},{10... | collective-permute-start | bytes 786440 | tf_op jit(solution)/shard_map/ppermute | solution.py:331
  34.8 12.9 %all-to-all-start = ((f32[32,4,128]{2,1,0:T(4,128)}), f32[32,4,128]{2,1,0:T(4,128)S(1)}, u32[]{:S(2)}, u32[]{:S(2)}) async-start(f32[32,4,128]{2,1,0:T(4,128)} %get-tuple-element.101), calls=%async_computation | async-start | bytes 131072 | tf_op jit(solution)/shard_map/all_to_all | solution.py:395
  40.4 5.0 %collective-permute-start.15 = (f32[16,4,128]{2,1,0:T(4,128)S(1)}, f32[16,4,128]{2,1,0:T(4,128)S(1)}, u32[]{:S(2)}, u32[]{:S(2)}) collective-permute-start(f32[16,4,128]{2,1,0:T(4,128)S(1)} %get-tuple-element.103), channel_id=1, source_target_pairs={{0,8},{8,0},{16,24},{24,16},{1,9},{9,1},{17,25},{25,17},{2,10},{10... | collective-permute-start | bytes 98312 | tf_op jit(solution)/shard_map/ppermute | solution.py:331
  40.7 4.7 %collective-permute-start.16 = (f32[16,4,128]{2,1,0:T(4,128)S(1)}, f32[16,4,128]{2,1,0:T(4,128)S(1)}, u32[]{:S(2)}, u32[]{:S(2)}) collective-permute-start(f32[16,4,128]{2,1,0:T(4,128)S(1)} %get-tuple-element.104), channel_id=1, source_target_pairs={{0,16},{8,24},{16,0},{24,8},{1,17},{9,25},{17,1},{25,9},{2,18},{10... | collective-permute-start | bytes 98312 | tf_op jit(solution)/shard_map/ppermute | solution.py:331
  42.4 3.5 %collective-permute-start.17 = (f32[16,4,128]{2,1,0:T(4,128)S(1)}, f32[16,4,128]{2,1,0:T(4,128)S(1)}, u32[]{:S(2)}, u32[]{:S(2)}) collective-permute-start(f32[16,4,128]{2,1,0:T(4,128)S(1)} %get-tuple-element.105), channel_id=1, source_target_pairs={{0,24},{8,16},{16,8},{24,0},{1,25},{9,17},{17,9},{25,1},{2,26},{10... | collective-permute-start | bytes 98312 | tf_op jit(solution)/shard_map/ppermute | solution.py:331

commit v10 on v8

--- a/solution.py
+++ b/solution.py
@@ -15,17 +15,20 @@
 BF16, F32 = jnp.bfloat16, jnp.float32
 
 
-def gate_kernel(pos_ref, left_ref, right_ref, *refs, reverse, sizes, ordered):
+def gate_kernel(pos_ref, left_ref, right_ref, *refs, reverse, sizes, ordered, window, peers):
     *outs, left, right, out, in_sem, out_sem = refs[ordered:]
-    local = left.shape[0] // LANES
+    local, wide = left.shape[0] // LANES, left.shape[1]
+    chip = jnp.right_shift(pos_ref[0], 1)
+    start = {"all": 0, "far": (1 - chip) * wide, "near": chip * wide}[window]
+    there = pl.ds(start if window == "all" else pl.multiple_of(start, wide), wide)
     per_device = sum(sizes)
     copies = []
     for i in range(local):
         here = pl.ds(i * LANES, LANES)
         copies.append(
             (
-                pltpu.make_async_copy(left_ref.at[0, here], left.at[here], in_sem.at[i, 0]),
-                pltpu.make_async_copy(right_ref.at[0, here], right.at[here], in_sem.at[i, 1]),
+                pltpu.make_async_copy(left_ref.at[0, here, there], left.at[here], in_sem.at[i, 0]),
+                pltpu.make_async_copy(right_ref.at[0, here, there], right.at[here], in_sem.at[i, 1]),
             )
         )
     for pair in copies:
@@ -46,7 +49,7 @@
         out[i % 2, i // 2] = value.reshape(out.shape[2:])
         for n, target in enumerate(outs):
             k, chunk = divmod(n, len(sizes))
-            first = jnp.bitwise_xor(pos_ref[0], k) * per_device + sum(sizes[:chunk])
+            first = jnp.bitwise_xor(pos_ref[0], peers[k]) * per_device - start // GROUP + sum(sizes[:chunk])
             send = pltpu.make_async_copy(
                 out.at[i % 2, i // 2, pl.ds(first, sizes[chunk])],
                 target.at[:, i % 2, i // 2],
@@ -299,21 +302,30 @@
     piece = jax.ShapeDtypeStruct((per_device,) + tail, BF16)
     lag_piece = jax.ShapeDtypeStruct((per_device, blocks // owners, LANES), F32)
 
-    def gate(left, right, after, reverse, sizes, limit, name):
+    def gate(left, right, after, reverse, sizes, limit, name, window="all", peers=None):
+        peers = peers or tuple(range(owners))
+        wide = chans if window == "all" else chans // 2
         parts = [jax.ShapeDtypeStruct((n,) + tail, BF16) for n in sizes]
         out = pl.pallas_call(
-            functools.partial(gate_kernel, reverse=reverse, sizes=sizes, ordered=len(after)),
+            functools.partial(
+                gate_kernel,
+                reverse=reverse,
+                sizes=sizes,
+                ordered=len(after),
+                window=window,
+                peers=peers,
+            ),
             in_specs=[smem] + [pl.BlockSpec(memory_space=pltpu.HBM)] * 2 + [vmem] * len(after),
-            out_specs=[anywhere] * (owners * len(sizes)),
-            out_shape=parts * owners,
+            out_specs=[anywhere] * (len(peers) * len(sizes)),
+            out_shape=parts * len(peers),
             scratch_shapes=[
-                pltpu.VMEM((block_len, chans), BF16),
-                pltpu.VMEM((block_len, chans), BF16),
-                pltpu.VMEM((2, local // 2, groups, GROUP, LANES), BF16),
+                pltpu.VMEM((block_len, wide), BF16),
+                pltpu.VMEM((block_len, wide), BF16),
+                pltpu.VMEM((2, local // 2, wide // GROUP, GROUP, LANES), BF16),
                 pltpu.SemaphoreType.DMA((local, 2)),
-                pltpu.SemaphoreType.DMA((local, owners * len(sizes))),
+                pltpu.SemaphoreType.DMA((local, len(peers) * len(sizes))),
             ],
-            cost_estimate=cost(block_len * chans, 3 * size),
+            cost_estimate=cost(block_len * wide, 6 * block_len * wide),
             compiler_params=pltpu.CompilerParams(vmem_limit_bytes=limit << 20),
             name=name,
         )(pos, left, right, *after)
@@ -326,9 +338,21 @@
         return out
 
     sizes = (8, 8) if per_device == 16 else (per_device,)
-    (grad_send,) = gate(grad_out, out_gate, (), False, (per_device,), 56, "gate_grad")
-    grad_got = swap(grad_send)
-    prod_send = gate(q_branch, k_branch, grad_send[:1], True, sizes, 12, "gate_prod")
+    if owners == 4:
+        (far,) = gate(
+            grad_out, out_gate, (), False, (per_device,), 56, "gate_far", "far", (2, 3)
+        )
+        far_send = far
+        far = [lax.ppermute(v, "ctx", [(i, i ^ k) for i in range(4)]) for k, v in zip((2, 3), far)]
+        prod_send = gate(q_branch, k_branch, (), True, sizes, 12, "gate_prod")
+        (near,) = gate(
+            grad_out, out_gate, prod_send[0][:1], False, (per_device,), 12, "gate_near", "near", (0, 1)
+        )
+        grad_got = [near[0], lax.ppermute(near[1], "ctx", [(i, i ^ 1) for i in range(4)]), *far]
+    else:
+        (grad_send,) = gate(grad_out, out_gate, (), False, (per_device,), 56, "gate_grad")
+        grad_got = swap(grad_send)
+        prod_send = gate(q_branch, k_branch, grad_send[:1], True, sizes, 12, "gate_prod")
     prod_got = []
     for part in prod_send:
         if prod_got:

time: 48.6 us -> 48.3 us (level)
  starting transfers between devices: 19.5 us -> 17.8 us
  local copies, waits for them, and re-layouts: 0.97 us -> 2.47 us
  waiting for transfers between devices: 6.33 us -> 5.7 us
    ppermute x15 -> x12, starting transfers between devices: 13.2 us -> 8.3 us  [swap(): lax.ppermute(values[k], 'ctx', [(i, i ^ k) for i in range(owners)])]
    ppermute x0 -> x3, starting transfers between devices: none -> 3.29 us  [the longest x2 3.03 us: on_device(): lax.ppermute(v, 'ctx', [(i, i ^ k) for i in range(4)])]
    ppermute x15 -> x12, waiting for transfers between devices: 4.21 us -> 2.02 us  [swap(): lax.ppermute(values[k], 'ctx', [(i, i ^ k) for i in range(owners)])]
    ppermute x0 -> x3, waiting for transfers between devices: none -> 1.55 us  [the longest x2 1.55 us: on_device(): lax.ppermute(v, 'ctx', [(i, i ^ k) for i in range(4)])]
    unnamed x10 -> x14, local copies, waits for them, and re-layouts: 0.97 us -> 2.47 us
    pallas_call x2 -> x3, Pallas kernels: 4.66 us -> 5.08 us  [gate(): pl.pallas_call(functools.partial(gate_kernel, reverse=reverse, sizes=size...]
  transfers between devices with their start and end apart: 16 -> 16, of which waited for: 5 -> 5; matrix products, arithmetic and copies ran while one was open for 0% -> 0% of each run, Pallas kernels for 36% -> 37%
where the time goes in v10:
time: 48.3 us; the launch traced here: 48.1 us
  Pallas kernels  21.3 us (44%)
  starting transfers between devices  17.8 us (37%)
  waiting for transfers between devices  5.7 us (12%)
  local copies, waits for them, and re-layouts  2.47 us (5%)
  between operations  0.78 us (2%)
    ppermute x12, starting transfers between devices, swap(): lax.ppermute(values[k], 'ctx', [(i, i ^ k) for i in range(owners)])  8.3 us
    all_to_all x1, starting transfers between devices, on_device(): total = lax.all_to_all(spread, both, 0, 0, tiled=True)  6.24 us
    pallas_call x2, Pallas kernels, on_device(): pl.pallas_call(functools.partial(lag_kernel, owners=owners, unroll=unroll...  6.04 us
    pallas_call x3, Pallas kernels, gate(): pl.pallas_call(functools.partial(gate_kernel, reverse=reverse, sizes=size...  5.08 us
    pallas_call x1, Pallas kernels, on_device(): pl.pallas_call(functools.partial(conv_kernel, owners=owners, unroll=unrol...  4.13 us
    pallas_call x1, Pallas kernels, on_device(): pl.pallas_call(blocks_kernel, in_specs=[smem, vmem], out_specs=[vmem] * u...  3.04 us
    ppermute x2, starting transfers between devices, on_device(): lax.ppermute(v, 'ctx', [(i, i ^ k) for i in range(4)])  3.03 us
    unnamed x14, local copies, waits for them, and re-layouts  2.47 us
  transfers between devices with their start and end apart: 16, of which 5 were waited for; matrix products, arithmetic and copies ran while one was open for 0% of the time, Pallas kernels for 37%

profile of v10, /device:TPU:0, one launch (start us, length us, event | category | flops | bytes accessed | tf_op | source)
XLA Modules:
  0.0 48.1 jit_solution(7999486180299374774)
XLA Ops:
  0.7 2.3 %gate_far.1 = (bf16[16,2,2,16,128]{4,3,2,1,0:T(8,128)(2,1)}, bf16[16,2,2,16,128]{4,3,2,1,0:T(8,128)(2,1)}) custom-call(s32[1]{0:T(128)} %bitcast.pos_ref, bf16[1,512,1024]{2,1,0:T(8,128)(2,1)} %left_ref.5, bf16[1,512,1024]{2,1,0:T(8,128)(2,1)} %right_ref.5), custom_call_target="tpu_custom_call" | custom-call | flops 262144 | bytes 1572864 | tf_op jit(solution)/shard_map/gate_far/pallas_call | solution.py:309
  3.0 3.0 %collective-permute-start.1 = (bf16[16,2,2,16,128]{4,3,2,1,0:T(8,128)(2,1)}, bf16[16,2,2,16,128]{4,3,2,1,0:T(8,128)(2,1)S(1)}, u32[]{:S(2)}, u32[]{:S(2)}) collective-permute-start(bf16[16,2,2,16,128]{4,3,2,1,0:T(8,128)(2,1)} %get-tuple-element.48), channel_id=1, source_target_pairs={{0,16},{8,24},{16,0},{24,8},{1,17},{9,25},{17,1},{25,9},{2,18},{10... | collective-permute-start | bytes 786440 | tf_op jit(solution)/shard_map/ppermute | solution.py:346
  6.0 0.0 collective-permute-start.2
  6.0 1.2 %copy-done.2 = bf16[1,512,1024]{2,1,0:T(8,128)(2,1)S(1)} copy-done((bf16[1,512,1024]{2,1,0:T(8,128)(2,1)S(1)}, bf16[1,512,1024]{2,1,0:T(8,128)(2,1)}, u32[]{:S(2)}) %copy-start.2) | copy-done | bytes 1048600
  7.2 1.2 %copy-done.4 = bf16[1,512,1024]{2,1,0:T(8,128)(2,1)S(1)} copy-done((bf16[1,512,1024]{2,1,0:T(8,128)(2,1)S(1)}, bf16[1,512,1024]{2,1,0:T(8,128)(2,1)}, u32[]{:S(2)}) %copy-start.4) | copy-done | bytes 1048600
  8.5 2.0 %gate_prod.1 = (bf16[8,2,2,16,128]{4,3,2,1,0:T(8,128)(2,1)S(1)}, bf16[8,2,2,16,128]{4,3,2,1,0:T(8,128)(2,1)S(1)}, bf16[8,2,2,16,128]{4,3,2,1,0:T(8,128)(2,1)S(1)...) custom-call(s32[1]{0:T(128)} %bitcast.pos_ref, ...), custom_call_target="tpu_custom_call" | custom-call | flops 524288 | bytes 3145728 | tf_op jit(solution)/shard_map/gate_prod/pallas_call | solution.py:309
  10.5 0.8 %gate_near.1 = (bf16[16,2,2,16,128]{4,3,2,1,0:T(8,128)(2,1)S(1)}, bf16[16,2,2,16,128]{4,3,2,1,0:T(8,128)(2,1)S(1)}) custom-call(s32[1]{0:T(128)} %bitcast.pos_ref, bf16[1,512,1024]{2,1,0:T(8,128)(2,1)S(1)} %copy-done, bf16[1,512,1024]{2,1,0:T(8,128)(2,1)S(1)} %copy-done.1, bf16[8,2,2,16,128]{4,3,2,1,0:T(8,128)(2,1)S(1)} %get-tuple-element.45.refs_0_.refs_4_), custom_call_target="tpu_custom_call" | custom-call | flops 262144 | bytes 1572864 | tf_op jit(solution)/shard_map/gate_near/pallas_call | solution.py:309
  11.3 0.3 collective-permute-start
  11.5 0.3 collective-permute-start.6
  11.8 1.7 %collective-permute-start.10 = (bf16[8,2,2,16,128]{4,3,2,1,0:T(8,128)(2,1)S(1)}, bf16[8,2,2,16,128]{4,3,2,1,0:T(8,128)(2,1)S(1)}, u32[]{:S(2)}, u32[]{:S(2)}) collective-permute-start(bf16[8,2,2,16,128]{4,3,2,1,0:T(8,128)(2,1)S(1)} %get-tuple-element.66), channel_id=1, source_target_pairs={{0,16},{8,24},{16,0},{24,8},{1,17},{9,25},{17,1},{25,9},{2,18},{10... | collective-permute-start | bytes 393224 | tf_op jit(solution)/shard_map/ppermute | solution.py:337
  13.6 3.0 %blocks.1 = (bf16[4,17,128,128]{3,2,1,0:T(8,128)(2,1)S(1)}, bf16[4,17,128,128]{3,2,1,0:T(8,128)(2,1)S(1)}, bf16[4,17,128,128]{3,2,1,0:T(8,128)(2,1)S(1)}, bf16[4,17,128,128]{3,2,1,0:T(8,128)(2,1)S(1)}) custom-call(s32[1]{0:T(128)} %bitcast.pos_ref, bf16[64,2048]{1,0:T(8,128)(2,1)S(1)} %copy-done.6), custom_call_target="tpu_custom_call" | custom-call | flops 1 | bytes 1 | tf_op jit(solution)/shard_map/blocks/pallas_call | solution.py:362
  16.6 0.0 collective-permute-done.6.refs_5_
  16.6 0.1 collective-permute-start.11
  16.7 0.4 collective-permute-start.7
  17.1 1.5 %collective-permute-done.2.refs_7_.refs_3_ = bf16[16,2,2,16,128]{4,3,2,1,0:T(8,128)(2,1)S(1)} collective-permute-done((bf16[16,2,2,16,128]{4,3,2,1,0:T(8,128)(2,1)}, bf16[16,2,2,16,128]{4,3,2,1,0:T(8,128)(2,1)S(1)}, u32[]{:S(2)}, u32[]{:S(2)}) %collective-permute-start.2) | collective-permute-done | bytes 262176 | tf_op jit(solution)/shard_map/ppermute | solution.py:346
  18.7 0.2 collective-permute-start.8
  18.8 1.7 %collective-permute-start.9 = (bf16[8,2,2,16,128]{4,3,2,1,0:T(8,128)(2,1)S(1)}, bf16[8,2,2,16,128]{4,3,2,1,0:T(8,128)(2,1)S(1)}, u32[]{:S(2)}, u32[]{:S(2)}) collective-permute-start(bf16[8,2,2,16,128]{4,3,2,1,0:T(8,128)(2,1)S(1)} %get-tuple-element.64), channel_id=1, source_target_pairs={{0,24},{8,16},{16,8},{24,0},{1,25},{9,17},{17,9},{25,1},{2,26},{10... | collective-permute-start | bytes 393224 | tf_op jit(solution)/shard_map/ppermute | solution.py:337
  20.5 4.1 %conv.1 = (bf16[16,2,2,16,128]{4,3,2,1,0:T(8,128)(2,1)S(1)}, bf16[16,2,2,16,128]{4,3,2,1,0:T(8,128)(2,1)}, bf16[16,2,2,16,128]{4,3,2,1,0:T(8,128)(2,1)}, bf16[16,2,2,16,128]{4,3,2,1,0:T(8,128)(2,1)}) custom-call(s32[1]{0:T(128)} %bitcast.pos_ref, bf16[4,17,128,128]{3,2,1,0:T(8,128)(2,1)S(1)} %get-tuple-element.41.refs_0_, ...), custom_call_target="tpu_custom_call" | custom-call | flops 17179869184 | bytes 2359296 | tf_op jit(solution)/shard_map/conv/pallas_call | solution.py:374
  24.6 0.3 collective-permute-start.3
  24.9 1.5 %collective-permute-start.4 = (bf16[16,2,2,16,128]{4,3,2,1,0:T(8,128)(2,1)}, bf16[16,2,2,16,128]{4,3,2,1,0:T(8,128)(2,1)S(1)}, u32[]{:S(2)}, u32[]{:S(2)}) collective-permute-start(bf16[16,2,2,16,128]{4,3,2,1,0:T(8,128)(2,1)} %get-tuple-element.52), channel_id=1, source_target_pairs={{0,16},{8,24},{16,0},{24,8},{1,17},{9,25},{17,1},{25,9},{2,18},{10... | collective-permute-start | bytes 786440 | tf_op jit(solution)/shard_map/ppermute | solution.py:337
  26.5 2.7 %lags.2 = (f32[16,4,128]{2,1,0:T(4,128)S(1)}, f32[16,4,128]{2,1,0:T(4,128)S(1)}, f32[16,4,128]{2,1,0:T(4,128)S(1)}, f32[16,4,128]{2,1,0:T(4,128)S(1)}, f32[4,128]{1,0:T(4,128)S(1)}) custom-call(s32[1]{0:T(128)} %bitcast.pos_ref, bf16[16,2,2,16,128]{4,3,2,1,0:T(8,128)(2,1)S(1)} %get-tuple-element.46.refs_4_.refs_0_, ...), custom_call_target="tpu_custom_call" | custom-call | flops 8589934592 | bytes 2097152 | tf_op jit(solution)/shard_map/lags/pallas_call | solution.py:392
  29.1 0.1 collective-permute-start.5
  29.3 0.5 %collective-permute-done.9.refs_7_ = bf16[8,2,2,16,128]{4,3,2,1,0:T(8,128)(2,1)S(1)} collective-permute-done((bf16[8,2,2,16,128]{4,3,2,1,0:T(8,128)(2,1)S(1)}, bf16[8,2,2,16,128]{4,3,2,1,0:T(8,128)(2,1)S(1)}, u32[]{:S(2)}, u32[]{:S(2)}) %collective-permute-start.9) | collective-permute-done | bytes 131104 | tf_op jit(solution)/shard_map/ppermute | solution.py:337
  29.8 3.4 %lags.3 = (f32[16,4,128]{2,1,0:T(4,128)S(1)}, f32[16,4,128]{2,1,0:T(4,128)S(1)}, f32[16,4,128]{2,1,0:T(4,128)S(1)}, f32[16,4,128]{2,1,0:T(4,128)S(1)}, f32[32,8,128]{2,1,0:T(8,128)}) custom-call(s32[1]{0:T(128)} %bitcast.pos_ref, ...), custom_call_target="tpu_custom_call", output_to_operand_aliasing={{0}: (9, {}), {1}: (10, {}), {2}: (11, {}), {3}: (12, {})} | custom-call | flops 8589934592 | bytes 2097152 | tf_op jit(solution)/shard_map/lags/pallas_call | solution.py:392
  33.2 6.2 %all-to-all-start = ((f32[32,8,128]{2,1,0:T(8,128)}), f32[32,8,128]{2,1,0:T(8,128)S(1)}, u32[]{:S(2)}, u32[]{:S(2)}) async-start(f32[32,8,128]{2,1,0:T(8,128)} %get-tuple-element.73), calls=%async_computation | async-start | bytes 262144 | tf_op jit(solution)/shard_map/all_to_all | solution.py:411
  39.4 0.3 collective-permute-start.12
  39.7 1.7 %collective-permute-start.13 = (f32[16,4,128]{2,1,0:T(4,128)S(1)}, f32[16,4,128]{2,1,0:T(4,128)S(1)}, u32[]{:S(2)}, u32[]{:S(2)}) collective-permute-start(f32[16,4,128]{2,1,0:T(4,128)S(1)} %get-tuple-element.76), channel_id=1, source_target_pairs={{0,16},{8,24},{16,0},{24,8},{1,17},{9,25},{17,1},{25,9},{2,18},{10... | collective-permute-start | bytes 98312 | tf_op jit(solution)/shard_map/ppermute | solution.py:337
  41.4 2.1 %ungate.1 = (bf16[1,512,1024]{2,1,0:T(8,128)(2,1)}, bf16[1,512,1024]{2,1,0:T(8,128)(2,1)}, f32[8,128]{1,0:T(8,128)S(1)}) custom-call(s32[1]{0:T(128)} %bitcast.pos_ref, bf16[1,512,1024]{2,1,0:T(8,128)(2,1)S(1)} %copy-done.3, bf16[1,512,1024]{2,1,0:T(8,128)(2,1)S(1)} %copy-done.5, bf16[16,2,2,16,128]{4,3,2,1,0:T(8,128)(2,1)S(1)} %get-tuple-element.50.refs_0_.refs_8_, ...), custom_call_target="tpu_custom_call" | custom-call | flops 1048576 | bytes 5242880 | tf_op jit(solution)/shard_map/ungate/pallas_call | solution.py:414
  43.5 0.2 collective-permute-done.13.refs_2_
  43.7 1.3 %collective-permute-done.14.refs_3_ = f32[16,4,128]{2,1,0:T(4,128)S(1)} collective-permute-done((f32[16,4,128]{2,1,0:T(4,128)S(1)}, f32[16,4,128]{2,1,0:T(4,128)S(1)}, u32[]{:S(2)}, u32[]{:S(2)}) %collective-permute-start.14) | collective-permute-done | bytes 32800 | tf_op jit(solution)/shard_map/ppermute | solution.py:337
  45.0 2.1 %all-to-all-done.total_ref = f32[32,8,128]{2,1,0:T(8,128)S(1)} async-done(((f32[32,8,128]{2,1,0:T(8,128)}), f32[32,8,128]{2,1,0:T(8,128)S(1)}, u32[]{:S(2)}, u32[]{:S(2)}) %all-to-all-start) | async-done | bytes 131104 | tf_op jit(solution)/shard_map/all_to_all | solution.py:411
  47.1 0.9 %clip.1 = f32[64,512]{1,0:T(8,128)} custom-call(s32[1]{0:T(128)} %bitcast.pos_ref, f32[32,8,128]{2,1,0:T(8,128)S(1)} %all-to-all-done.total_ref, f32[16,4,128]{2,1,0:T(4,128)S(1)} %get-tuple-element.74.refs_0_, f32[16,4,128]{2,1,0:T(4,128)S(1)} %collective-permute-done.12.refs_1_, f32[16,4,128]{2,1,0:T(4,128)S(1)} %collective-permute-done.13.refs_2_, ...), custom_call_target="tpu_custom_call" | custom-call | flops 131072 | bytes 524288 | tf_op jit(solution)/shard_map/clip/pallas_call | solution.py:433
  (23 shorter events, 0.1 us)
Async XLA Ops:
  0.6 9.8 %copy-start = (bf16[1,512,1024]{2,1,0:T(8,128)(2,1)S(1)}, bf16[1,512,1024]{2,1,0:T(8,128)(2,1)}, u32[]{:S(2)}) copy-start(bf16[1,512,1024]{2,1,0:T(8,128)(2,1)} %left_ref.5) | copy-start | bytes 3145732
  0.6 9.8 %copy-start.1 = (bf16[1,512,1024]{2,1,0:T(8,128)(2,1)S(1)}, bf16[1,512,1024]{2,1,0:T(8,128)(2,1)}, u32[]{:S(2)}) copy-start(bf16[1,512,1024]{2,1,0:T(8,128)(2,1)} %right_ref.5) | copy-start | bytes 3145732
  3.0 13.7 %collective-permute-start.1 = (bf16[16,2,2,16,128]{4,3,2,1,0:T(8,128)(2,1)}, bf16[16,2,2,16,128]{4,3,2,1,0:T(8,128)(2,1)S(1)}, u32[]{:S(2)}, u32[]{:S(2)}) collective-permute-start(bf16[16,2,2,16,128]{4,3,2,1,0:T(8,128)(2,1)} %get-tuple-element.48), channel_id=1, source_target_pairs={{0,16},{8,24},{16,0},{24,8},{1,17},{9,25},{17,1},{25,9},{2,18},{10... | collective-permute-start | bytes 786440 | tf_op jit(solution)/shard_map/ppermute | solution.py:346
  6.0 12.6 %collective-permute-start.2 = (bf16[16,2,2,16,128]{4,3,2,1,0:T(8,128)(2,1)}, bf16[16,2,2,16,128]{4,3,2,1,0:T(8,128)(2,1)S(1)}, u32[]{:S(2)}, u32[]{:S(2)}) collective-permute-start(bf16[16,2,2,16,128]{4,3,2,1,0:T(8,128)(2,1)} %get-tuple-element.49), channel_id=1, source_target_pairs={{0,24},{8,16},{16,8},{24,0},{1,25},{9,17},{17,9},{25,1},{2,26},{10... | collective-permute-start | bytes 786440 | tf_op jit(solution)/shard_map/ppermute | solution.py:346
  6.0 1.2 %copy-start.2 = (bf16[1,512,1024]{2,1,0:T(8,128)(2,1)S(1)}, bf16[1,512,1024]{2,1,0:T(8,128)(2,1)}, u32[]{:S(2)}) copy-start(bf16[1,512,1024]{2,1,0:T(8,128)(2,1)} %q_ref.1) | copy-start | bytes 3145732
  7.2 1.2 %copy-start.4 = (bf16[1,512,1024]{2,1,0:T(8,128)(2,1)S(1)}, bf16[1,512,1024]{2,1,0:T(8,128)(2,1)}, u32[]{:S(2)}) copy-start(bf16[1,512,1024]{2,1,0:T(8,128)(2,1)} %k_ref.1) | copy-start | bytes 3145732
  8.5 5.1 %copy-start.6 = (bf16[64,2048]{1,0:T(8,128)(2,1)S(1)}, bf16[64,2048]{1,0:T(8,128)(2,1)}, u32[]{:S(2)}) copy-start(bf16[64,2048]{1,0:T(8,128)(2,1)} %filt_ref.1) | copy-start | bytes 786436
  11.3 7.6 %collective-permute-start = (bf16[16,2,2,16,128]{4,3,2,1,0:T(8,128)(2,1)S(1)}, bf16[16,2,2,16,128]{4,3,2,1,0:T(8,128)(2,1)S(1)}, u32[]{:S(2)}, u32[]{:S(2)}) collective-permute-start(bf16[16,2,2,16,128]{4,3,2,1,0:T(8,128)(2,1)S(1)} %get-tuple-element.47), channel_id=1, source_target_pairs={{0,8},{8,0},{16,24},{24,16},{1,9},{9,1},{17,25},{25,17},{2,10},{10... | collective-permute-start | bytes 786440 | tf_op jit(solution)/shard_map/ppermute | solution.py:351
  11.5 5.1 %collective-permute-start.6 = (bf16[8,2,2,16,128]{4,3,2,1,0:T(8,128)(2,1)S(1)}, bf16[8,2,2,16,128]{4,3,2,1,0:T(8,128)(2,1)S(1)}, u32[]{:S(2)}, u32[]{:S(2)}) collective-permute-start(bf16[8,2,2,16,128]{4,3,2,1,0:T(8,128)(2,1)S(1)} %get-tuple-element.60), channel_id=1, source_target_pairs={{0,8},{8,0},{16,24},{24,16},{1,9},{9,1},{17,25},{25,17},{2,10},{10... | collective-permute-start | bytes 393224 | tf_op jit(solution)/shard_map/ppermute | solution.py:337
  11.8 12.8 %collective-permute-start.10 = (bf16[8,2,2,16,128]{4,3,2,1,0:T(8,128)(2,1)S(1)}, bf16[8,2,2,16,128]{4,3,2,1,0:T(8,128)(2,1)S(1)}, u32[]{:S(2)}, u32[]{:S(2)}) collective-permute-start(bf16[8,2,2,16,128]{4,3,2,1,0:T(8,128)(2,1)S(1)} %get-tuple-element.66), channel_id=1, source_target_pairs={{0,16},{8,24},{16,0},{24,8},{1,17},{9,25},{17,1},{25,9},{2,18},{10... | collective-permute-start | bytes 393224 | tf_op jit(solution)/shard_map/ppermute | solution.py:337
  16.6 8.3 %collective-permute-start.11 = (bf16[8,2,2,16,128]{4,3,2,1,0:T(8,128)(2,1)S(1)}, bf16[8,2,2,16,128]{4,3,2,1,0:T(8,128)(2,1)S(1)}, u32[]{:S(2)}, u32[]{:S(2)}) collective-permute-start(bf16[8,2,2,16,128]{4,3,2,1,0:T(8,128)(2,1)S(1)} %get-tuple-element.67), channel_id=1, source_target_pairs={{0,24},{8,16},{16,8},{24,0},{1,25},{9,17},{17,9},{25,1},{2,26},{10... | collective-permute-start | bytes 393224 | tf_op jit(solution)/shard_map/ppermute | solution.py:337
  16.7 12.4 %collective-permute-start.7 = (bf16[8,2,2,16,128]{4,3,2,1,0:T(8,128)(2,1)S(1)}, bf16[8,2,2,16,128]{4,3,2,1,0:T(8,128)(2,1)S(1)}, u32[]{:S(2)}, u32[]{:S(2)}) collective-permute-start(bf16[8,2,2,16,128]{4,3,2,1,0:T(8,128)(2,1)S(1)} %get-tuple-element.62), channel_id=1, source_target_pairs={{0,8},{8,0},{16,24},{24,16},{1,9},{9,1},{17,25},{25,17},{2,10},{10... | collective-permute-start | bytes 393224 | tf_op jit(solution)/shard_map/ppermute | solution.py:337
  18.7 10.6 %collective-permute-start.8 = (bf16[8,2,2,16,128]{4,3,2,1,0:T(8,128)(2,1)S(1)}, bf16[8,2,2,16,128]{4,3,2,1,0:T(8,128)(2,1)S(1)}, u32[]{:S(2)}, u32[]{:S(2)}) collective-permute-start(bf16[8,2,2,16,128]{4,3,2,1,0:T(8,128)(2,1)S(1)} %get-tuple-element.63), channel_id=1, source_target_pairs={{0,16},{8,24},{16,0},{24,8},{1,17},{9,25},{17,1},{25,9},{2,18},{10... | collective-permute-start | bytes 393224 | tf_op jit(solution)/shard_map/ppermute | solution.py:337
  18.8 11.0 %collective-permute-start.9 = (bf16[8,2,2,16,128]{4,3,2,1,0:T(8,128)(2,1)S(1)}, bf16[8,2,2,16,128]{4,3,2,1,0:T(8,128)(2,1)S(1)}, u32[]{:S(2)}, u32[]{:S(2)}) collective-permute-start(bf16[8,2,2,16,128]{4,3,2,1,0:T(8,128)(2,1)S(1)} %get-tuple-element.64), channel_id=1, source_target_pairs={{0,24},{8,16},{16,8},{24,0},{1,25},{9,17},{17,9},{25,1},{2,26},{10... | collective-permute-start | bytes 393224 | tf_op jit(solution)/shard_map/ppermute | solution.py:337
  24.6 16.8 %collective-permute-start.3 = (bf16[16,2,2,16,128]{4,3,2,1,0:T(8,128)(2,1)}, bf16[16,2,2,16,128]{4,3,2,1,0:T(8,128)(2,1)S(1)}, u32[]{:S(2)}, u32[]{:S(2)}) collective-permute-start(bf16[16,2,2,16,128]{4,3,2,1,0:T(8,128)(2,1)} %get-tuple-element.51), channel_id=1, source_target_pairs={{0,8},{8,0},{16,24},{24,16},{1,9},{9,1},{17,25},{25,17},{2,10},{10... | collective-permute-start | bytes 786440 | tf_op jit(solution)/shard_map/ppermute | solution.py:337
  24.9 16.5 %collective-permute-start.4 = (bf16[16,2,2,16,128]{4,3,2,1,0:T(8,128)(2,1)}, bf16[16,2,2,16,128]{4,3,2,1,0:T(8,128)(2,1)S(1)}, u32[]{:S(2)}, u32[]{:S(2)}) collective-permute-start(bf16[16,2,2,16,128]{4,3,2,1,0:T(8,128)(2,1)} %get-tuple-element.52), channel_id=1, source_target_pairs={{0,16},{8,24},{16,0},{24,8},{1,17},{9,25},{17,1},{25,9},{2,18},{10... | collective-permute-start | bytes 786440 | tf_op jit(solution)/shard_map/ppermute | solution.py:337
  29.1 12.3 %collective-permute-start.5 = (bf16[16,2,2,16,128]{4,3,2,1,0:T(8,128)(2,1)}, bf16[16,2,2,16,128]{4,3,2,1,0:T(8,128)(2,1)S(1)}, u32[]{:S(2)}, u32[]{:S(2)}) collective-permute-start(bf16[16,2,2,16,128]{4,3,2,1,0:T(8,128)(2,1)} %get-tuple-element.53), channel_id=1, source_target_pairs={{0,24},{8,16},{16,8},{24,0},{1,25},{9,17},{17,9},{25,1},{2,26},{10... | collective-permute-start | bytes 786440 | tf_op jit(solution)/shard_map/ppermute | solution.py:337
  29.8 11.6 %copy-start.3 = (bf16[1,512,1024]{2,1,0:T(8,128)(2,1)S(1)}, bf16[1,512,1024]{2,1,0:T(8,128)(2,1)}, u32[]{:S(2)}) copy-start(bf16[1,512,1024]{2,1,0:T(8,128)(2,1)} %q_ref.1) | copy-start | bytes 3145732
  29.8 11.6 %copy-start.5 = (bf16[1,512,1024]{2,1,0:T(8,128)(2,1)S(1)}, bf16[1,512,1024]{2,1,0:T(8,128)(2,1)}, u32[]{:S(2)}) copy-start(bf16[1,512,1024]{2,1,0:T(8,128)(2,1)} %k_ref.1) | copy-start | bytes 3145732
  33.2 14.0 %all-to-all-start = ((f32[32,8,128]{2,1,0:T(8,128)}), f32[32,8,128]{2,1,0:T(8,128)S(1)}, u32[]{:S(2)}, u32[]{:S(2)}) async-start(f32[32,8,128]{2,1,0:T(8,128)} %get-tuple-element.73), calls=%async_computation | async-start | bytes 262144 | tf_op jit(solution)/shard_map/all_to_all | solution.py:411
  39.4 4.1 %collective-permute-start.12 = (f32[16,4,128]{2,1,0:T(4,128)S(1)}, f32[16,4,128]{2,1,0:T(4,128)S(1)}, u32[]{:S(2)}, u32[]{:S(2)}) collective-permute-start(f32[16,4,128]{2,1,0:T(4,128)S(1)} %get-tuple-element.75), channel_id=1, source_target_pairs={{0,8},{8,0},{16,24},{24,16},{1,9},{9,1},{17,25},{25,17},{2,10},{10... | collective-permute-start | bytes 98312 | tf_op jit(solution)/shard_map/ppermute | solution.py:337
  39.7 4.0 %collective-permute-start.13 = (f32[16,4,128]{2,1,0:T(4,128)S(1)}, f32[16,4,128]{2,1,0:T(4,128)S(1)}, u32[]{:S(2)}, u32[]{:S(2)}) collective-permute-start(f32[16,4,128]{2,1,0:T(4,128)S(1)} %get-tuple-element.76), channel_id=1, source_target_pairs={{0,16},{8,24},{16,0},{24,8},{1,17},{9,25},{17,1},{25,9},{2,18},{10... | collective-permute-start | bytes 98312 | tf_op jit(solution)/shard_map/ppermute | solution.py:337
  41.4 3.6 %collective-permute-start.14 = (f32[16,4,128]{2,1,0:T(4,128)S(1)}, f32[16,4,128]{2,1,0:T(4,128)S(1)}, u32[]{:S(2)}, u32[]{:S(2)}) collective-permute-start(f32[16,4,128]{2,1,0:T(4,128)S(1)} %get-tuple-element.77), channel_id=1, source_target_pairs={{0,24},{8,16},{16,8},{24,0},{1,25},{9,17},{17,9},{25,1},{2,26},{10... | collective-permute-start | bytes 98312 | tf_op jit(solution)/shard_map/ppermute | solution.py:337

commit v11 on v10

--- a/solution.py
+++ b/solution.py
@@ -340,7 +340,8 @@
     sizes = (8, 8) if per_device == 16 else (per_device,)
     if owners == 4:
         (far,) = gate(
-            grad_out, out_gate, (), False, (per_device,), 56, "gate_far", "far", (2, 3)
+            *(pltpu.with_memory_space_constraint(v, pltpu.HBM) for v in (grad_out, out_gate)),
+            (), False, (per_device,), 12, "gate_far", "far", (2, 3)
         )
         far_send = far
         far = [lax.ppermute(v, "ctx", [(i, i ^ k) for i in range(4)]) for k, v in zip((2, 3), far)]
@@ -388,7 +389,7 @@
     for n, each in enumerate(sizes):
         last = n == len(sizes) - 1
         unroll = math.gcd(8, each)
-        sums = jax.ShapeDtypeStruct((count, 8, LANES) if last else (blocks // owners, LANES), F32)
+        sums = jax.ShapeDtypeStruct((count, 4, LANES) if last else (blocks // owners, LANES), F32)
         old = pl.pallas_call(
             functools.partial(
                 lag_kernel, owners=owners, unroll=unroll, scale=scale, first=sum(sizes[:n]), last=last

time: 48.3 us -> 47 us (0.973)
  waiting for transfers between devices: 5.7 us -> 4.93 us
  Pallas kernels: 21.3 us -> 20.7 us
    pallas_call x3, Pallas kernels: 5.08 us -> 4.49 us  [gate(): pl.pallas_call(functools.partial(gate_kernel, reverse=reverse, sizes=size...]
  transfers between devices with their start and end apart: 16 -> 16, of which waited for: 5 -> 5; matrix products, arithmetic and copies ran while one was open for 0% -> 0% of each run, Pallas kernels for 37% -> 38%
where the time goes in v11:
time: 47 us; the launch traced here: 46.8 us
  Pallas kernels  20.7 us (44%)
  starting transfers between devices  17.9 us (38%)
  waiting for transfers between devices  4.93 us (10%)
  local copies, waits for them, and re-layouts  2.47 us (5%)
  between operations  0.78 us (2%)
    ppermute x12, starting transfers between devices, swap(): lax.ppermute(values[k], 'ctx', [(i, i ^ k) for i in range(owners)])  8.41 us
    all_to_all x1, starting transfers between devices, on_device(): total = lax.all_to_all(spread, both, 0, 0, tiled=True)  6.24 us
    pallas_call x2, Pallas kernels, on_device(): pl.pallas_call(functools.partial(lag_kernel, owners=owners, unroll=unroll...  6.02 us
    pallas_call x3, Pallas kernels, gate(): pl.pallas_call(functools.partial(gate_kernel, reverse=reverse, sizes=size...  4.49 us
    pallas_call x1, Pallas kernels, on_device(): pl.pallas_call(functools.partial(conv_kernel, owners=owners, unroll=unrol...  4.13 us
    pallas_call x1, Pallas kernels, on_device(): pl.pallas_call(blocks_kernel, in_specs=[smem, vmem], out_specs=[vmem] * u...  3.04 us
    ppermute x2, starting transfers between devices, on_device(): lax.ppermute(v, 'ctx', [(i, i ^ k) for i in range(4)])  3.03 us
    unnamed x14, local copies, waits for them, and re-layouts  2.47 us
  transfers between devices with their start and end apart: 16, of which 5 were waited for; matrix products, arithmetic and copies ran while one was open for 0% of the time, Pallas kernels for 38%

profile of v11, /device:TPU:0, one launch (start us, length us, event | category | flops | bytes accessed | tf_op | source)
XLA Modules:
  0.0 46.8 jit_solution(13628351272809701343)
XLA Ops:
  0.7 1.7 %gate_far.1 = (bf16[16,2,2,16,128]{4,3,2,1,0:T(8,128)(2,1)S(1)}, bf16[16,2,2,16,128]{4,3,2,1,0:T(8,128)(2,1)S(1)}) custom-call(s32[1]{0:T(128)} %bitcast.pos_ref, bf16[1,512,1024]{2,1,0:T(8,128)(2,1)} %left_ref.5, bf16[1,512,1024]{2,1,0:T(8,128)(2,1)} %right_ref.5), custom_call_target="tpu_custom_call" | custom-call | flops 262144 | bytes 1572864 | tf_op jit(solution)/shard_map/gate_far/pallas_call | solution.py:309
  2.4 3.0 %collective-permute-start.1 = (bf16[16,2,2,16,128]{4,3,2,1,0:T(8,128)(2,1)S(1)}, bf16[16,2,2,16,128]{4,3,2,1,0:T(8,128)(2,1)S(1)}, u32[]{:S(2)}, u32[]{:S(2)}) collective-permute-start(bf16[16,2,2,16,128]{4,3,2,1,0:T(8,128)(2,1)S(1)} %get-tuple-element.48), channel_id=1, source_target_pairs={{0,16},{8,24},{16,0},{24,8},{1,17},{9,25},{17,1},{25,9},{2,18},{10... | collective-permute-start | bytes 786440 | tf_op jit(solution)/shard_map/ppermute | solution.py:347
  5.4 1.2 %copy-done.2 = bf16[1,512,1024]{2,1,0:T(8,128)(2,1)S(1)} copy-done((bf16[1,512,1024]{2,1,0:T(8,128)(2,1)S(1)}, bf16[1,512,1024]{2,1,0:T(8,128)(2,1)}, u32[]{:S(2)}) %copy-start.2) | copy-done | bytes 1048600
  6.7 1.2 %copy-done.4 = bf16[1,512,1024]{2,1,0:T(8,128)(2,1)S(1)} copy-done((bf16[1,512,1024]{2,1,0:T(8,128)(2,1)S(1)}, bf16[1,512,1024]{2,1,0:T(8,128)(2,1)}, u32[]{:S(2)}) %copy-start.4) | copy-done | bytes 1048600
  7.9 2.0 %gate_prod.1 = (bf16[8,2,2,16,128]{4,3,2,1,0:T(8,128)(2,1)S(1)}, bf16[8,2,2,16,128]{4,3,2,1,0:T(8,128)(2,1)S(1)}, bf16[8,2,2,16,128]{4,3,2,1,0:T(8,128)(2,1)S(1)...) custom-call(s32[1]{0:T(128)} %bitcast.pos_ref, ...), custom_call_target="tpu_custom_call" | custom-call | flops 524288 | bytes 3145728 | tf_op jit(solution)/shard_map/gate_prod/pallas_call | solution.py:309
  9.9 0.8 %gate_near.1 = (bf16[16,2,2,16,128]{4,3,2,1,0:T(8,128)(2,1)S(1)}, bf16[16,2,2,16,128]{4,3,2,1,0:T(8,128)(2,1)S(1)}) custom-call(s32[1]{0:T(128)} %bitcast.pos_ref, bf16[1,512,1024]{2,1,0:T(8,128)(2,1)S(1)} %copy-done, bf16[1,512,1024]{2,1,0:T(8,128)(2,1)S(1)} %copy-done.1, bf16[8,2,2,16,128]{4,3,2,1,0:T(8,128)(2,1)S(1)} %get-tuple-element.45.refs_0_.refs_4_), custom_call_target="tpu_custom_call" | custom-call | flops 262144 | bytes 1572864 | tf_op jit(solution)/shard_map/gate_near/pallas_call | solution.py:309
  10.7 0.3 collective-permute-start
  10.9 0.3 collective-permute-start.6
  11.3 1.7 %collective-permute-start.10 = (bf16[8,2,2,16,128]{4,3,2,1,0:T(8,128)(2,1)S(1)}, bf16[8,2,2,16,128]{4,3,2,1,0:T(8,128)(2,1)S(1)}, u32[]{:S(2)}, u32[]{:S(2)}) collective-permute-start(bf16[8,2,2,16,128]{4,3,2,1,0:T(8,128)(2,1)S(1)} %get-tuple-element.66), channel_id=1, source_target_pairs={{0,16},{8,24},{16,0},{24,8},{1,17},{9,25},{17,1},{25,9},{2,18},{10... | collective-permute-start | bytes 393224 | tf_op jit(solution)/shard_map/ppermute | solution.py:337
  13.0 3.0 %blocks.1 = (bf16[4,17,128,128]{3,2,1,0:T(8,128)(2,1)S(1)}, bf16[4,17,128,128]{3,2,1,0:T(8,128)(2,1)S(1)}, bf16[4,17,128,128]{3,2,1,0:T(8,128)(2,1)S(1)}, bf16[4,17,128,128]{3,2,1,0:T(8,128)(2,1)S(1)}) custom-call(s32[1]{0:T(128)} %bitcast.pos_ref, bf16[64,2048]{1,0:T(8,128)(2,1)S(1)} %copy-done.6), custom_call_target="tpu_custom_call" | custom-call | flops 1 | bytes 1 | tf_op jit(solution)/shard_map/blocks/pallas_call | solution.py:363
  16.0 0.0 collective-permute-done.6.refs_5_
  16.0 0.1 collective-permute-start.11
  16.1 0.4 collective-permute-start.7
  16.5 1.2 %collective-permute-done.2.refs_7_.refs_3_ = bf16[16,2,2,16,128]{4,3,2,1,0:T(8,128)(2,1)S(1)} collective-permute-done((bf16[16,2,2,16,128]{4,3,2,1,0:T(8,128)(2,1)S(1)}, bf16[16,2,2,16,128]{4,3,2,1,0:T(8,128)(2,1)S(1)}, u32[]{:S(2)}, u32[]{:S(2)}) %collective-permute-start.2) | collective-permute-done | bytes 262176 | tf_op jit(solution)/shard_map/ppermute | solution.py:347
  17.8 0.5 %collective-permute-start.8 = (bf16[8,2,2,16,128]{4,3,2,1,0:T(8,128)(2,1)S(1)}, bf16[8,2,2,16,128]{4,3,2,1,0:T(8,128)(2,1)S(1)}, u32[]{:S(2)}, u32[]{:S(2)}) collective-permute-start(bf16[8,2,2,16,128]{4,3,2,1,0:T(8,128)(2,1)S(1)} %get-tuple-element.63), channel_id=1, source_target_pairs={{0,16},{8,24},{16,0},{24,8},{1,17},{9,25},{17,1},{25,9},{2,18},{10... | collective-permute-start | bytes 393224 | tf_op jit(solution)/shard_map/ppermute | solution.py:337
  18.2 1.5 %collective-permute-start.9 = (bf16[8,2,2,16,128]{4,3,2,1,0:T(8,128)(2,1)S(1)}, bf16[8,2,2,16,128]{4,3,2,1,0:T(8,128)(2,1)S(1)}, u32[]{:S(2)}, u32[]{:S(2)}) collective-permute-start(bf16[8,2,2,16,128]{4,3,2,1,0:T(8,128)(2,1)S(1)} %get-tuple-element.64), channel_id=1, source_target_pairs={{0,24},{8,16},{16,8},{24,0},{1,25},{9,17},{17,9},{25,1},{2,26},{10... | collective-permute-start | bytes 393224 | tf_op jit(solution)/shard_map/ppermute | solution.py:337
  19.7 4.1 %conv.1 = (bf16[16,2,2,16,128]{4,3,2,1,0:T(8,128)(2,1)S(1)}, bf16[16,2,2,16,128]{4,3,2,1,0:T(8,128)(2,1)}, bf16[16,2,2,16,128]{4,3,2,1,0:T(8,128)(2,1)}, bf16[16,2,2,16,128]{4,3,2,1,0:T(8,128)(2,1)}) custom-call(s32[1]{0:T(128)} %bitcast.pos_ref, bf16[4,17,128,128]{3,2,1,0:T(8,128)(2,1)S(1)} %get-tuple-element.41.refs_0_, ...), custom_call_target="tpu_custom_call" | custom-call | flops 17179869184 | bytes 2359296 | tf_op jit(solution)/shard_map/conv/pallas_call | solution.py:375
  23.8 0.2 collective-permute-start.3
  24.0 1.6 %collective-permute-start.4 = (bf16[16,2,2,16,128]{4,3,2,1,0:T(8,128)(2,1)}, bf16[16,2,2,16,128]{4,3,2,1,0:T(8,128)(2,1)S(1)}, u32[]{:S(2)}, u32[]{:S(2)}) collective-permute-start(bf16[16,2,2,16,128]{4,3,2,1,0:T(8,128)(2,1)} %get-tuple-element.52), channel_id=1, source_target_pairs={{0,16},{8,24},{16,0},{24,8},{1,17},{9,25},{17,1},{25,9},{2,18},{10... | collective-permute-start | bytes 786440 | tf_op jit(solution)/shard_map/ppermute | solution.py:337
  25.7 2.7 %lags.2 = (f32[16,4,128]{2,1,0:T(4,128)S(1)}, f32[16,4,128]{2,1,0:T(4,128)S(1)}, f32[16,4,128]{2,1,0:T(4,128)S(1)}, f32[16,4,128]{2,1,0:T(4,128)S(1)}, f32[4,128]{1,0:T(4,128)S(1)}) custom-call(s32[1]{0:T(128)} %bitcast.pos_ref, bf16[16,2,2,16,128]{4,3,2,1,0:T(8,128)(2,1)S(1)} %get-tuple-element.46.refs_4_.refs_0_, ...), custom_call_target="tpu_custom_call" | custom-call | flops 8589934592 | bytes 2097152 | tf_op jit(solution)/shard_map/lags/pallas_call | solution.py:393
  28.3 0.0 collective-permute-done.7.refs_5_
  28.3 0.1 collective-permute-start.5
  28.5 0.5 %collective-permute-done.9.refs_7_ = bf16[8,2,2,16,128]{4,3,2,1,0:T(8,128)(2,1)S(1)} collective-permute-done((bf16[8,2,2,16,128]{4,3,2,1,0:T(8,128)(2,1)S(1)}, bf16[8,2,2,16,128]{4,3,2,1,0:T(8,128)(2,1)S(1)}, u32[]{:S(2)}, u32[]{:S(2)}) %collective-permute-start.9) | collective-permute-done | bytes 131104 | tf_op jit(solution)/shard_map/ppermute | solution.py:337
  29.0 3.3 %lags.3 = (f32[16,4,128]{2,1,0:T(4,128)S(1)}, f32[16,4,128]{2,1,0:T(4,128)S(1)}, f32[16,4,128]{2,1,0:T(4,128)S(1)}, f32[16,4,128]{2,1,0:T(4,128)S(1)}, f32[32,4,128]{2,1,0:T(4,128)}) custom-call(s32[1]{0:T(128)} %bitcast.pos_ref, ...), custom_call_target="tpu_custom_call", output_to_operand_aliasing={{0}: (9, {}), {1}: (10, {}), {2}: (11, {}), {3}: (12, {})} | custom-call | flops 8589934592 | bytes 2097152 | tf_op jit(solution)/shard_map/lags/pallas_call | solution.py:393
  32.3 6.2 %all-to-all-start = ((f32[32,4,128]{2,1,0:T(4,128)}), f32[32,4,128]{2,1,0:T(4,128)S(1)}, u32[]{:S(2)}, u32[]{:S(2)}) async-start(f32[32,4,128]{2,1,0:T(4,128)} %get-tuple-element.73), calls=%async_computation | async-start | bytes 131072 | tf_op jit(solution)/shard_map/all_to_all | solution.py:412
  38.6 0.3 collective-permute-start.12
  38.9 1.7 %collective-permute-start.13 = (f32[16,4,128]{2,1,0:T(4,128)S(1)}, f32[16,4,128]{2,1,0:T(4,128)S(1)}, u32[]{:S(2)}, u32[]{:S(2)}) collective-permute-start(f32[16,4,128]{2,1,0:T(4,128)S(1)} %get-tuple-element.76), channel_id=1, source_target_pairs={{0,16},{8,24},{16,0},{24,8},{1,17},{9,25},{17,1},{25,9},{2,18},{10... | collective-permute-start | bytes 98312 | tf_op jit(solution)/shard_map/ppermute | solution.py:337
  40.6 2.1 %ungate.1 = (bf16[1,512,1024]{2,1,0:T(8,128)(2,1)}, bf16[1,512,1024]{2,1,0:T(8,128)(2,1)}, f32[8,128]{1,0:T(8,128)S(1)}) custom-call(s32[1]{0:T(128)} %bitcast.pos_ref, bf16[1,512,1024]{2,1,0:T(8,128)(2,1)S(1)} %copy-done.3, bf16[1,512,1024]{2,1,0:T(8,128)(2,1)S(1)} %copy-done.5, bf16[16,2,2,16,128]{4,3,2,1,0:T(8,128)(2,1)S(1)} %get-tuple-element.50.refs_0_.refs_8_, ...), custom_call_target="tpu_custom_call" | custom-call | flops 1048576 | bytes 5242880 | tf_op jit(solution)/shard_map/ungate/pallas_call | solution.py:415
  42.7 0.1 collective-permute-done.13.refs_2_
  42.8 1.3 %collective-permute-done.14.refs_3_ = f32[16,4,128]{2,1,0:T(4,128)S(1)} collective-permute-done((f32[16,4,128]{2,1,0:T(4,128)S(1)}, f32[16,4,128]{2,1,0:T(4,128)S(1)}, u32[]{:S(2)}, u32[]{:S(2)}) %collective-permute-start.14) | collective-permute-done | bytes 32800 | tf_op jit(solution)/shard_map/ppermute | solution.py:337
  44.1 1.7 %all-to-all-done.total_ref = f32[32,4,128]{2,1,0:T(4,128)S(1)} async-done(((f32[32,4,128]{2,1,0:T(4,128)}), f32[32,4,128]{2,1,0:T(4,128)S(1)}, u32[]{:S(2)}, u32[]{:S(2)}) %all-to-all-start) | async-done | bytes 65568 | tf_op jit(solution)/shard_map/all_to_all | solution.py:412
  45.9 0.9 %clip.1 = f32[64,512]{1,0:T(8,128)} custom-call(s32[1]{0:T(128)} %bitcast.pos_ref, f32[32,4,128]{2,1,0:T(4,128)S(1)} %all-to-all-done.total_ref, f32[16,4,128]{2,1,0:T(4,128)S(1)} %get-tuple-element.74.refs_0_, f32[16,4,128]{2,1,0:T(4,128)S(1)} %collective-permute-done.12.refs_1_, f32[16,4,128]{2,1,0:T(4,128)S(1)} %collective-permute-done.13.refs_2_, ...), custom_call_target="tpu_custom_call" | custom-call | flops 131072 | bytes 524288 | tf_op jit(solution)/shard_map/clip/pallas_call | solution.py:434
  (23 shorter events, 0.1 us)
Async XLA Ops:
  0.6 9.3 %copy-start = (bf16[1,512,1024]{2,1,0:T(8,128)(2,1)S(1)}, bf16[1,512,1024]{2,1,0:T(8,128)(2,1)}, u32[]{:S(2)}) copy-start(bf16[1,512,1024]{2,1,0:T(8,128)(2,1)} %left_ref.5) | copy-start | bytes 3145732
  0.6 9.3 %copy-start.1 = (bf16[1,512,1024]{2,1,0:T(8,128)(2,1)S(1)}, bf16[1,512,1024]{2,1,0:T(8,128)(2,1)}, u32[]{:S(2)}) copy-start(bf16[1,512,1024]{2,1,0:T(8,128)(2,1)} %right_ref.5) | copy-start | bytes 3145732
  2.4 13.7 %collective-permute-start.1 = (bf16[16,2,2,16,128]{4,3,2,1,0:T(8,128)(2,1)S(1)}, bf16[16,2,2,16,128]{4,3,2,1,0:T(8,128)(2,1)S(1)}, u32[]{:S(2)}, u32[]{:S(2)}) collective-permute-start(bf16[16,2,2,16,128]{4,3,2,1,0:T(8,128)(2,1)S(1)} %get-tuple-element.48), channel_id=1, source_target_pairs={{0,16},{8,24},{16,0},{24,8},{1,17},{9,25},{17,1},{25,9},{2,18},{10... | collective-permute-start | bytes 786440 | tf_op jit(solution)/shard_map/ppermute | solution.py:347
  5.4 12.3 %collective-permute-start.2 = (bf16[16,2,2,16,128]{4,3,2,1,0:T(8,128)(2,1)S(1)}, bf16[16,2,2,16,128]{4,3,2,1,0:T(8,128)(2,1)S(1)}, u32[]{:S(2)}, u32[]{:S(2)}) collective-permute-start(bf16[16,2,2,16,128]{4,3,2,1,0:T(8,128)(2,1)S(1)} %get-tuple-element.49), channel_id=1, source_target_pairs={{0,24},{8,16},{16,8},{24,0},{1,25},{9,17},{17,9},{25,1},{2,26},{10... | collective-permute-start | bytes 786440 | tf_op jit(solution)/shard_map/ppermute | solution.py:347
  5.4 1.2 %copy-start.2 = (bf16[1,512,1024]{2,1,0:T(8,128)(2,1)S(1)}, bf16[1,512,1024]{2,1,0:T(8,128)(2,1)}, u32[]{:S(2)}) copy-start(bf16[1,512,1024]{2,1,0:T(8,128)(2,1)} %q_ref.1) | copy-start | bytes 3145732
  6.7 1.2 %copy-start.4 = (bf16[1,512,1024]{2,1,0:T(8,128)(2,1)S(1)}, bf16[1,512,1024]{2,1,0:T(8,128)(2,1)}, u32[]{:S(2)}) copy-start(bf16[1,512,1024]{2,1,0:T(8,128)(2,1)} %k_ref.1) | copy-start | bytes 3145732
  7.9 5.1 %copy-start.6 = (bf16[64,2048]{1,0:T(8,128)(2,1)S(1)}, bf16[64,2048]{1,0:T(8,128)(2,1)}, u32[]{:S(2)}) copy-start(bf16[64,2048]{1,0:T(8,128)(2,1)} %filt_ref.1) | copy-start | bytes 786436
  10.7 7.6 %collective-permute-start = (bf16[16,2,2,16,128]{4,3,2,1,0:T(8,128)(2,1)S(1)}, bf16[16,2,2,16,128]{4,3,2,1,0:T(8,128)(2,1)S(1)}, u32[]{:S(2)}, u32[]{:S(2)}) collective-permute-start(bf16[16,2,2,16,128]{4,3,2,1,0:T(8,128)(2,1)S(1)} %get-tuple-element.47), channel_id=1, source_target_pairs={{0,8},{8,0},{16,24},{24,16},{1,9},{9,1},{17,25},{25,17},{2,10},{10... | collective-permute-start | bytes 786440 | tf_op jit(solution)/shard_map/ppermute | solution.py:352
  10.9 5.1 %collective-permute-start.6 = (bf16[8,2,2,16,128]{4,3,2,1,0:T(8,128)(2,1)S(1)}, bf16[8,2,2,16,128]{4,3,2,1,0:T(8,128)(2,1)S(1)}, u32[]{:S(2)}, u32[]{:S(2)}) collective-permute-start(bf16[8,2,2,16,128]{4,3,2,1,0:T(8,128)(2,1)S(1)} %get-tuple-element.60), channel_id=1, source_target_pairs={{0,8},{8,0},{16,24},{24,16},{1,9},{9,1},{17,25},{25,17},{2,10},{10... | collective-permute-start | bytes 393224 | tf_op jit(solution)/shard_map/ppermute | solution.py:337
  11.3 12.6 %collective-permute-start.10 = (bf16[8,2,2,16,128]{4,3,2,1,0:T(8,128)(2,1)S(1)}, bf16[8,2,2,16,128]{4,3,2,1,0:T(8,128)(2,1)S(1)}, u32[]{:S(2)}, u32[]{:S(2)}) collective-permute-start(bf16[8,2,2,16,128]{4,3,2,1,0:T(8,128)(2,1)S(1)} %get-tuple-element.66), channel_id=1, source_target_pairs={{0,16},{8,24},{16,0},{24,8},{1,17},{9,25},{17,1},{25,9},{2,18},{10... | collective-permute-start | bytes 393224 | tf_op jit(solution)/shard_map/ppermute | solution.py:337
  16.0 8.0 %collective-permute-start.11 = (bf16[8,2,2,16,128]{4,3,2,1,0:T(8,128)(2,1)S(1)}, bf16[8,2,2,16,128]{4,3,2,1,0:T(8,128)(2,1)S(1)}, u32[]{:S(2)}, u32[]{:S(2)}) collective-permute-start(bf16[8,2,2,16,128]{4,3,2,1,0:T(8,128)(2,1)S(1)} %get-tuple-element.67), channel_id=1, source_target_pairs={{0,24},{8,16},{16,8},{24,0},{1,25},{9,17},{17,9},{25,1},{2,26},{10... | collective-permute-start | bytes 393224 | tf_op jit(solution)/shard_map/ppermute | solution.py:337
  16.1 12.2 %collective-permute-start.7 = (bf16[8,2,2,16,128]{4,3,2,1,0:T(8,128)(2,1)S(1)}, bf16[8,2,2,16,128]{4,3,2,1,0:T(8,128)(2,1)S(1)}, u32[]{:S(2)}, u32[]{:S(2)}) collective-permute-start(bf16[8,2,2,16,128]{4,3,2,1,0:T(8,128)(2,1)S(1)} %get-tuple-element.62), channel_id=1, source_target_pairs={{0,8},{8,0},{16,24},{24,16},{1,9},{9,1},{17,25},{25,17},{2,10},{10... | collective-permute-start | bytes 393224 | tf_op jit(solution)/shard_map/ppermute | solution.py:337
  17.8 10.7 %collective-permute-start.8 = (bf16[8,2,2,16,128]{4,3,2,1,0:T(8,128)(2,1)S(1)}, bf16[8,2,2,16,128]{4,3,2,1,0:T(8,128)(2,1)S(1)}, u32[]{:S(2)}, u32[]{:S(2)}) collective-permute-start(bf16[8,2,2,16,128]{4,3,2,1,0:T(8,128)(2,1)S(1)} %get-tuple-element.63), channel_id=1, source_target_pairs={{0,16},{8,24},{16,0},{24,8},{1,17},{9,25},{17,1},{25,9},{2,18},{10... | collective-permute-start | bytes 393224 | tf_op jit(solution)/shard_map/ppermute | solution.py:337
  18.2 10.7 %collective-permute-start.9 = (bf16[8,2,2,16,128]{4,3,2,1,0:T(8,128)(2,1)S(1)}, bf16[8,2,2,16,128]{4,3,2,1,0:T(8,128)(2,1)S(1)}, u32[]{:S(2)}, u32[]{:S(2)}) collective-permute-start(bf16[8,2,2,16,128]{4,3,2,1,0:T(8,128)(2,1)S(1)} %get-tuple-element.64), channel_id=1, source_target_pairs={{0,24},{8,16},{16,8},{24,0},{1,25},{9,17},{17,9},{25,1},{2,26},{10... | collective-permute-start | bytes 393224 | tf_op jit(solution)/shard_map/ppermute | solution.py:337
  23.8 16.8 %collective-permute-start.3 = (bf16[16,2,2,16,128]{4,3,2,1,0:T(8,128)(2,1)}, bf16[16,2,2,16,128]{4,3,2,1,0:T(8,128)(2,1)S(1)}, u32[]{:S(2)}, u32[]{:S(2)}) collective-permute-start(bf16[16,2,2,16,128]{4,3,2,1,0:T(8,128)(2,1)} %get-tuple-element.51), channel_id=1, source_target_pairs={{0,8},{8,0},{16,24},{24,16},{1,9},{9,1},{17,25},{25,17},{2,10},{10... | collective-permute-start | bytes 786440 | tf_op jit(solution)/shard_map/ppermute | solution.py:337
  24.0 16.5 %collective-permute-start.4 = (bf16[16,2,2,16,128]{4,3,2,1,0:T(8,128)(2,1)}, bf16[16,2,2,16,128]{4,3,2,1,0:T(8,128)(2,1)S(1)}, u32[]{:S(2)}, u32[]{:S(2)}) collective-permute-start(bf16[16,2,2,16,128]{4,3,2,1,0:T(8,128)(2,1)} %get-tuple-element.52), channel_id=1, source_target_pairs={{0,16},{8,24},{16,0},{24,8},{1,17},{9,25},{17,1},{25,9},{2,18},{10... | collective-permute-start | bytes 786440 | tf_op jit(solution)/shard_map/ppermute | solution.py:337
  28.3 12.3 %collective-permute-start.5 = (bf16[16,2,2,16,128]{4,3,2,1,0:T(8,128)(2,1)}, bf16[16,2,2,16,128]{4,3,2,1,0:T(8,128)(2,1)S(1)}, u32[]{:S(2)}, u32[]{:S(2)}) collective-permute-start(bf16[16,2,2,16,128]{4,3,2,1,0:T(8,128)(2,1)} %get-tuple-element.53), channel_id=1, source_target_pairs={{0,24},{8,16},{16,8},{24,0},{1,25},{9,17},{17,9},{25,1},{2,26},{10... | collective-permute-start | bytes 786440 | tf_op jit(solution)/shard_map/ppermute | solution.py:337
  29.0 11.6 %copy-start.3 = (bf16[1,512,1024]{2,1,0:T(8,128)(2,1)S(1)}, bf16[1,512,1024]{2,1,0:T(8,128)(2,1)}, u32[]{:S(2)}) copy-start(bf16[1,512,1024]{2,1,0:T(8,128)(2,1)} %q_ref.1) | copy-start | bytes 3145732
  29.0 11.6 %copy-start.5 = (bf16[1,512,1024]{2,1,0:T(8,128)(2,1)S(1)}, bf16[1,512,1024]{2,1,0:T(8,128)(2,1)}, u32[]{:S(2)}) copy-start(bf16[1,512,1024]{2,1,0:T(8,128)(2,1)} %k_ref.1) | copy-start | bytes 3145732
  32.3 13.5 %all-to-all-start = ((f32[32,4,128]{2,1,0:T(4,128)}), f32[32,4,128]{2,1,0:T(4,128)S(1)}, u32[]{:S(2)}, u32[]{:S(2)}) async-start(f32[32,4,128]{2,1,0:T(4,128)} %get-tuple-element.73), calls=%async_computation | async-start | bytes 131072 | tf_op jit(solution)/shard_map/all_to_all | solution.py:412
  38.6 4.1 %collective-permute-start.12 = (f32[16,4,128]{2,1,0:T(4,128)S(1)}, f32[16,4,128]{2,1,0:T(4,128)S(1)}, u32[]{:S(2)}, u32[]{:S(2)}) collective-permute-start(f32[16,4,128]{2,1,0:T(4,128)S(1)} %get-tuple-element.75), channel_id=1, source_target_pairs={{0,8},{8,0},{16,24},{24,16},{1,9},{9,1},{17,25},{25,17},{2,10},{10... | collective-permute-start | bytes 98312 | tf_op jit(solution)/shard_map/ppermute | solution.py:337
  38.9 3.9 %collective-permute-start.13 = (f32[16,4,128]{2,1,0:T(4,128)S(1)}, f32[16,4,128]{2,1,0:T(4,128)S(1)}, u32[]{:S(2)}, u32[]{:S(2)}) collective-permute-start(f32[16,4,128]{2,1,0:T(4,128)S(1)} %get-tuple-element.76), channel_id=1, source_target_pairs={{0,16},{8,24},{16,0},{24,8},{1,17},{9,25},{17,1},{25,9},{2,18},{10... | collective-permute-start | bytes 98312 | tf_op jit(solution)/shard_map/ppermute | solution.py:337
  40.6 3.5 %collective-permute-start.14 = (f32[16,4,128]{2,1,0:T(4,128)S(1)}, f32[16,4,128]{2,1,0:T(4,128)S(1)}, u32[]{:S(2)}, u32[]{:S(2)}) collective-permute-start(f32[16,4,128]{2,1,0:T(4,128)S(1)} %get-tuple-element.77), channel_id=1, source_target_pairs={{0,24},{8,16},{16,8},{24,0},{1,25},{9,17},{17,9},{25,1},{2,26},{10... | collective-permute-start | bytes 98312 | tf_op jit(solution)/shard_map/ppermute | solution.py:337

commit v12 on v11

--- a/solution.py
+++ b/solution.py
@@ -278,6 +278,10 @@
     sum_ref[:, :1] = jnp.broadcast_to(squares[None], (sum_ref.shape[0], 1, LANES))
 
 
+def in_hbm(value):
+    return pltpu.with_memory_space_constraint(value, pltpu.HBM)
+
+
 def cost(flops, moved):
     return pl.CostEstimate(flops=int(flops), bytes_accessed=int(moved), transcendentals=0)
 
@@ -340,12 +344,11 @@
     sizes = (8, 8) if per_device == 16 else (per_device,)
     if owners == 4:
         (far,) = gate(
-            *(pltpu.with_memory_space_constraint(v, pltpu.HBM) for v in (grad_out, out_gate)),
-            (), False, (per_device,), 12, "gate_far", "far", (2, 3)
+            in_hbm(grad_out), in_hbm(out_gate), (), False, (per_device,), 12, "gate_far", "far", (2, 3)
         )
         far_send = far
         far = [lax.ppermute(v, "ctx", [(i, i ^ k) for i in range(4)]) for k, v in zip((2, 3), far)]
-        prod_send = gate(q_branch, k_branch, (), True, sizes, 12, "gate_prod")
+        prod_send = gate(in_hbm(q_branch), in_hbm(k_branch), (), True, sizes, 12, "gate_prod")
         (near,) = gate(
             grad_out, out_gate, prod_send[0][:1], False, (per_device,), 12, "gate_near", "near", (0, 1)
         )

time: 47 us -> 47 us (level)
  local copies, waits for them, and re-layouts: 2.47 us -> 0.02 us
  waiting for transfers between devices: 4.93 us -> 6.5 us
  Pallas kernels: 20.7 us -> 21.5 us
    unnamed x14 -> x10, local copies, waits for them, and re-layouts: 2.47 us -> 0.02 us
    ppermute x2, waiting for transfers between devices: 1.24 us -> 2.81 us  [on_device(): lax.ppermute(v, 'ctx', [(i, i ^ k) for i in range(4)])]
    pallas_call x3, Pallas kernels: 4.49 us -> 5.37 us  [gate(): pl.pallas_call(functools.partial(gate_kernel, reverse=reverse, sizes=size...]
  transfers between devices with their start and end apart: 16 -> 16, of which waited for: 5 -> 5; matrix products, arithmetic and copies ran while one was open for 0% -> 0% of each run, Pallas kernels for 38% -> 40%
where the time goes in v12:
time: 47 us; the launch traced here: 46.8 us
  Pallas kernels  21.5 us (46%)
  starting transfers between devices  17.9 us (38%)
  waiting for transfers between devices  6.5 us (14%)
  between operations  0.79 us (2%)
    ppermute x12, starting transfers between devices, swap(): lax.ppermute(values[k], 'ctx', [(i, i ^ k) for i in range(owners)])  8.41 us
    all_to_all x1, starting transfers between devices, on_device(): total = lax.all_to_all(spread, both, 0, 0, tiled=True)  6.24 us
    pallas_call x2, Pallas kernels, on_device(): pl.pallas_call(functools.partial(lag_kernel, owners=owners, unroll=unroll...  6.02 us
    pallas_call x3, Pallas kernels, gate(): pl.pallas_call(functools.partial(gate_kernel, reverse=reverse, sizes=size...  5.37 us
    pallas_call x1, Pallas kernels, on_device(): pl.pallas_call(functools.partial(conv_kernel, owners=owners, unroll=unrol...  4.12 us
    pallas_call x1, Pallas kernels, on_device(): pl.pallas_call(blocks_kernel, in_specs=[smem, vmem], out_specs=[vmem] * u...  3.04 us
    ppermute x2, starting transfers between devices, on_device(): lax.ppermute(v, 'ctx', [(i, i ^ k) for i in range(4)])  3.03 us
    ppermute x2, waiting for transfers between devices, on_device(): lax.ppermute(v, 'ctx', [(i, i ^ k) for i in range(4)])  2.81 us
  transfers between devices with their start and end apart: 16, of which 5 were waited for; matrix products, arithmetic and copies ran while one was open for 0% of the time, Pallas kernels for 40%

profile of v12, /device:TPU:0, one launch (start us, length us, event | category | flops | bytes accessed | tf_op | source)
XLA Modules:
  0.0 46.8 jit_solution(14608380002600438089)
XLA Ops:
  0.7 1.7 %gate_far.1 = (bf16[16,2,2,16,128]{4,3,2,1,0:T(8,128)(2,1)S(1)}, bf16[16,2,2,16,128]{4,3,2,1,0:T(8,128)(2,1)S(1)}) custom-call(s32[1]{0:T(128)} %bitcast.pos_ref, bf16[1,512,1024]{2,1,0:T(8,128)(2,1)} %left_ref.5, bf16[1,512,1024]{2,1,0:T(8,128)(2,1)} %right_ref.5), custom_call_target="tpu_custom_call" | custom-call | flops 262144 | bytes 1572864 | tf_op jit(solution)/shard_map/gate_far/pallas_call | solution.py:313
  2.4 0.0 copy-start.4
  2.4 3.0 %collective-permute-start.1 = (bf16[16,2,2,16,128]{4,3,2,1,0:T(8,128)(2,1)S(1)}, bf16[16,2,2,16,128]{4,3,2,1,0:T(8,128)(2,1)S(1)}, u32[]{:S(2)}, u32[]{:S(2)}) collective-permute-start(bf16[16,2,2,16,128]{4,3,2,1,0:T(8,128)(2,1)S(1)} %get-tuple-element.48), channel_id=1, source_target_pairs={{0,16},{8,24},{16,0},{24,8},{1,17},{9,25},{17,1},{25,9},{2,18},{10... | collective-permute-start | bytes 786440 | tf_op jit(solution)/shard_map/ppermute | solution.py:350
  5.4 2.9 %gate_prod.1 = (bf16[8,2,2,16,128]{4,3,2,1,0:T(8,128)(2,1)S(1)}, bf16[8,2,2,16,128]{4,3,2,1,0:T(8,128)(2,1)S(1)}, bf16[8,2,2,16,128]{4,3,2,1,0:T(8,128)(2,1)S(1)...) custom-call(s32[1]{0:T(128)} %bitcast.pos_ref, ...), custom_call_target="tpu_custom_call" | custom-call | flops 524288 | bytes 3145728 | tf_op jit(solution)/shard_map/gate_prod/pallas_call | solution.py:313
  8.3 0.8 %gate_near.1 = (bf16[16,2,2,16,128]{4,3,2,1,0:T(8,128)(2,1)S(1)}, bf16[16,2,2,16,128]{4,3,2,1,0:T(8,128)(2,1)S(1)}) custom-call(s32[1]{0:T(128)} %bitcast.pos_ref, bf16[1,512,1024]{2,1,0:T(8,128)(2,1)S(1)} %copy-done, bf16[1,512,1024]{2,1,0:T(8,128)(2,1)S(1)} %copy-done.1, bf16[8,2,2,16,128]{4,3,2,1,0:T(8,128)(2,1)S(1)} %get-tuple-element.45.refs_0_.refs_4_), custom_call_target="tpu_custom_call" | custom-call | flops 262144 | bytes 1572864 | tf_op jit(solution)/shard_map/gate_near/pallas_call | solution.py:313
  9.1 0.3 collective-permute-start
  9.4 0.3 collective-permute-start.6
  9.7 1.7 %collective-permute-start.10 = (bf16[8,2,2,16,128]{4,3,2,1,0:T(8,128)(2,1)S(1)}, bf16[8,2,2,16,128]{4,3,2,1,0:T(8,128)(2,1)S(1)}, u32[]{:S(2)}, u32[]{:S(2)}) collective-permute-start(bf16[8,2,2,16,128]{4,3,2,1,0:T(8,128)(2,1)S(1)} %get-tuple-element.66), channel_id=1, source_target_pairs={{0,16},{8,24},{16,0},{24,8},{1,17},{9,25},{17,1},{25,9},{2,18},{10... | collective-permute-start | bytes 393224 | tf_op jit(solution)/shard_map/ppermute | solution.py:341
  11.4 3.0 %blocks.1 = (bf16[4,17,128,128]{3,2,1,0:T(8,128)(2,1)S(1)}, bf16[4,17,128,128]{3,2,1,0:T(8,128)(2,1)S(1)}, bf16[4,17,128,128]{3,2,1,0:T(8,128)(2,1)S(1)}, bf16[4,17,128,128]{3,2,1,0:T(8,128)(2,1)S(1)}) custom-call(s32[1]{0:T(128)} %bitcast.pos_ref, bf16[64,2048]{1,0:T(8,128)(2,1)S(1)} %copy-done.4), custom_call_target="tpu_custom_call" | custom-call | flops 1 | bytes 1 | tf_op jit(solution)/shard_map/blocks/pallas_call | solution.py:366
  14.5 0.0 collective-permute-done.6.refs_5_
  14.5 0.1 collective-permute-start.11
  14.6 0.0 collective-permute-done.1.refs_6_.refs_2_
  14.6 0.4 collective-permute-start.7
  15.0 2.8 %collective-permute-done.2.refs_7_.refs_3_ = bf16[16,2,2,16,128]{4,3,2,1,0:T(8,128)(2,1)S(1)} collective-permute-done((bf16[16,2,2,16,128]{4,3,2,1,0:T(8,128)(2,1)S(1)}, bf16[16,2,2,16,128]{4,3,2,1,0:T(8,128)(2,1)S(1)}, u32[]{:S(2)}, u32[]{:S(2)}) %collective-permute-start.2) | collective-permute-done | bytes 262176 | tf_op jit(solution)/shard_map/ppermute | solution.py:350
  17.8 0.2 collective-permute-start.8
  18.0 1.8 %collective-permute-start.9 = (bf16[8,2,2,16,128]{4,3,2,1,0:T(8,128)(2,1)S(1)}, bf16[8,2,2,16,128]{4,3,2,1,0:T(8,128)(2,1)S(1)}, u32[]{:S(2)}, u32[]{:S(2)}) collective-permute-start(bf16[8,2,2,16,128]{4,3,2,1,0:T(8,128)(2,1)S(1)} %get-tuple-element.64), channel_id=1, source_target_pairs={{0,24},{8,16},{16,8},{24,0},{1,25},{9,17},{17,9},{25,1},{2,26},{10... | collective-permute-start | bytes 393224 | tf_op jit(solution)/shard_map/ppermute | solution.py:341
  19.7 4.1 %conv.1 = (bf16[16,2,2,16,128]{4,3,2,1,0:T(8,128)(2,1)S(1)}, bf16[16,2,2,16,128]{4,3,2,1,0:T(8,128)(2,1)}, bf16[16,2,2,16,128]{4,3,2,1,0:T(8,128)(2,1)}, bf16[16,2,2,16,128]{4,3,2,1,0:T(8,128)(2,1)}) custom-call(s32[1]{0:T(128)} %bitcast.pos_ref, bf16[4,17,128,128]{3,2,1,0:T(8,128)(2,1)S(1)} %get-tuple-element.41.refs_0_, ...), custom_call_target="tpu_custom_call" | custom-call | flops 17179869184 | bytes 2359296 | tf_op jit(solution)/shard_map/conv/pallas_call | solution.py:378
  23.8 0.0 collective-permute-done.10.refs_6_
  23.8 0.2 collective-permute-start.3
  24.1 1.6 %collective-permute-start.4 = (bf16[16,2,2,16,128]{4,3,2,1,0:T(8,128)(2,1)}, bf16[16,2,2,16,128]{4,3,2,1,0:T(8,128)(2,1)S(1)}, u32[]{:S(2)}, u32[]{:S(2)}) collective-permute-start(bf16[16,2,2,16,128]{4,3,2,1,0:T(8,128)(2,1)} %get-tuple-element.52), channel_id=1, source_target_pairs={{0,16},{8,24},{16,0},{24,8},{1,17},{9,25},{17,1},{25,9},{2,18},{10... | collective-permute-start | bytes 786440 | tf_op jit(solution)/shard_map/ppermute | solution.py:341
  25.7 2.7 %lags.2 = (f32[16,4,128]{2,1,0:T(4,128)S(1)}, f32[16,4,128]{2,1,0:T(4,128)S(1)}, f32[16,4,128]{2,1,0:T(4,128)S(1)}, f32[16,4,128]{2,1,0:T(4,128)S(1)}, f32[4,128]{1,0:T(4,128)S(1)}) custom-call(s32[1]{0:T(128)} %bitcast.pos_ref, bf16[16,2,2,16,128]{4,3,2,1,0:T(8,128)(2,1)S(1)} %get-tuple-element.46.refs_4_.refs_0_, ...), custom_call_target="tpu_custom_call" | custom-call | flops 8589934592 | bytes 2097152 | tf_op jit(solution)/shard_map/lags/pallas_call | solution.py:396
  28.4 0.1 collective-permute-start.5
  28.5 0.5 %collective-permute-done.9.refs_7_ = bf16[8,2,2,16,128]{4,3,2,1,0:T(8,128)(2,1)S(1)} collective-permute-done((bf16[8,2,2,16,128]{4,3,2,1,0:T(8,128)(2,1)S(1)}, bf16[8,2,2,16,128]{4,3,2,1,0:T(8,128)(2,1)S(1)}, u32[]{:S(2)}, u32[]{:S(2)}) %collective-permute-start.9) | collective-permute-done | bytes 131104 | tf_op jit(solution)/shard_map/ppermute | solution.py:341
  29.0 3.3 %lags.3 = (f32[16,4,128]{2,1,0:T(4,128)S(1)}, f32[16,4,128]{2,1,0:T(4,128)S(1)}, f32[16,4,128]{2,1,0:T(4,128)S(1)}, f32[16,4,128]{2,1,0:T(4,128)S(1)}, f32[32,4,128]{2,1,0:T(4,128)}) custom-call(s32[1]{0:T(128)} %bitcast.pos_ref, ...), custom_call_target="tpu_custom_call", output_to_operand_aliasing={{0}: (9, {}), {1}: (10, {}), {2}: (11, {}), {3}: (12, {})} | custom-call | flops 8589934592 | bytes 2097152 | tf_op jit(solution)/shard_map/lags/pallas_call | solution.py:396
  32.3 6.2 %all-to-all-start = ((f32[32,4,128]{2,1,0:T(4,128)}), f32[32,4,128]{2,1,0:T(4,128)S(1)}, u32[]{:S(2)}, u32[]{:S(2)}) async-start(f32[32,4,128]{2,1,0:T(4,128)} %get-tuple-element.73), calls=%async_computation | async-start | bytes 131072 | tf_op jit(solution)/shard_map/all_to_all | solution.py:415
  38.6 0.3 collective-permute-start.12
  38.9 1.7 %collective-permute-start.13 = (f32[16,4,128]{2,1,0:T(4,128)S(1)}, f32[16,4,128]{2,1,0:T(4,128)S(1)}, u32[]{:S(2)}, u32[]{:S(2)}) collective-permute-start(f32[16,4,128]{2,1,0:T(4,128)S(1)} %get-tuple-element.76), channel_id=1, source_target_pairs={{0,16},{8,24},{16,0},{24,8},{1,17},{9,25},{17,1},{25,9},{2,18},{10... | collective-permute-start | bytes 98312 | tf_op jit(solution)/shard_map/ppermute | solution.py:341
  40.6 2.1 %ungate.1 = (bf16[1,512,1024]{2,1,0:T(8,128)(2,1)}, bf16[1,512,1024]{2,1,0:T(8,128)(2,1)}, f32[8,128]{1,0:T(8,128)S(1)}) custom-call(s32[1]{0:T(128)} %bitcast.pos_ref, bf16[1,512,1024]{2,1,0:T(8,128)(2,1)S(1)} %copy-done.2, bf16[1,512,1024]{2,1,0:T(8,128)(2,1)S(1)} %copy-done.3, bf16[16,2,2,16,128]{4,3,2,1,0:T(8,128)(2,1)S(1)} %get-tuple-element.50.refs_0_.refs_8_, ...), custom_call_target="tpu_custom_call" | custom-call | flops 1048576 | bytes 5242880 | tf_op jit(solution)/shard_map/ungate/pallas_call | solution.py:418
  42.7 0.1 collective-permute-done.13.refs_2_
  42.8 1.3 %collective-permute-done.14.refs_3_ = f32[16,4,128]{2,1,0:T(4,128)S(1)} collective-permute-done((f32[16,4,128]{2,1,0:T(4,128)S(1)}, f32[16,4,128]{2,1,0:T(4,128)S(1)}, u32[]{:S(2)}, u32[]{:S(2)}) %collective-permute-start.14) | collective-permute-done | bytes 32800 | tf_op jit(solution)/shard_map/ppermute | solution.py:341
  44.1 1.7 %all-to-all-done.total_ref = f32[32,4,128]{2,1,0:T(4,128)S(1)} async-done(((f32[32,4,128]{2,1,0:T(4,128)}), f32[32,4,128]{2,1,0:T(4,128)S(1)}, u32[]{:S(2)}, u32[]{:S(2)}) %all-to-all-start) | async-done | bytes 65568 | tf_op jit(solution)/shard_map/all_to_all | solution.py:415
  45.9 0.9 %clip.1 = f32[64,512]{1,0:T(8,128)} custom-call(s32[1]{0:T(128)} %bitcast.pos_ref, f32[32,4,128]{2,1,0:T(4,128)S(1)} %all-to-all-done.total_ref, f32[16,4,128]{2,1,0:T(4,128)S(1)} %get-tuple-element.74.refs_0_, f32[16,4,128]{2,1,0:T(4,128)S(1)} %collective-permute-done.12.refs_1_, f32[16,4,128]{2,1,0:T(4,128)S(1)} %collective-permute-done.13.refs_2_, ...), custom_call_target="tpu_custom_call" | custom-call | flops 131072 | bytes 524288 | tf_op jit(solution)/shard_map/clip/pallas_call | solution.py:437
  (19 shorter events, 0.0 us)
Async XLA Ops:
  0.6 7.7 %copy-start = (bf16[1,512,1024]{2,1,0:T(8,128)(2,1)S(1)}, bf16[1,512,1024]{2,1,0:T(8,128)(2,1)}, u32[]{:S(2)}) copy-start(bf16[1,512,1024]{2,1,0:T(8,128)(2,1)} %left_ref.5) | copy-start | bytes 3145732
  0.6 7.7 %copy-start.1 = (bf16[1,512,1024]{2,1,0:T(8,128)(2,1)S(1)}, bf16[1,512,1024]{2,1,0:T(8,128)(2,1)}, u32[]{:S(2)}) copy-start(bf16[1,512,1024]{2,1,0:T(8,128)(2,1)} %right_ref.5) | copy-start | bytes 3145732
  2.4 9.0 %copy-start.4 = (bf16[64,2048]{1,0:T(8,128)(2,1)S(1)}, bf16[64,2048]{1,0:T(8,128)(2,1)}, u32[]{:S(2)}) copy-start(bf16[64,2048]{1,0:T(8,128)(2,1)} %filt_ref.1) | copy-start | bytes 786436
  2.4 12.2 %collective-permute-start.1 = (bf16[16,2,2,16,128]{4,3,2,1,0:T(8,128)(2,1)S(1)}, bf16[16,2,2,16,128]{4,3,2,1,0:T(8,128)(2,1)S(1)}, u32[]{:S(2)}, u32[]{:S(2)}) collective-permute-start(bf16[16,2,2,16,128]{4,3,2,1,0:T(8,128)(2,1)S(1)} %get-tuple-element.48), channel_id=1, source_target_pairs={{0,16},{8,24},{16,0},{24,8},{1,17},{9,25},{17,1},{25,9},{2,18},{10... | collective-permute-start | bytes 786440 | tf_op jit(solution)/shard_map/ppermute | solution.py:350
  5.4 12.3 %collective-permute-start.2 = (bf16[16,2,2,16,128]{4,3,2,1,0:T(8,128)(2,1)S(1)}, bf16[16,2,2,16,128]{4,3,2,1,0:T(8,128)(2,1)S(1)}, u32[]{:S(2)}, u32[]{:S(2)}) collective-permute-start(bf16[16,2,2,16,128]{4,3,2,1,0:T(8,128)(2,1)S(1)} %get-tuple-element.49), channel_id=1, source_target_pairs={{0,24},{8,16},{16,8},{24,0},{1,25},{9,17},{17,9},{25,1},{2,26},{10... | collective-permute-start | bytes 786440 | tf_op jit(solution)/shard_map/ppermute | solution.py:350
  9.1 8.8 %collective-permute-start = (bf16[16,2,2,16,128]{4,3,2,1,0:T(8,128)(2,1)S(1)}, bf16[16,2,2,16,128]{4,3,2,1,0:T(8,128)(2,1)S(1)}, u32[]{:S(2)}, u32[]{:S(2)}) collective-permute-start(bf16[16,2,2,16,128]{4,3,2,1,0:T(8,128)(2,1)S(1)} %get-tuple-element.47), channel_id=1, source_target_pairs={{0,8},{8,0},{16,24},{24,16},{1,9},{9,1},{17,25},{25,17},{2,10},{10... | collective-permute-start | bytes 786440 | tf_op jit(solution)/shard_map/ppermute | solution.py:355
  9.4 5.1 %collective-permute-start.6 = (bf16[8,2,2,16,128]{4,3,2,1,0:T(8,128)(2,1)S(1)}, bf16[8,2,2,16,128]{4,3,2,1,0:T(8,128)(2,1)S(1)}, u32[]{:S(2)}, u32[]{:S(2)}) collective-permute-start(bf16[8,2,2,16,128]{4,3,2,1,0:T(8,128)(2,1)S(1)} %get-tuple-element.60), channel_id=1, source_target_pairs={{0,8},{8,0},{16,24},{24,16},{1,9},{9,1},{17,25},{25,17},{2,10},{10... | collective-permute-start | bytes 393224 | tf_op jit(solution)/shard_map/ppermute | solution.py:341
  9.7 14.1 %collective-permute-start.10 = (bf16[8,2,2,16,128]{4,3,2,1,0:T(8,128)(2,1)S(1)}, bf16[8,2,2,16,128]{4,3,2,1,0:T(8,128)(2,1)S(1)}, u32[]{:S(2)}, u32[]{:S(2)}) collective-permute-start(bf16[8,2,2,16,128]{4,3,2,1,0:T(8,128)(2,1)S(1)} %get-tuple-element.66), channel_id=1, source_target_pairs={{0,16},{8,24},{16,0},{24,8},{1,17},{9,25},{17,1},{25,9},{2,18},{10... | collective-permute-start | bytes 393224 | tf_op jit(solution)/shard_map/ppermute | solution.py:341
  14.5 9.6 %collective-permute-start.11 = (bf16[8,2,2,16,128]{4,3,2,1,0:T(8,128)(2,1)S(1)}, bf16[8,2,2,16,128]{4,3,2,1,0:T(8,128)(2,1)S(1)}, u32[]{:S(2)}, u32[]{:S(2)}) collective-permute-start(bf16[8,2,2,16,128]{4,3,2,1,0:T(8,128)(2,1)S(1)} %get-tuple-element.67), channel_id=1, source_target_pairs={{0,24},{8,16},{16,8},{24,0},{1,25},{9,17},{17,9},{25,1},{2,26},{10... | collective-permute-start | bytes 393224 | tf_op jit(solution)/shard_map/ppermute | solution.py:341
  14.6 13.8 %collective-permute-start.7 = (bf16[8,2,2,16,128]{4,3,2,1,0:T(8,128)(2,1)S(1)}, bf16[8,2,2,16,128]{4,3,2,1,0:T(8,128)(2,1)S(1)}, u32[]{:S(2)}, u32[]{:S(2)}) collective-permute-start(bf16[8,2,2,16,128]{4,3,2,1,0:T(8,128)(2,1)S(1)} %get-tuple-element.62), channel_id=1, source_target_pairs={{0,8},{8,0},{16,24},{24,16},{1,9},{9,1},{17,25},{25,17},{2,10},{10... | collective-permute-start | bytes 393224 | tf_op jit(solution)/shard_map/ppermute | solution.py:341
  17.8 10.7 %collective-permute-start.8 = (bf16[8,2,2,16,128]{4,3,2,1,0:T(8,128)(2,1)S(1)}, bf16[8,2,2,16,128]{4,3,2,1,0:T(8,128)(2,1)S(1)}, u32[]{:S(2)}, u32[]{:S(2)}) collective-permute-start(bf16[8,2,2,16,128]{4,3,2,1,0:T(8,128)(2,1)S(1)} %get-tuple-element.63), channel_id=1, source_target_pairs={{0,16},{8,24},{16,0},{24,8},{1,17},{9,25},{17,1},{25,9},{2,18},{10... | collective-permute-start | bytes 393224 | tf_op jit(solution)/shard_map/ppermute | solution.py:341
  18.0 11.0 %collective-permute-start.9 = (bf16[8,2,2,16,128]{4,3,2,1,0:T(8,128)(2,1)S(1)}, bf16[8,2,2,16,128]{4,3,2,1,0:T(8,128)(2,1)S(1)}, u32[]{:S(2)}, u32[]{:S(2)}) collective-permute-start(bf16[8,2,2,16,128]{4,3,2,1,0:T(8,128)(2,1)S(1)} %get-tuple-element.64), channel_id=1, source_target_pairs={{0,24},{8,16},{16,8},{24,0},{1,25},{9,17},{17,9},{25,1},{2,26},{10... | collective-permute-start | bytes 393224 | tf_op jit(solution)/shard_map/ppermute | solution.py:341
  23.8 16.8 %collective-permute-start.3 = (bf16[16,2,2,16,128]{4,3,2,1,0:T(8,128)(2,1)}, bf16[16,2,2,16,128]{4,3,2,1,0:T(8,128)(2,1)S(1)}, u32[]{:S(2)}, u32[]{:S(2)}) collective-permute-start(bf16[16,2,2,16,128]{4,3,2,1,0:T(8,128)(2,1)} %get-tuple-element.51), channel_id=1, source_target_pairs={{0,8},{8,0},{16,24},{24,16},{1,9},{9,1},{17,25},{25,17},{2,10},{10... | collective-permute-start | bytes 786440 | tf_op jit(solution)/shard_map/ppermute | solution.py:341
  24.1 16.5 %collective-permute-start.4 = (bf16[16,2,2,16,128]{4,3,2,1,0:T(8,128)(2,1)}, bf16[16,2,2,16,128]{4,3,2,1,0:T(8,128)(2,1)S(1)}, u32[]{:S(2)}, u32[]{:S(2)}) collective-permute-start(bf16[16,2,2,16,128]{4,3,2,1,0:T(8,128)(2,1)} %get-tuple-element.52), channel_id=1, source_target_pairs={{0,16},{8,24},{16,0},{24,8},{1,17},{9,25},{17,1},{25,9},{2,18},{10... | collective-permute-start | bytes 786440 | tf_op jit(solution)/shard_map/ppermute | solution.py:341
  28.4 12.2 %collective-permute-start.5 = (bf16[16,2,2,16,128]{4,3,2,1,0:T(8,128)(2,1)}, bf16[16,2,2,16,128]{4,3,2,1,0:T(8,128)(2,1)S(1)}, u32[]{:S(2)}, u32[]{:S(2)}) collective-permute-start(bf16[16,2,2,16,128]{4,3,2,1,0:T(8,128)(2,1)} %get-tuple-element.53), channel_id=1, source_target_pairs={{0,24},{8,16},{16,8},{24,0},{1,25},{9,17},{17,9},{25,1},{2,26},{10... | collective-permute-start | bytes 786440 | tf_op jit(solution)/shard_map/ppermute | solution.py:341
  29.0 11.6 %copy-start.2 = (bf16[1,512,1024]{2,1,0:T(8,128)(2,1)S(1)}, bf16[1,512,1024]{2,1,0:T(8,128)(2,1)}, u32[]{:S(2)}) copy-start(bf16[1,512,1024]{2,1,0:T(8,128)(2,1)} %q_ref.1) | copy-start | bytes 3145732
  29.0 11.6 %copy-start.3 = (bf16[1,512,1024]{2,1,0:T(8,128)(2,1)S(1)}, bf16[1,512,1024]{2,1,0:T(8,128)(2,1)}, u32[]{:S(2)}) copy-start(bf16[1,512,1024]{2,1,0:T(8,128)(2,1)} %k_ref.1) | copy-start | bytes 3145732
  32.3 13.5 %all-to-all-start = ((f32[32,4,128]{2,1,0:T(4,128)}), f32[32,4,128]{2,1,0:T(4,128)S(1)}, u32[]{:S(2)}, u32[]{:S(2)}) async-start(f32[32,4,128]{2,1,0:T(4,128)} %get-tuple-element.73), calls=%async_computation | async-start | bytes 131072 | tf_op jit(solution)/shard_map/all_to_all | solution.py:415
  38.6 4.1 %collective-permute-start.12 = (f32[16,4,128]{2,1,0:T(4,128)S(1)}, f32[16,4,128]{2,1,0:T(4,128)S(1)}, u32[]{:S(2)}, u32[]{:S(2)}) collective-permute-start(f32[16,4,128]{2,1,0:T(4,128)S(1)} %get-tuple-element.75), channel_id=1, source_target_pairs={{0,8},{8,0},{16,24},{24,16},{1,9},{9,1},{17,25},{25,17},{2,10},{10... | collective-permute-start | bytes 98312 | tf_op jit(solution)/shard_map/ppermute | solution.py:341
  38.9 3.9 %collective-permute-start.13 = (f32[16,4,128]{2,1,0:T(4,128)S(1)}, f32[16,4,128]{2,1,0:T(4,128)S(1)}, u32[]{:S(2)}, u32[]{:S(2)}) collective-permute-start(f32[16,4,128]{2,1,0:T(4,128)S(1)} %get-tuple-element.76), channel_id=1, source_target_pairs={{0,16},{8,24},{16,0},{24,8},{1,17},{9,25},{17,1},{25,9},{2,18},{10... | collective-permute-start | bytes 98312 | tf_op jit(solution)/shard_map/ppermute | solution.py:341
  40.6 3.5 %collective-permute-start.14 = (f32[16,4,128]{2,1,0:T(4,128)S(1)}, f32[16,4,128]{2,1,0:T(4,128)S(1)}, u32[]{:S(2)}, u32[]{:S(2)}) collective-permute-start(f32[16,4,128]{2,1,0:T(4,128)S(1)} %get-tuple-element.77), channel_id=1, source_target_pairs={{0,24},{8,16},{16,8},{24,0},{1,25},{9,17},{17,9},{25,1},{2,26},{10... | collective-permute-start | bytes 98312 | tf_op jit(solution)/shard_map/ppermute | solution.py:341

commit v13 on v12

--- a/solution.py
+++ b/solution.py
@@ -360,7 +360,7 @@
     prod_got = []
     for part in prod_send:
         if prod_got:
-            part, prod_got[-1][1] = lax.optimization_barrier((part, prod_got[-1][1]))
+            part, grad_got[2] = lax.optimization_barrier((part, grad_got[2]))
         prod_got.append(swap(part))
     unroll = math.gcd(4, per_device)
     toeps = pl.pallas_call(

time: 47 us -> 47 us (level)
  waiting for transfers between devices: 6.5 us -> 7.26 us
  starting transfers between devices: 17.9 us -> 17.2 us
    all_to_all x1, starting transfers between devices: 6.24 us -> 5.23 us  [on_device(): total = lax.all_to_all(spread, both, 0, 0, tiled=True)]
where the time goes in v13:
time: 47 us; the launch traced here: 46.8 us
  Pallas kernels  21.5 us (46%)
  starting transfers between devices  17.2 us (37%)
  waiting for transfers between devices  7.26 us (15%)
  between operations  0.79 us (2%)
    ppermute x12, starting transfers between devices, swap(): lax.ppermute(values[k], 'ctx', [(i, i ^ k) for i in range(owners)])  8.64 us
    pallas_call x2, Pallas kernels, on_device(): pl.pallas_call(functools.partial(lag_kernel, owners=owners, unroll=unroll...  6.02 us
    pallas_call x3, Pallas kernels, gate(): pl.pallas_call(functools.partial(gate_kernel, reverse=reverse, sizes=size...  5.37 us
    all_to_all x1, starting transfers between devices, on_device(): total = lax.all_to_all(spread, both, 0, 0, tiled=True)  5.23 us
    pallas_call x1, Pallas kernels, on_device(): pl.pallas_call(functools.partial(conv_kernel, owners=owners, unroll=unrol...  4.12 us
    ppermute x2, waiting for transfers between devices, on_device(): lax.ppermute(v, 'ctx', [(i, i ^ k) for i in range(4)])  3.2 us
    pallas_call x1, Pallas kernels, on_device(): pl.pallas_call(blocks_kernel, in_specs=[smem, vmem], out_specs=[vmem] * u...  3.04 us
    ppermute x2, starting transfers between devices, on_device(): lax.ppermute(v, 'ctx', [(i, i ^ k) for i in range(4)])  3.03 us
  transfers between devices with their start and end apart: 16, of which 5 were waited for; matrix products, arithmetic and copies ran while one was open for 0% of the time, Pallas kernels for 40%

profile of v13, /device:TPU:0, one launch (start us, length us, event | category | flops | bytes accessed | tf_op | source)
XLA Modules:
  0.0 46.8 jit_solution(17212881449627164459)
XLA Ops:
  0.7 1.7 %gate_far.1 = (bf16[16,2,2,16,128]{4,3,2,1,0:T(8,128)(2,1)S(1)}, bf16[16,2,2,16,128]{4,3,2,1,0:T(8,128)(2,1)S(1)}) custom-call(s32[1]{0:T(128)} %bitcast.pos_ref, bf16[1,512,1024]{2,1,0:T(8,128)(2,1)} %left_ref.5, bf16[1,512,1024]{2,1,0:T(8,128)(2,1)} %right_ref.5), custom_call_target="tpu_custom_call" | custom-call | flops 262144 | bytes 1572864 | tf_op jit(solution)/shard_map/gate_far/pallas_call | solution.py:313
  2.4 0.0 copy-start.4
  2.4 3.0 %collective-permute-start.1 = (bf16[16,2,2,16,128]{4,3,2,1,0:T(8,128)(2,1)S(1)}, bf16[16,2,2,16,128]{4,3,2,1,0:T(8,128)(2,1)S(1)}, u32[]{:S(2)}, u32[]{:S(2)}) collective-permute-start(bf16[16,2,2,16,128]{4,3,2,1,0:T(8,128)(2,1)S(1)} %get-tuple-element.52), channel_id=1, source_target_pairs={{0,16},{8,24},{16,0},{24,8},{1,17},{9,25},{17,1},{25,9},{2,18},{10... | collective-permute-start | bytes 786440 | tf_op jit(solution)/shard_map/ppermute | solution.py:350
  5.4 2.9 %gate_prod.1 = (bf16[8,2,2,16,128]{4,3,2,1,0:T(8,128)(2,1)S(1)}, bf16[8,2,2,16,128]{4,3,2,1,0:T(8,128)(2,1)S(1)}, bf16[8,2,2,16,128]{4,3,2,1,0:T(8,128)(2,1)S(1)...) custom-call(s32[1]{0:T(128)} %bitcast.pos_ref, ...), custom_call_target="tpu_custom_call" | custom-call | flops 524288 | bytes 3145728 | tf_op jit(solution)/shard_map/gate_prod/pallas_call | solution.py:313
  8.3 0.8 %gate_near.1 = (bf16[16,2,2,16,128]{4,3,2,1,0:T(8,128)(2,1)S(1)}, bf16[16,2,2,16,128]{4,3,2,1,0:T(8,128)(2,1)S(1)}) custom-call(s32[1]{0:T(128)} %bitcast.pos_ref, bf16[1,512,1024]{2,1,0:T(8,128)(2,1)S(1)} %copy-done, bf16[1,512,1024]{2,1,0:T(8,128)(2,1)S(1)} %copy-done.1, bf16[8,2,2,16,128]{4,3,2,1,0:T(8,128)(2,1)S(1)} %get-tuple-element.45.refs_0_.refs_4_), custom_call_target="tpu_custom_call" | custom-call | flops 262144 | bytes 1572864 | tf_op jit(solution)/shard_map/gate_near/pallas_call | solution.py:313
  9.1 0.3 collective-permute-start
  9.4 0.3 collective-permute-start.9
  9.7 1.7 %collective-permute-start.10 = (bf16[8,2,2,16,128]{4,3,2,1,0:T(8,128)(2,1)S(1)}, bf16[8,2,2,16,128]{4,3,2,1,0:T(8,128)(2,1)S(1)}, u32[]{:S(2)}, u32[]{:S(2)}) collective-permute-start(bf16[8,2,2,16,128]{4,3,2,1,0:T(8,128)(2,1)S(1)} %get-tuple-element.66), channel_id=1, source_target_pairs={{0,16},{8,24},{16,0},{24,8},{1,17},{9,25},{17,1},{25,9},{2,18},{10... | collective-permute-start | bytes 393224 | tf_op jit(solution)/shard_map/ppermute | solution.py:341
  11.4 3.0 %blocks.1 = (bf16[4,17,128,128]{3,2,1,0:T(8,128)(2,1)S(1)}, bf16[4,17,128,128]{3,2,1,0:T(8,128)(2,1)S(1)}, bf16[4,17,128,128]{3,2,1,0:T(8,128)(2,1)S(1)}, bf16[4,17,128,128]{3,2,1,0:T(8,128)(2,1)S(1)}) custom-call(s32[1]{0:T(128)} %bitcast.pos_ref, bf16[64,2048]{1,0:T(8,128)(2,1)S(1)} %copy-done.4), custom_call_target="tpu_custom_call" | custom-call | flops 1 | bytes 1 | tf_op jit(solution)/shard_map/blocks/pallas_call | solution.py:366
  14.5 0.0 collective-permute-done.1.refs_6_.refs_2_
  14.5 0.1 collective-permute-start.11
  14.6 3.2 %collective-permute-done.2.refs_7_.refs_3_ = bf16[16,2,2,16,128]{4,3,2,1,0:T(8,128)(2,1)S(1)} collective-permute-done((bf16[16,2,2,16,128]{4,3,2,1,0:T(8,128)(2,1)S(1)}, bf16[16,2,2,16,128]{4,3,2,1,0:T(8,128)(2,1)S(1)}, u32[]{:S(2)}, u32[]{:S(2)}) %collective-permute-start.2) | collective-permute-done | bytes 262176 | tf_op jit(solution)/shard_map/ppermute | solution.py:350
  17.8 0.2 collective-permute-start.6
  18.0 0.0 collective-permute-done.refs_5_.refs_1_
  18.0 2.1 %collective-permute-start.7 = (bf16[8,2,2,16,128]{4,3,2,1,0:T(8,128)(2,1)S(1)}, bf16[8,2,2,16,128]{4,3,2,1,0:T(8,128)(2,1)S(1)}, u32[]{:S(2)}, u32[]{:S(2)}) collective-permute-start(bf16[8,2,2,16,128]{4,3,2,1,0:T(8,128)(2,1)S(1)} %get-tuple-element.63), channel_id=1, source_target_pairs={{0,16},{8,24},{16,0},{24,8},{1,17},{9,25},{17,1},{25,9},{2,18},{10... | collective-permute-start | bytes 393224 | tf_op jit(solution)/shard_map/ppermute | solution.py:341
  20.1 4.1 %conv.1 = (bf16[16,2,2,16,128]{4,3,2,1,0:T(8,128)(2,1)S(1)}, bf16[16,2,2,16,128]{4,3,2,1,0:T(8,128)(2,1)}, bf16[16,2,2,16,128]{4,3,2,1,0:T(8,128)(2,1)}, bf16[16,2,2,16,128]{4,3,2,1,0:T(8,128)(2,1)}) custom-call(s32[1]{0:T(128)} %bitcast.pos_ref, bf16[4,17,128,128]{3,2,1,0:T(8,128)(2,1)S(1)} %get-tuple-element.41.refs_0_, ...), custom_call_target="tpu_custom_call" | custom-call | flops 17179869184 | bytes 2359296 | tf_op jit(solution)/shard_map/conv/pallas_call | solution.py:378
  24.2 0.0 collective-permute-start.8
  24.2 0.0 collective-permute-done.10.refs_6_
  24.2 0.2 collective-permute-start.3
  24.4 2.0 %collective-permute-start.4 = (bf16[16,2,2,16,128]{4,3,2,1,0:T(8,128)(2,1)}, bf16[16,2,2,16,128]{4,3,2,1,0:T(8,128)(2,1)S(1)}, u32[]{:S(2)}, u32[]{:S(2)}) collective-permute-start(bf16[16,2,2,16,128]{4,3,2,1,0:T(8,128)(2,1)} %get-tuple-element.57), channel_id=1, source_target_pairs={{0,16},{8,24},{16,0},{24,8},{1,17},{9,25},{17,1},{25,9},{2,18},{10... | collective-permute-start | bytes 786440 | tf_op jit(solution)/shard_map/ppermute | solution.py:341
  26.3 2.7 %lags.2 = (f32[16,4,128]{2,1,0:T(4,128)S(1)}, f32[16,4,128]{2,1,0:T(4,128)S(1)}, f32[16,4,128]{2,1,0:T(4,128)S(1)}, f32[16,4,128]{2,1,0:T(4,128)S(1)}, f32[4,128]{1,0:T(4,128)S(1)}) custom-call(s32[1]{0:T(128)} %bitcast.pos_ref, bf16[16,2,2,16,128]{4,3,2,1,0:T(8,128)(2,1)S(1)} %get-tuple-element.46.refs_4_.refs_0_, ...), custom_call_target="tpu_custom_call" | custom-call | flops 8589934592 | bytes 2097152 | tf_op jit(solution)/shard_map/lags/pallas_call | solution.py:396
  29.0 0.1 collective-permute-start.5
  29.1 0.9 %collective-permute-done.8.refs_7_ = bf16[8,2,2,16,128]{4,3,2,1,0:T(8,128)(2,1)S(1)} collective-permute-done((bf16[8,2,2,16,128]{4,3,2,1,0:T(8,128)(2,1)S(1)}, bf16[8,2,2,16,128]{4,3,2,1,0:T(8,128)(2,1)S(1)}, u32[]{:S(2)}, u32[]{:S(2)}) %collective-permute-start.8) | collective-permute-done | bytes 131104 | tf_op jit(solution)/shard_map/ppermute | solution.py:341
  30.0 3.3 %lags.3 = (f32[16,4,128]{2,1,0:T(4,128)S(1)}, f32[16,4,128]{2,1,0:T(4,128)S(1)}, f32[16,4,128]{2,1,0:T(4,128)S(1)}, f32[16,4,128]{2,1,0:T(4,128)S(1)}, f32[32,4,128]{2,1,0:T(4,128)}) custom-call(s32[1]{0:T(128)} %bitcast.pos_ref, ...), custom_call_target="tpu_custom_call", output_to_operand_aliasing={{0}: (9, {}), {1}: (10, {}), {2}: (11, {}), {3}: (12, {})} | custom-call | flops 8589934592 | bytes 2097152 | tf_op jit(solution)/shard_map/lags/pallas_call | solution.py:396
  33.3 5.2 %all-to-all-start = ((f32[32,4,128]{2,1,0:T(4,128)}), f32[32,4,128]{2,1,0:T(4,128)S(1)}, u32[]{:S(2)}, u32[]{:S(2)}) async-start(f32[32,4,128]{2,1,0:T(4,128)} %get-tuple-element.73), calls=%async_computation | async-start | bytes 131072 | tf_op jit(solution)/shard_map/all_to_all | solution.py:415
  38.6 0.3 collective-permute-start.12
  38.9 1.7 %collective-permute-start.13 = (f32[16,4,128]{2,1,0:T(4,128)S(1)}, f32[16,4,128]{2,1,0:T(4,128)S(1)}, u32[]{:S(2)}, u32[]{:S(2)}) collective-permute-start(f32[16,4,128]{2,1,0:T(4,128)S(1)} %get-tuple-element.76), channel_id=1, source_target_pairs={{0,16},{8,24},{16,0},{24,8},{1,17},{9,25},{17,1},{25,9},{2,18},{10... | collective-permute-start | bytes 98312 | tf_op jit(solution)/shard_map/ppermute | solution.py:341
  40.6 0.6 %collective-permute-done.5.refs_3_ = bf16[16,2,2,16,128]{4,3,2,1,0:T(8,128)(2,1)S(1)} collective-permute-done((bf16[16,2,2,16,128]{4,3,2,1,0:T(8,128)(2,1)}, bf16[16,2,2,16,128]{4,3,2,1,0:T(8,128)(2,1)S(1)}, u32[]{:S(2)}, u32[]{:S(2)}) %collective-permute-start.5) | collective-permute-done | bytes 262176 | tf_op jit(solution)/shard_map/ppermute | solution.py:341
  41.2 2.1 %ungate.1 = (bf16[1,512,1024]{2,1,0:T(8,128)(2,1)}, bf16[1,512,1024]{2,1,0:T(8,128)(2,1)}, f32[8,128]{1,0:T(8,128)S(1)}) custom-call(s32[1]{0:T(128)} %bitcast.pos_ref, bf16[1,512,1024]{2,1,0:T(8,128)(2,1)S(1)} %copy-done.2, bf16[1,512,1024]{2,1,0:T(8,128)(2,1)S(1)} %copy-done.3, bf16[16,2,2,16,128]{4,3,2,1,0:T(8,128)(2,1)S(1)} %get-tuple-element.55.refs_0_.refs_8_, ...), custom_call_target="tpu_custom_call" | custom-call | flops 1048576 | bytes 5242880 | tf_op jit(solution)/shard_map/ungate/pallas_call | solution.py:418
  43.2 0.9 %collective-permute-done.14.refs_3_ = f32[16,4,128]{2,1,0:T(4,128)S(1)} collective-permute-done((f32[16,4,128]{2,1,0:T(4,128)S(1)}, f32[16,4,128]{2,1,0:T(4,128)S(1)}, u32[]{:S(2)}, u32[]{:S(2)}) %collective-permute-start.14) | collective-permute-done | bytes 32800 | tf_op jit(solution)/shard_map/ppermute | solution.py:341
  44.1 1.7 %all-to-all-done.total_ref = f32[32,4,128]{2,1,0:T(4,128)S(1)} async-done(((f32[32,4,128]{2,1,0:T(4,128)}), f32[32,4,128]{2,1,0:T(4,128)S(1)}, u32[]{:S(2)}, u32[]{:S(2)}) %all-to-all-start) | async-done | bytes 65568 | tf_op jit(solution)/shard_map/all_to_all | solution.py:415
  45.9 0.9 %clip.1 = f32[64,512]{1,0:T(8,128)} custom-call(s32[1]{0:T(128)} %bitcast.pos_ref, f32[32,4,128]{2,1,0:T(4,128)S(1)} %all-to-all-done.total_ref, f32[16,4,128]{2,1,0:T(4,128)S(1)} %get-tuple-element.74.refs_0_, f32[16,4,128]{2,1,0:T(4,128)S(1)} %collective-permute-done.12.refs_1_, f32[16,4,128]{2,1,0:T(4,128)S(1)} %collective-permute-done.13.refs_2_, ...), custom_call_target="tpu_custom_call" | custom-call | flops 131072 | bytes 524288 | tf_op jit(solution)/shard_map/clip/pallas_call | solution.py:437
  (19 shorter events, 0.0 us)
Async XLA Ops:
  0.6 7.7 %copy-start = (bf16[1,512,1024]{2,1,0:T(8,128)(2,1)S(1)}, bf16[1,512,1024]{2,1,0:T(8,128)(2,1)}, u32[]{:S(2)}) copy-start(bf16[1,512,1024]{2,1,0:T(8,128)(2,1)} %left_ref.5) | copy-start | bytes 3145732
  0.6 7.7 %copy-start.1 = (bf16[1,512,1024]{2,1,0:T(8,128)(2,1)S(1)}, bf16[1,512,1024]{2,1,0:T(8,128)(2,1)}, u32[]{:S(2)}) copy-start(bf16[1,512,1024]{2,1,0:T(8,128)(2,1)} %right_ref.5) | copy-start | bytes 3145732
  2.4 9.0 %copy-start.4 = (bf16[64,2048]{1,0:T(8,128)(2,1)S(1)}, bf16[64,2048]{1,0:T(8,128)(2,1)}, u32[]{:S(2)}) copy-start(bf16[64,2048]{1,0:T(8,128)(2,1)} %filt_ref.1) | copy-start | bytes 786436
  2.4 12.0 %collective-permute-start.1 = (bf16[16,2,2,16,128]{4,3,2,1,0:T(8,128)(2,1)S(1)}, bf16[16,2,2,16,128]{4,3,2,1,0:T(8,128)(2,1)S(1)}, u32[]{:S(2)}, u32[]{:S(2)}) collective-permute-start(bf16[16,2,2,16,128]{4,3,2,1,0:T(8,128)(2,1)S(1)} %get-tuple-element.52), channel_id=1, source_target_pairs={{0,16},{8,24},{16,0},{24,8},{1,17},{9,25},{17,1},{25,9},{2,18},{10... | collective-permute-start | bytes 786440 | tf_op jit(solution)/shard_map/ppermute | solution.py:350
  5.4 12.3 %collective-permute-start.2 = (bf16[16,2,2,16,128]{4,3,2,1,0:T(8,128)(2,1)S(1)}, bf16[16,2,2,16,128]{4,3,2,1,0:T(8,128)(2,1)S(1)}, u32[]{:S(2)}, u32[]{:S(2)}) collective-permute-start(bf16[16,2,2,16,128]{4,3,2,1,0:T(8,128)(2,1)S(1)} %get-tuple-element.54), channel_id=1, source_target_pairs={{0,24},{8,16},{16,8},{24,0},{1,25},{9,17},{17,9},{25,1},{2,26},{10... | collective-permute-start | bytes 786440 | tf_op jit(solution)/shard_map/ppermute | solution.py:350
  9.1 8.9 %collective-permute-start = (bf16[16,2,2,16,128]{4,3,2,1,0:T(8,128)(2,1)S(1)}, bf16[16,2,2,16,128]{4,3,2,1,0:T(8,128)(2,1)S(1)}, u32[]{:S(2)}, u32[]{:S(2)}) collective-permute-start(bf16[16,2,2,16,128]{4,3,2,1,0:T(8,128)(2,1)S(1)} %get-tuple-element.47), channel_id=1, source_target_pairs={{0,8},{8,0},{16,24},{24,16},{1,9},{9,1},{17,25},{25,17},{2,10},{10... | collective-permute-start | bytes 786440 | tf_op jit(solution)/shard_map/ppermute | solution.py:355
  9.4 14.8 %collective-permute-start.9 = (bf16[8,2,2,16,128]{4,3,2,1,0:T(8,128)(2,1)S(1)}, bf16[8,2,2,16,128]{4,3,2,1,0:T(8,128)(2,1)S(1)}, u32[]{:S(2)}, u32[]{:S(2)}) collective-permute-start(bf16[8,2,2,16,128]{4,3,2,1,0:T(8,128)(2,1)S(1)} %get-tuple-element.65), channel_id=1, source_target_pairs={{0,8},{8,0},{16,24},{24,16},{1,9},{9,1},{17,25},{25,17},{2,10},{10... | collective-permute-start | bytes 393224 | tf_op jit(solution)/shard_map/ppermute | solution.py:341
  9.7 14.5 %collective-permute-start.10 = (bf16[8,2,2,16,128]{4,3,2,1,0:T(8,128)(2,1)S(1)}, bf16[8,2,2,16,128]{4,3,2,1,0:T(8,128)(2,1)S(1)}, u32[]{:S(2)}, u32[]{:S(2)}) collective-permute-start(bf16[8,2,2,16,128]{4,3,2,1,0:T(8,128)(2,1)S(1)} %get-tuple-element.66), channel_id=1, source_target_pairs={{0,16},{8,24},{16,0},{24,8},{1,17},{9,25},{17,1},{25,9},{2,18},{10... | collective-permute-start | bytes 393224 | tf_op jit(solution)/shard_map/ppermute | solution.py:341
  14.5 9.9 %collective-permute-start.11 = (bf16[8,2,2,16,128]{4,3,2,1,0:T(8,128)(2,1)S(1)}, bf16[8,2,2,16,128]{4,3,2,1,0:T(8,128)(2,1)S(1)}, u32[]{:S(2)}, u32[]{:S(2)}) collective-permute-start(bf16[8,2,2,16,128]{4,3,2,1,0:T(8,128)(2,1)S(1)} %get-tuple-element.67), channel_id=1, source_target_pairs={{0,24},{8,16},{16,8},{24,0},{1,25},{9,17},{17,9},{25,1},{2,26},{10... | collective-permute-start | bytes 393224 | tf_op jit(solution)/shard_map/ppermute | solution.py:341
  17.8 11.3 %collective-permute-start.6 = (bf16[8,2,2,16,128]{4,3,2,1,0:T(8,128)(2,1)S(1)}, bf16[8,2,2,16,128]{4,3,2,1,0:T(8,128)(2,1)S(1)}, u32[]{:S(2)}, u32[]{:S(2)}) collective-permute-start(bf16[8,2,2,16,128]{4,3,2,1,0:T(8,128)(2,1)S(1)} %get-tuple-element.62), channel_id=1, source_target_pairs={{0,8},{8,0},{16,24},{24,16},{1,9},{9,1},{17,25},{25,17},{2,10},{10... | collective-permute-start | bytes 393224 | tf_op jit(solution)/shard_map/ppermute | solution.py:341
  18.0 11.1 %collective-permute-start.7 = (bf16[8,2,2,16,128]{4,3,2,1,0:T(8,128)(2,1)S(1)}, bf16[8,2,2,16,128]{4,3,2,1,0:T(8,128)(2,1)S(1)}, u32[]{:S(2)}, u32[]{:S(2)}) collective-permute-start(bf16[8,2,2,16,128]{4,3,2,1,0:T(8,128)(2,1)S(1)} %get-tuple-element.63), channel_id=1, source_target_pairs={{0,16},{8,24},{16,0},{24,8},{1,17},{9,25},{17,1},{25,9},{2,18},{10... | collective-permute-start | bytes 393224 | tf_op jit(solution)/shard_map/ppermute | solution.py:341
  24.2 5.8 %collective-permute-start.8 = (bf16[8,2,2,16,128]{4,3,2,1,0:T(8,128)(2,1)S(1)}, bf16[8,2,2,16,128]{4,3,2,1,0:T(8,128)(2,1)S(1)}, u32[]{:S(2)}, u32[]{:S(2)}) collective-permute-start(bf16[8,2,2,16,128]{4,3,2,1,0:T(8,128)(2,1)S(1)} %get-tuple-element.64), channel_id=1, source_target_pairs={{0,24},{8,16},{16,8},{24,0},{1,25},{9,17},{17,9},{25,1},{2,26},{10... | collective-permute-start | bytes 393224 | tf_op jit(solution)/shard_map/ppermute | solution.py:341
  24.2 16.4 %collective-permute-start.3 = (bf16[16,2,2,16,128]{4,3,2,1,0:T(8,128)(2,1)}, bf16[16,2,2,16,128]{4,3,2,1,0:T(8,128)(2,1)S(1)}, u32[]{:S(2)}, u32[]{:S(2)}) collective-permute-start(bf16[16,2,2,16,128]{4,3,2,1,0:T(8,128)(2,1)} %get-tuple-element.56), channel_id=1, source_target_pairs={{0,8},{8,0},{16,24},{24,16},{1,9},{9,1},{17,25},{25,17},{2,10},{10... | collective-permute-start | bytes 786440 | tf_op jit(solution)/shard_map/ppermute | solution.py:341
  24.4 16.2 %collective-permute-start.4 = (bf16[16,2,2,16,128]{4,3,2,1,0:T(8,128)(2,1)}, bf16[16,2,2,16,128]{4,3,2,1,0:T(8,128)(2,1)S(1)}, u32[]{:S(2)}, u32[]{:S(2)}) collective-permute-start(bf16[16,2,2,16,128]{4,3,2,1,0:T(8,128)(2,1)} %get-tuple-element.57), channel_id=1, source_target_pairs={{0,16},{8,24},{16,0},{24,8},{1,17},{9,25},{17,1},{25,9},{2,18},{10... | collective-permute-start | bytes 786440 | tf_op jit(solution)/shard_map/ppermute | solution.py:341
  29.0 12.1 %collective-permute-start.5 = (bf16[16,2,2,16,128]{4,3,2,1,0:T(8,128)(2,1)}, bf16[16,2,2,16,128]{4,3,2,1,0:T(8,128)(2,1)S(1)}, u32[]{:S(2)}, u32[]{:S(2)}) collective-permute-start(bf16[16,2,2,16,128]{4,3,2,1,0:T(8,128)(2,1)} %get-tuple-element.58), channel_id=1, source_target_pairs={{0,24},{8,16},{16,8},{24,0},{1,25},{9,17},{17,9},{25,1},{2,26},{10... | collective-permute-start | bytes 786440 | tf_op jit(solution)/shard_map/ppermute | solution.py:341
  30.0 11.2 %copy-start.2 = (bf16[1,512,1024]{2,1,0:T(8,128)(2,1)S(1)}, bf16[1,512,1024]{2,1,0:T(8,128)(2,1)}, u32[]{:S(2)}) copy-start(bf16[1,512,1024]{2,1,0:T(8,128)(2,1)} %q_ref.1) | copy-start | bytes 3145732
  30.0 11.2 %copy-start.3 = (bf16[1,512,1024]{2,1,0:T(8,128)(2,1)S(1)}, bf16[1,512,1024]{2,1,0:T(8,128)(2,1)}, u32[]{:S(2)}) copy-start(bf16[1,512,1024]{2,1,0:T(8,128)(2,1)} %k_ref.1) | copy-start | bytes 3145732
  33.3 12.5 %all-to-all-start = ((f32[32,4,128]{2,1,0:T(4,128)}), f32[32,4,128]{2,1,0:T(4,128)S(1)}, u32[]{:S(2)}, u32[]{:S(2)}) async-start(f32[32,4,128]{2,1,0:T(4,128)} %get-tuple-element.73), calls=%async_computation | async-start | bytes 131072 | tf_op jit(solution)/shard_map/all_to_all | solution.py:415
  38.6 4.7 %collective-permute-start.12 = (f32[16,4,128]{2,1,0:T(4,128)S(1)}, f32[16,4,128]{2,1,0:T(4,128)S(1)}, u32[]{:S(2)}, u32[]{:S(2)}) collective-permute-start(f32[16,4,128]{2,1,0:T(4,128)S(1)} %get-tuple-element.75), channel_id=1, source_target_pairs={{0,8},{8,0},{16,24},{24,16},{1,9},{9,1},{17,25},{25,17},{2,10},{10... | collective-permute-start | bytes 98312 | tf_op jit(solution)/shard_map/ppermute | solution.py:341
  38.9 4.3 %collective-permute-start.13 = (f32[16,4,128]{2,1,0:T(4,128)S(1)}, f32[16,4,128]{2,1,0:T(4,128)S(1)}, u32[]{:S(2)}, u32[]{:S(2)}) collective-permute-start(f32[16,4,128]{2,1,0:T(4,128)S(1)} %get-tuple-element.76), channel_id=1, source_target_pairs={{0,16},{8,24},{16,0},{24,8},{1,17},{9,25},{17,1},{25,9},{2,18},{10... | collective-permute-start | bytes 98312 | tf_op jit(solution)/shard_map/ppermute | solution.py:341
  40.6 3.5 %collective-permute-start.14 = (f32[16,4,128]{2,1,0:T(4,128)S(1)}, f32[16,4,128]{2,1,0:T(4,128)S(1)}, u32[]{:S(2)}, u32[]{:S(2)}) collective-permute-start(f32[16,4,128]{2,1,0:T(4,128)S(1)} %get-tuple-element.77), channel_id=1, source_target_pairs={{0,24},{8,16},{16,8},{24,0},{1,25},{9,17},{17,9},{25,1},{2,26},{10... | collective-permute-start | bytes 98312 | tf_op jit(solution)/shard_map/ppermute | solution.py:341

commit v14 on v13

--- a/solution.py
+++ b/solution.py
@@ -357,11 +357,7 @@
         (grad_send,) = gate(grad_out, out_gate, (), False, (per_device,), 56, "gate_grad")
         grad_got = swap(grad_send)
         prod_send = gate(q_branch, k_branch, grad_send[:1], True, sizes, 12, "gate_prod")
-    prod_got = []
-    for part in prod_send:
-        if prod_got:
-            part, grad_got[2] = lax.optimization_barrier((part, grad_got[2]))
-        prod_got.append(swap(part))
+    first_got = swap(prod_send[0])
     unroll = math.gcd(4, per_device)
     toeps = pl.pallas_call(
         blocks_kernel,
@@ -385,6 +381,10 @@
         compiler_params=pltpu.CompilerParams(vmem_limit_bytes=16 << 20),
         name="conv",
     )(pos, *toeps, *grad_got)
+    conv, prod_got = list(conv), [first_got]
+    for part in prod_send[1:]:
+        part, conv[0] = lax.optimization_barrier((part, conv[0]))
+        prod_got.append(swap(part))
     back = swap(conv)
     both = ("ctx", "ch")
     count = lax.axis_size(both)

time: 47 us -> 48.9 us (1.040)
  starting transfers between devices: 17.2 us -> 18.2 us
  waiting for transfers between devices: 7.26 us -> 8.14 us
    all_to_all x1, starting transfers between devices: 5.23 us -> 6.24 us  [on_device(): total = lax.all_to_all(spread, both, 0, 0, tiled=True)]
    ppermute x12, waiting for transfers between devices: 2.31 us -> 3.19 us  [swap(): lax.ppermute(values[k], 'ctx', [(i, i ^ k) for i in range(owners)])]
  transfers between devices with their start and end apart: 16 -> 16, of which waited for: 5 -> 5; matrix products, arithmetic and copies ran while one was open for 0% -> 0% of each run, Pallas kernels for 40% -> 39%
where the time goes in v14:
time: 48.9 us; the launch traced here: 48.7 us
  Pallas kernels  21.5 us (44%)
  starting transfers between devices  18.2 us (37%)
  waiting for transfers between devices  8.14 us (17%)
  between operations  0.8 us (2%)
    ppermute x12, starting transfers between devices, swap(): lax.ppermute(values[k], 'ctx', [(i, i ^ k) for i in range(owners)])  8.66 us
    all_to_all x1, starting transfers between devices, on_device(): total = lax.all_to_all(spread, both, 0, 0, tiled=True)  6.24 us
    pallas_call x2, Pallas kernels, on_device(): pl.pallas_call(functools.partial(lag_kernel, owners=owners, unroll=unroll...  6.01 us
    pallas_call x3, Pallas kernels, gate(): pl.pallas_call(functools.partial(gate_kernel, reverse=reverse, sizes=size...  5.37 us
    pallas_call x1, Pallas kernels, on_device(): pl.pallas_call(functools.partial(conv_kernel, owners=owners, unroll=unrol...  4.12 us
    ppermute x2, waiting for transfers between devices, on_device(): lax.ppermute(v, 'ctx', [(i, i ^ k) for i in range(4)])  3.2 us
    ppermute x12, waiting for transfers between devices, swap(): lax.ppermute(values[k], 'ctx', [(i, i ^ k) for i in range(owners)])  3.19 us
    pallas_call x1, Pallas kernels, on_device(): pl.pallas_call(blocks_kernel, in_specs=[smem, vmem], out_specs=[vmem] * u...  3.04 us
  transfers between devices with their start and end apart: 16, of which 5 were waited for; matrix products, arithmetic and copies ran while one was open for 0% of the time, Pallas kernels for 39%

profile of v14, /device:TPU:0, one launch (start us, length us, event | category | flops | bytes accessed | tf_op | source)
XLA Modules:
  0.0 48.7 jit_solution(13630125056330625333)
XLA Ops:
  0.7 1.7 %gate_far.1 = (bf16[16,2,2,16,128]{4,3,2,1,0:T(8,128)(2,1)S(1)}, bf16[16,2,2,16,128]{4,3,2,1,0:T(8,128)(2,1)S(1)}) custom-call(s32[1]{0:T(128)} %bitcast.pos_ref, bf16[1,512,1024]{2,1,0:T(8,128)(2,1)} %left_ref.5, bf16[1,512,1024]{2,1,0:T(8,128)(2,1)} %right_ref.5), custom_call_target="tpu_custom_call" | custom-call | flops 262144 | bytes 1572864 | tf_op jit(solution)/shard_map/gate_far/pallas_call | solution.py:313
  2.4 0.0 copy-start.4
  2.4 3.0 %collective-permute-start.1 = (bf16[16,2,2,16,128]{4,3,2,1,0:T(8,128)(2,1)S(1)}, bf16[16,2,2,16,128]{4,3,2,1,0:T(8,128)(2,1)S(1)}, u32[]{:S(2)}, u32[]{:S(2)}) collective-permute-start(bf16[16,2,2,16,128]{4,3,2,1,0:T(8,128)(2,1)S(1)} %get-tuple-element.52), channel_id=1, source_target_pairs={{0,16},{8,24},{16,0},{24,8},{1,17},{9,25},{17,1},{25,9},{2,18},{10... | collective-permute-start | bytes 786440 | tf_op jit(solution)/shard_map/ppermute | solution.py:350
  5.4 2.9 %gate_prod.1 = (bf16[8,2,2,16,128]{4,3,2,1,0:T(8,128)(2,1)S(1)}, bf16[8,2,2,16,128]{4,3,2,1,0:T(8,128)(2,1)S(1)}, bf16[8,2,2,16,128]{4,3,2,1,0:T(8,128)(2,1)S(1)...) custom-call(s32[1]{0:T(128)} %bitcast.pos_ref, ...), custom_call_target="tpu_custom_call" | custom-call | flops 524288 | bytes 3145728 | tf_op jit(solution)/shard_map/gate_prod/pallas_call | solution.py:313
  8.3 0.8 %gate_near.1 = (bf16[16,2,2,16,128]{4,3,2,1,0:T(8,128)(2,1)S(1)}, bf16[16,2,2,16,128]{4,3,2,1,0:T(8,128)(2,1)S(1)}) custom-call(s32[1]{0:T(128)} %bitcast.pos_ref, bf16[1,512,1024]{2,1,0:T(8,128)(2,1)S(1)} %copy-done, bf16[1,512,1024]{2,1,0:T(8,128)(2,1)S(1)} %copy-done.1, bf16[8,2,2,16,128]{4,3,2,1,0:T(8,128)(2,1)S(1)} %get-tuple-element.49.refs_0_.refs_4_), custom_call_target="tpu_custom_call" | custom-call | flops 262144 | bytes 1572864 | tf_op jit(solution)/shard_map/gate_near/pallas_call | solution.py:313
  9.1 0.3 collective-permute-start
  9.4 0.3 collective-permute-start.9
  9.7 1.7 %collective-permute-start.10 = (bf16[8,2,2,16,128]{4,3,2,1,0:T(8,128)(2,1)S(1)}, bf16[8,2,2,16,128]{4,3,2,1,0:T(8,128)(2,1)S(1)}, u32[]{:S(2)}, u32[]{:S(2)}) collective-permute-start(bf16[8,2,2,16,128]{4,3,2,1,0:T(8,128)(2,1)S(1)} %get-tuple-element.66), channel_id=1, source_target_pairs={{0,16},{8,24},{16,0},{24,8},{1,17},{9,25},{17,1},{25,9},{2,18},{10... | collective-permute-start | bytes 393224 | tf_op jit(solution)/shard_map/ppermute | solution.py:341
  11.4 3.0 %blocks.1 = (bf16[4,17,128,128]{3,2,1,0:T(8,128)(2,1)S(1)}, bf16[4,17,128,128]{3,2,1,0:T(8,128)(2,1)S(1)}, bf16[4,17,128,128]{3,2,1,0:T(8,128)(2,1)S(1)}, bf16[4,17,128,128]{3,2,1,0:T(8,128)(2,1)S(1)}) custom-call(s32[1]{0:T(128)} %bitcast.pos_ref, bf16[64,2048]{1,0:T(8,128)(2,1)S(1)} %copy-done.4), custom_call_target="tpu_custom_call" | custom-call | flops 1 | bytes 1 | tf_op jit(solution)/shard_map/blocks/pallas_call | solution.py:362
  14.5 0.0 collective-permute-done.1.refs_6_.refs_2_
  14.5 0.1 collective-permute-start.11
  14.6 3.2 %collective-permute-done.2.refs_7_.refs_3_ = bf16[16,2,2,16,128]{4,3,2,1,0:T(8,128)(2,1)S(1)} collective-permute-done((bf16[16,2,2,16,128]{4,3,2,1,0:T(8,128)(2,1)S(1)}, bf16[16,2,2,16,128]{4,3,2,1,0:T(8,128)(2,1)S(1)}, u32[]{:S(2)}, u32[]{:S(2)}) %collective-permute-start.2) | collective-permute-done | bytes 262176 | tf_op jit(solution)/shard_map/ppermute | solution.py:350
  17.8 4.1 %conv.1 = (bf16[16,2,2,16,128]{4,3,2,1,0:T(8,128)(2,1)S(1)}, bf16[16,2,2,16,128]{4,3,2,1,0:T(8,128)(2,1)}, bf16[16,2,2,16,128]{4,3,2,1,0:T(8,128)(2,1)}, bf16[16,2,2,16,128]{4,3,2,1,0:T(8,128)(2,1)}) custom-call(s32[1]{0:T(128)} %bitcast.pos_ref, bf16[4,17,128,128]{3,2,1,0:T(8,128)(2,1)S(1)} %get-tuple-element.45.refs_0_, ...), custom_call_target="tpu_custom_call" | custom-call | flops 17179869184 | bytes 2359296 | tf_op jit(solution)/shard_map/conv/pallas_call | solution.py:374
  21.9 0.3 collective-permute-start.6
  22.2 2.1 %collective-permute-start.7 = (bf16[8,2,2,16,128]{4,3,2,1,0:T(8,128)(2,1)S(1)}, bf16[8,2,2,16,128]{4,3,2,1,0:T(8,128)(2,1)S(1)}, u32[]{:S(2)}, u32[]{:S(2)}) collective-permute-start(bf16[8,2,2,16,128]{4,3,2,1,0:T(8,128)(2,1)S(1)} %get-tuple-element.63), channel_id=1, source_target_pairs={{0,16},{8,24},{16,0},{24,8},{1,17},{9,25},{17,1},{25,9},{2,18},{10... | collective-permute-start | bytes 393224 | tf_op jit(solution)/shard_map/ppermute | solution.py:341
  24.2 0.0 collective-permute-done.9.refs_5_
  24.2 0.0 collective-permute-start.8
  24.2 0.0 collective-permute-done.10.refs_6_
  24.2 0.1 collective-permute-start.3
  24.4 2.0 %collective-permute-start.4 = (bf16[16,2,2,16,128]{4,3,2,1,0:T(8,128)(2,1)}, bf16[16,2,2,16,128]{4,3,2,1,0:T(8,128)(2,1)S(1)}, u32[]{:S(2)}, u32[]{:S(2)}) collective-permute-start(bf16[16,2,2,16,128]{4,3,2,1,0:T(8,128)(2,1)} %get-tuple-element.57), channel_id=1, source_target_pairs={{0,16},{8,24},{16,0},{24,8},{1,17},{9,25},{17,1},{25,9},{2,18},{10... | collective-permute-start | bytes 786440 | tf_op jit(solution)/shard_map/ppermute | solution.py:341
  26.4 2.7 %lags.2 = (f32[16,4,128]{2,1,0:T(4,128)S(1)}, f32[16,4,128]{2,1,0:T(4,128)S(1)}, f32[16,4,128]{2,1,0:T(4,128)S(1)}, f32[16,4,128]{2,1,0:T(4,128)S(1)}, f32[4,128]{1,0:T(4,128)S(1)}) custom-call(s32[1]{0:T(128)} %bitcast.pos_ref, bf16[16,2,2,16,128]{4,3,2,1,0:T(8,128)(2,1)S(1)} %get-tuple-element.50.refs_4_.refs_0_, ...), custom_call_target="tpu_custom_call" | custom-call | flops 8589934592 | bytes 2097152 | tf_op jit(solution)/shard_map/lags/pallas_call | solution.py:396
  29.1 0.1 collective-permute-start.5
  29.1 1.8 %collective-permute-done.8.refs_7_ = bf16[8,2,2,16,128]{4,3,2,1,0:T(8,128)(2,1)S(1)} collective-permute-done((bf16[8,2,2,16,128]{4,3,2,1,0:T(8,128)(2,1)S(1)}, bf16[8,2,2,16,128]{4,3,2,1,0:T(8,128)(2,1)S(1)}, u32[]{:S(2)}, u32[]{:S(2)}) %collective-permute-start.8) | collective-permute-done | bytes 131104 | tf_op jit(solution)/shard_map/ppermute | solution.py:341
  30.9 3.3 %lags.3 = (f32[16,4,128]{2,1,0:T(4,128)S(1)}, f32[16,4,128]{2,1,0:T(4,128)S(1)}, f32[16,4,128]{2,1,0:T(4,128)S(1)}, f32[16,4,128]{2,1,0:T(4,128)S(1)}, f32[32,4,128]{2,1,0:T(4,128)}) custom-call(s32[1]{0:T(128)} %bitcast.pos_ref, ...), custom_call_target="tpu_custom_call", output_to_operand_aliasing={{0}: (9, {}), {1}: (10, {}), {2}: (11, {}), {3}: (12, {})} | custom-call | flops 8589934592 | bytes 2097152 | tf_op jit(solution)/shard_map/lags/pallas_call | solution.py:396
  34.2 6.2 %all-to-all-start = ((f32[32,4,128]{2,1,0:T(4,128)}), f32[32,4,128]{2,1,0:T(4,128)S(1)}, u32[]{:S(2)}, u32[]{:S(2)}) async-start(f32[32,4,128]{2,1,0:T(4,128)} %get-tuple-element.73), calls=%async_computation | async-start | bytes 131072 | tf_op jit(solution)/shard_map/all_to_all | solution.py:415
  40.5 0.3 collective-permute-start.12
  40.8 1.7 %collective-permute-start.13 = (f32[16,4,128]{2,1,0:T(4,128)S(1)}, f32[16,4,128]{2,1,0:T(4,128)S(1)}, u32[]{:S(2)}, u32[]{:S(2)}) collective-permute-start(f32[16,4,128]{2,1,0:T(4,128)S(1)} %get-tuple-element.76), channel_id=1, source_target_pairs={{0,16},{8,24},{16,0},{24,8},{1,17},{9,25},{17,1},{25,9},{2,18},{10... | collective-permute-start | bytes 98312 | tf_op jit(solution)/shard_map/ppermute | solution.py:341
  42.5 2.1 %ungate.1 = (bf16[1,512,1024]{2,1,0:T(8,128)(2,1)}, bf16[1,512,1024]{2,1,0:T(8,128)(2,1)}, f32[8,128]{1,0:T(8,128)S(1)}) custom-call(s32[1]{0:T(128)} %bitcast.pos_ref, bf16[1,512,1024]{2,1,0:T(8,128)(2,1)S(1)} %copy-done.2, bf16[1,512,1024]{2,1,0:T(8,128)(2,1)S(1)} %copy-done.3, bf16[16,2,2,16,128]{4,3,2,1,0:T(8,128)(2,1)S(1)} %get-tuple-element.55.refs_0_.refs_8_, ...), custom_call_target="tpu_custom_call" | custom-call | flops 1048576 | bytes 5242880 | tf_op jit(solution)/shard_map/ungate/pallas_call | solution.py:418
  44.6 0.1 collective-permute-done.13.refs_2_
  44.7 1.3 %collective-permute-done.14.refs_3_ = f32[16,4,128]{2,1,0:T(4,128)S(1)} collective-permute-done((f32[16,4,128]{2,1,0:T(4,128)S(1)}, f32[16,4,128]{2,1,0:T(4,128)S(1)}, u32[]{:S(2)}, u32[]{:S(2)}) %collective-permute-start.14) | collective-permute-done | bytes 32800 | tf_op jit(solution)/shard_map/ppermute | solution.py:341
  46.0 1.7 %all-to-all-done.total_ref = f32[32,4,128]{2,1,0:T(4,128)S(1)} async-done(((f32[32,4,128]{2,1,0:T(4,128)}), f32[32,4,128]{2,1,0:T(4,128)S(1)}, u32[]{:S(2)}, u32[]{:S(2)}) %all-to-all-start) | async-done | bytes 65568 | tf_op jit(solution)/shard_map/all_to_all | solution.py:415
  47.8 0.9 %clip.1 = f32[64,512]{1,0:T(8,128)} custom-call(s32[1]{0:T(128)} %bitcast.pos_ref, f32[32,4,128]{2,1,0:T(4,128)S(1)} %all-to-all-done.total_ref, f32[16,4,128]{2,1,0:T(4,128)S(1)} %get-tuple-element.74.refs_0_, f32[16,4,128]{2,1,0:T(4,128)S(1)} %collective-permute-done.12.refs_1_, f32[16,4,128]{2,1,0:T(4,128)S(1)} %collective-permute-done.13.refs_2_, ...), custom_call_target="tpu_custom_call" | custom-call | flops 131072 | bytes 524288 | tf_op jit(solution)/shard_map/clip/pallas_call | solution.py:437
  (19 shorter events, 0.0 us)
Async XLA Ops:
  0.6 7.7 %copy-start = (bf16[1,512,1024]{2,1,0:T(8,128)(2,1)S(1)}, bf16[1,512,1024]{2,1,0:T(8,128)(2,1)}, u32[]{:S(2)}) copy-start(bf16[1,512,1024]{2,1,0:T(8,128)(2,1)} %left_ref.5) | copy-start | bytes 3145732
  0.6 7.7 %copy-start.1 = (bf16[1,512,1024]{2,1,0:T(8,128)(2,1)S(1)}, bf16[1,512,1024]{2,1,0:T(8,128)(2,1)}, u32[]{:S(2)}) copy-start(bf16[1,512,1024]{2,1,0:T(8,128)(2,1)} %right_ref.5) | copy-start | bytes 3145732
  2.4 9.0 %copy-start.4 = (bf16[64,2048]{1,0:T(8,128)(2,1)S(1)}, bf16[64,2048]{1,0:T(8,128)(2,1)}, u32[]{:S(2)}) copy-start(bf16[64,2048]{1,0:T(8,128)(2,1)} %filt_ref.1) | copy-start | bytes 786436
  2.4 12.0 %collective-permute-start.1 = (bf16[16,2,2,16,128]{4,3,2,1,0:T(8,128)(2,1)S(1)}, bf16[16,2,2,16,128]{4,3,2,1,0:T(8,128)(2,1)S(1)}, u32[]{:S(2)}, u32[]{:S(2)}) collective-permute-start(bf16[16,2,2,16,128]{4,3,2,1,0:T(8,128)(2,1)S(1)} %get-tuple-element.52), channel_id=1, source_target_pairs={{0,16},{8,24},{16,0},{24,8},{1,17},{9,25},{17,1},{25,9},{2,18},{10... | collective-permute-start | bytes 786440 | tf_op jit(solution)/shard_map/ppermute | solution.py:350
  5.4 12.3 %collective-permute-start.2 = (bf16[16,2,2,16,128]{4,3,2,1,0:T(8,128)(2,1)S(1)}, bf16[16,2,2,16,128]{4,3,2,1,0:T(8,128)(2,1)S(1)}, u32[]{:S(2)}, u32[]{:S(2)}) collective-permute-start(bf16[16,2,2,16,128]{4,3,2,1,0:T(8,128)(2,1)S(1)} %get-tuple-element.53), channel_id=1, source_target_pairs={{0,24},{8,16},{16,8},{24,0},{1,25},{9,17},{17,9},{25,1},{2,26},{10... | collective-permute-start | bytes 786440 | tf_op jit(solution)/shard_map/ppermute | solution.py:350
  9.1 8.7 %collective-permute-start = (bf16[16,2,2,16,128]{4,3,2,1,0:T(8,128)(2,1)S(1)}, bf16[16,2,2,16,128]{4,3,2,1,0:T(8,128)(2,1)S(1)}, u32[]{:S(2)}, u32[]{:S(2)}) collective-permute-start(bf16[16,2,2,16,128]{4,3,2,1,0:T(8,128)(2,1)S(1)} %get-tuple-element.51), channel_id=1, source_target_pairs={{0,8},{8,0},{16,24},{24,16},{1,9},{9,1},{17,25},{25,17},{2,10},{10... | collective-permute-start | bytes 786440 | tf_op jit(solution)/shard_map/ppermute | solution.py:355
  9.4 14.8 %collective-permute-start.9 = (bf16[8,2,2,16,128]{4,3,2,1,0:T(8,128)(2,1)S(1)}, bf16[8,2,2,16,128]{4,3,2,1,0:T(8,128)(2,1)S(1)}, u32[]{:S(2)}, u32[]{:S(2)}) collective-permute-start(bf16[8,2,2,16,128]{4,3,2,1,0:T(8,128)(2,1)S(1)} %get-tuple-element.65), channel_id=1, source_target_pairs={{0,8},{8,0},{16,24},{24,16},{1,9},{9,1},{17,25},{25,17},{2,10},{10... | collective-permute-start | bytes 393224 | tf_op jit(solution)/shard_map/ppermute | solution.py:341
  9.7 14.5 %collective-permute-start.10 = (bf16[8,2,2,16,128]{4,3,2,1,0:T(8,128)(2,1)S(1)}, bf16[8,2,2,16,128]{4,3,2,1,0:T(8,128)(2,1)S(1)}, u32[]{:S(2)}, u32[]{:S(2)}) collective-permute-start(bf16[8,2,2,16,128]{4,3,2,1,0:T(8,128)(2,1)S(1)} %get-tuple-element.66), channel_id=1, source_target_pairs={{0,16},{8,24},{16,0},{24,8},{1,17},{9,25},{17,1},{25,9},{2,18},{10... | collective-permute-start | bytes 393224 | tf_op jit(solution)/shard_map/ppermute | solution.py:341
  14.5 9.9 %collective-permute-start.11 = (bf16[8,2,2,16,128]{4,3,2,1,0:T(8,128)(2,1)S(1)}, bf16[8,2,2,16,128]{4,3,2,1,0:T(8,128)(2,1)S(1)}, u32[]{:S(2)}, u32[]{:S(2)}) collective-permute-start(bf16[8,2,2,16,128]{4,3,2,1,0:T(8,128)(2,1)S(1)} %get-tuple-element.67), channel_id=1, source_target_pairs={{0,24},{8,16},{16,8},{24,0},{1,25},{9,17},{17,9},{25,1},{2,26},{10... | collective-permute-start | bytes 393224 | tf_op jit(solution)/shard_map/ppermute | solution.py:341
  21.9 7.2 %collective-permute-start.6 = (bf16[8,2,2,16,128]{4,3,2,1,0:T(8,128)(2,1)S(1)}, bf16[8,2,2,16,128]{4,3,2,1,0:T(8,128)(2,1)S(1)}, u32[]{:S(2)}, u32[]{:S(2)}) collective-permute-start(bf16[8,2,2,16,128]{4,3,2,1,0:T(8,128)(2,1)S(1)} %get-tuple-element.62), channel_id=1, source_target_pairs={{0,8},{8,0},{16,24},{24,16},{1,9},{9,1},{17,25},{25,17},{2,10},{10... | collective-permute-start | bytes 393224 | tf_op jit(solution)/shard_map/ppermute | solution.py:341
  22.2 7.0 %collective-permute-start.7 = (bf16[8,2,2,16,128]{4,3,2,1,0:T(8,128)(2,1)S(1)}, bf16[8,2,2,16,128]{4,3,2,1,0:T(8,128)(2,1)S(1)}, u32[]{:S(2)}, u32[]{:S(2)}) collective-permute-start(bf16[8,2,2,16,128]{4,3,2,1,0:T(8,128)(2,1)S(1)} %get-tuple-element.63), channel_id=1, source_target_pairs={{0,16},{8,24},{16,0},{24,8},{1,17},{9,25},{17,1},{25,9},{2,18},{10... | collective-permute-start | bytes 393224 | tf_op jit(solution)/shard_map/ppermute | solution.py:341
  24.2 6.7 %collective-permute-start.8 = (bf16[8,2,2,16,128]{4,3,2,1,0:T(8,128)(2,1)S(1)}, bf16[8,2,2,16,128]{4,3,2,1,0:T(8,128)(2,1)S(1)}, u32[]{:S(2)}, u32[]{:S(2)}) collective-permute-start(bf16[8,2,2,16,128]{4,3,2,1,0:T(8,128)(2,1)S(1)} %get-tuple-element.64), channel_id=1, source_target_pairs={{0,24},{8,16},{16,8},{24,0},{1,25},{9,17},{17,9},{25,1},{2,26},{10... | collective-permute-start | bytes 393224 | tf_op jit(solution)/shard_map/ppermute | solution.py:341
  24.2 18.3 %collective-permute-start.3 = (bf16[16,2,2,16,128]{4,3,2,1,0:T(8,128)(2,1)}, bf16[16,2,2,16,128]{4,3,2,1,0:T(8,128)(2,1)S(1)}, u32[]{:S(2)}, u32[]{:S(2)}) collective-permute-start(bf16[16,2,2,16,128]{4,3,2,1,0:T(8,128)(2,1)} %get-tuple-element.56), channel_id=1, source_target_pairs={{0,8},{8,0},{16,24},{24,16},{1,9},{9,1},{17,25},{25,17},{2,10},{10... | collective-permute-start | bytes 786440 | tf_op jit(solution)/shard_map/ppermute | solution.py:341
  24.4 18.1 %collective-permute-start.4 = (bf16[16,2,2,16,128]{4,3,2,1,0:T(8,128)(2,1)}, bf16[16,2,2,16,128]{4,3,2,1,0:T(8,128)(2,1)S(1)}, u32[]{:S(2)}, u32[]{:S(2)}) collective-permute-start(bf16[16,2,2,16,128]{4,3,2,1,0:T(8,128)(2,1)} %get-tuple-element.57), channel_id=1, source_target_pairs={{0,16},{8,24},{16,0},{24,8},{1,17},{9,25},{17,1},{25,9},{2,18},{10... | collective-permute-start | bytes 786440 | tf_op jit(solution)/shard_map/ppermute | solution.py:341
  29.1 13.4 %collective-permute-start.5 = (bf16[16,2,2,16,128]{4,3,2,1,0:T(8,128)(2,1)}, bf16[16,2,2,16,128]{4,3,2,1,0:T(8,128)(2,1)S(1)}, u32[]{:S(2)}, u32[]{:S(2)}) collective-permute-start(bf16[16,2,2,16,128]{4,3,2,1,0:T(8,128)(2,1)} %get-tuple-element.58), channel_id=1, source_target_pairs={{0,24},{8,16},{16,8},{24,0},{1,25},{9,17},{17,9},{25,1},{2,26},{10... | collective-permute-start | bytes 786440 | tf_op jit(solution)/shard_map/ppermute | solution.py:341
  30.9 11.6 %copy-start.2 = (bf16[1,512,1024]{2,1,0:T(8,128)(2,1)S(1)}, bf16[1,512,1024]{2,1,0:T(8,128)(2,1)}, u32[]{:S(2)}) copy-start(bf16[1,512,1024]{2,1,0:T(8,128)(2,1)} %q_ref.1) | copy-start | bytes 3145732
  30.9 11.6 %copy-start.3 = (bf16[1,512,1024]{2,1,0:T(8,128)(2,1)S(1)}, bf16[1,512,1024]{2,1,0:T(8,128)(2,1)}, u32[]{:S(2)}) copy-start(bf16[1,512,1024]{2,1,0:T(8,128)(2,1)} %k_ref.1) | copy-start | bytes 3145732
  34.2 13.5 %all-to-all-start = ((f32[32,4,128]{2,1,0:T(4,128)}), f32[32,4,128]{2,1,0:T(4,128)S(1)}, u32[]{:S(2)}, u32[]{:S(2)}) async-start(f32[32,4,128]{2,1,0:T(4,128)} %get-tuple-element.73), calls=%async_computation | async-start | bytes 131072 | tf_op jit(solution)/shard_map/all_to_all | solution.py:415
  40.5 4.1 %collective-permute-start.12 = (f32[16,4,128]{2,1,0:T(4,128)S(1)}, f32[16,4,128]{2,1,0:T(4,128)S(1)}, u32[]{:S(2)}, u32[]{:S(2)}) collective-permute-start(f32[16,4,128]{2,1,0:T(4,128)S(1)} %get-tuple-element.75), channel_id=1, source_target_pairs={{0,8},{8,0},{16,24},{24,16},{1,9},{9,1},{17,25},{25,17},{2,10},{10... | collective-permute-start | bytes 98312 | tf_op jit(solution)/shard_map/ppermute | solution.py:341
  40.8 3.9 %collective-permute-start.13 = (f32[16,4,128]{2,1,0:T(4,128)S(1)}, f32[16,4,128]{2,1,0:T(4,128)S(1)}, u32[]{:S(2)}, u32[]{:S(2)}) collective-permute-start(f32[16,4,128]{2,1,0:T(4,128)S(1)} %get-tuple-element.76), channel_id=1, source_target_pairs={{0,16},{8,24},{16,0},{24,8},{1,17},{9,25},{17,1},{25,9},{2,18},{10... | collective-permute-start | bytes 98312 | tf_op jit(solution)/shard_map/ppermute | solution.py:341
  42.5 3.5 %collective-permute-start.14 = (f32[16,4,128]{2,1,0:T(4,128)S(1)}, f32[16,4,128]{2,1,0:T(4,128)S(1)}, u32[]{:S(2)}, u32[]{:S(2)}) collective-permute-start(f32[16,4,128]{2,1,0:T(4,128)S(1)} %get-tuple-element.77), channel_id=1, source_target_pairs={{0,24},{8,16},{16,8},{24,0},{1,25},{9,17},{17,9},{25,1},{2,26},{10... | collective-permute-start | bytes 98312 | tf_op jit(solution)/shard_map/ppermute | solution.py:341

commit v15 on v12

--- a/solution.py
+++ b/solution.py
@@ -391,7 +391,7 @@
     old = [conv[0]]
     for n, each in enumerate(sizes):
         last = n == len(sizes) - 1
-        unroll = math.gcd(8, each)
+        unroll = math.gcd(4, each)
         sums = jax.ShapeDtypeStruct((count, 4, LANES) if last else (blocks // owners, LANES), F32)
         old = pl.pallas_call(
             functools.partial(

time: 47 us -> 47.3 us (level)
  Pallas kernels: 21.5 us -> 22.1 us
    pallas_call x2, Pallas kernels: 6.02 us -> 6.61 us  [on_device(): pl.pallas_call(functools.partial(lag_kernel, owners=owners, unroll=unroll...]
  transfers between devices with their start and end apart: 16 -> 16, of which waited for: 5 -> 5; matrix products, arithmetic and copies ran while one was open for 0% -> 0% of each run, Pallas kernels for 40% -> 41%
where the time goes in v15:
time: 47.3 us; the launch traced here: 47.1 us
  Pallas kernels  22.1 us (47%)
  starting transfers between devices  17.9 us (38%)
  waiting for transfers between devices  6.2 us (13%)
  between operations  0.78 us (2%)
    ppermute x12, starting transfers between devices, swap(): lax.ppermute(values[k], 'ctx', [(i, i ^ k) for i in range(owners)])  8.41 us
    pallas_call x2, Pallas kernels, on_device(): pl.pallas_call(functools.partial(lag_kernel, owners=owners, unroll=unroll...  6.61 us
    all_to_all x1, starting transfers between devices, on_device(): total = lax.all_to_all(spread, both, 0, 0, tiled=True)  6.24 us
    pallas_call x3, Pallas kernels, gate(): pl.pallas_call(functools.partial(gate_kernel, reverse=reverse, sizes=size...  5.37 us
    pallas_call x1, Pallas kernels, on_device(): pl.pallas_call(functools.partial(conv_kernel, owners=owners, unroll=unrol...  4.12 us
    pallas_call x1, Pallas kernels, on_device(): pl.pallas_call(blocks_kernel, in_specs=[smem, vmem], out_specs=[vmem] * u...  3.04 us
    ppermute x2, starting transfers between devices, on_device(): lax.ppermute(v, 'ctx', [(i, i ^ k) for i in range(4)])  3.03 us
    ppermute x2, waiting for transfers between devices, on_device(): lax.ppermute(v, 'ctx', [(i, i ^ k) for i in range(4)])  2.81 us
  transfers between devices with their start and end apart: 16, of which 5 were waited for; matrix products, arithmetic and copies ran while one was open for 0% of the time, Pallas kernels for 41%

profile of v15, /device:TPU:0, one launch (start us, length us, event | category | flops | bytes accessed | tf_op | source)
XLA Modules:
  0.0 47.1 jit_solution(11500239345858442911)
XLA Ops:
  0.7 1.7 %gate_far.1 = (bf16[16,2,2,16,128]{4,3,2,1,0:T(8,128)(2,1)S(1)}, bf16[16,2,2,16,128]{4,3,2,1,0:T(8,128)(2,1)S(1)}) custom-call(s32[1]{0:T(128)} %bitcast.pos_ref, bf16[1,512,1024]{2,1,0:T(8,128)(2,1)} %left_ref.5, bf16[1,512,1024]{2,1,0:T(8,128)(2,1)} %right_ref.5), custom_call_target="tpu_custom_call" | custom-call | flops 262144 | bytes 1572864 | tf_op jit(solution)/shard_map/gate_far/pallas_call | solution.py:313
  2.4 0.0 copy-start.4
  2.4 3.0 %collective-permute-start.1 = (bf16[16,2,2,16,128]{4,3,2,1,0:T(8,128)(2,1)S(1)}, bf16[16,2,2,16,128]{4,3,2,1,0:T(8,128)(2,1)S(1)}, u32[]{:S(2)}, u32[]{:S(2)}) collective-permute-start(bf16[16,2,2,16,128]{4,3,2,1,0:T(8,128)(2,1)S(1)} %get-tuple-element.48), channel_id=1, source_target_pairs={{0,16},{8,24},{16,0},{24,8},{1,17},{9,25},{17,1},{25,9},{2,18},{10... | collective-permute-start | bytes 786440 | tf_op jit(solution)/shard_map/ppermute | solution.py:350
  5.4 2.9 %gate_prod.1 = (bf16[8,2,2,16,128]{4,3,2,1,0:T(8,128)(2,1)S(1)}, bf16[8,2,2,16,128]{4,3,2,1,0:T(8,128)(2,1)S(1)}, bf16[8,2,2,16,128]{4,3,2,1,0:T(8,128)(2,1)S(1)...) custom-call(s32[1]{0:T(128)} %bitcast.pos_ref, ...), custom_call_target="tpu_custom_call" | custom-call | flops 524288 | bytes 3145728 | tf_op jit(solution)/shard_map/gate_prod/pallas_call | solution.py:313
  8.3 0.8 %gate_near.1 = (bf16[16,2,2,16,128]{4,3,2,1,0:T(8,128)(2,1)S(1)}, bf16[16,2,2,16,128]{4,3,2,1,0:T(8,128)(2,1)S(1)}) custom-call(s32[1]{0:T(128)} %bitcast.pos_ref, bf16[1,512,1024]{2,1,0:T(8,128)(2,1)S(1)} %copy-done, bf16[1,512,1024]{2,1,0:T(8,128)(2,1)S(1)} %copy-done.1, bf16[8,2,2,16,128]{4,3,2,1,0:T(8,128)(2,1)S(1)} %get-tuple-element.45.refs_0_.refs_4_), custom_call_target="tpu_custom_call" | custom-call | flops 262144 | bytes 1572864 | tf_op jit(solution)/shard_map/gate_near/pallas_call | solution.py:313
  9.1 0.3 collective-permute-start
  9.4 0.3 collective-permute-start.6
  9.7 1.7 %collective-permute-start.10 = (bf16[8,2,2,16,128]{4,3,2,1,0:T(8,128)(2,1)S(1)}, bf16[8,2,2,16,128]{4,3,2,1,0:T(8,128)(2,1)S(1)}, u32[]{:S(2)}, u32[]{:S(2)}) collective-permute-start(bf16[8,2,2,16,128]{4,3,2,1,0:T(8,128)(2,1)S(1)} %get-tuple-element.66), channel_id=1, source_target_pairs={{0,16},{8,24},{16,0},{24,8},{1,17},{9,25},{17,1},{25,9},{2,18},{10... | collective-permute-start | bytes 393224 | tf_op jit(solution)/shard_map/ppermute | solution.py:341
  11.4 3.0 %blocks.1 = (bf16[4,17,128,128]{3,2,1,0:T(8,128)(2,1)S(1)}, bf16[4,17,128,128]{3,2,1,0:T(8,128)(2,1)S(1)}, bf16[4,17,128,128]{3,2,1,0:T(8,128)(2,1)S(1)}, bf16[4,17,128,128]{3,2,1,0:T(8,128)(2,1)S(1)}) custom-call(s32[1]{0:T(128)} %bitcast.pos_ref, bf16[64,2048]{1,0:T(8,128)(2,1)S(1)} %copy-done.4), custom_call_target="tpu_custom_call" | custom-call | flops 1 | bytes 1 | tf_op jit(solution)/shard_map/blocks/pallas_call | solution.py:366
  14.5 0.0 collective-permute-done.6.refs_5_
  14.5 0.1 collective-permute-start.11
  14.6 0.0 collective-permute-done.1.refs_6_.refs_2_
  14.6 0.4 collective-permute-start.7
  15.0 2.8 %collective-permute-done.2.refs_7_.refs_3_ = bf16[16,2,2,16,128]{4,3,2,1,0:T(8,128)(2,1)S(1)} collective-permute-done((bf16[16,2,2,16,128]{4,3,2,1,0:T(8,128)(2,1)S(1)}, bf16[16,2,2,16,128]{4,3,2,1,0:T(8,128)(2,1)S(1)}, u32[]{:S(2)}, u32[]{:S(2)}) %collective-permute-start.2) | collective-permute-done | bytes 262176 | tf_op jit(solution)/shard_map/ppermute | solution.py:350
  17.8 0.2 collective-permute-start.8
  18.0 1.8 %collective-permute-start.9 = (bf16[8,2,2,16,128]{4,3,2,1,0:T(8,128)(2,1)S(1)}, bf16[8,2,2,16,128]{4,3,2,1,0:T(8,128)(2,1)S(1)}, u32[]{:S(2)}, u32[]{:S(2)}) collective-permute-start(bf16[8,2,2,16,128]{4,3,2,1,0:T(8,128)(2,1)S(1)} %get-tuple-element.64), channel_id=1, source_target_pairs={{0,24},{8,16},{16,8},{24,0},{1,25},{9,17},{17,9},{25,1},{2,26},{10... | collective-permute-start | bytes 393224 | tf_op jit(solution)/shard_map/ppermute | solution.py:341
  19.7 4.1 %conv.1 = (bf16[16,2,2,16,128]{4,3,2,1,0:T(8,128)(2,1)S(1)}, bf16[16,2,2,16,128]{4,3,2,1,0:T(8,128)(2,1)}, bf16[16,2,2,16,128]{4,3,2,1,0:T(8,128)(2,1)}, bf16[16,2,2,16,128]{4,3,2,1,0:T(8,128)(2,1)}) custom-call(s32[1]{0:T(128)} %bitcast.pos_ref, bf16[4,17,128,128]{3,2,1,0:T(8,128)(2,1)S(1)} %get-tuple-element.41.refs_0_, ...), custom_call_target="tpu_custom_call" | custom-call | flops 17179869184 | bytes 2359296 | tf_op jit(solution)/shard_map/conv/pallas_call | solution.py:378
  23.8 0.0 collective-permute-done.10.refs_6_
  23.8 0.2 collective-permute-start.3
  24.1 1.6 %collective-permute-start.4 = (bf16[16,2,2,16,128]{4,3,2,1,0:T(8,128)(2,1)}, bf16[16,2,2,16,128]{4,3,2,1,0:T(8,128)(2,1)S(1)}, u32[]{:S(2)}, u32[]{:S(2)}) collective-permute-start(bf16[16,2,2,16,128]{4,3,2,1,0:T(8,128)(2,1)} %get-tuple-element.52), channel_id=1, source_target_pairs={{0,16},{8,24},{16,0},{24,8},{1,17},{9,25},{17,1},{25,9},{2,18},{10... | collective-permute-start | bytes 786440 | tf_op jit(solution)/shard_map/ppermute | solution.py:341
  25.7 3.0 %lags.2 = (f32[16,4,128]{2,1,0:T(4,128)S(1)}, f32[16,4,128]{2,1,0:T(4,128)S(1)}, f32[16,4,128]{2,1,0:T(4,128)S(1)}, f32[16,4,128]{2,1,0:T(4,128)S(1)}, f32[4,128]{1,0:T(4,128)S(1)}) custom-call(s32[1]{0:T(128)} %bitcast.pos_ref, bf16[16,2,2,16,128]{4,3,2,1,0:T(8,128)(2,1)S(1)} %get-tuple-element.46.refs_4_.refs_0_, ...), custom_call_target="tpu_custom_call" | custom-call | flops 8589934592 | bytes 2097152 | tf_op jit(solution)/shard_map/lags/pallas_call | solution.py:396
  28.7 0.1 collective-permute-start.5
  28.8 0.2 collective-permute-done.9.refs_7_
  29.0 3.6 %lags.3 = (f32[16,4,128]{2,1,0:T(4,128)S(1)}, f32[16,4,128]{2,1,0:T(4,128)S(1)}, f32[16,4,128]{2,1,0:T(4,128)S(1)}, f32[16,4,128]{2,1,0:T(4,128)S(1)}, f32[32,4,128]{2,1,0:T(4,128)}) custom-call(s32[1]{0:T(128)} %bitcast.pos_ref, ...), custom_call_target="tpu_custom_call", output_to_operand_aliasing={{0}: (9, {}), {1}: (10, {}), {2}: (11, {}), {3}: (12, {})} | custom-call | flops 8589934592 | bytes 2097152 | tf_op jit(solution)/shard_map/lags/pallas_call | solution.py:396
  32.6 6.2 %all-to-all-start = ((f32[32,4,128]{2,1,0:T(4,128)}), f32[32,4,128]{2,1,0:T(4,128)S(1)}, u32[]{:S(2)}, u32[]{:S(2)}) async-start(f32[32,4,128]{2,1,0:T(4,128)} %get-tuple-element.73), calls=%async_computation | async-start | bytes 131072 | tf_op jit(solution)/shard_map/all_to_all | solution.py:415
  38.9 0.3 collective-permute-start.12
  39.2 1.7 %collective-permute-start.13 = (f32[16,4,128]{2,1,0:T(4,128)S(1)}, f32[16,4,128]{2,1,0:T(4,128)S(1)}, u32[]{:S(2)}, u32[]{:S(2)}) collective-permute-start(f32[16,4,128]{2,1,0:T(4,128)S(1)} %get-tuple-element.76), channel_id=1, source_target_pairs={{0,16},{8,24},{16,0},{24,8},{1,17},{9,25},{17,1},{25,9},{2,18},{10... | collective-permute-start | bytes 98312 | tf_op jit(solution)/shard_map/ppermute | solution.py:341
  40.9 2.1 %ungate.1 = (bf16[1,512,1024]{2,1,0:T(8,128)(2,1)}, bf16[1,512,1024]{2,1,0:T(8,128)(2,1)}, f32[8,128]{1,0:T(8,128)S(1)}) custom-call(s32[1]{0:T(128)} %bitcast.pos_ref, bf16[1,512,1024]{2,1,0:T(8,128)(2,1)S(1)} %copy-done.2, bf16[1,512,1024]{2,1,0:T(8,128)(2,1)S(1)} %copy-done.3, bf16[16,2,2,16,128]{4,3,2,1,0:T(8,128)(2,1)S(1)} %get-tuple-element.50.refs_0_.refs_8_, ...), custom_call_target="tpu_custom_call" | custom-call | flops 1048576 | bytes 5242880 | tf_op jit(solution)/shard_map/ungate/pallas_call | solution.py:418
  43.0 0.1 collective-permute-done.13.refs_2_
  43.1 1.3 %collective-permute-done.14.refs_3_ = f32[16,4,128]{2,1,0:T(4,128)S(1)} collective-permute-done((f32[16,4,128]{2,1,0:T(4,128)S(1)}, f32[16,4,128]{2,1,0:T(4,128)S(1)}, u32[]{:S(2)}, u32[]{:S(2)}) %collective-permute-start.14) | collective-permute-done | bytes 32800 | tf_op jit(solution)/shard_map/ppermute | solution.py:341
  44.4 1.7 %all-to-all-done.total_ref = f32[32,4,128]{2,1,0:T(4,128)S(1)} async-done(((f32[32,4,128]{2,1,0:T(4,128)}), f32[32,4,128]{2,1,0:T(4,128)S(1)}, u32[]{:S(2)}, u32[]{:S(2)}) %all-to-all-start) | async-done | bytes 65568 | tf_op jit(solution)/shard_map/all_to_all | solution.py:415
  46.2 0.9 %clip.1 = f32[64,512]{1,0:T(8,128)} custom-call(s32[1]{0:T(128)} %bitcast.pos_ref, f32[32,4,128]{2,1,0:T(4,128)S(1)} %all-to-all-done.total_ref, f32[16,4,128]{2,1,0:T(4,128)S(1)} %get-tuple-element.74.refs_0_, f32[16,4,128]{2,1,0:T(4,128)S(1)} %collective-permute-done.12.refs_1_, f32[16,4,128]{2,1,0:T(4,128)S(1)} %collective-permute-done.13.refs_2_, ...), custom_call_target="tpu_custom_call" | custom-call | flops 131072 | bytes 524288 | tf_op jit(solution)/shard_map/clip/pallas_call | solution.py:437
  (19 shorter events, 0.0 us)
Async XLA Ops:
  0.6 7.7 %copy-start = (bf16[1,512,1024]{2,1,0:T(8,128)(2,1)S(1)}, bf16[1,512,1024]{2,1,0:T(8,128)(2,1)}, u32[]{:S(2)}) copy-start(bf16[1,512,1024]{2,1,0:T(8,128)(2,1)} %left_ref.5) | copy-start | bytes 3145732
  0.6 7.7 %copy-start.1 = (bf16[1,512,1024]{2,1,0:T(8,128)(2,1)S(1)}, bf16[1,512,1024]{2,1,0:T(8,128)(2,1)}, u32[]{:S(2)}) copy-start(bf16[1,512,1024]{2,1,0:T(8,128)(2,1)} %right_ref.5) | copy-start | bytes 3145732
  2.4 9.0 %copy-start.4 = (bf16[64,2048]{1,0:T(8,128)(2,1)S(1)}, bf16[64,2048]{1,0:T(8,128)(2,1)}, u32[]{:S(2)}) copy-start(bf16[64,2048]{1,0:T(8,128)(2,1)} %filt_ref.1) | copy-start | bytes 786436
  2.4 12.2 %collective-permute-start.1 = (bf16[16,2,2,16,128]{4,3,2,1,0:T(8,128)(2,1)S(1)}, bf16[16,2,2,16,128]{4,3,2,1,0:T(8,128)(2,1)S(1)}, u32[]{:S(2)}, u32[]{:S(2)}) collective-permute-start(bf16[16,2,2,16,128]{4,3,2,1,0:T(8,128)(2,1)S(1)} %get-tuple-element.48), channel_id=1, source_target_pairs={{0,16},{8,24},{16,0},{24,8},{1,17},{9,25},{17,1},{25,9},{2,18},{10... | collective-permute-start | bytes 786440 | tf_op jit(solution)/shard_map/ppermute | solution.py:350
  5.4 12.3 %collective-permute-start.2 = (bf16[16,2,2,16,128]{4,3,2,1,0:T(8,128)(2,1)S(1)}, bf16[16,2,2,16,128]{4,3,2,1,0:T(8,128)(2,1)S(1)}, u32[]{:S(2)}, u32[]{:S(2)}) collective-permute-start(bf16[16,2,2,16,128]{4,3,2,1,0:T(8,128)(2,1)S(1)} %get-tuple-element.49), channel_id=1, source_target_pairs={{0,24},{8,16},{16,8},{24,0},{1,25},{9,17},{17,9},{25,1},{2,26},{10... | collective-permute-start | bytes 786440 | tf_op jit(solution)/shard_map/ppermute | solution.py:350
  9.1 8.8 %collective-permute-start = (bf16[16,2,2,16,128]{4,3,2,1,0:T(8,128)(2,1)S(1)}, bf16[16,2,2,16,128]{4,3,2,1,0:T(8,128)(2,1)S(1)}, u32[]{:S(2)}, u32[]{:S(2)}) collective-permute-start(bf16[16,2,2,16,128]{4,3,2,1,0:T(8,128)(2,1)S(1)} %get-tuple-element.47), channel_id=1, source_target_pairs={{0,8},{8,0},{16,24},{24,16},{1,9},{9,1},{17,25},{25,17},{2,10},{10... | collective-permute-start | bytes 786440 | tf_op jit(solution)/shard_map/ppermute | solution.py:355
  9.4 5.1 %collective-permute-start.6 = (bf16[8,2,2,16,128]{4,3,2,1,0:T(8,128)(2,1)S(1)}, bf16[8,2,2,16,128]{4,3,2,1,0:T(8,128)(2,1)S(1)}, u32[]{:S(2)}, u32[]{:S(2)}) collective-permute-start(bf16[8,2,2,16,128]{4,3,2,1,0:T(8,128)(2,1)S(1)} %get-tuple-element.60), channel_id=1, source_target_pairs={{0,8},{8,0},{16,24},{24,16},{1,9},{9,1},{17,25},{25,17},{2,10},{10... | collective-permute-start | bytes 393224 | tf_op jit(solution)/shard_map/ppermute | solution.py:341
  9.7 14.1 %collective-permute-start.10 = (bf16[8,2,2,16,128]{4,3,2,1,0:T(8,128)(2,1)S(1)}, bf16[8,2,2,16,128]{4,3,2,1,0:T(8,128)(2,1)S(1)}, u32[]{:S(2)}, u32[]{:S(2)}) collective-permute-start(bf16[8,2,2,16,128]{4,3,2,1,0:T(8,128)(2,1)S(1)} %get-tuple-element.66), channel_id=1, source_target_pairs={{0,16},{8,24},{16,0},{24,8},{1,17},{9,25},{17,1},{25,9},{2,18},{10... | collective-permute-start | bytes 393224 | tf_op jit(solution)/shard_map/ppermute | solution.py:341
  14.5 9.6 %collective-permute-start.11 = (bf16[8,2,2,16,128]{4,3,2,1,0:T(8,128)(2,1)S(1)}, bf16[8,2,2,16,128]{4,3,2,1,0:T(8,128)(2,1)S(1)}, u32[]{:S(2)}, u32[]{:S(2)}) collective-permute-start(bf16[8,2,2,16,128]{4,3,2,1,0:T(8,128)(2,1)S(1)} %get-tuple-element.67), channel_id=1, source_target_pairs={{0,24},{8,16},{16,8},{24,0},{1,25},{9,17},{17,9},{25,1},{2,26},{10... | collective-permute-start | bytes 393224 | tf_op jit(solution)/shard_map/ppermute | solution.py:341
  14.6 14.1 %collective-permute-start.7 = (bf16[8,2,2,16,128]{4,3,2,1,0:T(8,128)(2,1)S(1)}, bf16[8,2,2,16,128]{4,3,2,1,0:T(8,128)(2,1)S(1)}, u32[]{:S(2)}, u32[]{:S(2)}) collective-permute-start(bf16[8,2,2,16,128]{4,3,2,1,0:T(8,128)(2,1)S(1)} %get-tuple-element.62), channel_id=1, source_target_pairs={{0,8},{8,0},{16,24},{24,16},{1,9},{9,1},{17,25},{25,17},{2,10},{10... | collective-permute-start | bytes 393224 | tf_op jit(solution)/shard_map/ppermute | solution.py:341
  17.8 11.0 %collective-permute-start.8 = (bf16[8,2,2,16,128]{4,3,2,1,0:T(8,128)(2,1)S(1)}, bf16[8,2,2,16,128]{4,3,2,1,0:T(8,128)(2,1)S(1)}, u32[]{:S(2)}, u32[]{:S(2)}) collective-permute-start(bf16[8,2,2,16,128]{4,3,2,1,0:T(8,128)(2,1)S(1)} %get-tuple-element.63), channel_id=1, source_target_pairs={{0,16},{8,24},{16,0},{24,8},{1,17},{9,25},{17,1},{25,9},{2,18},{10... | collective-permute-start | bytes 393224 | tf_op jit(solution)/shard_map/ppermute | solution.py:341
  18.0 11.0 %collective-permute-start.9 = (bf16[8,2,2,16,128]{4,3,2,1,0:T(8,128)(2,1)S(1)}, bf16[8,2,2,16,128]{4,3,2,1,0:T(8,128)(2,1)S(1)}, u32[]{:S(2)}, u32[]{:S(2)}) collective-permute-start(bf16[8,2,2,16,128]{4,3,2,1,0:T(8,128)(2,1)S(1)} %get-tuple-element.64), channel_id=1, source_target_pairs={{0,24},{8,16},{16,8},{24,0},{1,25},{9,17},{17,9},{25,1},{2,26},{10... | collective-permute-start | bytes 393224 | tf_op jit(solution)/shard_map/ppermute | solution.py:341
  23.8 17.1 %collective-permute-start.3 = (bf16[16,2,2,16,128]{4,3,2,1,0:T(8,128)(2,1)}, bf16[16,2,2,16,128]{4,3,2,1,0:T(8,128)(2,1)S(1)}, u32[]{:S(2)}, u32[]{:S(2)}) collective-permute-start(bf16[16,2,2,16,128]{4,3,2,1,0:T(8,128)(2,1)} %get-tuple-element.51), channel_id=1, source_target_pairs={{0,8},{8,0},{16,24},{24,16},{1,9},{9,1},{17,25},{25,17},{2,10},{10... | collective-permute-start | bytes 786440 | tf_op jit(solution)/shard_map/ppermute | solution.py:341
  24.1 16.8 %collective-permute-start.4 = (bf16[16,2,2,16,128]{4,3,2,1,0:T(8,128)(2,1)}, bf16[16,2,2,16,128]{4,3,2,1,0:T(8,128)(2,1)S(1)}, u32[]{:S(2)}, u32[]{:S(2)}) collective-permute-start(bf16[16,2,2,16,128]{4,3,2,1,0:T(8,128)(2,1)} %get-tuple-element.52), channel_id=1, source_target_pairs={{0,16},{8,24},{16,0},{24,8},{1,17},{9,25},{17,1},{25,9},{2,18},{10... | collective-permute-start | bytes 786440 | tf_op jit(solution)/shard_map/ppermute | solution.py:341
  28.7 12.2 %collective-permute-start.5 = (bf16[16,2,2,16,128]{4,3,2,1,0:T(8,128)(2,1)}, bf16[16,2,2,16,128]{4,3,2,1,0:T(8,128)(2,1)S(1)}, u32[]{:S(2)}, u32[]{:S(2)}) collective-permute-start(bf16[16,2,2,16,128]{4,3,2,1,0:T(8,128)(2,1)} %get-tuple-element.53), channel_id=1, source_target_pairs={{0,24},{8,16},{16,8},{24,0},{1,25},{9,17},{17,9},{25,1},{2,26},{10... | collective-permute-start | bytes 786440 | tf_op jit(solution)/shard_map/ppermute | solution.py:341
  29.0 11.9 %copy-start.2 = (bf16[1,512,1024]{2,1,0:T(8,128)(2,1)S(1)}, bf16[1,512,1024]{2,1,0:T(8,128)(2,1)}, u32[]{:S(2)}) copy-start(bf16[1,512,1024]{2,1,0:T(8,128)(2,1)} %q_ref.1) | copy-start | bytes 3145732
  29.0 11.9 %copy-start.3 = (bf16[1,512,1024]{2,1,0:T(8,128)(2,1)S(1)}, bf16[1,512,1024]{2,1,0:T(8,128)(2,1)}, u32[]{:S(2)}) copy-start(bf16[1,512,1024]{2,1,0:T(8,128)(2,1)} %k_ref.1) | copy-start | bytes 3145732
  32.6 13.5 %all-to-all-start = ((f32[32,4,128]{2,1,0:T(4,128)}), f32[32,4,128]{2,1,0:T(4,128)S(1)}, u32[]{:S(2)}, u32[]{:S(2)}) async-start(f32[32,4,128]{2,1,0:T(4,128)} %get-tuple-element.73), calls=%async_computation | async-start | bytes 131072 | tf_op jit(solution)/shard_map/all_to_all | solution.py:415
  38.9 4.1 %collective-permute-start.12 = (f32[16,4,128]{2,1,0:T(4,128)S(1)}, f32[16,4,128]{2,1,0:T(4,128)S(1)}, u32[]{:S(2)}, u32[]{:S(2)}) collective-permute-start(f32[16,4,128]{2,1,0:T(4,128)S(1)} %get-tuple-element.75), channel_id=1, source_target_pairs={{0,8},{8,0},{16,24},{24,16},{1,9},{9,1},{17,25},{25,17},{2,10},{10... | collective-permute-start | bytes 98312 | tf_op jit(solution)/shard_map/ppermute | solution.py:341
  39.2 3.9 %collective-permute-start.13 = (f32[16,4,128]{2,1,0:T(4,128)S(1)}, f32[16,4,128]{2,1,0:T(4,128)S(1)}, u32[]{:S(2)}, u32[]{:S(2)}) collective-permute-start(f32[16,4,128]{2,1,0:T(4,128)S(1)} %get-tuple-element.76), channel_id=1, source_target_pairs={{0,16},{8,24},{16,0},{24,8},{1,17},{9,25},{17,1},{25,9},{2,18},{10... | collective-permute-start | bytes 98312 | tf_op jit(solution)/shard_map/ppermute | solution.py:341
  40.9 3.5 %collective-permute-start.14 = (f32[16,4,128]{2,1,0:T(4,128)S(1)}, f32[16,4,128]{2,1,0:T(4,128)S(1)}, u32[]{:S(2)}, u32[]{:S(2)}) collective-permute-start(f32[16,4,128]{2,1,0:T(4,128)S(1)} %get-tuple-element.77), channel_id=1, source_target_pairs={{0,24},{8,16},{16,8},{24,0},{1,25},{9,17},{17,9},{25,1},{2,26},{10... | collective-permute-start | bytes 98312 | tf_op jit(solution)/shard_map/ppermute | solution.py:341
